TPU v7x, 256 devices: a whole 4x4x8 slice. The times are simulated.
256 devices in a mesh: expert: 64 (over y, z_hi, x, core), tensor: 4 (over z_lo).
Axes of the slice: x: 4, y: 4, z: 8 (z_hi: 2, z_lo: 4; z = z_hi * 4 + z_lo), core: 2. Of those that a mesh axis runs over, the one named last changes fastest.
Arguments:
- tokens: bfloat16 [8192, 2048], P('expert'), may hold values from -6 to 6
- expert_ids: int32 [8192, 8], P('expert'), may hold values from 0 to 127, as said below
- gate_values: float32 [8192, 8], P('expert'), may hold values from 0.25 to 1
- hot_ids: int32 [4], replicated, may hold values from 0 to 127, as said below
- w_gate: bfloat16 [128, 768, 2048], P('expert', 'tensor'), may hold values from -0.125 to 0.125
- w_up: bfloat16 [128, 768, 2048], P('expert', 'tensor'), may hold values from -0.125 to 0.125
- w_down: bfloat16 [128, 768, 2048], P('expert', 'tensor'), may hold values from -0.21875 to 0.21875
Outputs:
- mixed: bfloat16 [8192, 2048], P('expert', 'tensor')
Inputs may be any that keep to these rules, and one draw needn't show every extreme that they name: `expert_ids`: rows are taken in micro-spans: micro-span c of a device is its rows c * 32 to (c + 1) * 32 - 1 within each aligned block of 128 rows. Each row names 8 different experts. Every row of micro-span c names hot_ids[c] once. In each micro-span of each device every other expert is named by at least 1 and at most 2 rows, and some by exactly 2. hot_ids[c] is the popular expert of micro-span c; the micro-spans' popular experts are different, and expert 128 - 1 is the popular one of some micro-span.
All inputs are finite; a program needn't handle non-finite values.
Results may differ from a plain program's by a relative error of at most 0.015.
Values may be sent and summed in bfloat16 or wider, within the bound.
No kernel may reach another device: no remote copies, remote signals or barrier semaphores. Data moves between devices by JAX's collectives and lax.ppermute only.
A program may use at most 128 MiB of HBM per device.

v0:
```python
import jax
import jax.numpy as jnp
from jax import lax
from jax.sharding import PartitionSpec as P

SPANS = 4


def broadcast(value, axis, source):
    kept = jnp.where(lax.axis_index(axis) == source, value, 0).astype(value.dtype)
    return lax.psum(kept, axis)


def expert_block(row_block, w_gate, w_up, w_down):
    gate_proj = jnp.einsum("necd,efd->necf", row_block, w_gate, preferred_element_type=jnp.float32)
    up_proj = jnp.einsum("necd,efd->necf", row_block, w_up, preferred_element_type=jnp.float32)
    hidden = (jax.nn.silu(gate_proj) * up_proj).astype(jnp.bfloat16)
    return jnp.einsum("necf,efd->necd", hidden, w_down, preferred_element_type=jnp.float32)


def fetch_hot(hot_ids, span_idx, w_gate, w_up, w_down):
    exp_dev = w_gate.shape[0]
    expert = hot_ids[span_idx]
    owner_dev = expert // exp_dev
    local_idx = expert % exp_dev
    pieces = (
        lax.dynamic_index_in_dim(w_gate, local_idx, 0, keepdims=False),
        lax.dynamic_index_in_dim(w_up, local_idx, 0, keepdims=False),
        lax.dynamic_index_in_dim(w_down, local_idx, 0, keepdims=False),
    )
    return (
        broadcast(pieces[0], "expert", owner_dev),
        broadcast(pieces[1], "expert", owner_dev),
        broadcast(pieces[2], "expert", owner_dev),
    )


def per_device(tokens, expert_ids, gate_values, hot_ids, w_gate, w_up, w_down):
    n_expert = lax.axis_size("expert")
    n_tensor = lax.axis_size("tensor")
    tok_dev, model_width = tokens.shape
    exp_dev = w_gate.shape[0]
    num_experts = exp_dev * n_expert
    top_k = expert_ids.shape[1]
    span_rows = tok_dev // SPANS
    capacity = (span_rows * (top_k - 1) + num_experts - 2) // (num_experts - 1)
    slice_width = model_width // n_tensor
    pair_count = span_rows * top_k
    expert_iota = jnp.arange(num_experts, dtype=jnp.int32)
    outputs = []
    for span_idx in range(SPANS):
        hot_gate, hot_up, hot_down = fetch_hot(hot_ids, span_idx, w_gate, w_up, w_down)
        start_row = span_idx * span_rows
        span_tok = tokens[start_row : start_row + span_rows]
        span_ids = expert_ids[start_row : start_row + span_rows]
        span_gates = gate_values[start_row : start_row + span_rows]
        hot_expert = hot_ids[span_idx]
        flat_ids = span_ids.reshape(pair_count)
        is_hot = flat_ids == hot_expert
        one_hot = (
            (flat_ids[:, None] == expert_iota[None, :]) & jnp.logical_not(is_hot)[:, None]
        ).astype(jnp.int32)
        rank_before = jnp.cumsum(one_hot, axis=0) - one_hot
        slot_pos = jnp.sum(rank_before * one_hot, axis=1)
        target = jnp.where(is_hot, num_experts * capacity, flat_ids * capacity + slot_pos)
        send_width = span_tok.shape[1]
        send_buf = jnp.zeros((num_experts * capacity, send_width), jnp.bfloat16)
        send_buf = send_buf.at[target].set(jnp.repeat(span_tok, top_k, axis=0), mode="drop")
        send_buf = send_buf.reshape(n_expert, exp_dev, capacity, send_width)
        received = lax.all_to_all(send_buf, "expert", split_axis=0, concat_axis=0, tiled=True)
        expert_part = expert_block(received, w_gate, w_up, w_down)
        hot_gproj = jnp.einsum("cd,fd->cf", span_tok, hot_gate, preferred_element_type=jnp.float32)
        hot_uproj = jnp.einsum("cd,fd->cf", span_tok, hot_up, preferred_element_type=jnp.float32)
        hot_hidden = (jax.nn.silu(hot_gproj) * hot_uproj).astype(jnp.bfloat16)
        hot_part = jnp.dot(hot_hidden, hot_down, preferred_element_type=jnp.float32)
        summed, hot_summed = (
            lax.psum_scatter(
                expert_part.astype(jnp.bfloat16), "tensor", scatter_dimension=3, tiled=True
            ).astype(jnp.float32),
            lax.psum_scatter(
                hot_part.astype(jnp.bfloat16), "tensor", scatter_dimension=1, tiled=True
            ).astype(jnp.float32),
        )
        returned = lax.all_to_all(
            summed.astype(jnp.bfloat16), "expert", split_axis=0, concat_axis=0, tiled=True
        )
        returned = returned.reshape(num_experts * capacity, slice_width)
        safe_target = jnp.where(is_hot, 0, target)
        pair_out = (
            jnp.take(returned, safe_target, axis=0)
            .astype(jnp.float32)
            .reshape(span_rows, top_k, slice_width)
        )
        weights_cold = jnp.where(is_hot, 0.0, span_gates.reshape(pair_count)).reshape(
            span_rows, top_k
        )
        hot_weight = jnp.sum(jnp.where(span_ids == hot_expert, span_gates, 0.0), axis=1)
        hot_rounded = lax.optimization_barrier(hot_summed.astype(jnp.bfloat16)).astype(jnp.float32)
        mixed_rows = (
            jnp.sum(pair_out * weights_cold[:, :, None], axis=1) + hot_weight[:, None] * hot_rounded
        )
        outputs.append(mixed_rows.astype(jnp.bfloat16))
    return jnp.concatenate(outputs, axis=0)


def solution(mesh):
    in_specs = (
        P("expert", None),
        P("expert", None),
        P("expert", None),
        P(),
        P("expert", "tensor", None),
        P("expert", "tensor", None),
        P("expert", "tensor", None),
    )
    out_specs = P("expert", "tensor")
    return jax.shard_map(
        per_device, mesh=mesh, in_specs=in_specs, out_specs=out_specs, check_vma=False
    )
```

profile of v0, /device:TPU:2, one launch (start us, length us, event | category | flops | bytes accessed | tf_op | source)
XLA Modules:
  0.0 1163.0 jit_solution(1350965413087568314)
XLA Ops:
  22.9 14.6 %all-to-all-start = ((bf16[64,2,2,2048]{3,2,1,0:T(2,128)(2,1)}), bf16[64,2,2,2048]{3,2,1,0:T(2,128)(2,1)S(1)}, u32[]{:S(2)}, u32[]{:S(2)}) async-start(bf16[64,2,2,2048]{3,2,1,0:T(2,128)(2,1)} %reshape.411), calls=%async_computation | async-start | bytes 2097152 | tf_op jit(solution)/shard_map/all_to_all | solution.py:70
  44.6 16.5 %all-to-all-done = bf16[64,2,2,2048]{3,2,1,0:T(2,128)(2,1)S(1)} async-done(((bf16[64,2,2,2048]{3,2,1,0:T(2,128)(2,1)}), bf16[64,2,2,2048]{3,2,1,0:T(2,128)(2,1)S(1)}, u32[]{:S(2)}, u32[]{:S(2)}) %all-to-all-start) | async-done | bytes 1048608 | tf_op jit(solution)/shard_map/all_to_all | solution.py:70
  62.2 6.6 all-to-all-start.2
  72.7 4.5 fusion
  93.2 13.0 %all-to-all-start.4 = ((bf16[64,2,2,2048]{3,2,1,0:T(2,128)(2,1)}), bf16[64,2,2,2048]{3,2,1,0:T(2,128)(2,1)}, u32[]{:S(2)}, u32[]{:S(2)}) async-start(bf16[64,2,2,2048]{3,2,1,0:T(2,128)(2,1)} %reshape.423), calls=%async_computation.8 | async-start | bytes 2097152 | tf_op jit(solution)/shard_map/all_to_all | solution.py:70
  109.8 4.5 fusion.1
  120.0 26.7 %all-to-all-done.4 = bf16[64,2,2,2048]{3,2,1,0:T(2,128)(2,1)} async-done(((bf16[64,2,2,2048]{3,2,1,0:T(2,128)(2,1)}), bf16[64,2,2,2048]{3,2,1,0:T(2,128)(2,1)}, u32[]{:S(2)}, u32[]{:S(2)}) %all-to-all-start.4) | async-done | bytes 1048608 | tf_op jit(solution)/shard_map/all_to_all | solution.py:70
  146.7 5.1 all-to-all-start.6
  155.2 4.5 fusion.2
  160.0 24.9 %all-to-all-done.6 = bf16[64,2,2,2048]{3,2,1,0:T(2,128)(2,1)} async-done(((bf16[64,2,2,2048]{3,2,1,0:T(2,128)(2,1)}), bf16[64,2,2,2048]{3,2,1,0:T(2,128)(2,1)}, u32[]{:S(2)}, u32[]{:S(2)}) %all-to-all-start.6) | async-done | bytes 1048608 | tf_op jit(solution)/shard_map/all_to_all | solution.py:70
  188.2 4.5 fusion.3
  209.9 5.9 all-to-all-start.1
  217.8 10.7 all-to-all-done.1
  228.5 5.6 all-to-all-start.3
  237.0 13.2 %all-to-all-done.3 = bf16[64,2,2,512]{3,2,1,0:T(2,128)(2,1)S(1)} async-done(((bf16[64,2,2,512]{3,2,1,0:T(2,128)(2,1)}), bf16[64,2,2,512]{3,2,1,0:T(2,128)(2,1)S(1)}, u32[]{:S(2)}, u32[]{:S(2)}) %all-to-all-start.3) | async-done | bytes 262176 | tf_op jit(solution)/shard_map/all_to_all | solution.py:84
  250.3 5.3 all-to-all-start.5
  258.8 10.1 all-to-all-done.5
  268.9 6.2 all-to-all-start.7
  280.0 8.3 all-to-all-done.7
  290.5 754.2 %all-reduce.3.cloned.1.call-done = (bf16[192,2048]{1,0:T(8,128)(2,1)}, bf16[192,2048]{1,0:T(8,128)(2,1)}, bf16[192,2048]{1,0:T(8,128)(2,1)}, bf16[192,2048]{1,0:...) async-done(((bf16[192,2048]{1,0:T(8,128)(2,1)}, ...) | async-done | bytes 9437200 | tf_op jit(solution)/shard_map/psum | solution.py:11
  1057.3 19.6 %reduce-scatter.11.cloned.1.call-done = bf16[32,512]{1,0:T(8,128)(2,1)} async-done(((bf16[32,2048]{1,0:T(8,128)(2,1)}), bf16[32,512]{1,0:T(8,128)(2,1)}) %reduce-scatter.11.cloned.1.call-update) | async-done | bytes 32784 | tf_op jit(solution)/shard_map/reduce_scatter | solution.py:80
  1077.7 24.7 %reduce-scatter.15.cloned.1.call-done = bf16[32,512]{1,0:T(8,128)(2,1)} async-done(((bf16[32,2048]{1,0:T(8,128)(2,1)}), bf16[32,512]{1,0:T(8,128)(2,1)}) %reduce-scatter.15.cloned.1.call-update) | async-done | bytes 32784 | tf_op jit(solution)/shard_map/reduce_scatter | solution.py:80
  1103.2 24.7 %reduce-scatter.19.cloned.1.call-done = bf16[32,512]{1,0:T(8,128)(2,1)} async-done(((bf16[32,2048]{1,0:T(8,128)(2,1)}), bf16[32,512]{1,0:T(8,128)(2,1)}) %reduce-scatter.19.cloned.1.call-update) | async-done | bytes 32784 | tf_op jit(solution)/shard_map/reduce_scatter | solution.py:80
  1128.8 24.8 %reduce-scatter.23.cloned.1.call-done = bf16[32,512]{1,0:T(8,128)(2,1)} async-done(((bf16[32,2048]{1,0:T(8,128)(2,1)}), bf16[32,512]{1,0:T(8,128)(2,1)}) %reduce-scatter.23.cloned.1.call-update) | async-done | bytes 32784 | tf_op jit(solution)/shard_map/reduce_scatter | solution.py:80
  (220 shorter events, 98.1 us)
Async XLA Ops:
  22.9 38.3 %all-to-all-start = ((bf16[64,2,2,2048]{3,2,1,0:T(2,128)(2,1)}), bf16[64,2,2,2048]{3,2,1,0:T(2,128)(2,1)S(1)}, u32[]{:S(2)}, u32[]{:S(2)}) async-start(bf16[64,2,2,2048]{3,2,1,0:T(2,128)(2,1)} %reshape.411), calls=%async_computation | async-start | bytes 2097152 | tf_op jit(solution)/shard_map/all_to_all | solution.py:70
  41.5 27.9 %copy-start = (bf16[2,192,2048]{2,1,0:T(8,128)(2,1)S(1)}, bf16[2,192,2048]{2,1,0:T(8,128)(2,1)}, u32[]{:S(2)}) copy-start(bf16[2,192,2048]{2,1,0:T(8,128)(2,1)} %param.13) | copy-start | bytes 4718596
  62.2 31.0 %all-to-all-start.2 = ((bf16[64,2,2,2048]{3,2,1,0:T(2,128)(2,1)}), bf16[64,2,2,2048]{3,2,1,0:T(2,128)(2,1)}, u32[]{:S(2)}, u32[]{:S(2)}) async-start(bf16[64,2,2,2048]{3,2,1,0:T(2,128)(2,1)} %reshape.417), calls=%async_computation.4 | async-start | bytes 2097152 | tf_op jit(solution)/shard_map/all_to_all | solution.py:70
  68.8 139.2 %reduce-scatter.9.cloned.1.call-start = ((), (), s32[]{:S(2)}) async-start(), calls=%async_computation.16 | async-start | bytes 1310720 | tf_op jit(solution)/shard_map/reduce_scatter | solution.py:77
  93.2 53.5 %all-to-all-start.4 = ((bf16[64,2,2,2048]{3,2,1,0:T(2,128)(2,1)}), bf16[64,2,2,2048]{3,2,1,0:T(2,128)(2,1)}, u32[]{:S(2)}, u32[]{:S(2)}) async-start(bf16[64,2,2,2048]{3,2,1,0:T(2,128)(2,1)} %reshape.423), calls=%async_computation.8 | async-start | bytes 2097152 | tf_op jit(solution)/shard_map/all_to_all | solution.py:70
  106.2 109.7 %reduce-scatter.13.cloned.1.call-start = ((), (), s32[]{:S(2)}) async-start(), calls=%async_computation.18 | async-start | bytes 1310720 | tf_op jit(solution)/shard_map/reduce_scatter | solution.py:77
  146.7 38.1 %all-to-all-start.6 = ((bf16[64,2,2,2048]{3,2,1,0:T(2,128)(2,1)}), bf16[64,2,2,2048]{3,2,1,0:T(2,128)(2,1)}, u32[]{:S(2)}, u32[]{:S(2)}) async-start(bf16[64,2,2,2048]{3,2,1,0:T(2,128)(2,1)} %reshape.429), calls=%async_computation.12 | async-start | bytes 2097152 | tf_op jit(solution)/shard_map/all_to_all | solution.py:70
  151.8 83.3 %reduce-scatter.17.cloned.1.call-start = ((), (), s32[]{:S(2)}) async-start(), calls=%async_computation.20 | async-start | bytes 1310720 | tf_op jit(solution)/shard_map/reduce_scatter | solution.py:77
  159.7 97.1 %reduce-scatter.21.cloned.1.call-start = ((), (), s32[]{:S(2)}) async-start(), calls=%async_computation.22 | async-start | bytes 1310720 | tf_op jit(solution)/shard_map/reduce_scatter | solution.py:77
  192.7 852.0 %all-reduce.3.cloned.1.call-start = ((), (), s32[]{:S(2)}) async-start(), calls=%async_computation.24 | async-start | bytes 18874368 | tf_op jit(solution)/shard_map/psum | solution.py:11
  208.0 47.6 %copy-start.20 = (s32[256]{0:T(256)S(1)}, s32[256]{0:T(256)}, u32[]{:S(2)}) copy-start(s32[256]{0:T(256)} %copy-done.19) | copy-start | bytes 3076
  208.0 48.2 %copy-start.15 = (s32[256]{0:T(256)S(1)}, s32[256]{0:T(256)}, u32[]{:S(2)}) copy-start(s32[256]{0:T(256)} %eq.288) | copy-start | bytes 3076
  209.9 18.6 %all-to-all-start.1 = ((bf16[64,2,2,512]{3,2,1,0:T(2,128)(2,1)}), bf16[64,2,2,512]{3,2,1,0:T(2,128)(2,1)S(1)}, u32[]{:S(2)}, u32[]{:S(2)}) async-start(bf16[64,2,2,512]{3,2,1,0:T(2,128)(2,1)} %copy.61), calls=%async_computation.2 | async-start | bytes 524288 | tf_op jit(solution)/shard_map/all_to_all | solution.py:84
  228.5 21.7 %all-to-all-start.3 = ((bf16[64,2,2,512]{3,2,1,0:T(2,128)(2,1)}), bf16[64,2,2,512]{3,2,1,0:T(2,128)(2,1)S(1)}, u32[]{:S(2)}, u32[]{:S(2)}) async-start(bf16[64,2,2,512]{3,2,1,0:T(2,128)(2,1)} %copy.72), calls=%async_computation.6 | async-start | bytes 524288 | tf_op jit(solution)/shard_map/all_to_all | solution.py:84
  250.3 18.7 %all-to-all-start.5 = ((bf16[64,2,2,512]{3,2,1,0:T(2,128)(2,1)}), bf16[64,2,2,512]{3,2,1,0:T(2,128)(2,1)S(1)}, u32[]{:S(2)}, u32[]{:S(2)}) async-start(bf16[64,2,2,512]{3,2,1,0:T(2,128)(2,1)} %copy.83), calls=%async_computation.10 | async-start | bytes 524288 | tf_op jit(solution)/shard_map/all_to_all | solution.py:84
  268.9 19.3 %all-to-all-start.7 = ((bf16[64,2,2,512]{3,2,1,0:T(2,128)(2,1)}), bf16[64,2,2,512]{3,2,1,0:T(2,128)(2,1)S(1)}, u32[]{:S(2)}, u32[]{:S(2)}) async-start(bf16[64,2,2,512]{3,2,1,0:T(2,128)(2,1)} %copy.94), calls=%async_computation.14 | async-start | bytes 524288 | tf_op jit(solution)/shard_map/all_to_all | solution.py:84
  275.1 801.7 %reduce-scatter.11.cloned.1.call-start = ((), (), s32[]{:S(2)}) async-start(), calls=%async_computation.17 | async-start | bytes 163840 | tf_op jit(solution)/shard_map/reduce_scatter | solution.py:80
  288.3 756.3 %copy-start.4 = (bf16[128,2048]{1,0:T(8,128)(2,1)S(1)}, bf16[128,2048]{1,0:T(8,128)(2,1)}, u32[]{:S(2)}) copy-start(bf16[128,2048]{1,0:T(8,128)(2,1)} %param.9) | copy-start | bytes 1572868
  1049.1 53.3 %reduce-scatter.15.cloned.1.call-start = ((), (), s32[]{:S(2)}) async-start(), calls=%async_computation.19 | async-start | bytes 163840 | tf_op jit(solution)/shard_map/reduce_scatter | solution.py:80
  1053.2 74.7 %reduce-scatter.19.cloned.1.call-start = ((), (), s32[]{:S(2)}) async-start(), calls=%async_computation.21 | async-start | bytes 163840 | tf_op jit(solution)/shard_map/reduce_scatter | solution.py:80
  1055.8 46.6 %copy-start.27 = (f32[32]{0:T(128)S(1)}, f32[32]{0:T(128)}, u32[]{:S(2)}) copy-start(f32[32]{0:T(128)} %get-tuple-element.7) | copy-start | bytes 388
  1055.8 72.1 %copy-start.26 = (f32[32]{0:T(128)S(1)}, f32[32]{0:T(128)}, u32[]{:S(2)}) copy-start(f32[32]{0:T(128)} %get-tuple-element.8) | copy-start | bytes 388
  1055.8 97.8 %copy-start.25 = (f32[32]{0:T(128)S(1)}, f32[32]{0:T(128)}, u32[]{:S(2)}) copy-start(f32[32]{0:T(128)} %get-tuple-element.9) | copy-start | bytes 388
  1055.8 97.8 %reduce-scatter.23.cloned.1.call-start = ((), (), s32[]{:S(2)}) async-start(), calls=%async_computation.23 | async-start | bytes 163840 | tf_op jit(solution)/shard_map/reduce_scatter | solution.py:80
  (22 other events, 228.3 us)
Sparse Core Ops, SparseCore 0:
  77.3 50.7 reduce-scatter.8
  130.9 47.3 reduce-scatter.12
  180.8 32.7 reduce-scatter.16
  216.2 36.9 reduce-scatter.20
  1049.3 27.5 reduce-scatter.10
  1079.4 22.9 reduce-scatter.14
  1104.9 22.9 reduce-scatter.18
  1130.6 22.9 reduce-scatter.22
Sparse Core Ops, SparseCore 1:
  208.0 836.6 all-reduce.2
where the time goes:
time: 1170 us; the launch traced here: 1160 us
  waiting for transfers between devices  959 us (82%)
  starting transfers between devices  63.8 us (5%)
  local copies, waits for them, and re-layouts  43.8 us (4%)
  matrix products  43.6 us (4%)
  other arithmetic  27 us (2%)
  between operations  26.1 us (2%)
    psum x1, waiting for transfers between devices, broadcast(): return lax.psum(kept, axis)  754 us
    reduce_scatter x4, waiting for transfers between devices, per_device(): lax.psum_scatter(hot_part.astype(jnp.bfloat16), 'tensor', scatter_dimensi...  93.8 us
    all_to_all x4, waiting for transfers between devices, per_device(): lax.all_to_all(send_buf, 'expert', split_axis=0, concat_axis=0, tiled=True)  68.1 us
    all_to_all x4, waiting for transfers between devices, per_device(): lax.all_to_all(summed.astype(jnp.bfloat16), 'expert', split_axis=0, conca...  42.3 us
    all_to_all x4, starting transfers between devices, per_device(): lax.all_to_all(send_buf, 'expert', split_axis=0, concat_axis=0, tiled=True)  39.3 us
  transfers between devices with their start and end apart: 17, of which 12 were waited for; matrix products, arithmetic and copies ran while one was open for 8% of the time, Pallas kernels for 0%

commit v1 on v0

v1 whole, which is shorter than its diff:
```python
import jax
import jax.numpy as jnp
from jax import lax
from jax.sharding import Mesh, PartitionSpec as P

SPANS = 4
CAPACITY = 2
SWAP = ((0, 1), (1, 0))


def dot(a, b, dims):
    return lax.dot_general(a, b, (dims, ((), ())), preferred_element_type=jnp.float32)


def hot_round(turn, held, wanted, chunks, zh, c):
    chip_of, core_of, local_of, order_of = wanted
    my_chip = (lax.axis_index("y") * 2 + zh) * 4 + lax.axis_index("x")
    mine = (chip_of == my_chip) & (order_of == turn)
    local = jnp.sum(jnp.where(mine, local_of, 0))
    core = jnp.sum(jnp.where(mine, core_of, 0))
    rows = jnp.concatenate(
        [lax.dynamic_index_in_dim(w, local, 0, keepdims=False) for w in held], axis=0
    )
    half = rows.shape[0] // 2
    keep = lax.dynamic_slice_in_dim(rows, c * half, half, 0)
    give = lax.dynamic_slice_in_dim(rows, (1 - c) * half, half, 0)
    got = lax.ppermute(give, "c", SWAP)
    part = jnp.where(core == c, keep, got)
    part = part.reshape(half, 16, -1).transpose(1, 0, 2)
    part = lax.all_to_all(part, ("y", "x"), 0, 0, tiled=True)
    new = []
    for span in range(SPANS):
        chip = chip_of[span]
        source = chip // 8 * 4 + chip % 4
        here = (chip // 4 % 2 == zh) & (order_of[span] == turn)
        found = lax.dynamic_index_in_dim(part, source, 0, keepdims=False)
        new.append(jnp.where(here, found, chunks[span]))
    return jnp.stack(new)


def fetch_hot(hot_ids, held, zh, c):
    device_of = hot_ids // 2
    chip_of, core_of, local_of = device_of // 2, device_of % 2, hot_ids % 2
    before = jnp.arange(SPANS)[None, :] < jnp.arange(SPANS)[:, None]
    order_of = jnp.sum((chip_of[:, None] == chip_of[None, :]) & before, axis=1)
    wanted = (chip_of, core_of, local_of, order_of)
    half = 3 * held[0].shape[1] // 2
    width = held[0].shape[2] // 16
    chunks = jnp.zeros((SPANS, half, width), jnp.bfloat16)
    chunks = hot_round(0, held, wanted, chunks, zh, c)
    turns = jnp.max(order_of) + 1
    chunks = lax.fori_loop(
        1, turns, lambda turn, got: hot_round(turn, held, wanted, got, zh, c), chunks
    )
    give = lax.dynamic_slice_in_dim(chunks, 2 * (1 - zh), 2, 0)
    got = lax.ppermute(give, "zh", SWAP)
    keep = lax.dynamic_slice_in_dim(chunks, 2 * zh, 2, 0)
    zh_of = lax.dynamic_slice_in_dim(chip_of // 4 % 2, 2 * zh, 2, 0)
    pair = jnp.where((zh_of == zh)[:, None, None], keep, got)
    mine = lax.dynamic_index_in_dim(pair, c, 0, keepdims=False)
    give = lax.dynamic_index_in_dim(pair, 1 - c, 0, keepdims=False)
    got = lax.ppermute(give, "c", SWAP)
    whole = jnp.where(c == 0, jnp.stack([mine, got]), jnp.stack([got, mine]))
    whole = whole.reshape(2 * half, width)
    return lax.all_gather(whole, ("y", "x"), axis=0, tiled=False)


def per_device(tokens, expert_ids, gate_values, hot_ids, w_gate, w_up, w_down):
    zh = lax.axis_index("zh")
    c = lax.axis_index("c")
    tok_dev, model_width = tokens.shape
    top_k = expert_ids.shape[1]
    span_rows = tok_dev // SPANS
    units = w_gate.shape[1]

    hot_parts = fetch_hot(hot_ids, (w_gate, w_up, w_down), zh, c)

    meta = jnp.concatenate([expert_ids.astype(jnp.float32), gate_values], axis=1).T
    tok_z = lax.ppermute(tokens, "zh", SWAP)
    meta_z = lax.ppermute(meta, "zh", SWAP)
    tok_c = lax.ppermute(tokens, "c", SWAP)
    tok_zc = lax.ppermute(tok_z, "c", SWAP)
    meta_c, meta_zc = jnp.split(
        lax.ppermute(jnp.concatenate([meta, meta_z], axis=1), "c", SWAP), 2, axis=1
    )
    tok = jnp.concatenate([tokens, tok_c, tok_z, tok_zc], axis=0)
    meta = jnp.concatenate([meta, meta_c, meta_z, meta_zc], axis=1)
    n_tok = 4 * tok_dev
    ids = meta[:top_k].astype(jnp.int32)
    gates = meta[top_k:]

    group = jnp.arange(n_tok, dtype=jnp.int32) // span_rows
    span_of = group % SPANS
    hot_of = sum(jnp.where(span_of == s, hot_ids[s], 0) for s in range(SPANS))
    is_hot = ids == hot_of[None, :]
    hot_weight = jnp.sum(jnp.where(is_hot, gates, 0.0), axis=0)

    place = jnp.arange(32, dtype=jnp.int32)
    experts = ((place // 8 * 2 + zh) * 4 + place // 2 % 4) * 4 + c * 2 + place % 2
    match = (ids[None] == experts[:, None, None]) & jnp.logical_not(is_hot)[None]
    named = jnp.any(match, axis=1)
    named_gate = jnp.sum(jnp.where(match, gates[None], 0.0), axis=1)
    row = jnp.arange(n_tok, dtype=jnp.int32)
    earlier = (group[:, None] == group[None, :]) & (row[:, None] < row[None, :])
    rank = dot(named.astype(jnp.bfloat16), earlier.astype(jnp.bfloat16), ((1,), (0,)))
    n_group = 4 * SPANS
    slot_group = jnp.arange(n_group * CAPACITY, dtype=jnp.int32) // CAPACITY
    slot_rank = (jnp.arange(n_group * CAPACITY, dtype=jnp.int32) % CAPACITY).astype(jnp.float32)
    chosen = (
        named[:, None, :]
        & (slot_group[:, None] == group[None, :])[None]
        & (rank[:, None, :] == slot_rank[None, :, None])
    )
    n_slot = 32 * n_group * CAPACITY
    pick = chosen.astype(jnp.bfloat16).reshape(n_slot, n_tok)
    mix = jnp.where(chosen, named_gate[:, None, :], 0.0).astype(jnp.bfloat16)
    mix = mix.reshape(n_slot, n_tok)

    send = dot(pick, tok, ((1,), (0,))).astype(jnp.bfloat16)
    send = send.reshape(16, n_slot // 16, model_width)
    received = lax.all_to_all(send, ("y", "x"), 0, 0, tiled=True)
    received = received.reshape(16, 2, n_slot // 32, model_width)
    gate_proj = jnp.einsum("nerd,efd->nerf", received, w_gate, preferred_element_type=jnp.float32)
    up_proj = jnp.einsum("nerd,efd->nerf", received, w_up, preferred_element_type=jnp.float32)
    hidden = (jax.nn.silu(gate_proj) * up_proj).astype(jnp.bfloat16)
    part = jnp.einsum("nerf,efd->nerd", hidden, w_down, preferred_element_type=jnp.float32)
    part = part.astype(jnp.bfloat16).reshape(16, n_slot // 16, model_width)
    returned = lax.all_to_all(part, ("y", "x"), 0, 0, tiled=True)
    returned = returned.reshape(n_slot, model_width)

    my_span = 2 * zh + c
    hot_w = hot_parts.transpose(1, 0, 2).reshape(3 * units, model_width)
    hot_tok = lax.dynamic_slice_in_dim(
        tok.reshape(4, tok_dev, model_width), my_span * span_rows, span_rows, 1
    ).reshape(4 * span_rows, model_width)
    hot_gate = dot(hot_tok, hot_w[:units], ((1,), (1,)))
    hot_up = dot(hot_tok, hot_w[units : 2 * units], ((1,), (1,)))
    hot_hidden = (jax.nn.silu(hot_gate) * hot_up).astype(jnp.bfloat16)
    hot_out = dot(hot_hidden, hot_w[2 * units :], ((1,), (0,))).astype(jnp.bfloat16)
    hot_row = jnp.arange(4 * span_rows, dtype=jnp.int32)
    hot_row = hot_row // span_rows * tok_dev + my_span * span_rows + hot_row % span_rows
    hot_mix = jnp.where(hot_row[:, None] == row[None, :], hot_weight[None, :], 0.0)
    hot_mix = hot_mix.astype(jnp.bfloat16)

    summed = dot(mix, returned, ((0,), (0,))) + dot(hot_mix, hot_out, ((0,), (0,)))
    summed = summed.reshape(2, 2, tok_dev, model_width)
    other = lax.ppermute(summed[:, 1].astype(jnp.bfloat16), "c", SWAP)
    summed = summed[:, 0] + other.astype(jnp.float32)
    summed = jnp.where(zh == 0, summed, summed[::-1]).astype(jnp.bfloat16)
    summed = summed.reshape(2, tok_dev, 4, model_width // 4).transpose(0, 2, 1, 3)
    summed = summed.reshape(8, tok_dev, model_width // 4)
    pieces = lax.all_to_all(summed, ("zh", "t"), 0, 0, tiled=True)
    return jnp.sum(pieces.astype(jnp.float32), axis=0).astype(jnp.bfloat16)


def solution(mesh):
    fine = Mesh(mesh.devices.reshape(4, 2, 4, 2, 4), ("y", "zh", "x", "c", "t"))
    owner = ("y", "zh", "x", "c")
    in_specs = (
        P(owner, None),
        P(owner, None),
        P(owner, None),
        P(),
        P(owner, "t", None),
        P(owner, "t", None),
        P(owner, "t", None),
    )
    return jax.shard_map(
        per_device, mesh=fine, in_specs=in_specs, out_specs=P(owner, "t"), check_vma=False
    )
```

time: 1170 us -> 308 us (0.26)
  waiting for transfers between devices: 959 us -> 126 us
  blocking collectives: 0 us -> 33.2 us
  starting transfers between devices: 63.8 us -> 38.4 us
  local copies, waits for them, and re-layouts: 43.8 us -> 24.7 us
  matrix products: 43.6 us -> 29.3 us
    psum x1 -> x0, waiting for transfers between devices: 754 us -> none  [broadcast(): return lax.psum(kept, axis)]
    reduce_scatter x8 -> x0, waiting for transfers between devices: 93.9 us -> none  [the longest x4 93.8 us: per_device(): lax.psum_scatter(hot_part.astype(jnp.bfloat16), 'tensor', scatter_dimensi...]
    all_to_all x8 -> x3, starting transfers between devices: 62.3 us -> 24.5 us  [the longest x1 9.14 us: per_device(): returned = lax.all_to_all(part, ('y', 'x'), 0, 0, tiled=True)]
    all_to_all x0 -> x1, blocking collectives: none -> 33.2 us  [per_device(): pieces = lax.all_to_all(summed, ('zh', 't'), 0, 0, tiled=True)]
    dot_general x16 -> x8, matrix products: 43.6 us -> 29.3 us  [the longest x6 17.8 us: dot(): lax.dot_general(a, b, (dims, ((), ())), preferred_element_type=jnp.float32)]
    ppermute x0 -> x9, starting transfers between devices: none -> 13.9 us  [the longest x1 7.19 us: per_device(): tok_z = lax.ppermute(tokens, 'zh', SWAP)]
    all_to_all x8 -> x3, waiting for transfers between devices: 110 us -> 114 us  [the longest x1 53.3 us: per_device(): returned = lax.all_to_all(part, ('y', 'x'), 0, 0, tiled=True)]
  transfers between devices with their start and end apart: 17 -> 13, of which waited for: 12 -> 7; matrix products, arithmetic and copies ran while one was open for 8% -> 20% of each run, Pallas kernels for 0% -> 0%
where the time goes in v1:
time: 308 us; the launch traced here: 304 us
  waiting for transfers between devices  126 us (41%)
  starting transfers between devices  38.4 us (12%)
  blocking collectives  33.2 us (11%)
  between operations  29.4 us (10%)
  matrix products  29.3 us (10%)
  local copies, waits for them, and re-layouts  24.7 us (8%)
  other arithmetic  23.4 us (8%)
    all_to_all x1, waiting for transfers between devices, per_device(): returned = lax.all_to_all(part, ('y', 'x'), 0, 0, tiled=True)  53.3 us
    all_to_all x1, waiting for transfers between devices, per_device(): received = lax.all_to_all(send, ('y', 'x'), 0, 0, tiled=True)  49.3 us
    all_to_all x1, blocking collectives, per_device(): pieces = lax.all_to_all(summed, ('zh', 't'), 0, 0, tiled=True)  33.2 us
    dot_general x6, matrix products, dot(): lax.dot_general(a, b, (dims, ((), ())), preferred_element_type=jnp.float32)  17.8 us
    all_to_all x1, waiting for transfers between devices, hot_round(): part = lax.all_to_all(part, ('y', 'x'), 0, 0, tiled=True)  11.9 us
    all_to_all x1, starting transfers between devices, per_device(): returned = lax.all_to_all(part, ('y', 'x'), 0, 0, tiled=True)  9.14 us
    all_to_all x1, starting transfers between devices, per_device(): received = lax.all_to_all(send, ('y', 'x'), 0, 0, tiled=True)  7.86 us
    dot_general x1, matrix products, per_device(): jnp.einsum('nerf,efd->nerd', hidden, w_down, preferred_element_type=jnp.f...  7.54 us
  transfers between devices with their start and end apart: 13, of which 7 were waited for; matrix products, arithmetic and copies ran while one was open for 20% of the time, Pallas kernels for 0%

profile of v1, /device:TPU:2, one launch (start us, length us, event | category | flops | bytes accessed | tf_op | source)
XLA Modules:
  0.0 304.5 jit_solution(17376394947448392668)
XLA Ops:
  6.5 7.2 %collective-permute-start.4 = (bf16[128,2048]{1,0:T(8,128)(2,1)}, bf16[128,2048]{1,0:T(8,128)(2,1)}, u32[]{:S(2)}, u32[]{:S(2)}) collective-permute-start(bf16[128,2048]{1,0:T(8,128)(2,1)} %param.9), channel_id=1, source_target_pairs={{0,32},{32,0},{1,33},{33,1},{2,34},{34,2},{3,35},{35,3},{4,36},{36... | collective-permute-start | bytes 1572872 | tf_op jit(solution)/shard_map/ppermute | solution.py:79
  15.2 1.9 select_reduce_fusion.5
  20.2 2.7 dynamic-slice_bitcast_fusion.3
  29.4 3.2 %select_add_fusion = s32[512]{0:T(512)} fusion(s32[]{:T(128)} %bitcast.12, s32[]{:T(128)} %bitcast.11, s32[]{:T(128)} %bitcast.10, s32[]{:T(128)} %bitcast.9), kind=kLoop, calls=%fused_computation.113 | loop fusion | flops 15360 | bytes 2064 | tf_op jit(solution)/shard_map/add | solution.py:94
  32.6 3.5 %collective-permute-done.1 = f32[16,128]{1,0:T(8,128)} collective-permute-done((f32[16,128]{1,0:T(8,128)S(1)}, f32[16,128]{1,0:T(8,128)}, u32[]{:S(2)}, u32[]{:S(2)}) %collective-permute-start.1) | collective-permute-done | bytes 8224 | tf_op jit(solution)/shard_map/ppermute | solution.py:80
  55.4 1.8 select_reduce_fusion.3
  60.2 2.0 fusion.6
  64.8 7.5 %all-to-all-start.3 = ((bf16[16,288,128]{2,1,0:T(8,128)(2,1)}), bf16[16,288,128]{2,1,0:T(8,128)(2,1)S(1)}, u32[]{:S(2)}, u32[]{:S(2)}) async-start(bf16[16,288,128]{2,1,0:T(8,128)(2,1)} %copy.34), calls=%async_computation.3 | async-start | bytes 2359296 | tf_op jit(solution)/shard_map/all_to_all | solution.py:30
  75.6 4.3 %convolution_convert_fusion = bf16[1024,2048]{1,0:T(8,128)(2,1)} fusion(pred[1024,512]{1,0:T(32,128)(4,1)S(1)} %copy-done.5, bf16[512,2048]{1,0:T(8,128)(2,1)S(1)} %constant_dynamic-update-slice_fusion), kind=kOutput, calls=%fused_computation.15 | convolution fusion | flops 2149580800 | bytes 6815744 | tf_op jit(solution)/shard_map/dot_general | solution.py:12
  79.9 11.9 %all-to-all-done.3 = bf16[16,288,128]{2,1,0:T(8,128)(2,1)S(1)} async-done(((bf16[16,288,128]{2,1,0:T(8,128)(2,1)}), bf16[16,288,128]{2,1,0:T(8,128)(2,1)S(1)}, u32[]{:S(2)}, u32[]{:S(2)}) %all-to-all-start.3) | async-done | bytes 1179680 | tf_op jit(solution)/shard_map/all_to_all | solution.py:30
  92.6 7.9 %all-to-all-start.1 = ((bf16[16,64,2048]{2,1,0:T(8,128)(2,1)}), bf16[16,64,2048]{2,1,0:T(8,128)(2,1)}, u32[]{:S(2)}, u32[]{:S(2)}) async-start(bf16[16,64,2048]{2,1,0:T(8,128)(2,1)} %bitcast.151), calls=%async_computation.1 | async-start | bytes 8388608 | tf_op jit(solution)/shard_map/all_to_all | solution.py:121
  100.6 5.3 %collective-permute-start.7 = (bf16[2,288,128]{2,1,0:T(8,128)(2,1)S(1)}, bf16[2,288,128]{2,1,0:T(8,128)(2,1)S(1)}, u32[]{:S(2)}, u32[]{:S(2)}) collective-permute-start(bf16[2,288,128]{2,1,0:T(8,128)(2,1)S(1)} %constant_dynamic-slice_fusion.2), channel_id=1, source_target_pairs={{0,32},{32,0},{1,33},{33,1},{2,34},{34,2},{3,35},{35,3},{4,36},{36... | collective-permute-start | bytes 442376 | tf_op jit(solution)/shard_map/ppermute | solution.py:56
  105.9 4.3 %collective-permute-done.7 = bf16[2,288,128]{2,1,0:T(8,128)(2,1)S(1)} collective-permute-done((bf16[2,288,128]{2,1,0:T(8,128)(2,1)S(1)}, bf16[2,288,128]{2,1,0:T(8,128)(2,1)S(1)}, u32[]{:S(2)}, u32[]{:S(2)}) %collective-permute-start.7) | collective-permute-done | bytes 147488 | tf_op jit(solution)/shard_map/ppermute | solution.py:56
  112.4 49.3 %all-to-all-done.1 = bf16[16,64,2048]{2,1,0:T(8,128)(2,1)} async-done(((bf16[16,64,2048]{2,1,0:T(8,128)(2,1)}), bf16[16,64,2048]{2,1,0:T(8,128)(2,1)}, u32[]{:S(2)}, u32[]{:S(2)}) %all-to-all-start.1) | async-done | bytes 4194336 | tf_op jit(solution)/shard_map/all_to_all | solution.py:121
  161.7 3.9 %fusion.10 = f32[16,2,32,192]{3,2,0,1:T(8,128)S(1)} fusion(bf16[2,192,2048]{2,1,0:T(8,128)(2,1)} %param.13, bf16[16,2,32,2048]{3,2,1,0:T(8,128)(2,1)} %bitcast.17), kind=kOutput, calls=%fused_computation.34 | convolution fusion | flops 805306368 | bytes 6553600 | tf_op jit(solution)/shard_map/nerd,efd->nerf/dot_general | solution.py:123
  165.7 7.5 %convert_bitcast_fusion = bf16[16,2,32,2048]{3,2,0,1:T(8,128)(2,1)} fusion(bf16[2,192,2048]{2,1,0:T(8,128)(2,1)} %param.15, bf16[2,192,2048]{2,1,0:T(8,128)(2,1)} %param.14, bf16[16,2,32,2048]{3,2,1,0:T(8,128)(2,1)} %bitcast.17, f32[16,2,32,192]{3,2,0,1:T(8,128)S(1)} %fusion.10), kind=kOutput, calls=%fused_computation.14 | convolution fusion | flops 1613889536 | bytes 12320768 | tf_op jit(solution)/shard_map/nerf,efd->nerd/dot_general | solution.py:126
  173.2 4.8 %copy.33 = bf16[16,2,32,2048]{3,2,1,0:T(8,128)(2,1)} copy(bf16[16,2,32,2048]{3,2,0,1:T(8,128)(2,1)} %convert_bitcast_fusion) | data formatting | bytes 8388608 | tf_op jit(solution)/shard_map/convert_element_type | solution.py:127
  178.0 9.1 %all-to-all-start.2 = ((bf16[16,64,2048]{2,1,0:T(8,128)(2,1)}), bf16[16,64,2048]{2,1,0:T(8,128)(2,1)}, u32[]{:S(2)}, u32[]{:S(2)}) async-start(bf16[16,64,2048]{2,1,0:T(8,128)(2,1)} %bitcast.146), calls=%async_computation.2 | async-start | bytes 8388608 | tf_op jit(solution)/shard_map/all_to_all | solution.py:128
  191.8 53.3 %all-to-all-done.2 = bf16[16,64,2048]{2,1,0:T(8,128)(2,1)} async-done(((bf16[16,64,2048]{2,1,0:T(8,128)(2,1)}), bf16[16,64,2048]{2,1,0:T(8,128)(2,1)}, u32[]{:S(2)}, u32[]{:S(2)}) %all-to-all-start.2) | async-done | bytes 4194336 | tf_op jit(solution)/shard_map/all_to_all | solution.py:128
  245.1 6.6 %fusion.84 = f32[512,2048]{1,0:T(8,128)} fusion(bf16[1024,512]{1,0:T(8,128)(2,1)S(1)} %bitcast.149, bf16[1024,2048]{1,0:T(8,128)(2,1)} %bitcast.28), kind=kOutput, calls=%fused_computation.170 | convolution fusion | flops 2147483648 | bytes 9437184 | tf_op jit(solution)/shard_map/dot_general | solution.py:12
  251.7 5.1 %convolution_add_fusion = f32[512,2048]{1,0:T(8,128)} fusion(f32[512,2048]{1,0:T(8,128)} %fusion.84, bf16[128,192]{0,1:T(8,128)(2,1)S(1)} %fusion.30, bf16[16,24,8,128]{3,2,1,0:T(8,128)(2,1)S(1)} %get-tuple-element.1323, bf16[512]{0:T(512)(128)(2,1)S(1)} %copy-done.19, s32[128]{0:T(128)S(1)} %fusion.63), kind=kOutput, calls=%fused_computation.20 | convolution fusion | flops 370540544 | bytes 9225728 | tf_op jit(solution)/shard_map/dot_general | solution.py:12
  258.7 2.6 collective-permute-done.9
  261.3 1.9 fusion.5
  263.6 33.2 %all_to_all.30 = bf16[8,128,512]{2,1,0:T(8,128)(2,1)S(1)} all-to-all(bf16[8,128,512]{2,1,0:T(8,128)(2,1)S(1)} %bitcast.152), channel_id=1, replica_groups=mesh['y'=4,'zh'=2,'x'=4,'c'=2,'t'=4] {'zh','t'}, dimensions={0} | all-to-all | bytes 2097152 | tf_op jit(solution)/shard_map/all_to_all | solution.py:152
  (112 shorter events, 34.3 us)
Async XLA Ops:
  6.5 55.7 %collective-permute-start.4 = (bf16[128,2048]{1,0:T(8,128)(2,1)}, bf16[128,2048]{1,0:T(8,128)(2,1)}, u32[]{:S(2)}, u32[]{:S(2)}) collective-permute-start(bf16[128,2048]{1,0:T(8,128)(2,1)} %param.9), channel_id=1, source_target_pairs={{0,32},{32,0},{1,33},{33,1},{2,34},{34,2},{3,35},{35,3},{4,36},{36... | collective-permute-start | bytes 1572872 | tf_op jit(solution)/shard_map/ppermute | solution.py:79
  13.7 58.5 %collective-permute-start.3 = (bf16[128,2048]{1,0:T(8,128)(2,1)}, bf16[128,2048]{1,0:T(8,128)(2,1)}, u32[]{:S(2)}, u32[]{:S(2)}) collective-permute-start(bf16[128,2048]{1,0:T(8,128)(2,1)} %param.9), channel_id=1, source_target_pairs={{0,4},{4,0},{1,5},{5,1},{2,6},{6,2},{3,7},{7,3},{8,12},{12,8},{9,1... | collective-permute-start | bytes 1572872 | tf_op jit(solution)/shard_map/ppermute | solution.py:81
  24.7 38.0 %collective-permute-start.6 = (bf16[288,2048]{1,0:T(8,128)(2,1)S(1)}, bf16[288,2048]{1,0:T(8,128)(2,1)}, u32[]{:S(2)}, u32[]{:S(2)}) collective-permute-start(bf16[288,2048]{1,0:T(8,128)(2,1)S(1)} %constant_dynamic-slice_fusion.3), channel_id=1, source_target_pairs={{0,4},{4,0},{1,5},{5,1},{2,6},{6,2},{3,7},{7,3},{8,12},{12,8},{9,1... | collective-permute-start | bytes 3538952 | tf_op jit(solution)/shard_map/ppermute | solution.py:27
  25.3 10.8 %collective-permute-start.1 = (f32[16,128]{1,0:T(8,128)S(1)}, f32[16,128]{1,0:T(8,128)}, u32[]{:S(2)}, u32[]{:S(2)}) collective-permute-start(f32[16,128]{1,0:T(8,128)S(1)} %maximum_bitcast_fusion), channel_id=1, source_target_pairs={{0,32},{32,0},{1,33},{33,1},{2,34},{34,2},{3,35},{35,3},{4,36},{36... | collective-permute-start | bytes 24584 | tf_op jit(solution)/shard_map/ppermute | solution.py:80
  37.4 16.6 %collective-permute-start.2 = (f32[16,256]{1,0:T(8,128)}, f32[16,256]{1,0:T(8,128)}, u32[]{:S(2)}, u32[]{:S(2)}) collective-permute-start(f32[16,256]{1,0:T(8,128)} %pad_maximum_fusion.6), channel_id=1, source_target_pairs={{0,4},{4,0},{1,5},{5,1},{2,6},{6,2},{3,7},{7,3},{8,12},{12,8},{9,1... | collective-permute-start | bytes 49160 | tf_op jit(solution)/shard_map/ppermute | solution.py:84
  62.2 12.3 %collective-permute-start.5 = (bf16[128,2048]{1,0:T(8,128)(2,1)}, bf16[128,2048]{1,0:T(8,128)(2,1)}, u32[]{:S(2)}, u32[]{:S(2)}) collective-permute-start(bf16[128,2048]{1,0:T(8,128)(2,1)} %collective-permute-done.4), channel_id=1, source_target_pairs={{0,4},{4,0},{1,5},{5,1},{2,6},{6,2},{3,7},{7,3},{8,12},{12,8},{9,1... | collective-permute-start | bytes 1572872 | tf_op jit(solution)/shard_map/ppermute | solution.py:82
  63.4 8.9 %copy-start.2 = (bf16[512,2048]{1,0:T(8,128)(2,1)S(1)}, bf16[512,2048]{1,0:T(8,128)(2,1)}, u32[]{:S(2)}) copy-start(bf16[512,2048]{1,0:T(8,128)(2,1)} %constant_dynamic-update-slice_fusion.3) | copy-start | bytes 6291460
  64.8 27.0 %all-to-all-start.3 = ((bf16[16,288,128]{2,1,0:T(8,128)(2,1)}), bf16[16,288,128]{2,1,0:T(8,128)(2,1)S(1)}, u32[]{:S(2)}, u32[]{:S(2)}) async-start(bf16[16,288,128]{2,1,0:T(8,128)(2,1)} %copy.34), calls=%async_computation.3 | async-start | bytes 2359296 | tf_op jit(solution)/shard_map/all_to_all | solution.py:30
  75.6 17.0 %copy-start.15 = (s32[4]{0:T(128)S(1)}, s32[4]{0:T(128)}, u32[]{:S(2)}) copy-start(s32[4]{0:T(128)} %get-tuple-element.1523) | copy-start | bytes 52
  75.6 17.0 %copy-start.16 = (s32[4]{0:T(128)S(1)}, s32[4]{0:T(128)}, u32[]{:S(2)}) copy-start(s32[4]{0:T(128)} %get-tuple-element.1521) | copy-start | bytes 52
  92.6 13.3 %copy-start.24 = (s32[4]{0:T(128)S(1)}, s32[4]{0:T(128)}, u32[]{:S(2)}) copy-start(s32[4]{0:T(128)} %get-tuple-element.1308) | copy-start | bytes 52
  92.6 69.1 %all-to-all-start.1 = ((bf16[16,64,2048]{2,1,0:T(8,128)(2,1)}), bf16[16,64,2048]{2,1,0:T(8,128)(2,1)}, u32[]{:S(2)}, u32[]{:S(2)}) async-start(bf16[16,64,2048]{2,1,0:T(8,128)(2,1)} %bitcast.151), calls=%async_computation.1 | async-start | bytes 8388608 | tf_op jit(solution)/shard_map/all_to_all | solution.py:121
  100.5 88.8 %all-gather.2.cloned.1.call-start = ((), (), s32[]{:S(2)}) async-start(), calls=%async_computation.5 | async-start | bytes 2506752 | tf_op jit(solution)/shard_map/all_gather | solution.py:65
  100.6 9.7 %collective-permute-start.7 = (bf16[2,288,128]{2,1,0:T(8,128)(2,1)S(1)}, bf16[2,288,128]{2,1,0:T(8,128)(2,1)S(1)}, u32[]{:S(2)}, u32[]{:S(2)}) collective-permute-start(bf16[2,288,128]{2,1,0:T(8,128)(2,1)S(1)} %constant_dynamic-slice_fusion.2), channel_id=1, source_target_pairs={{0,32},{32,0},{1,33},{33,1},{2,34},{34,2},{3,35},{35,3},{4,36},{36... | collective-permute-start | bytes 442376 | tf_op jit(solution)/shard_map/ppermute | solution.py:56
  110.3 1.4 collective-permute-start.8
  178.0 9.2 %copy-start.12 = (s32[8,512]{1,0:T(8,128)S(1)}, s32[8,512]{1,0:T(8,128)}, u32[]{:S(2)}) copy-start(s32[8,512]{1,0:T(8,128)} %copy-done.11) | copy-start | bytes 49156
  178.0 9.2 %copy-start.13 = (f32[8,512]{1,0:T(8,128)S(1)}, f32[8,512]{1,0:T(8,128)}, u32[]{:S(2)}) copy-start(f32[8,512]{1,0:T(8,128)} %get-tuple-element.1336) | copy-start | bytes 49156
  178.0 9.2 %copy-start.22 = (s32[32]{0:T(128)S(1)}, s32[32]{0:T(128)}, u32[]{:S(2)}) copy-start(s32[32]{0:T(128)} %fusion.70) | copy-start | bytes 388
  178.0 9.5 %copy-start.7 = (f32[32,512]{1,0:T(8,128)S(1)}, f32[32,512]{1,0:T(8,128)}, u32[]{:S(2)}) copy-start(f32[32,512]{1,0:T(8,128)} %copy-done.6) | copy-start | bytes 196612
  178.0 9.5 %copy-start.9 = (pred[32,512]{1,0:T(8,128)(4,1)S(1)}, pred[32,512]{1,0:T(8,128)(4,1)}, u32[]{:S(2)}) copy-start(pred[32,512]{1,0:T(8,128)(4,1)} %copy-done.8) | copy-start | bytes 49156
  178.0 9.5 %copy-start.10 = (pred[32,512]{1,0:T(8,128)(4,1)S(1)}, pred[32,512]{1,0:T(8,128)(4,1)}, u32[]{:S(2)}) copy-start(pred[32,512]{1,0:T(8,128)(4,1)} %broadcast_compare_fusion) | copy-start | bytes 49156
  178.0 9.5 %copy-start.23 = (f32[32]{0:T(128)S(1)}, f32[32]{0:T(128)}, u32[]{:S(2)}) copy-start(f32[32]{0:T(128)} %get-tuple-element.1353) | copy-start | bytes 388
  178.0 67.1 %all-to-all-start.2 = ((bf16[16,64,2048]{2,1,0:T(8,128)(2,1)}), bf16[16,64,2048]{2,1,0:T(8,128)(2,1)}, u32[]{:S(2)}, u32[]{:S(2)}) async-start(bf16[16,64,2048]{2,1,0:T(8,128)(2,1)} %bitcast.146), calls=%async_computation.2 | async-start | bytes 8388608 | tf_op jit(solution)/shard_map/all_to_all | solution.py:128
  258.6 2.7 collective-permute-start.9
  (12 other events, 34.8 us)
Sparse Core Ops, SparseCore 0:
  112.5 74.4 all-gather.1

commit v2 on v1

v2 whole, which is shorter than its diff:
```python
import jax
import jax.numpy as jnp
from jax import lax
from jax.experimental import pallas as pl
from jax.experimental.pallas import tpu as pltpu
from jax.sharding import Mesh, PartitionSpec as P

SPANS = 4
CAPACITY = 2
SWAP = ((0, 1), (1, 0))
VMEM_LIMIT = 32 * 1024 * 1024


def dot(a, b, contract_a, contract_b):
    dims = (((contract_a,), (contract_b,)), ((), ()))
    return lax.dot_general(a, b, dims, preferred_element_type=jnp.float32)


def iota(shape, dim):
    return lax.broadcasted_iota(jnp.int32, shape, dim)


def cost(flops, moved):
    return pl.CostEstimate(flops=flops, bytes_accessed=moved, transcendentals=0)


PARAMS = pltpu.CompilerParams(vmem_limit_bytes=VMEM_LIMIT)


def whole(shape):
    return pl.BlockSpec(shape, lambda *_: (0,) * len(shape))


def chunk_kernel(info, gate_ref, up_ref, down_ref, keep_ref, give_ref):
    units = gate_ref.shape[1]
    mid = units // 2

    def first(out):
        out[0, :units] = gate_ref[0]
        out[0, units:] = up_ref[0, :mid]

    def second(out):
        out[0, :mid] = up_ref[0, mid:]
        out[0, mid:] = down_ref[0]

    @pl.when(info[1] == 0)
    def _():
        first(keep_ref)
        second(give_ref)

    @pl.when(info[1] == 1)
    def _():
        second(keep_ref)
        first(give_ref)


def cut_chunks(local, c, held):
    _, units, width = held[0].shape
    lane = width // 16
    half = 3 * units // 2
    spec = pl.BlockSpec((1, units, lane), lambda n, info: (info[0], 0, n))
    out = pl.BlockSpec((1, half, lane), lambda n, info: (n, 0, 0))
    shape = jax.ShapeDtypeStruct((16, half, lane), jnp.bfloat16)
    return pl.pallas_call(
        chunk_kernel,
        out_shape=(shape, shape),
        grid_spec=pltpu.PrefetchScalarGridSpec(
            num_scalar_prefetch=1, grid=(16,), in_specs=[spec] * 3, out_specs=(out, out)
        ),
        compiler_params=PARAMS,
        cost_estimate=cost(0, 4 * 3 * units * width),
    )(jnp.stack([local, c]).astype(jnp.int32), *held)


def hot_round(turn, held, wanted, chunks, zh, c):
    chip_of, core_of, local_of, order_of = wanted
    my_chip = (lax.axis_index("y") * 2 + zh) * 4 + lax.axis_index("x")
    mine = (chip_of == my_chip) & (order_of == turn)
    local = jnp.sum(jnp.where(mine, local_of, 0))
    core = jnp.sum(jnp.where(mine, core_of, 0))
    keep, give = cut_chunks(local, c, held)
    got = lax.ppermute(give, "c", SWAP)
    part = jnp.where(core == c, keep, got)
    part = lax.all_to_all(part, ("y", "x"), 0, 0, tiled=True)
    new = []
    for span in range(SPANS):
        chip = chip_of[span]
        source = chip // 8 * 4 + chip % 4
        here = (chip // 4 % 2 == zh) & (order_of[span] == turn)
        found = lax.dynamic_index_in_dim(part, source, 0, keepdims=False)
        new.append(jnp.where(here, found, chunks[span]))
    return jnp.stack(new)


def fetch_hot(hot_ids, held, zh, c):
    device_of = hot_ids // 2
    chip_of, core_of, local_of = device_of // 2, device_of % 2, hot_ids % 2
    before = jnp.arange(SPANS)[None, :] < jnp.arange(SPANS)[:, None]
    order_of = jnp.sum((chip_of[:, None] == chip_of[None, :]) & before, axis=1)
    wanted = (chip_of, core_of, local_of, order_of)
    half = 3 * held[0].shape[1] // 2
    width = held[0].shape[2] // 16
    chunks = jnp.zeros((SPANS, half, width), jnp.bfloat16)
    chunks = hot_round(0, held, wanted, chunks, zh, c)
    turns = jnp.max(order_of) + 1
    chunks = lax.fori_loop(
        1, turns, lambda turn, got: hot_round(turn, held, wanted, got, zh, c), chunks
    )
    give = lax.dynamic_slice_in_dim(chunks, 2 * (1 - zh), 2, 0)
    got = lax.ppermute(give, "zh", SWAP)
    keep = lax.dynamic_slice_in_dim(chunks, 2 * zh, 2, 0)
    zh_of = lax.dynamic_slice_in_dim(chip_of // 4 % 2, 2 * zh, 2, 0)
    pair = jnp.where((zh_of == zh)[:, None, None], keep, got)
    mine = lax.dynamic_index_in_dim(pair, c, 0, keepdims=False)
    give = lax.dynamic_index_in_dim(pair, 1 - c, 0, keepdims=False)
    got = lax.ppermute(give, "c", SWAP)
    both = jnp.where(c == 0, jnp.stack([mine, got]), jnp.stack([got, mine]))
    both = both.reshape(2 * half, width)
    return lax.all_gather(both, ("y", "x"), axis=0, tiled=False)


def hot_kernel(info, *refs):
    *tok_refs, w_ref, near_ref, far_ref = refs
    tok = jnp.concatenate([r[...] for r in tok_refs], axis=0)
    units = w_ref.shape[1] // 3
    lane = w_ref.shape[2]
    n_chunk = w_ref.shape[0]
    proj = sum(
        dot(tok[:, n * lane : (n + 1) * lane], w_ref[n, : 2 * units], 1, 1) for n in range(n_chunk)
    )
    hidden = (jax.nn.silu(proj[:, :units]) * proj[:, units:]).astype(jnp.bfloat16)
    half = tok.shape[0] // 2
    for n in range(n_chunk):
        out = dot(hidden, w_ref[n, 2 * units :], 1, 0).astype(jnp.bfloat16)
        near_ref[:, n * lane : (n + 1) * lane] = out[:half]
        far_ref[:, n * lane : (n + 1) * lane] = out[half:]


def hot_ffn(info, blocks, hot_w):
    tok_dev, width = blocks[0].shape
    rows = tok_dev // SPANS
    spec = pl.BlockSpec((rows, width), lambda i, info: (2 * info[4] + info[5], 0))
    shape = jax.ShapeDtypeStruct((2 * rows, width), jnp.bfloat16)
    return pl.pallas_call(
        hot_kernel,
        out_shape=(shape, shape),
        grid_spec=pltpu.PrefetchScalarGridSpec(
            num_scalar_prefetch=1,
            grid=(1,),
            in_specs=[spec] * 4 + [whole(hot_w.shape)],
            out_specs=(whole(shape.shape), whole(shape.shape)),
        ),
        compiler_params=PARAMS,
        cost_estimate=cost(8 * rows * hot_w.size, 2 * hot_w.size + 16 * rows * width),
    )(info, *blocks, hot_w)


def route_kernel(info, meta_ref, a_ref, b_ref, send_ref, mix_ref, hot_mix_ref):
    zh, c = info[4], info[5]
    n_tok = meta_ref.shape[1]
    n_slot = send_ref.shape[0]
    top_k = meta_ref.shape[0] // 2
    tok_dev = n_tok // 2
    span_rows = tok_dev // SPANS

    row = iota((1, n_tok), 1)
    group = row // span_rows
    span = group % SPANS
    hot = sum(jnp.where(span == s, info[s], 0) for s in range(SPANS)).astype(jnp.float32)

    slot = pl.program_id(0) * n_slot + iota((n_slot, 1), 0)
    dest, local = slot // 32, slot // 16 % 2
    expert = ((dest // 4 * 2 + zh) * 4 + dest % 4) * 4 + c * 2 + local
    expert = expert.astype(jnp.float32)
    gate = jnp.zeros((n_slot, n_tok), jnp.float32)
    hits = jnp.zeros((n_slot, n_tok), jnp.float32)
    hot_gate = jnp.zeros((1, n_tok), jnp.float32)
    for k in range(top_k):
        ids, gates = meta_ref[k : k + 1], meta_ref[top_k + k : top_k + k + 1]
        same = expert == ids
        gate = jnp.where(same, gates, gate)
        hits = jnp.where(same, 1.0, hits)
        hot_gate += jnp.where(ids == hot, gates, 0.0)
    named = jnp.where(expert == hot, 0.0, hits)
    before, after = iota((n_tok, n_tok), 0), iota((n_tok, n_tok), 1)
    earlier = (before // span_rows == after // span_rows) & (before < after)
    earlier = jnp.where(earlier, 1.0, 0.0).astype(jnp.bfloat16)
    rank = dot(named.astype(jnp.bfloat16), earlier, 1, 0)
    at = (slot // CAPACITY % (2 * SPANS)) == group
    chosen = (named > 0.5) & at & (rank == (slot % CAPACITY).astype(jnp.float32))
    pick = jnp.where(chosen, 1.0, 0.0).astype(jnp.bfloat16)
    sent = dot(pick[:, :tok_dev], a_ref[...], 1, 0) + dot(pick[:, tok_dev:], b_ref[...], 1, 0)
    send_ref[...] = sent.astype(jnp.bfloat16)
    mix_ref[...] = jnp.where(chosen, gate, 0.0).astype(jnp.bfloat16)
    hot_row = iota((2 * span_rows, 1), 0)
    hot_row = hot_row // span_rows * tok_dev + (2 * zh + c) * span_rows + hot_row % span_rows
    hot_mix_ref[...] = jnp.where(hot_row == row, hot_gate, 0.0).astype(jnp.bfloat16)


def route(info, meta, a, b):
    tok_dev, width = a.shape
    n_slot = 32 * 2 * SPANS * CAPACITY
    steps = 4
    span_rows = tok_dev // SPANS
    shapes = (
        jax.ShapeDtypeStruct((n_slot, width), jnp.bfloat16),
        jax.ShapeDtypeStruct((n_slot, 2 * tok_dev), jnp.bfloat16),
        jax.ShapeDtypeStruct((2 * span_rows, 2 * tok_dev), jnp.bfloat16),
    )
    return pl.pallas_call(
        route_kernel,
        out_shape=shapes,
        grid_spec=pltpu.PrefetchScalarGridSpec(
            num_scalar_prefetch=1,
            grid=(steps,),
            in_specs=[whole(meta.shape), whole(a.shape), whole(b.shape)],
            out_specs=(
                pl.BlockSpec((n_slot // steps, width), lambda i, info: (i, 0)),
                pl.BlockSpec((n_slot // steps, 2 * tok_dev), lambda i, info: (i, 0)),
                whole(shapes[2].shape),
            ),
        ),
        compiler_params=PARAMS,
        cost_estimate=cost(4 * n_slot * tok_dev * width, 2 * width * (n_slot + 2 * tok_dev)),
    )(info, meta, a, b)


def ffn_kernel(x_ref, gate_ref, up_ref, down_ref, out_ref):
    n_src, rows, width = x_ref.shape
    x = x_ref[...].reshape(n_src * rows, width)
    gate = dot(x, gate_ref[0], 1, 1)
    up = dot(x, up_ref[0], 1, 1)
    hidden = (jax.nn.silu(gate) * up).astype(jnp.bfloat16)
    out = dot(hidden, down_ref[0], 1, 0).astype(jnp.bfloat16)
    out_ref[...] = out.reshape(n_src, rows, width)


def ffn(x, w_gate, w_up, w_down):
    n_src, rows, width = x.shape
    exp_dev, units, _ = w_gate.shape
    steps = 2
    block = pl.BlockSpec((n_src // steps, rows // exp_dev, width), lambda e, i: (i, e, 0))
    w_spec = pl.BlockSpec((1, units, width), lambda e, i: (e, 0, 0))
    return pl.pallas_call(
        ffn_kernel,
        out_shape=jax.ShapeDtypeStruct(x.shape, jnp.bfloat16),
        grid=(exp_dev, steps),
        in_specs=[block, w_spec, w_spec, w_spec],
        out_specs=block,
        compiler_params=PARAMS,
        cost_estimate=cost(6 * n_src * rows * units * width, 4 * x.size + 6 * w_gate.size),
    )(x, w_gate, w_up, w_down)


def mix_kernel(mix_ref, hot_mix_ref, ret_ref, hot_ref, own_ref, other_ref):
    out = dot(mix_ref[...], ret_ref[...], 0, 0) + dot(hot_mix_ref[...], hot_ref[...], 0, 0)
    out = out.astype(jnp.bfloat16)
    half = out.shape[0] // 2
    own_ref[0] = out[:half]
    other_ref[0] = out[half:]


def mix_rows(mix, hot_mix, returned, hot):
    n_slot, n_tok = mix.shape
    width = returned.shape[1]
    n_group = lax.axis_size("t")
    cols = width // n_group
    shape = jax.ShapeDtypeStruct((n_group, n_tok // 2, cols), jnp.bfloat16)
    out = pl.BlockSpec((1, n_tok // 2, cols), lambda i: (i, 0, 0))
    return pl.pallas_call(
        mix_kernel,
        out_shape=(shape, shape),
        grid=(n_group,),
        in_specs=[
            whole(mix.shape),
            whole(hot_mix.shape),
            pl.BlockSpec((n_slot, cols), lambda i: (0, i)),
            pl.BlockSpec((hot.shape[0], cols), lambda i: (0, i)),
        ],
        out_specs=(out, out),
        compiler_params=PARAMS,
        cost_estimate=cost(2 * n_slot * n_tok * width, 2 * width * (n_slot + n_tok)),
    )(mix, hot_mix, returned, hot)


def exchange(send):
    rows, width = send.shape
    out = lax.all_to_all(send.reshape(16, rows // 16, width), ("y", "x"), 0, 0, tiled=True)
    return out


def pieces_of(own, other, t, axes, perm_of, first):
    got = lax.ppermute(other, "c", SWAP)
    pieces = []
    n_group = own.shape[0]
    for shift in range(n_group):
        q = (t + shift) % n_group
        piece = lax.dynamic_index_in_dim(own, q, 0, keepdims=False).astype(jnp.float32)
        piece += lax.dynamic_index_in_dim(got, q, 0, keepdims=False).astype(jnp.float32)
        if shift >= first:
            piece = lax.ppermute(piece.astype(jnp.bfloat16), axes, perm_of(shift))
        pieces.append(piece.astype(jnp.float32))
    return pieces


def per_device(tokens, expert_ids, gate_values, hot_ids, w_gate, w_up, w_down):
    zh = lax.axis_index("zh")
    c = lax.axis_index("c")
    t = lax.axis_index("t")
    n_t = lax.axis_size("t")
    info = jnp.concatenate([hot_ids, jnp.stack([zh, c]).astype(jnp.int32)])

    meta = jnp.concatenate([expert_ids.astype(jnp.float32), gate_values], axis=1).T
    tok_z = lax.ppermute(tokens, "zh", SWAP)
    meta_z = lax.ppermute(meta, "zh", SWAP)
    tok_c = lax.ppermute(tokens, "c", SWAP)
    meta_c = lax.ppermute(meta, "c", SWAP)
    tok_zc = lax.ppermute(tok_z, "c", SWAP)
    meta_zc = lax.ppermute(meta_z, "c", SWAP)

    hot_w = fetch_hot(hot_ids, (w_gate, w_up, w_down), zh, c)

    near, near_mix, near_hot_mix = route(
        info, jnp.concatenate([meta, meta_c], axis=1), tokens, tok_c
    )
    near = exchange(near)
    far, far_mix, far_hot_mix = route(
        info, jnp.concatenate([meta_z, meta_zc], axis=1), tok_z, tok_zc
    )
    far = exchange(far)
    n_slot = near_mix.shape[0]
    width = tokens.shape[1]
    near = exchange(ffn(near, w_gate, w_up, w_down).reshape(n_slot, width)).reshape(n_slot, width)
    far = exchange(ffn(far, w_gate, w_up, w_down).reshape(n_slot, width)).reshape(n_slot, width)

    near_hot, far_hot = hot_ffn(info, (tokens, tok_c, tok_z, tok_zc), hot_w)
    own, other = mix_rows(near_mix, near_hot_mix, near, near_hot)
    pieces = pieces_of(
        own, other, t, "t", lambda k: [(i, (i + k) % n_t) for i in range(n_t)], 1
    )
    own, other = mix_rows(far_mix, far_hot_mix, far, far_hot)
    pieces += pieces_of(
        own,
        other,
        t,
        ("zh", "t"),
        lambda k: [(z * n_t + i, (1 - z) * n_t + (i + k) % n_t) for z in (0, 1) for i in range(n_t)],
        0,
    )
    return sum(pieces).astype(jnp.bfloat16)


def solution(mesh):
    fine = Mesh(mesh.devices.reshape(4, 2, 4, 2, 4), ("y", "zh", "x", "c", "t"))
    owner = ("y", "zh", "x", "c")
    in_specs = (
        P(owner, None),
        P(owner, None),
        P(owner, None),
        P(),
        P(owner, "t", None),
        P(owner, "t", None),
        P(owner, "t", None),
    )
    return jax.shard_map(
        per_device, mesh=fine, in_specs=in_specs, out_specs=P(owner, "t"), check_vma=False
    )
```

time: 308 us -> 285 us (0.925)
  starting transfers between devices: 38.4 us -> 88.9 us
  Pallas kernels: 0 us -> 38.3 us
  blocking collectives: 33.2 us -> 0 us
  matrix products: 29.3 us -> 0 us
  waiting for transfers between devices: 126 us -> 101 us
  other arithmetic: 23.4 us -> 9.26 us
  local copies, waits for them, and re-layouts: 24.7 us -> 16.8 us
    all_to_all x2 -> x4, waiting for transfers between devices: 103 us -> 43.3 us  [exchange(): lax.all_to_all(send.reshape(16, rows // 16, width), ('y', 'x'), 0, 0, til...]
    pallas_call x0 -> x8, Pallas kernels: none -> 38.3 us  [the longest x2 13.7 us: ffn(): pl.pallas_call(ffn_kernel, out_shape=jax.ShapeDtypeStruct(x.shape, jnp.bf...]
    all_to_all x1 -> x0, blocking collectives: 33.2 us -> none  [per_device(): pieces = lax.all_to_all(summed, ('zh', 't'), 0, 0, tiled=True)]
    dot_general x8 -> x0, matrix products: 29.3 us -> none  [the longest x6 17.8 us: dot(): lax.dot_general(a, b, (dims, ((), ())), preferred_element_type=jnp.float32)]
    all_gather x1, waiting for transfers between devices: 0.02 us -> 29.2 us  [fetch_hot(): return lax.all_gather(both, ('y', 'x'), axis=0, tiled=False)]
    ppermute x2 -> x11, starting transfers between devices: 0.1 us -> 25.9 us  [the longest x7 24.6 us: pieces_of(): piece = lax.ppermute(piece.astype(jnp.bfloat16), axes, perm_of(shift))]
    all_to_all x2 -> x4, starting transfers between devices: 17 us -> 32.5 us  [exchange(): lax.all_to_all(send.reshape(16, rows // 16, width), ('y', 'x'), 0, 0, til...]
    ppermute x1, starting transfers between devices: 0.09 us -> 14.1 us  [per_device(): meta_z = lax.ppermute(meta, 'zh', SWAP)]
  transfers between devices with their start and end apart: 13 -> 24, of which waited for: 7 -> 12; matrix products, arithmetic and copies ran while one was open for 20% -> 3% of each run, Pallas kernels for 0% -> 10%
where the time goes in v2:
time: 285 us; the launch traced here: 282 us
  waiting for transfers between devices  101 us (35%)
  starting transfers between devices  88.9 us (31%)
  Pallas kernels  38.3 us (13%)
  between operations  28 us (10%)
  local copies, waits for them, and re-layouts  16.8 us (6%)
  other arithmetic  9.26 us (3%)
    all_to_all x4, waiting for transfers between devices, exchange(): lax.all_to_all(send.reshape(16, rows // 16, width), ('y', 'x'), 0, 0, til...  43.3 us
    all_to_all x4, starting transfers between devices, exchange(): lax.all_to_all(send.reshape(16, rows // 16, width), ('y', 'x'), 0, 0, til...  32.5 us
    all_gather x1, waiting for transfers between devices, fetch_hot(): return lax.all_gather(both, ('y', 'x'), axis=0, tiled=False)  29.2 us
    ppermute x7, starting transfers between devices, pieces_of(): piece = lax.ppermute(piece.astype(jnp.bfloat16), axes, perm_of(shift))  24.6 us
    ppermute x1, starting transfers between devices, per_device(): meta_z = lax.ppermute(meta, 'zh', SWAP)  14.1 us
    pallas_call x2, Pallas kernels, ffn(): pl.pallas_call(ffn_kernel, out_shape=jax.ShapeDtypeStruct(x.shape, jnp.bf...  13.7 us
    unnamed x38, local copies, waits for them, and re-layouts  13.3 us
    ppermute x7, waiting for transfers between devices, pieces_of(): piece = lax.ppermute(piece.astype(jnp.bfloat16), axes, perm_of(shift))  12.1 us
  transfers between devices with their start and end apart: 24, of which 12 were waited for; matrix products, arithmetic and copies ran while one was open for 3% of the time, Pallas kernels for 10%

profile of v2, /device:TPU:2, one launch (start us, length us, event | category | flops | bytes accessed | tf_op | source)
XLA Modules:
  0.0 282.4 jit_solution(17021988399855009905)
XLA Ops:
  9.6 9.6 %shard_map.75 = (bf16[16,288,128]{2,1,0:T(8,128)(2,1)S(1)}, bf16[16,288,128]{2,1,0:T(8,128)(2,1)}) custom-call(s32[2]{0:T(128)S(1)} %pad_add_fusion.2.info, bf16[2,192,2048]{2,1,0:T(8,128)(2,1)} %gate_ref.5, bf16[2,192,2048]{2,1,0:T(8,128)(2,1)} %up_ref.5, bf16[2,192,2048]{2,1,0:T(8,128)(2,1)} %down_ref.5), custom_call_target="tpu_custom_call" | custom-call | bytes 4718592 | tf_op jit(solution)/shard_map/pallas_call | solution.py:64
  19.2 7.3 %collective-permute-start.3 = (bf16[128,2048]{1,0:T(8,128)(2,1)S(1)}, bf16[128,2048]{1,0:T(8,128)(2,1)S(1)}, u32[]{:S(2)}, u32[]{:S(2)}) collective-permute-start(bf16[128,2048]{1,0:T(8,128)(2,1)S(1)} %copy-done.6), channel_id=1, source_target_pairs={{0,32},{32,0},{1,33},{33,1},{2,34},{34,2},{3,35},{35,3},{4,36},{36... | collective-permute-start | bytes 1572872 | tf_op jit(solution)/shard_map/ppermute | solution.py:314
  28.3 7.6 %all-to-all-start.3 = ((bf16[16,288,128]{2,1,0:T(8,128)(2,1)}), bf16[16,288,128]{2,1,0:T(8,128)(2,1)S(1)}, u32[]{:S(2)}, u32[]{:S(2)}) async-start(bf16[16,288,128]{2,1,0:T(8,128)(2,1)} %broadcast_select_fusion.1), calls=%async_computation.3 | async-start | bytes 2359296 | tf_op jit(solution)/shard_map/all_to_all | solution.py:84
  35.9 5.3 %collective-permute-done.3.refs_2_.a_ref = bf16[128,2048]{1,0:T(8,128)(2,1)S(1)} collective-permute-done((bf16[128,2048]{1,0:T(8,128)(2,1)S(1)}, bf16[128,2048]{1,0:T(8,128)(2,1)S(1)}, u32[]{:S(2)}, u32[]{:S(2)}) %collective-permute-start.3) | collective-permute-done | bytes 524320 | tf_op jit(solution)/shard_map/ppermute | solution.py:314
  41.2 14.1 %collective-permute-start.12 = (f32[16,128]{1,0:T(8,128)S(1)}, f32[16,128]{1,0:T(8,128)S(1)}, u32[]{:S(2)}, u32[]{:S(2)}) collective-permute-start(f32[16,128]{1,0:T(8,128)S(1)} %maximum_bitcast_fusion), channel_id=1, source_target_pairs={{0,32},{32,0},{1,33},{33,1},{2,34},{34,2},{3,35},{35,3},{4,36},{36... | collective-permute-start | bytes 24584 | tf_op jit(solution)/shard_map/ppermute | solution.py:315
  70.7 4.0 %shard_map.78 = (bf16[512,2048]{1,0:T(8,128)(2,1)S(1)}, bf16[512,256]{1,0:T(8,128)(2,1)S(1)}, bf16[64,256]{1,0:T(8,128)(2,1)S(1)}) custom-call(s32[6]{0:T(128)S(1)} %pad_add_fusion.1.info, f32[16,256]{1,0:T(8,128)S(1)} %pad_maximum_fusion.3.meta_ref, bf16[128,2048]{1,0:T(8,128)(2,1)S(1)} %collective-permute-done.3.refs_2_.a_ref, ...), custom_call_target="tpu_custom_call" | custom-call | flops 536870912 | bytes 3145728 | tf_op jit(solution)/shard_map/pallas_call | solution.py:210
  76.9 7.5 %all-to-all-start.4 = ((bf16[16,32,2048]{2,1,0:T(8,128)(2,1)}), bf16[16,32,2048]{2,1,0:T(8,128)(2,1)S(1)}, u32[]{:S(2)}, u32[]{:S(2)}) async-start(bf16[16,32,2048]{2,1,0:T(8,128)(2,1)} %bitcast.71), calls=%async_computation.4 | async-start | bytes 4194304 | tf_op jit(solution)/shard_map/all_to_all | solution.py:288
  86.3 4.0 %shard_map.73 = (bf16[512,2048]{1,0:T(8,128)(2,1)S(1)}, bf16[512,256]{1,0:T(8,128)(2,1)S(1)}, bf16[64,256]{1,0:T(8,128)(2,1)S(1)}) custom-call(s32[6]{0:T(128)S(1)} %pad_add_fusion.1.info, f32[16,256]{1,0:T(8,128)S(1)} %pad_maximum_fusion.2.meta_ref, bf16[128,2048]{1,0:T(8,128)(2,1)S(1)} %copy-done.6, bf16[128,2048]{1,0:T(8,128)(2,1)S(1)} %collective-permute-done.2.b_ref.refs_1_), custom_call_target="tpu_custom_call" | custom-call | flops 536870912 | bytes 3145728 | tf_op jit(solution)/shard_map/pallas_call | solution.py:210
  93.1 20.2 %all-to-all-done.4.x_ref = bf16[16,32,2048]{2,1,0:T(8,128)(2,1)S(1)} async-done(((bf16[16,32,2048]{2,1,0:T(8,128)(2,1)}), bf16[16,32,2048]{2,1,0:T(8,128)(2,1)S(1)}, u32[]{:S(2)}, u32[]{:S(2)}) %all-to-all-start.4) | async-done | bytes 2097184 | tf_op jit(solution)/shard_map/all_to_all | solution.py:288
  113.3 9.1 %all-to-all-start.1 = ((bf16[16,32,2048]{2,1,0:T(8,128)(2,1)}), bf16[16,32,2048]{2,1,0:T(8,128)(2,1)}, u32[]{:S(2)}, u32[]{:S(2)}) async-start(bf16[16,32,2048]{2,1,0:T(8,128)(2,1)} %bitcast.72), calls=%async_computation.1 | async-start | bytes 4194304 | tf_op jit(solution)/shard_map/all_to_all | solution.py:288
  125.5 8.2 %collective-permute-done.6 = bf16[2,288,128]{2,1,0:T(8,128)(2,1)} collective-permute-done((bf16[2,288,128]{2,1,0:T(8,128)(2,1)}, bf16[2,288,128]{2,1,0:T(8,128)(2,1)}, u32[]{:S(2)}, u32[]{:S(2)}) %collective-permute-start.6) | collective-permute-done | bytes 147488 | tf_op jit(solution)/shard_map/ppermute | solution.py:110
  138.7 6.1 %shard_map.79 = bf16[16,32,2048]{2,1,0:T(8,128)(2,1)S(1)} custom-call(bf16[16,32,2048]{2,1,0:T(8,128)(2,1)S(1)} %all-to-all-done.4.x_ref, bf16[2,192,2048]{2,1,0:T(8,128)(2,1)} %get-tuple-element.1549, bf16[2,192,2048]{2,1,0:T(8,128)(2,1)} %get-tuple-element.1550, bf16[2,192,2048]{2,1,0:T(8,128)(2,1)} %get-tuple-element.1551), custom_call_target="tpu_custom_call" | custom-call | flops 1207959552 | bytes 8912896 | tf_op jit(solution)/shard_map/pallas_call | solution.py:244
  146.2 3.2 %all-to-all-done.1.x_ref = bf16[16,32,2048]{2,1,0:T(8,128)(2,1)} async-done(((bf16[16,32,2048]{2,1,0:T(8,128)(2,1)}), bf16[16,32,2048]{2,1,0:T(8,128)(2,1)}, u32[]{:S(2)}, u32[]{:S(2)}) %all-to-all-start.1) | async-done | bytes 2097184 | tf_op jit(solution)/shard_map/all_to_all | solution.py:288
  149.4 7.6 %all-to-all-start.5 = ((bf16[16,32,2048]{2,1,0:T(8,128)(2,1)}), bf16[16,32,2048]{2,1,0:T(8,128)(2,1)S(1)}, u32[]{:S(2)}, u32[]{:S(2)}) async-start(bf16[16,32,2048]{2,1,0:T(8,128)(2,1)} %copy-done), calls=%async_computation.5 | async-start | bytes 4194304 | tf_op jit(solution)/shard_map/all_to_all | solution.py:288
  156.9 7.6 %shard_map.74 = bf16[16,32,2048]{2,1,0:T(8,128)(2,1)} custom-call(bf16[16,32,2048]{2,1,0:T(8,128)(2,1)} %all-to-all-done.1.x_ref, bf16[2,192,2048]{2,1,0:T(8,128)(2,1)} %get-tuple-element.1549, bf16[2,192,2048]{2,1,0:T(8,128)(2,1)} %get-tuple-element.1550, bf16[2,192,2048]{2,1,0:T(8,128)(2,1)} %get-tuple-element.1551), custom_call_target="tpu_custom_call" | custom-call | flops 1207959552 | bytes 8912896 | tf_op jit(solution)/shard_map/pallas_call | solution.py:244
  164.5 20.0 %all-to-all-done.5 = bf16[16,32,2048]{2,1,0:T(8,128)(2,1)S(1)} async-done(((bf16[16,32,2048]{2,1,0:T(8,128)(2,1)}), bf16[16,32,2048]{2,1,0:T(8,128)(2,1)S(1)}, u32[]{:S(2)}, u32[]{:S(2)}) %all-to-all-start.5) | async-done | bytes 2097184 | tf_op jit(solution)/shard_map/all_to_all | solution.py:288
  185.9 8.3 %all-to-all-start.2 = ((bf16[16,32,2048]{2,1,0:T(8,128)(2,1)}), bf16[16,32,2048]{2,1,0:T(8,128)(2,1)S(1)}, u32[]{:S(2)}, u32[]{:S(2)}) async-start(bf16[16,32,2048]{2,1,0:T(8,128)(2,1)} %shard_map.74), calls=%async_computation.2 | async-start | bytes 4194304 | tf_op jit(solution)/shard_map/all_to_all | solution.py:288
  194.2 29.2 %all-gather.2.cloned.1.call-done.refs_4_ = bf16[16,576,128]{2,1,0:T(8,128)(2,1)} async-done(((bf16[1,576,128]{2,1,0:T(8,128)(2,1)}), bf16[16,576,128]{2,1,0:T(8,128)(2,1)}) %all-gather.2.cloned.1.call-update) | async-done | bytes 2359312 | tf_op jit(solution)/shard_map/all_gather | solution.py:119
  237.9 9.0 %collective-permute-start.15 = (bf16[128,512]{1,0:T(8,128)(2,1)S(1)}, bf16[128,512]{1,0:T(8,128)(2,1)S(1)}, u32[]{:S(2)}, u32[]{:S(2)}) collective-permute-start(bf16[128,512]{1,0:T(8,128)(2,1)S(1)} %get-tuple-element.1295), channel_id=1, source_target_pairs={{0,32},{1,33},{2,34},{3,35},{32,0},{33,1},{34,2},{35,3},{4,36},{5,... | collective-permute-start | bytes 393224 | tf_op jit(solution)/shard_map/ppermute | solution.py:301
  247.4 4.1 %collective-permute-start.17 = (bf16[128,512]{1,0:T(8,128)(2,1)S(1)}, bf16[128,512]{1,0:T(8,128)(2,1)S(1)}, u32[]{:S(2)}, u32[]{:S(2)}) collective-permute-start(bf16[128,512]{1,0:T(8,128)(2,1)S(1)} %get-tuple-element.1297), channel_id=1, source_target_pairs={{0,34},{1,35},{2,32},{3,33},{32,2},{33,3},{34,0},{35,1},{4,38},{5,... | collective-permute-start | bytes 393224 | tf_op jit(solution)/shard_map/ppermute | solution.py:301
  253.2 3.3 %collective-permute-start.11 = (bf16[128,512]{1,0:T(8,128)(2,1)S(1)}, bf16[128,512]{1,0:T(8,128)(2,1)S(1)}, u32[]{:S(2)}, u32[]{:S(2)}) collective-permute-start(bf16[128,512]{1,0:T(8,128)(2,1)S(1)} %get-tuple-element.1293), channel_id=1, source_target_pairs={{0,3},{1,0},{2,1},{3,2},{4,7},{5,4},{6,5},{7,6},{8,11},{9,8},{10,9... | collective-permute-start | bytes 393224 | tf_op jit(solution)/shard_map/ppermute | solution.py:301
  259.4 6.2 %collective-permute-start.10 = (bf16[128,512]{1,0:T(8,128)(2,1)S(1)}, bf16[128,512]{1,0:T(8,128)(2,1)S(1)}, u32[]{:S(2)}, u32[]{:S(2)}) collective-permute-start(bf16[128,512]{1,0:T(8,128)(2,1)S(1)} %get-tuple-element.1294), channel_id=1, source_target_pairs={{0,2},{1,3},{2,0},{3,1},{4,6},{5,7},{6,4},{7,5},{8,10},{9,11},{10,... | collective-permute-start | bytes 393224 | tf_op jit(solution)/shard_map/ppermute | solution.py:301
  265.6 3.2 %collective-permute-done.16 = bf16[128,512]{1,0:T(8,128)(2,1)S(1)} collective-permute-done((bf16[128,512]{1,0:T(8,128)(2,1)S(1)}, bf16[128,512]{1,0:T(8,128)(2,1)S(1)}, u32[]{:S(2)}, u32[]{:S(2)}) %collective-permute-start.16) | collective-permute-done | bytes 131104 | tf_op jit(solution)/shard_map/ppermute | solution.py:301
  268.7 6.0 %collective-permute-done.10 = bf16[128,512]{1,0:T(8,128)(2,1)S(1)} collective-permute-done((bf16[128,512]{1,0:T(8,128)(2,1)S(1)}, bf16[128,512]{1,0:T(8,128)(2,1)S(1)}, u32[]{:S(2)}, u32[]{:S(2)}) %collective-permute-start.10) | collective-permute-done | bytes 131104 | tf_op jit(solution)/shard_map/ppermute | solution.py:301
  (94 shorter events, 43.9 us)
Async XLA Ops:
  19.2 8.0 %collective-permute-start.5 = (bf16[16,288,128]{2,1,0:T(8,128)(2,1)}, bf16[16,288,128]{2,1,0:T(8,128)(2,1)}, u32[]{:S(2)}, u32[]{:S(2)}) collective-permute-start(bf16[16,288,128]{2,1,0:T(8,128)(2,1)} %get-tuple-element.1219), channel_id=1, source_target_pairs={{0,4},{4,0},{1,5},{5,1},{2,6},{6,2},{3,7},{7,3},{8,12},{12,8},{9,1... | collective-permute-start | bytes 3538952 | tf_op jit(solution)/shard_map/ppermute | solution.py:82
  19.2 22.0 %collective-permute-start.3 = (bf16[128,2048]{1,0:T(8,128)(2,1)S(1)}, bf16[128,2048]{1,0:T(8,128)(2,1)S(1)}, u32[]{:S(2)}, u32[]{:S(2)}) collective-permute-start(bf16[128,2048]{1,0:T(8,128)(2,1)S(1)} %copy-done.6), channel_id=1, source_target_pairs={{0,32},{32,0},{1,33},{33,1},{2,34},{34,2},{3,35},{35,3},{4,36},{36... | collective-permute-start | bytes 1572872 | tf_op jit(solution)/shard_map/ppermute | solution.py:314
  28.3 47.7 %all-to-all-start.3 = ((bf16[16,288,128]{2,1,0:T(8,128)(2,1)}), bf16[16,288,128]{2,1,0:T(8,128)(2,1)S(1)}, u32[]{:S(2)}, u32[]{:S(2)}) async-start(bf16[16,288,128]{2,1,0:T(8,128)(2,1)} %broadcast_select_fusion.1), calls=%async_computation.3 | async-start | bytes 2359296 | tf_op jit(solution)/shard_map/all_to_all | solution.py:84
  41.2 29.5 %collective-permute-start.4 = (bf16[128,2048]{1,0:T(8,128)(2,1)S(1)}, bf16[128,2048]{1,0:T(8,128)(2,1)S(1)}, u32[]{:S(2)}, u32[]{:S(2)}) collective-permute-start(bf16[128,2048]{1,0:T(8,128)(2,1)S(1)} %collective-permute-done.3.refs_2_.a_ref), channel_id=1, source_target_pairs={{0,4},{4,0},{1,5},{5,1},{2,6},{6,2},{3,7},{7,3},{8,12},{12,8},{9,1... | collective-permute-start | bytes 1572872 | tf_op jit(solution)/shard_map/ppermute | solution.py:318
  41.2 20.5 %collective-permute-start.12 = (f32[16,128]{1,0:T(8,128)S(1)}, f32[16,128]{1,0:T(8,128)S(1)}, u32[]{:S(2)}, u32[]{:S(2)}) collective-permute-start(f32[16,128]{1,0:T(8,128)S(1)} %maximum_bitcast_fusion), channel_id=1, source_target_pairs={{0,32},{32,0},{1,33},{33,1},{2,34},{34,2},{3,35},{35,3},{4,36},{36... | collective-permute-start | bytes 24584 | tf_op jit(solution)/shard_map/ppermute | solution.py:315
  61.7 8.9 %collective-permute-start.13 = (f32[16,128]{1,0:T(8,128)S(1)}, f32[16,128]{1,0:T(8,128)S(1)}, u32[]{:S(2)}, u32[]{:S(2)}) collective-permute-start(f32[16,128]{1,0:T(8,128)S(1)} %collective-permute-done.12), channel_id=1, source_target_pairs={{0,4},{4,0},{1,5},{5,1},{2,6},{6,2},{3,7},{7,3},{8,12},{12,8},{9,1... | collective-permute-start | bytes 24584 | tf_op jit(solution)/shard_map/ppermute | solution.py:319
  76.9 36.4 %all-to-all-start.4 = ((bf16[16,32,2048]{2,1,0:T(8,128)(2,1)}), bf16[16,32,2048]{2,1,0:T(8,128)(2,1)S(1)}, u32[]{:S(2)}, u32[]{:S(2)}) async-start(bf16[16,32,2048]{2,1,0:T(8,128)(2,1)} %bitcast.71), calls=%async_computation.4 | async-start | bytes 4194304 | tf_op jit(solution)/shard_map/all_to_all | solution.py:288
  84.4 1.9 collective-permute-start.2
  84.4 1.9 collective-permute-start.1
  113.3 36.1 %all-to-all-start.1 = ((bf16[16,32,2048]{2,1,0:T(8,128)(2,1)}), bf16[16,32,2048]{2,1,0:T(8,128)(2,1)}, u32[]{:S(2)}, u32[]{:S(2)}) async-start(bf16[16,32,2048]{2,1,0:T(8,128)(2,1)} %bitcast.72), calls=%async_computation.1 | async-start | bytes 4194304 | tf_op jit(solution)/shard_map/all_to_all | solution.py:288
  122.4 101.0 %all-gather.2.cloned.1.call-start = ((), (), s32[]{:S(2)}) async-start(), calls=%async_computation.6 | async-start | bytes 2506752 | tf_op jit(solution)/shard_map/all_gather | solution.py:119
  124.0 9.7 %collective-permute-start.6 = (bf16[2,288,128]{2,1,0:T(8,128)(2,1)}, bf16[2,288,128]{2,1,0:T(8,128)(2,1)}, u32[]{:S(2)}, u32[]{:S(2)}) collective-permute-start(bf16[2,288,128]{2,1,0:T(8,128)(2,1)} %constant_dynamic-slice_fusion.1), channel_id=1, source_target_pairs={{0,32},{32,0},{1,33},{33,1},{2,34},{34,2},{3,35},{35,3},{4,36},{36... | collective-permute-start | bytes 442376 | tf_op jit(solution)/shard_map/ppermute | solution.py:110
  135.4 1.6 collective-permute-start.7
  149.4 35.1 %all-to-all-start.5 = ((bf16[16,32,2048]{2,1,0:T(8,128)(2,1)}), bf16[16,32,2048]{2,1,0:T(8,128)(2,1)S(1)}, u32[]{:S(2)}, u32[]{:S(2)}) async-start(bf16[16,32,2048]{2,1,0:T(8,128)(2,1)} %copy-done), calls=%async_computation.5 | async-start | bytes 4194304 | tf_op jit(solution)/shard_map/all_to_all | solution.py:288
  185.9 45.7 %all-to-all-start.2 = ((bf16[16,32,2048]{2,1,0:T(8,128)(2,1)}), bf16[16,32,2048]{2,1,0:T(8,128)(2,1)S(1)}, u32[]{:S(2)}, u32[]{:S(2)}) async-start(bf16[16,32,2048]{2,1,0:T(8,128)(2,1)} %shard_map.74), calls=%async_computation.2 | async-start | bytes 4194304 | tf_op jit(solution)/shard_map/all_to_all | solution.py:288
  231.6 5.1 %collective-permute-start.14 = (bf16[4,128,512]{2,1,0:T(8,128)(2,1)}, bf16[4,128,512]{2,1,0:T(8,128)(2,1)}, u32[]{:S(2)}, u32[]{:S(2)}) collective-permute-start(bf16[4,128,512]{2,1,0:T(8,128)(2,1)} %get-tuple-element.1229), channel_id=1, source_target_pairs={{0,4},{4,0},{1,5},{5,1},{2,6},{6,2},{3,7},{7,3},{8,12},{12,8},{9,1... | collective-permute-start | bytes 1572872 | tf_op jit(solution)/shard_map/ppermute | solution.py:293
  236.2 15.8 %collective-permute-start.8 = (bf16[4,128,512]{2,1,0:T(8,128)(2,1)}, bf16[4,128,512]{2,1,0:T(8,128)(2,1)S(1)}, u32[]{:S(2)}, u32[]{:S(2)}) collective-permute-start(bf16[4,128,512]{2,1,0:T(8,128)(2,1)} %get-tuple-element.1223), channel_id=1, source_target_pairs={{0,4},{4,0},{1,5},{5,1},{2,6},{6,2},{3,7},{7,3},{8,12},{12,8},{9,1... | collective-permute-start | bytes 1572872 | tf_op jit(solution)/shard_map/ppermute | solution.py:293
  237.9 15.3 %collective-permute-start.15 = (bf16[128,512]{1,0:T(8,128)(2,1)S(1)}, bf16[128,512]{1,0:T(8,128)(2,1)S(1)}, u32[]{:S(2)}, u32[]{:S(2)}) collective-permute-start(bf16[128,512]{1,0:T(8,128)(2,1)S(1)} %get-tuple-element.1295), channel_id=1, source_target_pairs={{0,32},{1,33},{2,34},{3,35},{32,0},{33,1},{34,2},{35,3},{4,36},{5,... | collective-permute-start | bytes 393224 | tf_op jit(solution)/shard_map/ppermute | solution.py:301
  246.9 12.5 %collective-permute-start.18 = (bf16[128,512]{1,0:T(8,128)(2,1)S(1)}, bf16[128,512]{1,0:T(8,128)(2,1)S(1)}, u32[]{:S(2)}, u32[]{:S(2)}) collective-permute-start(bf16[128,512]{1,0:T(8,128)(2,1)S(1)} %get-tuple-element.1296), channel_id=1, source_target_pairs={{0,35},{1,32},{2,33},{3,34},{32,3},{33,0},{34,1},{35,2},{4,39},{5,... | collective-permute-start | bytes 393224 | tf_op jit(solution)/shard_map/ppermute | solution.py:301
  247.4 18.2 %collective-permute-start.17 = (bf16[128,512]{1,0:T(8,128)(2,1)S(1)}, bf16[128,512]{1,0:T(8,128)(2,1)S(1)}, u32[]{:S(2)}, u32[]{:S(2)}) collective-permute-start(bf16[128,512]{1,0:T(8,128)(2,1)S(1)} %get-tuple-element.1297), channel_id=1, source_target_pairs={{0,34},{1,35},{2,32},{3,33},{32,2},{33,3},{34,0},{35,1},{4,38},{5,... | collective-permute-start | bytes 393224 | tf_op jit(solution)/shard_map/ppermute | solution.py:301
  251.4 17.3 %collective-permute-start.16 = (bf16[128,512]{1,0:T(8,128)(2,1)S(1)}, bf16[128,512]{1,0:T(8,128)(2,1)S(1)}, u32[]{:S(2)}, u32[]{:S(2)}) collective-permute-start(bf16[128,512]{1,0:T(8,128)(2,1)S(1)} %get-tuple-element.1298), channel_id=1, source_target_pairs={{0,33},{1,34},{2,35},{3,32},{32,1},{33,2},{34,3},{35,0},{4,37},{5,... | collective-permute-start | bytes 393224 | tf_op jit(solution)/shard_map/ppermute | solution.py:301
  252.1 16.6 %collective-permute-start.9 = (bf16[128,512]{1,0:T(8,128)(2,1)S(1)}, bf16[128,512]{1,0:T(8,128)(2,1)S(1)}, u32[]{:S(2)}, u32[]{:S(2)}) collective-permute-start(bf16[128,512]{1,0:T(8,128)(2,1)S(1)} %get-tuple-element.1292), channel_id=1, source_target_pairs={{0,1},{1,2},{2,3},{3,0},{4,5},{5,6},{6,7},{7,4},{8,9},{9,10},{10,1... | collective-permute-start | bytes 393224 | tf_op jit(solution)/shard_map/ppermute | solution.py:301
  253.2 15.5 %collective-permute-start.11 = (bf16[128,512]{1,0:T(8,128)(2,1)S(1)}, bf16[128,512]{1,0:T(8,128)(2,1)S(1)}, u32[]{:S(2)}, u32[]{:S(2)}) collective-permute-start(bf16[128,512]{1,0:T(8,128)(2,1)S(1)} %get-tuple-element.1293), channel_id=1, source_target_pairs={{0,3},{1,0},{2,1},{3,2},{4,7},{5,4},{6,5},{7,6},{8,11},{9,8},{10,9... | collective-permute-start | bytes 393224 | tf_op jit(solution)/shard_map/ppermute | solution.py:301
  259.4 15.4 %collective-permute-start.10 = (bf16[128,512]{1,0:T(8,128)(2,1)S(1)}, bf16[128,512]{1,0:T(8,128)(2,1)S(1)}, u32[]{:S(2)}, u32[]{:S(2)}) collective-permute-start(bf16[128,512]{1,0:T(8,128)(2,1)S(1)} %get-tuple-element.1294), channel_id=1, source_target_pairs={{0,2},{1,3},{2,0},{3,1},{4,6},{5,7},{6,4},{7,5},{8,10},{9,11},{10,... | collective-permute-start | bytes 393224 | tf_op jit(solution)/shard_map/ppermute | solution.py:301
  (19 other events, 81.6 us)
Sparse Core Ops, SparseCore 0:
  138.8 84.5 all-gather.1

commit v3 on v2

v3 whole, which is shorter than its diff:
```python
import jax
import jax.numpy as jnp
from jax import lax
from jax.experimental import pallas as pl
from jax.experimental.pallas import tpu as pltpu
from jax.sharding import Mesh, PartitionSpec as P

SPANS = 4
CAPACITY = 2
TOP_K = 8
SWAP = ((0, 1), (1, 0))
VMEM_LIMIT = 32 * 1024 * 1024


def dot(a, b, contract_a, contract_b):
    dims = (((contract_a,), (contract_b,)), ((), ()))
    return lax.dot_general(a, b, dims, preferred_element_type=jnp.float32)


def iota(shape, dim):
    return lax.broadcasted_iota(jnp.int32, shape, dim)


def cost(flops, moved):
    return pl.CostEstimate(flops=flops, bytes_accessed=moved, transcendentals=0)


PARAMS = pltpu.CompilerParams(vmem_limit_bytes=VMEM_LIMIT)


def whole(shape):
    return pl.BlockSpec(shape, lambda *_: (0,) * len(shape))


CHIP, Z_HI, CORE, TENSOR, TURN = 4, 5, 6, 7, 8


def chip_of(expert):
    return expert >> 2


def order_of(info, span):
    chip = chip_of(info[span])
    return sum(((chip_of(info[s]) == chip) & (s < span)).astype(jnp.int32) for s in range(SPANS))


def my_turn(info):
    return sum(
        jnp.where((chip_of(info[s]) == info[CHIP]) & (order_of(info, s) == info[TURN]), info[s], 0)
        for s in range(SPANS)
    )


def chunk_kernel(info, gate_ref, up_ref, down_ref, keep_ref, give_ref):
    units = gate_ref.shape[1]
    mid = units // 2
    n_chunk, _, lane = keep_ref.shape

    def first(out):
        for n in range(n_chunk):
            at = slice(n * lane, (n + 1) * lane)
            out[n, :units] = gate_ref[0, :, at]
            out[n, units:] = up_ref[0, :mid, at]

    def second(out):
        for n in range(n_chunk):
            at = slice(n * lane, (n + 1) * lane)
            out[n, :mid] = up_ref[0, mid:, at]
            out[n, mid:] = down_ref[0, :, at]

    @pl.when(info[CORE] == 0)
    def _():
        first(keep_ref)
        second(give_ref)

    @pl.when(info[CORE] == 1)
    def _():
        second(keep_ref)
        first(give_ref)


def cut_chunks(info, held):
    _, units, width = held[0].shape
    steps = 4
    half, lane = 3 * units // 2, width // 16
    spec = pl.BlockSpec((1, units, width // steps), lambda n, info: (my_turn(info) & 1, 0, n))
    out = pl.BlockSpec((16 // steps, half, lane), lambda n, info: (n, 0, 0))
    shape = jax.ShapeDtypeStruct((16, half, lane), jnp.bfloat16)
    return pl.pallas_call(
        chunk_kernel,
        out_shape=(shape, shape),
        grid_spec=pltpu.PrefetchScalarGridSpec(
            num_scalar_prefetch=1, grid=(steps,), in_specs=[spec] * 3, out_specs=(out, out)
        ),
        compiler_params=PARAMS,
        cost_estimate=cost(0, 4 * 3 * units * width),
    )(info, *held)


def choose_kernel(info, keep_ref, got_ref, out_ref):
    held_here = ((my_turn(info) >> 1) & 1) == info[CORE]

    @pl.when(held_here)
    def _():
        out_ref[...] = keep_ref[...]

    @pl.when(jnp.logical_not(held_here))
    def _():
        out_ref[...] = got_ref[...]


def choose(info, keep, got):
    return pl.pallas_call(
        choose_kernel,
        out_shape=jax.ShapeDtypeStruct(keep.shape, keep.dtype),
        grid_spec=pltpu.PrefetchScalarGridSpec(
            num_scalar_prefetch=1,
            grid=(1,),
            in_specs=[whole(keep.shape)] * 2,
            out_specs=whole(keep.shape),
        ),
        compiler_params=PARAMS,
        cost_estimate=cost(0, 6 * keep.size),
    )(info, keep, got)


def span_at(info, i):
    return (2 * info[Z_HI] + info[CORE]) ^ i


def take_kernel(info, part_ref, *refs):
    *old_refs, out_ref = refs
    span = span_at(info, pl.program_id(0))
    expert = info[span]
    here = (((expert >> 4) & 1) == info[Z_HI]) & (order_of(info, span) == info[TURN])
    if old_refs:
        out_ref[...] = jnp.where(here, part_ref[...], old_refs[0][...])
    else:
        out_ref[...] = part_ref[...]


def take(info, part, *old):
    block = (1, *part.shape[1:])

    def source(i, info):
        expert = info[span_at(info, i)]
        return ((expert >> 5) * 4 + ((expert >> 2) & 3), 0, 0)

    def same(i, info):
        return (i, 0, 0)

    return pl.pallas_call(
        take_kernel,
        out_shape=jax.ShapeDtypeStruct((SPANS, *part.shape[1:]), part.dtype),
        grid_spec=pltpu.PrefetchScalarGridSpec(
            num_scalar_prefetch=1,
            grid=(SPANS,),
            in_specs=[pl.BlockSpec(block, source)] + [pl.BlockSpec(block, same)] * len(old),
            out_specs=pl.BlockSpec(block, same),
        ),
        compiler_params=PARAMS,
        cost_estimate=cost(0, 16 * block[1] * block[2]),
    )(info, part, *old)


def hot_round(info, held, *old):
    keep, give = cut_chunks(info, held)
    part = choose(info, keep, lax.ppermute(give, "c", SWAP))
    part = lax.all_to_all(part, ("y", "x"), 0, 0, tiled=True)
    return take(info, part, *old)


def pair_kernel(info, chunk_ref, got_ref, mine_ref, give_ref):
    for i, out_ref in enumerate((mine_ref, give_ref)):
        here = ((info[span_at(info, i)] >> 4) & 1) == info[Z_HI]
        out_ref[...] = jnp.where(here, chunk_ref[i], got_ref[i])


def pair(info, chunks, got):
    shape = jax.ShapeDtypeStruct(chunks.shape[1:], chunks.dtype)
    return pl.pallas_call(
        pair_kernel,
        out_shape=(shape, shape),
        grid_spec=pltpu.PrefetchScalarGridSpec(
            num_scalar_prefetch=1,
            grid=(1,),
            in_specs=[whole(got.shape)] * 2,
            out_specs=(whole(shape.shape), whole(shape.shape)),
        ),
        compiler_params=PARAMS,
        cost_estimate=cost(0, 12 * shape.size),
    )(info, chunks, got)


def fetch_hot(info, hot_ids, held, c):
    chips = chip_of(hot_ids)
    before = jnp.arange(SPANS)[None, :] < jnp.arange(SPANS)[:, None]
    turns = 1 + jnp.max(jnp.sum((chips[:, None] == chips[None, :]) & before, axis=1))
    chunks = hot_round(info, held)
    chunks = lax.fori_loop(
        1, turns, lambda turn, old: hot_round(info.at[TURN].set(turn), held, old), chunks
    )
    got = lax.ppermute(chunks[2:], "zh", SWAP)
    mine, give = pair(info, chunks, got)
    got = lax.ppermute(give, "c", SWAP)
    first, second = jnp.where(c == 0, mine, got), jnp.where(c == 0, got, mine)
    return jnp.concatenate([first, second], axis=0)


def along_y(chunk):
    n_y = lax.axis_size("y")
    column = [chunk]
    for k in range(1, n_y):
        column.append(lax.ppermute(chunk, "y", [(i, i ^ k) for i in range(n_y)]))
    return jnp.stack(column)


def shift_x(array, step):
    n_x = lax.axis_size("x")
    return lax.ppermute(array, "x", [(i, (i + step) % n_x) for i in range(n_x)])


def hot_kernel(info, *refs):
    *refs, near_ref, far_ref = refs
    tok_refs, w_refs = refs[:4], refs[4:]
    n_y, rows, lane = w_refs[0].shape
    units = rows // 3
    half = near_ref.shape[0]
    pieces = [(0, i, w_refs[0], i) for i in range(n_y)]
    pieces += [(3, i, w_refs[1], i) for i in range(n_y)]
    pieces += [(1, i, w_refs[2], i) for i in range(n_y)]
    pieces += [(2, i, w_refs[3 + i // 2], i % 2) for i in range(n_y)]

    def columns(far, i):
        start = ((info[CHIP] >> 3 ^ i) * 4 + ((info[CHIP] + far) & 3)) * lane
        return pl.ds(pl.multiple_of(start, lane), lane)

    proj = jnp.zeros((2 * half, 2 * units), jnp.float32)
    for far, i, w_ref, at in pieces:
        tok = jnp.concatenate([r[:, columns(far, i)] for r in tok_refs], axis=0)
        proj += dot(tok, w_ref[at, : 2 * units], 1, 1)
    hidden = (jax.nn.silu(proj[:, :units]) * proj[:, units:]).astype(jnp.bfloat16)
    for far, i, w_ref, at in pieces:
        out = dot(hidden, w_ref[at, 2 * units :], 1, 0).astype(jnp.bfloat16)
        near_ref[:, columns(far, i)] = out[:half]
        far_ref[:, columns(far, i)] = out[half:]


def hot_ffn(info, blocks, hot_w, rows):
    width = blocks[0].shape[1]
    w_size = sum(w.size for w in hot_w)
    spec = pl.BlockSpec((rows, width), lambda i, info: (span_at(info, 0), 0))
    shape = jax.ShapeDtypeStruct((2 * rows, width), jnp.bfloat16)
    return pl.pallas_call(
        hot_kernel,
        out_shape=(shape, shape),
        grid_spec=pltpu.PrefetchScalarGridSpec(
            num_scalar_prefetch=1,
            grid=(1,),
            in_specs=[spec] * 4 + [whole(w.shape) for w in hot_w],
            out_specs=(whole(shape.shape), whole(shape.shape)),
        ),
        compiler_params=PARAMS,
        cost_estimate=cost(8 * rows * w_size, 2 * w_size + 16 * rows * width),
    )(info, *blocks, *hot_w)


def pack(tokens, expert_ids, gate_values):
    tok_dev, width = tokens.shape
    meta = jnp.concatenate([expert_ids.astype(jnp.bfloat16), gate_values.astype(jnp.bfloat16)], axis=1)
    meta = meta.T.reshape(1, -1)
    meta = jnp.pad(meta, ((0, 7), (0, width - meta.shape[1])))
    return jnp.concatenate([tokens, meta], axis=0)


def route_kernel(info, a_ref, b_ref, send_ref, mix_ref, hot_mix_ref):
    zh, c = info[Z_HI], info[CORE]
    n_tok = mix_ref.shape[1]
    n_slot = send_ref.shape[0]
    tok_dev = n_tok // 2
    span_rows = tok_dev // SPANS

    def entry(k):
        at = slice(k * tok_dev, (k + 1) * tok_dev)
        row = jnp.concatenate(
            [a_ref[tok_dev : tok_dev + 8, at], b_ref[tok_dev : tok_dev + 8, at]], axis=1
        )
        return row.astype(jnp.float32)[:1]

    row = iota((1, n_tok), 1)
    group = row // span_rows
    span = group % SPANS
    hot = sum(jnp.where(span == s, info[s], 0) for s in range(SPANS)).astype(jnp.float32)

    slot = pl.program_id(0) * n_slot + iota((n_slot, 1), 0)
    dest, local = slot // 32, slot // 16 % 2
    expert = ((dest // 4 * 2 + zh) * 4 + dest % 4) * 4 + c * 2 + local
    expert = expert.astype(jnp.float32)
    gate = jnp.zeros((n_slot, n_tok), jnp.float32)
    hits = jnp.zeros((n_slot, n_tok), jnp.float32)
    hot_gate = jnp.zeros((1, n_tok), jnp.float32)
    for k in range(TOP_K):
        ids, gates = entry(k), entry(TOP_K + k)
        same = expert == ids
        gate = jnp.where(same, gates, gate)
        hits = jnp.where(same, 1.0, hits)
        hot_gate += jnp.where(ids == hot, gates, 0.0)
    named = jnp.where(expert == hot, 0.0, hits)
    before, after = iota((n_tok, n_tok), 0), iota((n_tok, n_tok), 1)
    earlier = (before // span_rows == after // span_rows) & (before < after)
    earlier = jnp.where(earlier, 1.0, 0.0).astype(jnp.bfloat16)
    rank = dot(named.astype(jnp.bfloat16), earlier, 1, 0)
    at = (slot // CAPACITY % (2 * SPANS)) == group
    chosen = (named > 0.5) & at & (rank == (slot % CAPACITY).astype(jnp.float32))
    pick = jnp.where(chosen, 1.0, 0.0).astype(jnp.bfloat16)
    sent = dot(pick[:, :tok_dev], a_ref[:tok_dev], 1, 0)
    sent += dot(pick[:, tok_dev:], b_ref[:tok_dev], 1, 0)
    send_ref[...] = sent.astype(jnp.bfloat16)
    mix_ref[...] = jnp.where(chosen, gate, 0.0).astype(jnp.bfloat16)
    hot_row = iota((2 * span_rows, 1), 0)
    hot_row = hot_row // span_rows * tok_dev + (2 * zh + c) * span_rows + hot_row % span_rows
    hot_mix_ref[...] = jnp.where(hot_row == row, hot_gate, 0.0).astype(jnp.bfloat16)


def route(info, a, b, tok_dev):
    width = a.shape[1]
    n_slot = 32 * 2 * SPANS * CAPACITY
    steps = 4
    span_rows = tok_dev // SPANS
    shapes = (
        jax.ShapeDtypeStruct((n_slot, width), jnp.bfloat16),
        jax.ShapeDtypeStruct((n_slot, 2 * tok_dev), jnp.bfloat16),
        jax.ShapeDtypeStruct((2 * span_rows, 2 * tok_dev), jnp.bfloat16),
    )
    return pl.pallas_call(
        route_kernel,
        out_shape=shapes,
        grid_spec=pltpu.PrefetchScalarGridSpec(
            num_scalar_prefetch=1,
            grid=(steps,),
            in_specs=[whole(a.shape), whole(b.shape)],
            out_specs=(
                pl.BlockSpec((n_slot // steps, width), lambda i, info: (i, 0)),
                pl.BlockSpec((n_slot // steps, 2 * tok_dev), lambda i, info: (i, 0)),
                whole(shapes[2].shape),
            ),
        ),
        compiler_params=PARAMS,
        cost_estimate=cost(4 * n_slot * tok_dev * width, 2 * width * (n_slot + 2 * tok_dev)),
    )(info, a, b)


def ffn_kernel(x_ref, gate_ref, up_ref, down_ref, out_ref):
    n_src, rows, width = x_ref.shape
    x = x_ref[...].reshape(n_src * rows, width)
    gate = dot(x, gate_ref[0], 1, 1)
    up = dot(x, up_ref[0], 1, 1)
    hidden = (jax.nn.silu(gate) * up).astype(jnp.bfloat16)
    out = dot(hidden, down_ref[0], 1, 0).astype(jnp.bfloat16)
    out_ref[...] = out.reshape(n_src, rows, width)


def ffn(x, w_gate, w_up, w_down):
    n_src, rows, width = x.shape
    exp_dev, units, _ = w_gate.shape
    steps = 2
    block = pl.BlockSpec((n_src // steps, rows // exp_dev, width), lambda e, i: (i, e, 0))
    w_spec = pl.BlockSpec((1, units, width), lambda e, i: (e, 0, 0))
    return pl.pallas_call(
        ffn_kernel,
        out_shape=jax.ShapeDtypeStruct(x.shape, jnp.bfloat16),
        grid=(exp_dev, steps),
        in_specs=[block, w_spec, w_spec, w_spec],
        out_specs=block,
        compiler_params=PARAMS,
        cost_estimate=cost(6 * n_src * rows * units * width, 4 * x.size + 6 * w_gate.size),
    )(x, w_gate, w_up, w_down)


def mix_kernel(info, mix_ref, hot_mix_ref, ret_ref, hot_ref, own_ref, other_ref):
    out = dot(mix_ref[...], ret_ref[...], 0, 0) + dot(hot_mix_ref[...], hot_ref[...], 0, 0)
    out = out.astype(jnp.bfloat16)
    half = out.shape[0] // 2
    own_ref[0] = out[:half]
    other_ref[0] = out[half:]


def mix_rows(info, mix, hot_mix, returned, hot):
    n_slot, n_tok = mix.shape
    width = returned.shape[1]
    n_group = lax.axis_size("t")
    cols = width // n_group
    shape = jax.ShapeDtypeStruct((n_group, n_tok // 2, cols), jnp.bfloat16)
    out = pl.BlockSpec((1, n_tok // 2, cols), lambda i, info: (i, 0, 0))
    return pl.pallas_call(
        mix_kernel,
        out_shape=(shape, shape),
        grid_spec=pltpu.PrefetchScalarGridSpec(
            num_scalar_prefetch=1,
            grid=(n_group,),
            in_specs=[
                whole(mix.shape),
                whole(hot_mix.shape),
                pl.BlockSpec((n_slot, cols), lambda i, info: (0, i ^ info[TENSOR])),
                pl.BlockSpec((hot.shape[0], cols), lambda i, info: (0, i ^ info[TENSOR])),
            ],
            out_specs=(out, out),
        ),
        compiler_params=PARAMS,
        cost_estimate=cost(2 * n_slot * n_tok * width, 2 * width * (n_slot + n_tok)),
    )(info, mix, hot_mix, returned, hot)


def exchange(send):
    rows, width = send.shape
    return lax.all_to_all(send.reshape(16, rows // 16, width), ("y", "x"), 0, 0, tiled=True)


def pieces_of(own, other, axes, perm_of, first):
    got = lax.ppermute(other, "c", SWAP)
    pieces = []
    for shift in range(own.shape[0]):
        piece = own[shift].astype(jnp.float32) + got[shift].astype(jnp.float32)
        if shift >= first:
            piece = lax.ppermute(piece.astype(jnp.bfloat16), axes, perm_of(shift))
        pieces.append(piece.astype(jnp.float32))
    return pieces


def per_device(tokens, expert_ids, gate_values, hot_ids, w_gate, w_up, w_down):
    y, zh, x, c, t = (lax.axis_index(name) for name in ("y", "zh", "x", "c", "t"))
    n_t = lax.axis_size("t")
    tok_dev, width = tokens.shape
    place = jnp.stack([(y * 2 + zh) * 4 + x, zh, c, t, 0]).astype(jnp.int32)
    info = jnp.concatenate([hot_ids, place])
    experts = (w_gate, w_up, w_down)

    own = pack(tokens, expert_ids, gate_values)
    own_z = lax.ppermute(own, "zh", SWAP)
    own_c = lax.ppermute(own, "c", SWAP)
    near, near_mix, near_hot_mix = route(info, own, own_c, tok_dev)
    n_slot = near.shape[0]

    hot_w = fetch_hot(info, hot_ids, experts, c)
    near, own_z = lax.optimization_barrier((near, own_z))
    near = exchange(near)
    hot_w = along_y(hot_w)
    own_zc = lax.ppermute(own_z, "c", SWAP)
    own_zc, hot_w = lax.optimization_barrier((own_zc, hot_w))
    far, far_mix, far_hot_mix = route(info, own_z, own_zc, tok_dev)
    far = exchange(far)
    hot_w = (hot_w, shift_x(hot_w, 1), shift_x(hot_w, -1))
    near, hot_w = lax.optimization_barrier((near, hot_w))
    near = exchange(ffn(near, *experts).reshape(n_slot, width)).reshape(n_slot, width)
    half = hot_w[0].shape[0] // 2
    hot_w += (shift_x(hot_w[1][:half], 1), shift_x(hot_w[2][half:], -1))
    far, hot_w = lax.optimization_barrier((far, hot_w))
    far = exchange(ffn(far, *experts).reshape(n_slot, width)).reshape(n_slot, width)

    near_hot, far_hot = hot_ffn(info, (own, own_c, own_z, own_zc), hot_w, tok_dev // SPANS)
    mine, other = mix_rows(info, near_mix, near_hot_mix, near, near_hot)
    pieces = pieces_of(mine, other, "t", lambda k: [(i, i ^ k) for i in range(n_t)], 1)
    far, pieces = lax.optimization_barrier((far, pieces))
    mine, other = mix_rows(info, far_mix, far_hot_mix, far, far_hot)
    pieces += pieces_of(
        mine,
        other,
        ("zh", "t"),
        lambda k: [(z * n_t + i, (1 - z) * n_t + (i ^ k)) for z in (0, 1) for i in range(n_t)],
        0,
    )
    return sum(pieces).astype(jnp.bfloat16)


def solution(mesh):
    fine = Mesh(mesh.devices.reshape(4, 2, 4, 2, 4), ("y", "zh", "x", "c", "t"))
    owner = ("y", "zh", "x", "c")
    in_specs = (
        P(owner, None),
        P(owner, None),
        P(owner, None),
        P(),
        P(owner, "t", None),
        P(owner, "t", None),
        P(owner, "t", None),
    )
    return jax.shard_map(
        per_device, mesh=fine, in_specs=in_specs, out_specs=P(owner, "t"), check_vma=False
    )
```

time: 285 us -> 272 us (0.954)
  between operations: 28 us -> 1.04 us
  waiting for transfers between devices: 101 us -> 118 us
  other arithmetic: 9.26 us -> 4.27 us
    ppermute x8 -> x12, waiting for transfers between devices: 14.9 us -> 88.6 us  [the longest x4 65.9 us: shift_x(): return lax.ppermute(array, 'x', [(i, (i + step) % n_x) for i in range(n_x)])]
    all_to_all x4, waiting for transfers between devices: 43.3 us -> 0.01 us  [exchange(): lax.all_to_all(send.reshape(16, rows // 16, width), ('y', 'x'), 0, 0, til...]
    all_gather x1 -> x0, waiting for transfers between devices: 29.2 us -> none  [fetch_hot(): return lax.all_gather(both, ('y', 'x'), axis=0, tiled=False)]
    ppermute x7, waiting for transfers between devices: 12.1 us -> 25.1 us  [pieces_of(): piece = lax.ppermute(piece.astype(jnp.bfloat16), axes, perm_of(shift))]
    ppermute x8 -> x12, starting transfers between devices: 23.6 us -> 31.2 us  [the longest x1 14.9 us: fetch_hot(): got = lax.ppermute(chunks[2:], 'zh', SWAP)]
    pallas_call x1, Pallas kernels: 9.6 us -> 3.32 us  [cut_chunks(): pl.pallas_call(chunk_kernel, out_shape=(shape, shape), grid_spec=pltpu.Pr...]
    select_n x5 -> x1, other arithmetic: 4.57 us -> 0.01 us  [fetch_hot(): first, second = (jnp.where(c == 0, mine, got), jnp.where(c == 0, got, mine))]
    all_to_all x4, starting transfers between devices: 32.5 us -> 28.2 us  [exchange(): lax.all_to_all(send.reshape(16, rows // 16, width), ('y', 'x'), 0, 0, til...]
  transfers between devices with their start and end apart: 24 -> 27, of which waited for: 12 -> 15; matrix products, arithmetic and copies ran while one was open for 3% -> 2% of each run, Pallas kernels for 10% -> 11%
where the time goes in v3:
time: 272 us; the launch traced here: 269 us
  waiting for transfers between devices  118 us (43%)
  starting transfers between devices  91.5 us (34%)
  Pallas kernels  36.8 us (14%)
  local copies, waits for them, and re-layouts  17.3 us (6%)
  other arithmetic  4.27 us (2%)
    ppermute x4, waiting for transfers between devices, shift_x(): return lax.ppermute(array, 'x', [(i, (i + step) % n_x) for i in range(n_x)])  65.9 us
    all_to_all x4, starting transfers between devices, exchange(): lax.all_to_all(send.reshape(16, rows // 16, width), ('y', 'x'), 0, 0, til...  28.2 us
    ppermute x7, waiting for transfers between devices, pieces_of(): piece = lax.ppermute(piece.astype(jnp.bfloat16), axes, perm_of(shift))  25.1 us
    ppermute x7, starting transfers between devices, pieces_of(): piece = lax.ppermute(piece.astype(jnp.bfloat16), axes, perm_of(shift))  24.2 us
    ppermute x1, starting transfers between devices, fetch_hot(): got = lax.ppermute(chunks[2:], 'zh', SWAP)  14.9 us
    unnamed x61, local copies, waits for them, and re-layouts  14.6 us
    pallas_call x2, Pallas kernels, ffn(): pl.pallas_call(ffn_kernel, out_shape=jax.ShapeDtypeStruct(x.shape, jnp.bf...  13.6 us
    pallas_call x2, Pallas kernels, route(): pl.pallas_call(route_kernel, out_shape=shapes, grid_spec=pltpu.PrefetchSc...  9.14 us
  transfers between devices with their start and end apart: 27, of which 15 were waited for; matrix products, arithmetic and copies ran while one was open for 2% of the time, Pallas kernels for 11%

profile of v3, /device:TPU:2, one launch (start us, length us, event | category | flops | bytes accessed | tf_op | source)
XLA Modules:
  0.0 269.2 jit_solution(14058681302328457294)
XLA Ops:
  0.7 3.3 %shard_map.74 = (bf16[16,288,128]{2,1,0:T(8,128)(2,1)S(1)}, bf16[16,288,128]{2,1,0:T(8,128)(2,1)S(1)}) custom-call(s32[9]{0:T(128)S(1)} %concatenate.14.info, bf16[2,192,2048]{2,1,0:T(8,128)(2,1)} %gate_ref.5, bf16[2,192,2048]{2,1,0:T(8,128)(2,1)} %up_ref.5, bf16[2,192,2048]{2,1,0:T(8,128)(2,1)} %down_ref.5), custom_call_target="tpu_custom_call" | custom-call | bytes 4718592 | tf_op jit(solution)/shard_map/pallas_call | solution.py:89
  8.7 7.6 %all-to-all-start.1 = ((bf16[16,288,128]{2,1,0:T(8,128)(2,1)}), bf16[16,288,128]{2,1,0:T(8,128)(2,1)S(1)}, u32[]{:S(2)}, u32[]{:S(2)}) async-start(bf16[16,288,128]{2,1,0:T(8,128)(2,1)} %shard_map.75), calls=%async_computation.1 | async-start | bytes 2359296 | tf_op jit(solution)/shard_map/all_to_all | solution.py:169
  16.5 7.3 %collective-permute-start.2 = (bf16[136,2048]{1,0:T(8,128)(2,1)S(1)}, bf16[136,2048]{1,0:T(8,128)(2,1)}, u32[]{:S(2)}, u32[]{:S(2)}) collective-permute-start(bf16[136,2048]{1,0:T(8,128)(2,1)S(1)} %fusion.1.a_ref.refs_0_), channel_id=1, source_target_pairs={{0,32},{32,0},{1,33},{33,1},{2,34},{34,2},{3,35},{35,3},{4,36},{36... | collective-permute-start | bytes 1671176 | tf_op jit(solution)/shard_map/ppermute | solution.py:439
  25.3 4.0 %shard_map.73 = (bf16[512,2048]{1,0:T(8,128)(2,1)S(1)}, bf16[512,256]{1,0:T(8,128)(2,1)S(1)}, bf16[64,256]{1,0:T(8,128)(2,1)S(1)}) custom-call(s32[9]{0:T(128)S(1)} %concatenate.14.info, bf16[136,2048]{1,0:T(8,128)(2,1)S(1)} %fusion.1.a_ref.refs_0_, bf16[136,2048]{1,0:T(8,128)(2,1)S(1)} %collective-permute-done.1.b_ref.refs_1_), custom_call_target="tpu_custom_call" | custom-call | flops 536870912 | bytes 3145728 | tf_op jit(solution)/shard_map/pallas_call | solution.py:335
  32.0 7.3 %collective-permute-done.2.a_ref.refs_2_ = bf16[136,2048]{1,0:T(8,128)(2,1)} collective-permute-done((bf16[136,2048]{1,0:T(8,128)(2,1)S(1)}, bf16[136,2048]{1,0:T(8,128)(2,1)}, u32[]{:S(2)}, u32[]{:S(2)}) %collective-permute-start.2) | collective-permute-done | bytes 557088 | tf_op jit(solution)/shard_map/ppermute | solution.py:439
  40.1 7.2 %all-to-all-start.3 = ((bf16[16,32,2048]{2,1,0:T(8,128)(2,1)}), bf16[16,32,2048]{2,1,0:T(8,128)(2,1)S(1)}, u32[]{:S(2)}, u32[]{:S(2)}) async-start(bf16[16,32,2048]{2,1,0:T(8,128)(2,1)} %bitcast.41), calls=%async_computation.3 | async-start | bytes 4194304 | tf_op jit(solution)/shard_map/all_to_all | solution.py:416
  47.4 14.9 %collective-permute-start.5 = (bf16[2,288,128]{2,1,0:T(8,128)(2,1)S(1)}, bf16[2,288,128]{2,1,0:T(8,128)(2,1)S(1)}, u32[]{:S(2)}, u32[]{:S(2)}) collective-permute-start(bf16[2,288,128]{2,1,0:T(8,128)(2,1)S(1)} %slice.67), channel_id=1, source_target_pairs={{0,32},{32,0},{1,33},{33,1},{2,34},{34,2},{3,35},{35,3},{4,36},{36... | collective-permute-start | bytes 442376 | tf_op jit(solution)/shard_map/ppermute | solution.py:203
  62.2 4.3 %collective-permute-done.5.got_ref = bf16[2,288,128]{2,1,0:T(8,128)(2,1)S(1)} collective-permute-done((bf16[2,288,128]{2,1,0:T(8,128)(2,1)S(1)}, bf16[2,288,128]{2,1,0:T(8,128)(2,1)S(1)}, u32[]{:S(2)}, u32[]{:S(2)}) %collective-permute-start.5) | collective-permute-done | bytes 147488 | tf_op jit(solution)/shard_map/ppermute | solution.py:203
  72.7 5.7 %collective-permute-done.8 = bf16[576,128]{1,0:T(8,128)(2,1)S(1)} collective-permute-done((bf16[576,128]{1,0:T(8,128)(2,1)S(1)}, bf16[576,128]{1,0:T(8,128)(2,1)S(1)}, u32[]{:S(2)}, u32[]{:S(2)}) %collective-permute-start.8) | collective-permute-done | bytes 147488 | tf_op jit(solution)/shard_map/ppermute | solution.py:214
  81.0 5.1 %shard_map.78 = (bf16[512,2048]{1,0:T(8,128)(2,1)S(1)}, bf16[512,256]{1,0:T(8,128)(2,1)S(1)}, bf16[64,256]{1,0:T(8,128)(2,1)S(1)}) custom-call(s32[9]{0:T(128)S(1)} %get-tuple-element.334, bf16[136,2048]{1,0:T(8,128)(2,1)} %collective-permute-done.2.a_ref.refs_2_, bf16[136,2048]{1,0:T(8,128)(2,1)S(1)} %collective-permute-done.3.b_ref.refs_3_), custom_call_target="tpu_custom_call" | custom-call | flops 536870912 | bytes 3145728 | tf_op jit(solution)/shard_map/pallas_call | solution.py:335
  89.6 5.9 %all-to-all-start.2 = ((bf16[16,32,2048]{2,1,0:T(8,128)(2,1)}), bf16[16,32,2048]{2,1,0:T(8,128)(2,1)}, u32[]{:S(2)}, u32[]{:S(2)}) async-start(bf16[16,32,2048]{2,1,0:T(8,128)(2,1)} %bitcast.42), calls=%async_computation.2 | async-start | bytes 4194304 | tf_op jit(solution)/shard_map/all_to_all | solution.py:416
  97.5 37.5 %collective-permute-done.11.refs_6_ = bf16[4,576,128]{2,1,0:T(8,128)(2,1)S(1)} collective-permute-done((bf16[4,576,128]{2,1,0:T(8,128)(2,1)S(1)}, bf16[4,576,128]{2,1,0:T(8,128)(2,1)S(1)}, u32[]{:S(2)}, u32[]{:S(2)}) %collective-permute-start.11) | collective-permute-done | bytes 589856 | tf_op jit(solution)/shard_map/ppermute | solution.py:220
  135.8 6.1 %shard_map.80 = bf16[16,32,2048]{2,1,0:T(8,128)(2,1)S(1)} custom-call(bf16[16,32,2048]{2,1,0:T(8,128)(2,1)S(1)} %all-to-all-done.3.x_ref, bf16[2,192,2048]{2,1,0:T(8,128)(2,1)} %get-tuple-element.305, bf16[2,192,2048]{2,1,0:T(8,128)(2,1)} %get-tuple-element.306, bf16[2,192,2048]{2,1,0:T(8,128)(2,1)} %get-tuple-element.307), custom_call_target="tpu_custom_call" | custom-call | flops 1207959552 | bytes 8912896 | tf_op jit(solution)/shard_map/pallas_call | solution.py:369
  143.3 7.6 %all-to-all-start.5 = ((bf16[16,32,2048]{2,1,0:T(8,128)(2,1)}), bf16[16,32,2048]{2,1,0:T(8,128)(2,1)S(1)}, u32[]{:S(2)}, u32[]{:S(2)}) async-start(bf16[16,32,2048]{2,1,0:T(8,128)(2,1)} %copy-done), calls=%async_computation.5 | async-start | bytes 4194304 | tf_op jit(solution)/shard_map/all_to_all | solution.py:416
  155.0 28.4 %collective-permute-done.13.refs_8_ = bf16[2,576,128]{2,1,0:T(8,128)(2,1)S(1)} collective-permute-done((bf16[2,576,128]{2,1,0:T(8,128)(2,1)S(1)}, bf16[2,576,128]{2,1,0:T(8,128)(2,1)S(1)}, u32[]{:S(2)}, u32[]{:S(2)}) %collective-permute-start.13) | collective-permute-done | bytes 294944 | tf_op jit(solution)/shard_map/ppermute | solution.py:220
  184.1 7.5 %shard_map.79 = bf16[16,32,2048]{2,1,0:T(8,128)(2,1)} custom-call(bf16[16,32,2048]{2,1,0:T(8,128)(2,1)} %all-to-all-done.2.x_ref, bf16[2,192,2048]{2,1,0:T(8,128)(2,1)} %get-tuple-element.305, bf16[2,192,2048]{2,1,0:T(8,128)(2,1)} %get-tuple-element.306, bf16[2,192,2048]{2,1,0:T(8,128)(2,1)} %get-tuple-element.307), custom_call_target="tpu_custom_call" | custom-call | flops 1207959552 | bytes 8912896 | tf_op jit(solution)/shard_map/pallas_call | solution.py:369
  193.0 7.6 %all-to-all-start.4 = ((bf16[16,32,2048]{2,1,0:T(8,128)(2,1)}), bf16[16,32,2048]{2,1,0:T(8,128)(2,1)S(1)}, u32[]{:S(2)}, u32[]{:S(2)}) async-start(bf16[16,32,2048]{2,1,0:T(8,128)(2,1)} %shard_map.79), calls=%async_computation.4 | async-start | bytes 4194304 | tf_op jit(solution)/shard_map/all_to_all | solution.py:416
  204.7 3.1 %shard_map.81 = (bf16[64,2048]{1,0:T(8,128)(2,1)S(1)}, bf16[64,2048]{1,0:T(8,128)(2,1)S(1)}) custom-call(s32[9]{0:T(128)S(1)} %get-tuple-element.334, bf16[136,2048]{1,0:T(8,128)(2,1)S(1)} %fusion.1.a_ref.refs_0_, bf16[136,2048]{1,0:T(8,128)(2,1)S(1)} %copy-done.8, bf16[136,2048]{1,0:T(8,128)(2,1)} %collective-permute-done.2.a_ref.refs_2_, ...), custom_call_target="tpu_custom_call" | custom-call | flops 301989888 | bytes 3407872 | tf_op jit(solution)/shard_map/pallas_call | solution.py:254
  213.0 6.5 %collective-permute-start.17 = (bf16[128,512]{1,0:T(8,128)(2,1)S(1)}, bf16[128,512]{1,0:T(8,128)(2,1)S(1)}, u32[]{:S(2)}, u32[]{:S(2)}) collective-permute-start(bf16[128,512]{1,0:T(8,128)(2,1)S(1)} %get-tuple-element.197), channel_id=1, source_target_pairs={{0,3},{1,2},{2,1},{3,0},{4,7},{5,6},{6,5},{7,4},{8,11},{9,10},{10,... | collective-permute-start | bytes 393224 | tf_op jit(solution)/shard_map/ppermute | solution.py:425
  219.5 5.4 %collective-permute-start.16 = (bf16[128,512]{1,0:T(8,128)(2,1)S(1)}, bf16[128,512]{1,0:T(8,128)(2,1)S(1)}, u32[]{:S(2)}, u32[]{:S(2)}) collective-permute-start(bf16[128,512]{1,0:T(8,128)(2,1)S(1)} %get-tuple-element.198), channel_id=1, source_target_pairs={{0,2},{1,3},{2,0},{3,1},{4,6},{5,7},{6,4},{7,5},{8,10},{9,11},{10,... | collective-permute-start | bytes 393224 | tf_op jit(solution)/shard_map/ppermute | solution.py:425
  225.0 9.1 %collective-permute-done.16 = bf16[128,512]{1,0:T(8,128)(2,1)S(1)} collective-permute-done((bf16[128,512]{1,0:T(8,128)(2,1)S(1)}, bf16[128,512]{1,0:T(8,128)(2,1)S(1)}, u32[]{:S(2)}, u32[]{:S(2)}) %collective-permute-start.16) | collective-permute-done | bytes 131104 | tf_op jit(solution)/shard_map/ppermute | solution.py:425
  240.1 5.6 %collective-permute-start.19 = (bf16[128,512]{1,0:T(8,128)(2,1)S(1)}, bf16[128,512]{1,0:T(8,128)(2,1)S(1)}, u32[]{:S(2)}, u32[]{:S(2)}) collective-permute-start(bf16[128,512]{1,0:T(8,128)(2,1)S(1)} %get-tuple-element.193), channel_id=1, source_target_pairs={{0,32},{1,33},{2,34},{3,35},{32,0},{33,1},{34,2},{35,3},{4,36},{5,... | collective-permute-start | bytes 393224 | tf_op jit(solution)/shard_map/ppermute | solution.py:425
  245.7 6.4 %collective-permute-start.21 = (bf16[128,512]{1,0:T(8,128)(2,1)S(1)}, bf16[128,512]{1,0:T(8,128)(2,1)S(1)}, u32[]{:S(2)}, u32[]{:S(2)}) collective-permute-start(bf16[128,512]{1,0:T(8,128)(2,1)S(1)} %get-tuple-element.195), channel_id=1, source_target_pairs={{0,34},{1,35},{2,32},{3,33},{32,2},{33,3},{34,0},{35,1},{4,38},{5,... | collective-permute-start | bytes 393224 | tf_op jit(solution)/shard_map/ppermute | solution.py:425
  252.4 11.4 %collective-permute-done.22 = bf16[128,512]{1,0:T(8,128)(2,1)S(1)} collective-permute-done((bf16[128,512]{1,0:T(8,128)(2,1)S(1)}, bf16[128,512]{1,0:T(8,128)(2,1)S(1)}, u32[]{:S(2)}, u32[]{:S(2)}) %collective-permute-start.22) | collective-permute-done | bytes 131104 | tf_op jit(solution)/shard_map/ppermute | solution.py:425
  (123 shorter events, 53.5 us)
Async XLA Ops:
  4.1 2.9 %collective-permute-start.4 = (bf16[16,288,128]{2,1,0:T(8,128)(2,1)S(1)}, bf16[16,288,128]{2,1,0:T(8,128)(2,1)S(1)}, u32[]{:S(2)}, u32[]{:S(2)}) collective-permute-start(bf16[16,288,128]{2,1,0:T(8,128)(2,1)S(1)} %get-tuple-element.146), channel_id=1, source_target_pairs={{0,4},{4,0},{1,5},{5,1},{2,6},{6,2},{3,7},{7,3},{8,12},{12,8},{9,1... | collective-permute-start | bytes 3538952 | tf_op jit(solution)/shard_map/ppermute | solution.py:168
  8.7 30.7 %all-to-all-start.1 = ((bf16[16,288,128]{2,1,0:T(8,128)(2,1)}), bf16[16,288,128]{2,1,0:T(8,128)(2,1)S(1)}, u32[]{:S(2)}, u32[]{:S(2)}) async-start(bf16[16,288,128]{2,1,0:T(8,128)(2,1)} %shard_map.75), calls=%async_computation.1 | async-start | bytes 2359296 | tf_op jit(solution)/shard_map/all_to_all | solution.py:169
  16.4 8.9 %collective-permute-start.1 = (bf16[136,2048]{1,0:T(8,128)(2,1)S(1)}, bf16[136,2048]{1,0:T(8,128)(2,1)S(1)}, u32[]{:S(2)}, u32[]{:S(2)}) collective-permute-start(bf16[136,2048]{1,0:T(8,128)(2,1)S(1)} %fusion.1.a_ref.refs_0_), channel_id=1, source_target_pairs={{0,4},{4,0},{1,5},{5,1},{2,6},{6,2},{3,7},{7,3},{8,12},{12,8},{9,1... | collective-permute-start | bytes 1671176 | tf_op jit(solution)/shard_map/ppermute | solution.py:440
  16.5 22.8 %collective-permute-start.2 = (bf16[136,2048]{1,0:T(8,128)(2,1)S(1)}, bf16[136,2048]{1,0:T(8,128)(2,1)}, u32[]{:S(2)}, u32[]{:S(2)}) collective-permute-start(bf16[136,2048]{1,0:T(8,128)(2,1)S(1)} %fusion.1.a_ref.refs_0_), channel_id=1, source_target_pairs={{0,32},{32,0},{1,33},{33,1},{2,34},{34,2},{3,35},{35,3},{4,36},{36... | collective-permute-start | bytes 1671176 | tf_op jit(solution)/shard_map/ppermute | solution.py:439
  40.1 49.5 %all-to-all-start.3 = ((bf16[16,32,2048]{2,1,0:T(8,128)(2,1)}), bf16[16,32,2048]{2,1,0:T(8,128)(2,1)S(1)}, u32[]{:S(2)}, u32[]{:S(2)}) async-start(bf16[16,32,2048]{2,1,0:T(8,128)(2,1)} %bitcast.41), calls=%async_computation.3 | async-start | bytes 4194304 | tf_op jit(solution)/shard_map/all_to_all | solution.py:416
  47.4 19.1 %collective-permute-start.5 = (bf16[2,288,128]{2,1,0:T(8,128)(2,1)S(1)}, bf16[2,288,128]{2,1,0:T(8,128)(2,1)S(1)}, u32[]{:S(2)}, u32[]{:S(2)}) collective-permute-start(bf16[2,288,128]{2,1,0:T(8,128)(2,1)S(1)} %slice.67), channel_id=1, source_target_pairs={{0,32},{32,0},{1,33},{33,1},{2,34},{34,2},{3,35},{35,3},{4,36},{36... | collective-permute-start | bytes 442376 | tf_op jit(solution)/shard_map/ppermute | solution.py:203
  67.2 13.9 %collective-permute-start.3 = (bf16[136,2048]{1,0:T(8,128)(2,1)}, bf16[136,2048]{1,0:T(8,128)(2,1)S(1)}, u32[]{:S(2)}, u32[]{:S(2)}) collective-permute-start(bf16[136,2048]{1,0:T(8,128)(2,1)} %collective-permute-done.2.a_ref.refs_2_), channel_id=1, source_target_pairs={{0,4},{4,0},{1,5},{5,1},{2,6},{6,2},{3,7},{7,3},{8,12},{12,8},{9,1... | collective-permute-start | bytes 1671176 | tf_op jit(solution)/shard_map/ppermute | solution.py:448
  68.5 9.9 %collective-permute-start.8 = (bf16[576,128]{1,0:T(8,128)(2,1)S(1)}, bf16[576,128]{1,0:T(8,128)(2,1)S(1)}, u32[]{:S(2)}, u32[]{:S(2)}) collective-permute-start(bf16[576,128]{1,0:T(8,128)(2,1)S(1)} %get-tuple-element.202), channel_id=1, source_target_pairs={{0,128},{64,192},{128,0},{192,64},{1,129},{65,193},{129,1},{193,65... | collective-permute-start | bytes 442376 | tf_op jit(solution)/shard_map/ppermute | solution.py:214
  71.5 7.6 %collective-permute-start.7 = (bf16[576,128]{1,0:T(8,128)(2,1)S(1)}, bf16[576,128]{1,0:T(8,128)(2,1)S(1)}, u32[]{:S(2)}, u32[]{:S(2)}) collective-permute-start(bf16[576,128]{1,0:T(8,128)(2,1)S(1)} %get-tuple-element.202), channel_id=1, source_target_pairs={{0,64},{64,0},{128,192},{192,128},{1,65},{65,1},{129,193},{193,129... | collective-permute-start | bytes 442376 | tf_op jit(solution)/shard_map/ppermute | solution.py:214
  72.1 8.9 %collective-permute-start.9 = (bf16[576,128]{1,0:T(8,128)(2,1)S(1)}, bf16[576,128]{1,0:T(8,128)(2,1)S(1)}, u32[]{:S(2)}, u32[]{:S(2)}) collective-permute-start(bf16[576,128]{1,0:T(8,128)(2,1)S(1)} %get-tuple-element.202), channel_id=1, source_target_pairs={{0,192},{64,128},{128,64},{192,0},{1,193},{65,129},{129,65},{193,1... | collective-permute-start | bytes 442376 | tf_op jit(solution)/shard_map/ppermute | solution.py:214
  89.6 53.7 %all-to-all-start.2 = ((bf16[16,32,2048]{2,1,0:T(8,128)(2,1)}), bf16[16,32,2048]{2,1,0:T(8,128)(2,1)}, u32[]{:S(2)}, u32[]{:S(2)}) async-start(bf16[16,32,2048]{2,1,0:T(8,128)(2,1)} %bitcast.42), calls=%async_computation.2 | async-start | bytes 4194304 | tf_op jit(solution)/shard_map/all_to_all | solution.py:416
  95.5 39.5 %collective-permute-start.11 = (bf16[4,576,128]{2,1,0:T(8,128)(2,1)S(1)}, bf16[4,576,128]{2,1,0:T(8,128)(2,1)S(1)}, u32[]{:S(2)}, u32[]{:S(2)}) collective-permute-start(bf16[4,576,128]{2,1,0:T(8,128)(2,1)S(1)} %pad_maximum_fusion.refs_4_), channel_id=1, source_target_pairs={{0,24},{8,0},{16,8},{24,16},{1,25},{9,1},{17,9},{25,17},{2,26},{10... | collective-permute-start | bytes 1769480 | tf_op jit(solution)/shard_map/ppermute | solution.py:220
  95.7 40.1 %collective-permute-start.10 = (bf16[4,576,128]{2,1,0:T(8,128)(2,1)S(1)}, bf16[4,576,128]{2,1,0:T(8,128)(2,1)}, u32[]{:S(2)}, u32[]{:S(2)}) collective-permute-start(bf16[4,576,128]{2,1,0:T(8,128)(2,1)S(1)} %pad_maximum_fusion.refs_4_), channel_id=1, source_target_pairs={{0,8},{8,16},{16,24},{24,0},{1,9},{9,17},{17,25},{25,1},{2,10},{10... | collective-permute-start | bytes 1769480 | tf_op jit(solution)/shard_map/ppermute | solution.py:220
  143.3 48.3 %all-to-all-start.5 = ((bf16[16,32,2048]{2,1,0:T(8,128)(2,1)}), bf16[16,32,2048]{2,1,0:T(8,128)(2,1)S(1)}, u32[]{:S(2)}, u32[]{:S(2)}) async-start(bf16[16,32,2048]{2,1,0:T(8,128)(2,1)} %copy-done), calls=%async_computation.5 | async-start | bytes 4194304 | tf_op jit(solution)/shard_map/all_to_all | solution.py:416
  152.9 30.5 %collective-permute-start.13 = (bf16[2,576,128]{2,1,0:T(8,128)(2,1)S(1)}, bf16[2,576,128]{2,1,0:T(8,128)(2,1)S(1)}, u32[]{:S(2)}, u32[]{:S(2)}) collective-permute-start(bf16[2,576,128]{2,1,0:T(8,128)(2,1)S(1)} %slice.69), channel_id=1, source_target_pairs={{0,24},{8,0},{16,8},{24,16},{1,25},{9,1},{17,9},{25,17},{2,26},{10... | collective-permute-start | bytes 884744 | tf_op jit(solution)/shard_map/ppermute | solution.py:220
  153.1 30.3 %collective-permute-start.12 = (bf16[2,576,128]{2,1,0:T(8,128)(2,1)S(1)}, bf16[2,576,128]{2,1,0:T(8,128)(2,1)S(1)}, u32[]{:S(2)}, u32[]{:S(2)}) collective-permute-start(bf16[2,576,128]{2,1,0:T(8,128)(2,1)S(1)} %slice.68), channel_id=1, source_target_pairs={{0,8},{8,16},{16,24},{24,0},{1,9},{9,17},{17,25},{25,1},{2,10},{10... | collective-permute-start | bytes 884744 | tf_op jit(solution)/shard_map/ppermute | solution.py:220
  193.0 42.6 %all-to-all-start.4 = ((bf16[16,32,2048]{2,1,0:T(8,128)(2,1)}), bf16[16,32,2048]{2,1,0:T(8,128)(2,1)S(1)}, u32[]{:S(2)}, u32[]{:S(2)}) async-start(bf16[16,32,2048]{2,1,0:T(8,128)(2,1)} %shard_map.79), calls=%async_computation.4 | async-start | bytes 4194304 | tf_op jit(solution)/shard_map/all_to_all | solution.py:416
  213.0 12.0 %collective-permute-start.17 = (bf16[128,512]{1,0:T(8,128)(2,1)S(1)}, bf16[128,512]{1,0:T(8,128)(2,1)S(1)}, u32[]{:S(2)}, u32[]{:S(2)}) collective-permute-start(bf16[128,512]{1,0:T(8,128)(2,1)S(1)} %get-tuple-element.197), channel_id=1, source_target_pairs={{0,3},{1,2},{2,1},{3,0},{4,7},{5,6},{6,5},{7,4},{8,11},{9,10},{10,... | collective-permute-start | bytes 393224 | tf_op jit(solution)/shard_map/ppermute | solution.py:425
  219.5 14.6 %collective-permute-start.16 = (bf16[128,512]{1,0:T(8,128)(2,1)S(1)}, bf16[128,512]{1,0:T(8,128)(2,1)S(1)}, u32[]{:S(2)}, u32[]{:S(2)}) collective-permute-start(bf16[128,512]{1,0:T(8,128)(2,1)S(1)} %get-tuple-element.198), channel_id=1, source_target_pairs={{0,2},{1,3},{2,0},{3,1},{4,6},{5,7},{6,4},{7,5},{8,10},{9,11},{10,... | collective-permute-start | bytes 393224 | tf_op jit(solution)/shard_map/ppermute | solution.py:425
  225.0 9.9 %collective-permute-start.15 = (bf16[128,512]{1,0:T(8,128)(2,1)S(1)}, bf16[128,512]{1,0:T(8,128)(2,1)S(1)}, u32[]{:S(2)}, u32[]{:S(2)}) collective-permute-start(bf16[128,512]{1,0:T(8,128)(2,1)S(1)} %get-tuple-element.199), channel_id=1, source_target_pairs={{0,1},{1,0},{2,3},{3,2},{4,5},{5,4},{6,7},{7,6},{8,9},{9,8},{10,11... | collective-permute-start | bytes 393224 | tf_op jit(solution)/shard_map/ppermute | solution.py:425
  240.1 12.3 %collective-permute-start.19 = (bf16[128,512]{1,0:T(8,128)(2,1)S(1)}, bf16[128,512]{1,0:T(8,128)(2,1)S(1)}, u32[]{:S(2)}, u32[]{:S(2)}) collective-permute-start(bf16[128,512]{1,0:T(8,128)(2,1)S(1)} %get-tuple-element.193), channel_id=1, source_target_pairs={{0,32},{1,33},{2,34},{3,35},{32,0},{33,1},{34,2},{35,3},{4,36},{5,... | collective-permute-start | bytes 393224 | tf_op jit(solution)/shard_map/ppermute | solution.py:425
  245.7 18.1 %collective-permute-start.22 = (bf16[128,512]{1,0:T(8,128)(2,1)S(1)}, bf16[128,512]{1,0:T(8,128)(2,1)S(1)}, u32[]{:S(2)}, u32[]{:S(2)}) collective-permute-start(bf16[128,512]{1,0:T(8,128)(2,1)S(1)} %get-tuple-element.194), channel_id=1, source_target_pairs={{0,35},{1,34},{2,33},{3,32},{32,3},{33,2},{34,1},{35,0},{4,39},{5,... | collective-permute-start | bytes 393224 | tf_op jit(solution)/shard_map/ppermute | solution.py:425
  245.7 20.7 %collective-permute-start.21 = (bf16[128,512]{1,0:T(8,128)(2,1)S(1)}, bf16[128,512]{1,0:T(8,128)(2,1)S(1)}, u32[]{:S(2)}, u32[]{:S(2)}) collective-permute-start(bf16[128,512]{1,0:T(8,128)(2,1)S(1)} %get-tuple-element.195), channel_id=1, source_target_pairs={{0,34},{1,35},{2,32},{3,33},{32,2},{33,3},{34,0},{35,1},{4,38},{5,... | collective-permute-start | bytes 393224 | tf_op jit(solution)/shard_map/ppermute | solution.py:425
  252.1 16.3 %collective-permute-start.20 = (bf16[128,512]{1,0:T(8,128)(2,1)S(1)}, bf16[128,512]{1,0:T(8,128)(2,1)S(1)}, u32[]{:S(2)}, u32[]{:S(2)}) collective-permute-start(bf16[128,512]{1,0:T(8,128)(2,1)S(1)} %get-tuple-element.196), channel_id=1, source_target_pairs={{0,33},{1,32},{2,35},{3,34},{32,1},{33,0},{34,3},{35,2},{4,37},{5,... | collective-permute-start | bytes 393224 | tf_op jit(solution)/shard_map/ppermute | solution.py:425
  (33 other events, 246.0 us)

commit v4 on v3

--- a/solution.py
+++ b/solution.py
@@ -221,11 +221,12 @@
 
 
 def hot_kernel(info, *refs):
-    *refs, near_ref, far_ref = refs
-    tok_refs, w_refs = refs[:4], refs[4:]
+    *refs, far_ref, near_rows = refs
+    tok_refs, w_refs, near_refs = refs[:4], refs[4:9], refs[9:]
     n_y, rows, lane = w_refs[0].shape
     units = rows // 3
-    half = near_ref.shape[0]
+    half = far_ref.shape[0]
+    cols = near_refs[0].shape[1]
     pieces = [(0, i, w_refs[0], i) for i in range(n_y)]
     pieces += [(3, i, w_refs[1], i) for i in range(n_y)]
     pieces += [(1, i, w_refs[2], i) for i in range(n_y)]
@@ -242,27 +243,34 @@
     hidden = (jax.nn.silu(proj[:, :units]) * proj[:, units:]).astype(jnp.bfloat16)
     for far, i, w_ref, at in pieces:
         out = dot(hidden, w_ref[at, 2 * units :], 1, 0).astype(jnp.bfloat16)
-        near_ref[:, columns(far, i)] = out[:half]
+        near_rows[:, columns(far, i)] = out[:half]
         far_ref[:, columns(far, i)] = out[half:]
+    for i, near_ref in enumerate(near_refs):
+        start = pl.multiple_of((info[TENSOR] ^ i) * cols, cols)
+        near_ref[...] = near_rows[:, pl.ds(start, cols)]
 
 
 def hot_ffn(info, blocks, hot_w, rows):
     width = blocks[0].shape[1]
     w_size = sum(w.size for w in hot_w)
     spec = pl.BlockSpec((rows, width), lambda i, info: (span_at(info, 0), 0))
-    shape = jax.ShapeDtypeStruct((2 * rows, width), jnp.bfloat16)
-    return pl.pallas_call(
+    n_t = lax.axis_size("t")
+    shapes = [jax.ShapeDtypeStruct((2 * rows, width // n_t), jnp.bfloat16)] * n_t
+    shapes.append(jax.ShapeDtypeStruct((2 * rows, width), jnp.bfloat16))
+    *near, far = pl.pallas_call(
         hot_kernel,
-        out_shape=(shape, shape),
+        out_shape=shapes,
         grid_spec=pltpu.PrefetchScalarGridSpec(
             num_scalar_prefetch=1,
             grid=(1,),
             in_specs=[spec] * 4 + [whole(w.shape) for w in hot_w],
-            out_specs=(whole(shape.shape), whole(shape.shape)),
+            out_specs=[whole(shape.shape) for shape in shapes],
+            scratch_shapes=[pltpu.VMEM((2 * rows, width), jnp.bfloat16)],
         ),
         compiler_params=PARAMS,
         cost_estimate=cost(8 * rows * w_size, 2 * w_size + 16 * rows * width),
     )(info, *blocks, *hot_w)
+    return near, far
 
 
 def pack(tokens, expert_ids, gate_values):
@@ -350,31 +358,45 @@
     )(info, a, b)
 
 
-def ffn_kernel(x_ref, gate_ref, up_ref, down_ref, out_ref):
+def ffn_kernel(info, x_ref, gate_ref, up_ref, down_ref, *out_refs):
     n_src, rows, width = x_ref.shape
     x = x_ref[...].reshape(n_src * rows, width)
     gate = dot(x, gate_ref[0], 1, 1)
     up = dot(x, up_ref[0], 1, 1)
     hidden = (jax.nn.silu(gate) * up).astype(jnp.bfloat16)
-    out = dot(hidden, down_ref[0], 1, 0).astype(jnp.bfloat16)
-    out_ref[...] = out.reshape(n_src, rows, width)
-
-
-def ffn(x, w_gate, w_up, w_down):
+    if len(out_refs) == 1:
+        out = dot(hidden, down_ref[0], 1, 0).astype(jnp.bfloat16)
+        out_refs[0][...] = out.reshape(n_src, rows, width)
+        return
+    cols = width // len(out_refs)
+    for i, out_ref in enumerate(out_refs):
+        start = pl.multiple_of((info[TENSOR] ^ i) * cols, cols)
+        out = dot(hidden, down_ref[0, :, pl.ds(start, cols)], 1, 0).astype(jnp.bfloat16)
+        out_ref[...] = out.reshape(n_src, rows, cols)
+
+
+def ffn(info, x, w_gate, w_up, w_down, groups):
     n_src, rows, width = x.shape
     exp_dev, units, _ = w_gate.shape
     steps = 2
-    block = pl.BlockSpec((n_src // steps, rows // exp_dev, width), lambda e, i: (i, e, 0))
-    w_spec = pl.BlockSpec((1, units, width), lambda e, i: (e, 0, 0))
+
+    def block(cols):
+        return pl.BlockSpec((n_src // steps, rows // exp_dev, cols), lambda e, i, info: (i, e, 0))
+
+    w_spec = pl.BlockSpec((1, units, width), lambda e, i, info: (e, 0, 0))
+    cols = width // groups
     return pl.pallas_call(
         ffn_kernel,
-        out_shape=jax.ShapeDtypeStruct(x.shape, jnp.bfloat16),
-        grid=(exp_dev, steps),
-        in_specs=[block, w_spec, w_spec, w_spec],
-        out_specs=block,
+        out_shape=[jax.ShapeDtypeStruct((n_src, rows, cols), jnp.bfloat16)] * groups,
+        grid_spec=pltpu.PrefetchScalarGridSpec(
+            num_scalar_prefetch=1,
+            grid=(exp_dev, steps),
+            in_specs=[block(width), w_spec, w_spec, w_spec],
+            out_specs=[block(cols)] * groups,
+        ),
         compiler_params=PARAMS,
         cost_estimate=cost(6 * n_src * rows * units * width, 4 * x.size + 6 * w_gate.size),
-    )(x, w_gate, w_up, w_down)
+    )(info, x, w_gate, w_up, w_down)
 
 
 def mix_kernel(info, mix_ref, hot_mix_ref, ret_ref, hot_ref, own_ref, other_ref):
@@ -411,20 +433,37 @@
     )(info, mix, hot_mix, returned, hot)
 
 
+def mix_quarter_kernel(mix_ref, hot_mix_ref, ret_ref, hot_ref, own_ref, other_ref):
+    out = dot(mix_ref[...], ret_ref[...], 0, 0) + dot(hot_mix_ref[...], hot_ref[...], 0, 0)
+    half = out.shape[0] // 2
+    own_ref[...] = out[:half]
+    other_ref[...] = out[half:].astype(jnp.bfloat16)
+
+
+def mix_quarter(mix, hot_mix, returned, hot):
+    rows, cols = mix.shape[1] // 2, returned.shape[1]
+    return pl.pallas_call(
+        mix_quarter_kernel,
+        out_shape=(
+            jax.ShapeDtypeStruct((rows, cols), jnp.float32),
+            jax.ShapeDtypeStruct((rows, cols), jnp.bfloat16),
+        ),
+        compiler_params=PARAMS,
+        cost_estimate=cost(2 * mix.size * cols, 2 * (mix.size + returned.size)),
+    )(mix, hot_mix, returned, hot)
+
+
 def exchange(send):
-    rows, width = send.shape
-    return lax.all_to_all(send.reshape(16, rows // 16, width), ("y", "x"), 0, 0, tiled=True)
-
-
-def pieces_of(own, other, axes, perm_of, first):
-    got = lax.ppermute(other, "c", SWAP)
-    pieces = []
-    for shift in range(own.shape[0]):
-        piece = own[shift].astype(jnp.float32) + got[shift].astype(jnp.float32)
-        if shift >= first:
-            piece = lax.ppermute(piece.astype(jnp.bfloat16), axes, perm_of(shift))
-        pieces.append(piece.astype(jnp.float32))
-    return pieces
+    return lax.all_to_all(send, ("y", "x"), 0, 0, tiled=True)
+
+
+def to_t(groups, *shifts):
+    pairs = range(len(groups))
+    return tuple(lax.ppermute(groups[k], "t", [(i, i ^ k) for i in pairs]) for k in shifts)
+
+
+def total_of(parts):
+    return sum(part.astype(jnp.float32) for part in parts).astype(jnp.bfloat16)
 
 
 def per_device(tokens, expert_ids, gate_values, hot_ids, w_gate, w_up, w_down):
@@ -440,36 +479,41 @@
     own_c = lax.ppermute(own, "c", SWAP)
     near, near_mix, near_hot_mix = route(info, own, own_c, tok_dev)
     n_slot = near.shape[0]
+    slots = (16, n_slot // 16, width)
 
     hot_w = fetch_hot(info, hot_ids, experts, c)
     near, own_z = lax.optimization_barrier((near, own_z))
-    near = exchange(near)
+    near = exchange(near.reshape(slots))
     hot_w = along_y(hot_w)
     own_zc = lax.ppermute(own_z, "c", SWAP)
     own_zc, hot_w = lax.optimization_barrier((own_zc, hot_w))
     far, far_mix, far_hot_mix = route(info, own_z, own_zc, tok_dev)
+    far = exchange(far.reshape(slots))
+    hot_w = (hot_w, shift_x(hot_w, 1), shift_x(hot_w, -1))
+    near = ffn(info, near, *experts, n_t)
+    summands = (near[0], *to_t(near, 1, 2))
+    far, hot_w, summands = lax.optimization_barrier((far, hot_w, summands))
+    near = total_of(summands + to_t(near, 3))
+    (far,) = ffn(info, far, *experts, 1)
     far = exchange(far)
-    hot_w = (hot_w, shift_x(hot_w, 1), shift_x(hot_w, -1))
-    near, hot_w = lax.optimization_barrier((near, hot_w))
-    near = exchange(ffn(near, *experts).reshape(n_slot, width)).reshape(n_slot, width)
     half = hot_w[0].shape[0] // 2
     hot_w += (shift_x(hot_w[1][:half], 1), shift_x(hot_w[2][half:], -1))
-    far, hot_w = lax.optimization_barrier((far, hot_w))
-    far = exchange(ffn(far, *experts).reshape(n_slot, width)).reshape(n_slot, width)
-
     near_hot, far_hot = hot_ffn(info, (own, own_c, own_z, own_zc), hot_w, tok_dev // SPANS)
-    mine, other = mix_rows(info, near_mix, near_hot_mix, near, near_hot)
-    pieces = pieces_of(mine, other, "t", lambda k: [(i, i ^ k) for i in range(n_t)], 1)
-    far, pieces = lax.optimization_barrier((far, pieces))
-    mine, other = mix_rows(info, far_mix, far_hot_mix, far, far_hot)
-    pieces += pieces_of(
-        mine,
-        other,
-        ("zh", "t"),
-        lambda k: [(z * n_t + i, (1 - z) * n_t + (i ^ k)) for z in (0, 1) for i in range(n_t)],
-        0,
-    )
-    return sum(pieces).astype(jnp.bfloat16)
+    near_hot = total_of((near_hot[0], *to_t(near_hot, 1, 2, 3)))
+    far, near, near_hot, far_hot = lax.optimization_barrier((far, near, near_hot, far_hot))
+
+    near = exchange(near).reshape(n_slot, width // n_t)
+    mine, other = mix_rows(info, far_mix, far_hot_mix, far.reshape(n_slot, width), far_hot)
+    got = lax.ppermute(other, "c", SWAP)
+    total = jnp.zeros((tok_dev, width // n_t), jnp.float32)
+    for k in range(n_t):
+        piece = (mine[k].astype(jnp.float32) + got[k].astype(jnp.float32)).astype(jnp.bfloat16)
+        there = [(z * n_t + i, (1 - z) * n_t + (i ^ k)) for z in (0, 1) for i in range(n_t)]
+        total += lax.ppermute(piece, ("zh", "t"), there).astype(jnp.float32)
+    near, total = lax.optimization_barrier((near, total))
+    mine, other = mix_quarter(near_mix, near_hot_mix, near, near_hot)
+    got = lax.ppermute(other, "c", SWAP)
+    return (total + mine + got.astype(jnp.float32)).astype(jnp.bfloat16)
 
 
 def solution(mesh):

time: 272 us -> 252 us (0.926)
  waiting for transfers between devices: 118 us -> 91.1 us
  starting transfers between devices: 91.5 us -> 102 us
    ppermute x4, waiting for transfers between devices: 65.9 us -> 20.6 us  [shift_x(): return lax.ppermute(array, 'x', [(i, (i + step) % n_x) for i in range(n_x)])]
    ppermute x9 -> x12, waiting for transfers between devices: 28.9 us -> 46.4 us  [the longest x6 27.9 us: to_t(): lax.ppermute(groups[k], 't', [(i, i ^ k) for i in pairs])]
    ppermute x9 -> x12, starting transfers between devices: 24.4 us -> 33.1 us  [the longest x6 22.2 us: to_t(): lax.ppermute(groups[k], 't', [(i, i ^ k) for i in pairs])]
    unnamed x61 -> x57, local copies, waits for them, and re-layouts: 14.6 us -> 12.3 us
    pallas_call x3 -> x4, Pallas kernels: 16.7 us -> 17.6 us  [the longest x2 14.3 us: ffn(): pl.pallas_call(ffn_kernel, out_shape=[jax.ShapeDtypeStruct((n_src, rows,...]
  transfers between devices with their start and end apart: 27 -> 30, of which waited for: 15 -> 15; matrix products, arithmetic and copies ran while one was open for 2% -> 2% of each run, Pallas kernels for 11% -> 8%
where the time goes in v4:
time: 252 us; the launch traced here: 250 us
  starting transfers between devices  102 us (40%)
  waiting for transfers between devices  91.1 us (36%)
  Pallas kernels  37.1 us (15%)
  local copies, waits for them, and re-layouts  15.9 us (6%)
  other arithmetic  3.1 us (1%)
    all_to_all x4, starting transfers between devices, exchange(): return lax.all_to_all(send, ('y', 'x'), 0, 0, tiled=True)  29.7 us
    ppermute x6, waiting for transfers between devices, to_t(): lax.ppermute(groups[k], 't', [(i, i ^ k) for i in pairs])  27.9 us
    ppermute x6, starting transfers between devices, to_t(): lax.ppermute(groups[k], 't', [(i, i ^ k) for i in pairs])  22.2 us
    ppermute x4, waiting for transfers between devices, shift_x(): return lax.ppermute(array, 'x', [(i, (i + step) % n_x) for i in range(n_x)])  20.6 us
    ppermute x4, waiting for transfers between devices, per_device(): total += lax.ppermute(piece, ('zh', 't'), there).astype(jnp.float32)  17.2 us
    ppermute x1, starting transfers between devices, fetch_hot(): got = lax.ppermute(chunks[2:], 'zh', SWAP)  14.9 us
    pallas_call x2, Pallas kernels, ffn(): pl.pallas_call(ffn_kernel, out_shape=[jax.ShapeDtypeStruct((n_src, rows,...  14.3 us
    unnamed x57, local copies, waits for them, and re-layouts  12.3 us
  transfers between devices with their start and end apart: 30, of which 15 were waited for; matrix products, arithmetic and copies ran while one was open for 2% of the time, Pallas kernels for 8%

profile of v4, /device:TPU:2, one launch (start us, length us, event | category | flops | bytes accessed | tf_op | source)
XLA Modules:
  0.0 250.0 jit_solution(15703429836281662174)
XLA Ops:
  0.7 3.3 %shard_map.74 = (bf16[16,288,128]{2,1,0:T(8,128)(2,1)S(1)}, bf16[16,288,128]{2,1,0:T(8,128)(2,1)S(1)}) custom-call(s32[9]{0:T(128)S(1)} %concatenate.14.info, bf16[2,192,2048]{2,1,0:T(8,128)(2,1)} %gate_ref.5, bf16[2,192,2048]{2,1,0:T(8,128)(2,1)} %up_ref.5, bf16[2,192,2048]{2,1,0:T(8,128)(2,1)} %down_ref.5), custom_call_target="tpu_custom_call" | custom-call | bytes 4718592 | tf_op jit(solution)/shard_map/pallas_call | solution.py:89
  8.7 7.6 %all-to-all-start.1 = ((bf16[16,288,128]{2,1,0:T(8,128)(2,1)}), bf16[16,288,128]{2,1,0:T(8,128)(2,1)S(1)}, u32[]{:S(2)}, u32[]{:S(2)}) async-start(bf16[16,288,128]{2,1,0:T(8,128)(2,1)} %shard_map.75), calls=%async_computation.1 | async-start | bytes 2359296 | tf_op jit(solution)/shard_map/all_to_all | solution.py:169
  16.6 7.3 %collective-permute-start.2 = (bf16[136,2048]{1,0:T(8,128)(2,1)S(1)}, bf16[136,2048]{1,0:T(8,128)(2,1)}, u32[]{:S(2)}, u32[]{:S(2)}) collective-permute-start(bf16[136,2048]{1,0:T(8,128)(2,1)S(1)} %fusion.1.a_ref.refs_0_), channel_id=1, source_target_pairs={{0,32},{32,0},{1,33},{33,1},{2,34},{34,2},{3,35},{35,3},{4,36},{36... | collective-permute-start | bytes 1671176 | tf_op jit(solution)/shard_map/ppermute | solution.py:478
  25.3 4.0 %shard_map.73 = (bf16[512,2048]{1,0:T(8,128)(2,1)S(1)}, bf16[512,256]{1,0:T(8,128)(2,1)S(1)}, bf16[64,256]{1,0:T(8,128)(2,1)S(1)}) custom-call(s32[9]{0:T(128)S(1)} %concatenate.14.info, bf16[136,2048]{1,0:T(8,128)(2,1)S(1)} %fusion.1.a_ref.refs_0_, bf16[136,2048]{1,0:T(8,128)(2,1)S(1)} %collective-permute-done.1.b_ref.refs_1_), custom_call_target="tpu_custom_call" | custom-call | flops 536870912 | bytes 3145728 | tf_op jit(solution)/shard_map/pallas_call | solution.py:343
  30.7 8.7 %collective-permute-done.2.a_ref.refs_2_ = bf16[136,2048]{1,0:T(8,128)(2,1)} collective-permute-done((bf16[136,2048]{1,0:T(8,128)(2,1)S(1)}, bf16[136,2048]{1,0:T(8,128)(2,1)}, u32[]{:S(2)}, u32[]{:S(2)}) %collective-permute-start.2) | collective-permute-done | bytes 557088 | tf_op jit(solution)/shard_map/ppermute | solution.py:478
  40.8 7.2 %all-to-all-start.3 = ((bf16[16,32,2048]{2,1,0:T(8,128)(2,1)}), bf16[16,32,2048]{2,1,0:T(8,128)(2,1)S(1)}, u32[]{:S(2)}, u32[]{:S(2)}) async-start(bf16[16,32,2048]{2,1,0:T(8,128)(2,1)} %bitcast.33), calls=%async_computation.3 | async-start | bytes 4194304 | tf_op jit(solution)/shard_map/all_to_all | solution.py:457
  49.0 14.9 %collective-permute-start.5 = (bf16[2,288,128]{2,1,0:T(8,128)(2,1)S(1)}, bf16[2,288,128]{2,1,0:T(8,128)(2,1)S(1)}, u32[]{:S(2)}, u32[]{:S(2)}) collective-permute-start(bf16[2,288,128]{2,1,0:T(8,128)(2,1)S(1)} %slice.43), channel_id=1, source_target_pairs={{0,32},{32,0},{1,33},{33,1},{2,34},{34,2},{3,35},{35,3},{4,36},{36... | collective-permute-start | bytes 442376 | tf_op jit(solution)/shard_map/ppermute | solution.py:203
  63.8 4.3 %collective-permute-done.5.got_ref = bf16[2,288,128]{2,1,0:T(8,128)(2,1)S(1)} collective-permute-done((bf16[2,288,128]{2,1,0:T(8,128)(2,1)S(1)}, bf16[2,288,128]{2,1,0:T(8,128)(2,1)S(1)}, u32[]{:S(2)}, u32[]{:S(2)}) %collective-permute-start.5) | collective-permute-done | bytes 147488 | tf_op jit(solution)/shard_map/ppermute | solution.py:203
  75.2 4.4 %collective-permute-done.8 = bf16[576,128]{1,0:T(8,128)(2,1)S(1)} collective-permute-done((bf16[576,128]{1,0:T(8,128)(2,1)S(1)}, bf16[576,128]{1,0:T(8,128)(2,1)S(1)}, u32[]{:S(2)}, u32[]{:S(2)}) %collective-permute-start.8) | collective-permute-done | bytes 147488 | tf_op jit(solution)/shard_map/ppermute | solution.py:214
  82.8 5.1 %shard_map.78 = (bf16[512,2048]{1,0:T(8,128)(2,1)S(1)}, bf16[512,256]{1,0:T(8,128)(2,1)S(1)}, bf16[64,256]{1,0:T(8,128)(2,1)S(1)}) custom-call(s32[9]{0:T(128)S(1)} %get-tuple-element.346, bf16[136,2048]{1,0:T(8,128)(2,1)} %collective-permute-done.2.a_ref.refs_2_, bf16[136,2048]{1,0:T(8,128)(2,1)S(1)} %collective-permute-done.3.b_ref.refs_3_), custom_call_target="tpu_custom_call" | custom-call | flops 536870912 | bytes 3145728 | tf_op jit(solution)/shard_map/pallas_call | solution.py:343
  92.1 6.2 %all-to-all-start.2 = ((bf16[16,32,2048]{2,1,0:T(8,128)(2,1)}), bf16[16,32,2048]{2,1,0:T(8,128)(2,1)S(1)}, u32[]{:S(2)}, u32[]{:S(2)}) async-start(bf16[16,32,2048]{2,1,0:T(8,128)(2,1)} %bitcast.34), calls=%async_computation.2 | async-start | bytes 4194304 | tf_op jit(solution)/shard_map/all_to_all | solution.py:457
  101.9 6.7 %shard_map.79 = (bf16[16,32,512]{2,1,0:T(8,128)(2,1)S(1)}, bf16[16,32,512]{2,1,0:T(8,128)(2,1)S(1)}, bf16[16,32,512]{2,1,0:T(8,128)(2,1)S(1)}, bf16[16,32,512]{2,1,0:T(8,128)(2,1)S(1)}) custom-call(s32[9]{0:T(128)S(1)} %get-tuple-element.346, bf16[16,32,2048]{2,1,0:T(8,128)(2,1)S(1)} %copy-done.1, bf16[2,192,2048]{2,1,0:T(8,128)(2,1)} %get-tuple-element.315, ...), custom_call_target="tpu_custom_call" | custom-call | flops 1207959552 | bytes 8912896 | tf_op jit(solution)/shard_map/pallas_call | solution.py:388
  109.5 8.8 %collective-permute-start.12 = (bf16[16,32,512]{2,1,0:T(8,128)(2,1)S(1)}, bf16[16,32,512]{2,1,0:T(8,128)(2,1)S(1)}, u32[]{:S(2)}, u32[]{:S(2)}) collective-permute-start(bf16[16,32,512]{2,1,0:T(8,128)(2,1)S(1)} %get-tuple-element.160), channel_id=1, source_target_pairs={{0,1},{1,0},{2,3},{3,2},{4,5},{5,4},{6,7},{7,6},{8,9},{9,8},{10,11... | collective-permute-start | bytes 1572872 | tf_op jit(solution)/shard_map/ppermute | solution.py:462
  118.9 21.1 %collective-permute-done.12 = bf16[16,32,512]{2,1,0:T(8,128)(2,1)S(1)} collective-permute-done((bf16[16,32,512]{2,1,0:T(8,128)(2,1)S(1)}, bf16[16,32,512]{2,1,0:T(8,128)(2,1)S(1)}, u32[]{:S(2)}, u32[]{:S(2)}) %collective-permute-start.12) | collective-permute-done | bytes 524320 | tf_op jit(solution)/shard_map/ppermute | solution.py:462
  144.6 7.5 %shard_map.80 = bf16[16,32,2048]{2,1,0:T(8,128)(2,1)} custom-call(s32[9]{0:T(128)S(1)} %get-tuple-element.346, bf16[16,32,2048]{2,1,0:T(8,128)(2,1)S(1)} %all-to-all-done.2.x_ref, bf16[2,192,2048]{2,1,0:T(8,128)(2,1)} %get-tuple-element.315, bf16[2,192,2048]{2,1,0:T(8,128)(2,1)} %get-tuple-element.316, bf16[2,192,2048]{2,1,0:T(8,128)(2,1)} %get-tuple-element.317), custom_call_target="tpu_custom_call" | custom-call | flops 1207959552 | bytes 8912896 | tf_op jit(solution)/shard_map/pallas_call | solution.py:388
  152.2 8.1 %all-to-all-start.4 = ((bf16[16,32,2048]{2,1,0:T(8,128)(2,1)}), bf16[16,32,2048]{2,1,0:T(8,128)(2,1)S(1)}, u32[]{:S(2)}, u32[]{:S(2)}) async-start(bf16[16,32,2048]{2,1,0:T(8,128)(2,1)} %shard_map.80), calls=%async_computation.4 | async-start | bytes 4194304 | tf_op jit(solution)/shard_map/all_to_all | solution.py:457
  166.5 20.6 %collective-permute-done.16.refs_8_ = bf16[2,576,128]{2,1,0:T(8,128)(2,1)S(1)} collective-permute-done((bf16[2,576,128]{2,1,0:T(8,128)(2,1)S(1)}, bf16[2,576,128]{2,1,0:T(8,128)(2,1)S(1)}, u32[]{:S(2)}, u32[]{:S(2)}) %collective-permute-start.16) | collective-permute-done | bytes 294944 | tf_op jit(solution)/shard_map/ppermute | solution.py:220
  191.1 8.2 %collective-permute-start.17 = (bf16[64,512]{1,0:T(8,128)(2,1)S(1)}, bf16[64,512]{1,0:T(8,128)(2,1)S(1)}, u32[]{:S(2)}, u32[]{:S(2)}) collective-permute-start(bf16[64,512]{1,0:T(8,128)(2,1)S(1)} %get-tuple-element.171), channel_id=1, source_target_pairs={{0,1},{1,0},{2,3},{3,2},{4,5},{5,4},{6,7},{7,6},{8,9},{9,8},{10,11... | collective-permute-start | bytes 196616 | tf_op jit(solution)/shard_map/ppermute | solution.py:462
  203.0 3.8 %collective-permute-done.18 = bf16[64,512]{1,0:T(8,128)(2,1)S(1)} collective-permute-done((bf16[64,512]{1,0:T(8,128)(2,1)S(1)}, bf16[64,512]{1,0:T(8,128)(2,1)S(1)}, u32[]{:S(2)}, u32[]{:S(2)}) %collective-permute-start.18) | collective-permute-done | bytes 65568 | tf_op jit(solution)/shard_map/ppermute | solution.py:462
  207.8 3.2 %shard_map.82 = (bf16[4,128,512]{2,1,0:T(8,128)(2,1)S(1)}, bf16[4,128,512]{2,1,0:T(8,128)(2,1)}) custom-call(s32[9]{0:T(128)S(1)} %get-tuple-element.346, bf16[512,256]{1,0:T(8,128)(2,1)S(1)} %copy-done.13, bf16[64,256]{1,0:T(8,128)(2,1)S(1)} %get-tuple-element.177.hot_mix_ref, bf16[512,2048]{1,0:T(8,128)(2,1)S(1)} %bitcast.31, bf16[64,2048]{1,0:T(8,128)(2,1)S(1)} %copy-done.15), custom_call_target="tpu_custom_call" | custom-call | flops 536870912 | bytes 3145728 | tf_op jit(solution)/shard_map/pallas_call | solution.py:417
  211.0 8.1 %all-to-all-start.5 = ((bf16[16,32,512]{2,1,0:T(8,128)(2,1)}), bf16[16,32,512]{2,1,0:T(8,128)(2,1)S(1)}, u32[]{:S(2)}, u32[]{:S(2)}) async-start(bf16[16,32,512]{2,1,0:T(8,128)(2,1)} %add_convert_fusion), calls=%async_computation.5 | async-start | bytes 1048576 | tf_op jit(solution)/shard_map/all_to_all | solution.py:457
  219.3 5.5 %collective-permute-start.21 = (bf16[128,512]{1,0:T(8,128)(2,1)S(1)}, bf16[128,512]{1,0:T(8,128)(2,1)S(1)}, u32[]{:S(2)}, u32[]{:S(2)}) collective-permute-start(bf16[128,512]{1,0:T(8,128)(2,1)S(1)} %get-tuple-element.203), channel_id=1, source_target_pairs={{0,32},{1,33},{2,34},{3,35},{32,0},{33,1},{34,2},{35,3},{4,36},{5,... | collective-permute-start | bytes 393224 | tf_op jit(solution)/shard_map/ppermute | solution.py:512
  224.8 4.8 %collective-permute-start.23 = (bf16[128,512]{1,0:T(8,128)(2,1)S(1)}, bf16[128,512]{1,0:T(8,128)(2,1)S(1)}, u32[]{:S(2)}, u32[]{:S(2)}) collective-permute-start(bf16[128,512]{1,0:T(8,128)(2,1)S(1)} %get-tuple-element.205), channel_id=1, source_target_pairs={{0,34},{1,35},{2,32},{3,33},{32,2},{33,3},{34,0},{35,1},{4,38},{5,... | collective-permute-start | bytes 393224 | tf_op jit(solution)/shard_map/ppermute | solution.py:512
  230.1 12.4 %collective-permute-done.24 = bf16[128,512]{1,0:T(8,128)(2,1)S(1)} collective-permute-done((bf16[128,512]{1,0:T(8,128)(2,1)S(1)}, bf16[128,512]{1,0:T(8,128)(2,1)S(1)}, u32[]{:S(2)}, u32[]{:S(2)}) %collective-permute-start.24) | collective-permute-done | bytes 131104 | tf_op jit(solution)/shard_map/ppermute | solution.py:512
  (124 shorter events, 56.9 us)
Async XLA Ops:
  8.7 30.7 %all-to-all-start.1 = ((bf16[16,288,128]{2,1,0:T(8,128)(2,1)}), bf16[16,288,128]{2,1,0:T(8,128)(2,1)S(1)}, u32[]{:S(2)}, u32[]{:S(2)}) async-start(bf16[16,288,128]{2,1,0:T(8,128)(2,1)} %shard_map.75), calls=%async_computation.1 | async-start | bytes 2359296 | tf_op jit(solution)/shard_map/all_to_all | solution.py:169
  16.5 8.9 %collective-permute-start.1 = (bf16[136,2048]{1,0:T(8,128)(2,1)S(1)}, bf16[136,2048]{1,0:T(8,128)(2,1)S(1)}, u32[]{:S(2)}, u32[]{:S(2)}) collective-permute-start(bf16[136,2048]{1,0:T(8,128)(2,1)S(1)} %fusion.1.a_ref.refs_0_), channel_id=1, source_target_pairs={{0,4},{4,0},{1,5},{5,1},{2,6},{6,2},{3,7},{7,3},{8,12},{12,8},{9,1... | collective-permute-start | bytes 1671176 | tf_op jit(solution)/shard_map/ppermute | solution.py:479
  16.6 22.8 %collective-permute-start.2 = (bf16[136,2048]{1,0:T(8,128)(2,1)S(1)}, bf16[136,2048]{1,0:T(8,128)(2,1)}, u32[]{:S(2)}, u32[]{:S(2)}) collective-permute-start(bf16[136,2048]{1,0:T(8,128)(2,1)S(1)} %fusion.1.a_ref.refs_0_), channel_id=1, source_target_pairs={{0,32},{32,0},{1,33},{33,1},{2,34},{34,2},{3,35},{35,3},{4,36},{36... | collective-permute-start | bytes 1671176 | tf_op jit(solution)/shard_map/ppermute | solution.py:478
  40.8 49.9 %all-to-all-start.3 = ((bf16[16,32,2048]{2,1,0:T(8,128)(2,1)}), bf16[16,32,2048]{2,1,0:T(8,128)(2,1)S(1)}, u32[]{:S(2)}, u32[]{:S(2)}) async-start(bf16[16,32,2048]{2,1,0:T(8,128)(2,1)} %bitcast.33), calls=%async_computation.3 | async-start | bytes 4194304 | tf_op jit(solution)/shard_map/all_to_all | solution.py:457
  49.0 19.1 %collective-permute-start.5 = (bf16[2,288,128]{2,1,0:T(8,128)(2,1)S(1)}, bf16[2,288,128]{2,1,0:T(8,128)(2,1)S(1)}, u32[]{:S(2)}, u32[]{:S(2)}) collective-permute-start(bf16[2,288,128]{2,1,0:T(8,128)(2,1)S(1)} %slice.43), channel_id=1, source_target_pairs={{0,32},{32,0},{1,33},{33,1},{2,34},{34,2},{3,35},{35,3},{4,36},{36... | collective-permute-start | bytes 442376 | tf_op jit(solution)/shard_map/ppermute | solution.py:203
  69.7 13.1 %collective-permute-start.3 = (bf16[136,2048]{1,0:T(8,128)(2,1)}, bf16[136,2048]{1,0:T(8,128)(2,1)S(1)}, u32[]{:S(2)}, u32[]{:S(2)}) collective-permute-start(bf16[136,2048]{1,0:T(8,128)(2,1)} %collective-permute-done.2.a_ref.refs_2_), channel_id=1, source_target_pairs={{0,4},{4,0},{1,5},{5,1},{2,6},{6,2},{3,7},{7,3},{8,12},{12,8},{9,1... | collective-permute-start | bytes 1671176 | tf_op jit(solution)/shard_map/ppermute | solution.py:488
  71.0 8.6 %collective-permute-start.8 = (bf16[576,128]{1,0:T(8,128)(2,1)S(1)}, bf16[576,128]{1,0:T(8,128)(2,1)S(1)}, u32[]{:S(2)}, u32[]{:S(2)}) collective-permute-start(bf16[576,128]{1,0:T(8,128)(2,1)S(1)} %get-tuple-element.208), channel_id=1, source_target_pairs={{0,128},{64,192},{128,0},{192,64},{1,129},{65,193},{129,1},{193,65... | collective-permute-start | bytes 442376 | tf_op jit(solution)/shard_map/ppermute | solution.py:214
  74.6 8.1 %collective-permute-start.9 = (bf16[576,128]{1,0:T(8,128)(2,1)S(1)}, bf16[576,128]{1,0:T(8,128)(2,1)S(1)}, u32[]{:S(2)}, u32[]{:S(2)}) collective-permute-start(bf16[576,128]{1,0:T(8,128)(2,1)S(1)} %get-tuple-element.208), channel_id=1, source_target_pairs={{0,192},{64,128},{128,64},{192,0},{1,193},{65,129},{129,65},{193,1... | collective-permute-start | bytes 442376 | tf_op jit(solution)/shard_map/ppermute | solution.py:214
  92.1 52.5 %all-to-all-start.2 = ((bf16[16,32,2048]{2,1,0:T(8,128)(2,1)}), bf16[16,32,2048]{2,1,0:T(8,128)(2,1)S(1)}, u32[]{:S(2)}, u32[]{:S(2)}) async-start(bf16[16,32,2048]{2,1,0:T(8,128)(2,1)} %bitcast.34), calls=%async_computation.2 | async-start | bytes 4194304 | tf_op jit(solution)/shard_map/all_to_all | solution.py:457
  98.3 44.7 %collective-permute-start.11 = (bf16[4,576,128]{2,1,0:T(8,128)(2,1)S(1)}, bf16[4,576,128]{2,1,0:T(8,128)(2,1)S(1)}, u32[]{:S(2)}, u32[]{:S(2)}) collective-permute-start(bf16[4,576,128]{2,1,0:T(8,128)(2,1)S(1)} %pad_maximum_fusion.refs_4_), channel_id=1, source_target_pairs={{0,24},{8,0},{16,8},{24,16},{1,25},{9,1},{17,9},{25,17},{2,26},{10... | collective-permute-start | bytes 1769480 | tf_op jit(solution)/shard_map/ppermute | solution.py:220
  98.5 46.1 %collective-permute-start.10 = (bf16[4,576,128]{2,1,0:T(8,128)(2,1)S(1)}, bf16[4,576,128]{2,1,0:T(8,128)(2,1)}, u32[]{:S(2)}, u32[]{:S(2)}) collective-permute-start(bf16[4,576,128]{2,1,0:T(8,128)(2,1)S(1)} %pad_maximum_fusion.refs_4_), channel_id=1, source_target_pairs={{0,8},{8,16},{16,24},{24,0},{1,9},{9,17},{17,25},{25,1},{2,10},{10... | collective-permute-start | bytes 1769480 | tf_op jit(solution)/shard_map/ppermute | solution.py:220
  109.5 30.5 %collective-permute-start.12 = (bf16[16,32,512]{2,1,0:T(8,128)(2,1)S(1)}, bf16[16,32,512]{2,1,0:T(8,128)(2,1)S(1)}, u32[]{:S(2)}, u32[]{:S(2)}) collective-permute-start(bf16[16,32,512]{2,1,0:T(8,128)(2,1)S(1)} %get-tuple-element.160), channel_id=1, source_target_pairs={{0,1},{1,0},{2,3},{3,2},{4,5},{5,4},{6,7},{7,6},{8,9},{9,8},{10,11... | collective-permute-start | bytes 1572872 | tf_op jit(solution)/shard_map/ppermute | solution.py:462
  118.3 24.6 %collective-permute-start.13 = (bf16[16,32,512]{2,1,0:T(8,128)(2,1)S(1)}, bf16[16,32,512]{2,1,0:T(8,128)(2,1)S(1)}, u32[]{:S(2)}, u32[]{:S(2)}) collective-permute-start(bf16[16,32,512]{2,1,0:T(8,128)(2,1)S(1)} %get-tuple-element.161), channel_id=1, source_target_pairs={{0,2},{1,3},{2,0},{3,1},{4,6},{5,7},{6,4},{7,5},{8,10},{9,11},{10,... | collective-permute-start | bytes 1572872 | tf_op jit(solution)/shard_map/ppermute | solution.py:462
  152.2 54.6 %all-to-all-start.4 = ((bf16[16,32,2048]{2,1,0:T(8,128)(2,1)}), bf16[16,32,2048]{2,1,0:T(8,128)(2,1)S(1)}, u32[]{:S(2)}, u32[]{:S(2)}) async-start(bf16[16,32,2048]{2,1,0:T(8,128)(2,1)} %shard_map.80), calls=%async_computation.4 | async-start | bytes 4194304 | tf_op jit(solution)/shard_map/all_to_all | solution.py:457
  160.3 41.4 %collective-permute-start.14 = (bf16[16,32,512]{2,1,0:T(8,128)(2,1)}, bf16[16,32,512]{2,1,0:T(8,128)(2,1)S(1)}, u32[]{:S(2)}, u32[]{:S(2)}) collective-permute-start(bf16[16,32,512]{2,1,0:T(8,128)(2,1)} %copy-done.18), channel_id=1, source_target_pairs={{0,3},{1,2},{2,1},{3,0},{4,7},{5,6},{6,5},{7,4},{8,11},{9,10},{10,... | collective-permute-start | bytes 1572872 | tf_op jit(solution)/shard_map/ppermute | solution.py:462
  164.4 22.7 %collective-permute-start.16 = (bf16[2,576,128]{2,1,0:T(8,128)(2,1)S(1)}, bf16[2,576,128]{2,1,0:T(8,128)(2,1)S(1)}, u32[]{:S(2)}, u32[]{:S(2)}) collective-permute-start(bf16[2,576,128]{2,1,0:T(8,128)(2,1)S(1)} %slice.45), channel_id=1, source_target_pairs={{0,24},{8,0},{16,8},{24,16},{1,25},{9,1},{17,9},{25,17},{2,26},{10... | collective-permute-start | bytes 884744 | tf_op jit(solution)/shard_map/ppermute | solution.py:220
  164.6 22.5 %collective-permute-start.15 = (bf16[2,576,128]{2,1,0:T(8,128)(2,1)S(1)}, bf16[2,576,128]{2,1,0:T(8,128)(2,1)S(1)}, u32[]{:S(2)}, u32[]{:S(2)}) collective-permute-start(bf16[2,576,128]{2,1,0:T(8,128)(2,1)S(1)} %slice.44), channel_id=1, source_target_pairs={{0,8},{8,16},{16,24},{24,0},{1,9},{9,17},{17,25},{25,1},{2,10},{10... | collective-permute-start | bytes 884744 | tf_op jit(solution)/shard_map/ppermute | solution.py:220
  191.1 11.8 %collective-permute-start.17 = (bf16[64,512]{1,0:T(8,128)(2,1)S(1)}, bf16[64,512]{1,0:T(8,128)(2,1)S(1)}, u32[]{:S(2)}, u32[]{:S(2)}) collective-permute-start(bf16[64,512]{1,0:T(8,128)(2,1)S(1)} %get-tuple-element.171), channel_id=1, source_target_pairs={{0,1},{1,0},{2,3},{3,2},{4,5},{5,4},{6,7},{7,6},{8,9},{9,8},{10,11... | collective-permute-start | bytes 196616 | tf_op jit(solution)/shard_map/ppermute | solution.py:462
  211.0 8.1 %collective-permute-start.20 = (bf16[4,128,512]{2,1,0:T(8,128)(2,1)}, bf16[4,128,512]{2,1,0:T(8,128)(2,1)S(1)}, u32[]{:S(2)}, u32[]{:S(2)}) collective-permute-start(bf16[4,128,512]{2,1,0:T(8,128)(2,1)} %get-tuple-element.181), channel_id=1, source_target_pairs={{0,4},{4,0},{1,5},{5,1},{2,6},{6,2},{3,7},{7,3},{8,12},{12,8},{9,1... | collective-permute-start | bytes 1572872 | tf_op jit(solution)/shard_map/ppermute | solution.py:507
  211.0 36.4 %all-to-all-start.5 = ((bf16[16,32,512]{2,1,0:T(8,128)(2,1)}), bf16[16,32,512]{2,1,0:T(8,128)(2,1)S(1)}, u32[]{:S(2)}, u32[]{:S(2)}) async-start(bf16[16,32,512]{2,1,0:T(8,128)(2,1)} %add_convert_fusion), calls=%async_computation.5 | async-start | bytes 1048576 | tf_op jit(solution)/shard_map/all_to_all | solution.py:457
  219.3 10.8 %collective-permute-start.21 = (bf16[128,512]{1,0:T(8,128)(2,1)S(1)}, bf16[128,512]{1,0:T(8,128)(2,1)S(1)}, u32[]{:S(2)}, u32[]{:S(2)}) collective-permute-start(bf16[128,512]{1,0:T(8,128)(2,1)S(1)} %get-tuple-element.203), channel_id=1, source_target_pairs={{0,32},{1,33},{2,34},{3,35},{32,0},{33,1},{34,2},{35,3},{4,36},{5,... | collective-permute-start | bytes 393224 | tf_op jit(solution)/shard_map/ppermute | solution.py:512
  224.8 17.7 %collective-permute-start.24 = (bf16[128,512]{1,0:T(8,128)(2,1)S(1)}, bf16[128,512]{1,0:T(8,128)(2,1)S(1)}, u32[]{:S(2)}, u32[]{:S(2)}) collective-permute-start(bf16[128,512]{1,0:T(8,128)(2,1)S(1)} %get-tuple-element.204), channel_id=1, source_target_pairs={{0,35},{1,34},{2,33},{3,32},{32,3},{33,2},{34,1},{35,0},{4,39},{5,... | collective-permute-start | bytes 393224 | tf_op jit(solution)/shard_map/ppermute | solution.py:512
  224.8 20.5 %collective-permute-start.23 = (bf16[128,512]{1,0:T(8,128)(2,1)S(1)}, bf16[128,512]{1,0:T(8,128)(2,1)S(1)}, u32[]{:S(2)}, u32[]{:S(2)}) collective-permute-start(bf16[128,512]{1,0:T(8,128)(2,1)S(1)} %get-tuple-element.205), channel_id=1, source_target_pairs={{0,34},{1,35},{2,32},{3,33},{32,2},{33,3},{34,0},{35,1},{4,38},{5,... | collective-permute-start | bytes 393224 | tf_op jit(solution)/shard_map/ppermute | solution.py:512
  229.7 17.7 %collective-permute-start.22 = (bf16[128,512]{1,0:T(8,128)(2,1)S(1)}, bf16[128,512]{1,0:T(8,128)(2,1)S(1)}, u32[]{:S(2)}, u32[]{:S(2)}) collective-permute-start(bf16[128,512]{1,0:T(8,128)(2,1)S(1)} %get-tuple-element.206), channel_id=1, source_target_pairs={{0,33},{1,32},{2,35},{3,34},{32,1},{33,0},{34,3},{35,2},{4,37},{5,... | collective-permute-start | bytes 393224 | tf_op jit(solution)/shard_map/ppermute | solution.py:512
  (34 other events, 280.0 us)

commit v5 on v4

--- a/solution.py
+++ b/solution.py
@@ -128,46 +128,72 @@
     return (2 * info[Z_HI] + info[CORE]) ^ i
 
 
-def take_kernel(info, part_ref, *refs):
-    *old_refs, out_ref = refs
+def take_kernel(info, *refs):
+    *part_refs, out_ref = refs
+    rows = 0
+    for part_ref in part_refs:
+        out_ref[:, rows : rows + part_ref.shape[1]] = part_ref[...]
+        rows += part_ref.shape[1]
+
+
+def source_of(expert):
+    return (expert >> 5) * 4 + ((expert >> 2) & 3)
+
+
+def take(info, received, first, rows):
+    lane = received.shape[2]
+    sizes = (256, rows - 256)
+
+    def spec(size, start):
+        return pl.BlockSpec(
+            (1, size, lane), lambda i, info: (source_of(info[span_at(info, i)]), start // size, 0)
+        )
+
+    return pl.pallas_call(
+        take_kernel,
+        out_shape=jax.ShapeDtypeStruct((SPANS, rows, lane), received.dtype),
+        grid_spec=pltpu.PrefetchScalarGridSpec(
+            num_scalar_prefetch=1,
+            grid=(SPANS,),
+            in_specs=[spec(sizes[0], first), spec(sizes[1], first + sizes[0])],
+            out_specs=pl.BlockSpec((1, rows, lane), lambda i, info: (i, 0, 0)),
+        ),
+        compiler_params=PARAMS,
+        cost_estimate=cost(0, 16 * rows * lane),
+    )(info, received, received)
+
+
+def take_more_kernel(info, part_ref, old_ref, out_ref):
     span = span_at(info, pl.program_id(0))
-    expert = info[span]
-    here = (((expert >> 4) & 1) == info[Z_HI]) & (order_of(info, span) == info[TURN])
-    if old_refs:
-        out_ref[...] = jnp.where(here, part_ref[...], old_refs[0][...])
-    else:
-        out_ref[...] = part_ref[...]
-
-
-def take(info, part, *old):
+    here = (((info[span] >> 4) & 1) == info[Z_HI]) & (order_of(info, span) == info[TURN])
+    out_ref[...] = jnp.where(here, part_ref[...], old_ref[...])
+
+
+def take_more(info, part, old):
     block = (1, *part.shape[1:])
-
-    def source(i, info):
-        expert = info[span_at(info, i)]
-        return ((expert >> 5) * 4 + ((expert >> 2) & 3), 0, 0)
-
-    def same(i, info):
-        return (i, 0, 0)
-
-    return pl.pallas_call(
-        take_kernel,
-        out_shape=jax.ShapeDtypeStruct((SPANS, *part.shape[1:]), part.dtype),
+    same = pl.BlockSpec(block, lambda i, info: (i, 0, 0))
+    return pl.pallas_call(
+        take_more_kernel,
+        out_shape=jax.ShapeDtypeStruct(old.shape, old.dtype),
         grid_spec=pltpu.PrefetchScalarGridSpec(
             num_scalar_prefetch=1,
             grid=(SPANS,),
-            in_specs=[pl.BlockSpec(block, source)] + [pl.BlockSpec(block, same)] * len(old),
-            out_specs=pl.BlockSpec(block, same),
-        ),
-        compiler_params=PARAMS,
-        cost_estimate=cost(0, 16 * block[1] * block[2]),
-    )(info, part, *old)
-
-
-def hot_round(info, held, *old):
+            in_specs=[
+                pl.BlockSpec(block, lambda i, info: (source_of(info[span_at(info, i)]), 0, 0)),
+                same,
+            ],
+            out_specs=same,
+        ),
+        compiler_params=PARAMS,
+        cost_estimate=cost(0, 24 * block[1] * block[2]),
+    )(info, part, old)
+
+
+def later_turn(info, held, old):
     keep, give = cut_chunks(info, held)
     part = choose(info, keep, lax.ppermute(give, "c", SWAP))
     part = lax.all_to_all(part, ("y", "x"), 0, 0, tiled=True)
-    return take(info, part, *old)
+    return take_more(info, part, old)
 
 
 def pair_kernel(info, chunk_ref, got_ref, mine_ref, give_ref):
@@ -192,14 +218,16 @@
     )(info, chunks, got)
 
 
-def fetch_hot(info, hot_ids, held, c):
+def later_turns(info, hot_ids, held, chunks):
     chips = chip_of(hot_ids)
     before = jnp.arange(SPANS)[None, :] < jnp.arange(SPANS)[:, None]
     turns = 1 + jnp.max(jnp.sum((chips[:, None] == chips[None, :]) & before, axis=1))
-    chunks = hot_round(info, held)
-    chunks = lax.fori_loop(
-        1, turns, lambda turn, old: hot_round(info.at[TURN].set(turn), held, old), chunks
-    )
+    return lax.fori_loop(
+        1, turns, lambda turn, old: later_turn(info.at[TURN].set(turn), held, old), chunks
+    )
+
+
+def own_span(info, chunks, c):
     got = lax.ppermute(chunks[2:], "zh", SWAP)
     mine, give = pair(info, chunks, got)
     got = lax.ppermute(give, "c", SWAP)
@@ -281,10 +309,10 @@
     return jnp.concatenate([tokens, meta], axis=0)
 
 
-def route_kernel(info, a_ref, b_ref, send_ref, mix_ref, hot_mix_ref):
+def route_kernel(info, a_ref, b_ref, *refs):
+    *chunk_refs, send_ref, mix_ref, hot_mix_ref = refs
     zh, c = info[Z_HI], info[CORE]
-    n_tok = mix_ref.shape[1]
-    n_slot = send_ref.shape[0]
+    n_slot, n_tok = mix_ref.shape
     tok_dev = n_tok // 2
     span_rows = tok_dev // SPANS
 
@@ -323,44 +351,71 @@
     pick = jnp.where(chosen, 1.0, 0.0).astype(jnp.bfloat16)
     sent = dot(pick[:, :tok_dev], a_ref[:tok_dev], 1, 0)
     sent += dot(pick[:, tok_dev:], b_ref[:tok_dev], 1, 0)
-    send_ref[...] = sent.astype(jnp.bfloat16)
+    sent = sent.astype(jnp.bfloat16)
+    lane = send_ref.shape[2]
+    n_col = sent.shape[1] // lane
+    for d in range(n_slot // 32):
+        for e in range(2):
+            for n in range(n_col):
+                at = (e * n_col + n) * 16
+                send_ref[d, at : at + 16] = sent[d * 32 + e * 16 : d * 32 + e * 16 + 16, n * lane : (n + 1) * lane]
+    if chunk_refs:
+        keep_ref, got_ref = chunk_refs
+        held_here = ((my_turn(info) >> 1) & 1) == c
+        send_ref[:, 32 * n_col :] = jnp.where(held_here, keep_ref[...], got_ref[...])
     mix_ref[...] = jnp.where(chosen, gate, 0.0).astype(jnp.bfloat16)
     hot_row = iota((2 * span_rows, 1), 0)
     hot_row = hot_row // span_rows * tok_dev + (2 * zh + c) * span_rows + hot_row % span_rows
     hot_mix_ref[...] = jnp.where(hot_row == row, hot_gate, 0.0).astype(jnp.bfloat16)
 
 
-def route(info, a, b, tok_dev):
+def route(info, a, b, tok_dev, chunks=()):
     width = a.shape[1]
     n_slot = 32 * 2 * SPANS * CAPACITY
+    n_dest = 16
     steps = 4
+    lane = width // 16
     span_rows = tok_dev // SPANS
+    rows = n_slot // n_dest * 16
+    chunk_rows = chunks[0].shape[1] if chunks else 0
     shapes = (
-        jax.ShapeDtypeStruct((n_slot, width), jnp.bfloat16),
+        jax.ShapeDtypeStruct((n_dest, rows + chunk_rows, lane), jnp.bfloat16),
         jax.ShapeDtypeStruct((n_slot, 2 * tok_dev), jnp.bfloat16),
         jax.ShapeDtypeStruct((2 * span_rows, 2 * tok_dev), jnp.bfloat16),
     )
+
+    def some(rows):
+        return pl.BlockSpec((n_dest // steps, rows, lane), lambda i, info: (i, 0, 0))
+
     return pl.pallas_call(
         route_kernel,
         out_shape=shapes,
         grid_spec=pltpu.PrefetchScalarGridSpec(
             num_scalar_prefetch=1,
             grid=(steps,),
-            in_specs=[whole(a.shape), whole(b.shape)],
+            in_specs=[whole(a.shape), whole(b.shape)] + [some(chunk_rows)] * len(chunks),
             out_specs=(
-                pl.BlockSpec((n_slot // steps, width), lambda i, info: (i, 0)),
+                some(rows + chunk_rows),
                 pl.BlockSpec((n_slot // steps, 2 * tok_dev), lambda i, info: (i, 0)),
                 whole(shapes[2].shape),
             ),
         ),
         compiler_params=PARAMS,
         cost_estimate=cost(4 * n_slot * tok_dev * width, 2 * width * (n_slot + 2 * tok_dev)),
-    )(info, a, b)
+    )(info, a, b, *chunks)
 
 
 def ffn_kernel(info, x_ref, gate_ref, up_ref, down_ref, *out_refs):
-    n_src, rows, width = x_ref.shape
-    x = x_ref[...].reshape(n_src * rows, width)
+    n_src, _, lane = x_ref.shape
+    rows = out_refs[0].shape[1]
+    width = gate_ref.shape[2]
+    x = jnp.concatenate(
+        [
+            x_ref[:, n * rows : (n + 1) * rows].reshape(n_src * rows, lane)
+            for n in range(width // lane)
+        ],
+        axis=1,
+    )
     gate = dot(x, gate_ref[0], 1, 1)
     up = dot(x, up_ref[0], 1, 1)
     hidden = (jax.nn.silu(gate) * up).astype(jnp.bfloat16)
@@ -376,9 +431,13 @@
 
 
 def ffn(info, x, w_gate, w_up, w_down, groups):
-    n_src, rows, width = x.shape
-    exp_dev, units, _ = w_gate.shape
+    n_src, _, lane = x.shape
+    exp_dev, units, width = w_gate.shape
+    rows = exp_dev * 16
     steps = 2
+    x_spec = pl.BlockSpec(
+        (n_src // steps, 16 * width // lane, lane), lambda e, i, info: (i, e, 0)
+    )
 
     def block(cols):
         return pl.BlockSpec((n_src // steps, rows // exp_dev, cols), lambda e, i, info: (i, e, 0))
@@ -391,7 +450,7 @@
         grid_spec=pltpu.PrefetchScalarGridSpec(
             num_scalar_prefetch=1,
             grid=(exp_dev, steps),
-            in_specs=[block(width), w_spec, w_spec, w_spec],
+            in_specs=[x_spec, w_spec, w_spec, w_spec],
             out_specs=[block(cols)] * groups,
         ),
         compiler_params=PARAMS,
@@ -477,24 +536,25 @@
     own = pack(tokens, expert_ids, gate_values)
     own_z = lax.ppermute(own, "zh", SWAP)
     own_c = lax.ppermute(own, "c", SWAP)
-    near, near_mix, near_hot_mix = route(info, own, own_c, tok_dev)
-    n_slot = near.shape[0]
-    slots = (16, n_slot // 16, width)
-
-    hot_w = fetch_hot(info, hot_ids, experts, c)
-    near, own_z = lax.optimization_barrier((near, own_z))
-    near = exchange(near.reshape(slots))
-    hot_w = along_y(hot_w)
+    keep, give = cut_chunks(info, experts)
+    got = lax.ppermute(give, "c", SWAP)
+    near, near_mix, near_hot_mix = route(info, own, own_c, tok_dev, (keep, got))
+    near = exchange(near)
     own_zc = lax.ppermute(own_z, "c", SWAP)
-    own_zc, hot_w = lax.optimization_barrier((own_zc, hot_w))
     far, far_mix, far_hot_mix = route(info, own_z, own_zc, tok_dev)
-    far = exchange(far.reshape(slots))
-    hot_w = (hot_w, shift_x(hot_w, 1), shift_x(hot_w, -1))
+    n_slot = near_mix.shape[0]
+    chunks = take(info, near, far.shape[1], keep.shape[1])
+    chunks = later_turns(info, hot_ids, experts, chunks)
+    chunks, far = lax.optimization_barrier((chunks, far))
+    far = exchange(far)
+    hot_w = along_y(own_span(info, chunks, c))
     near = ffn(info, near, *experts, n_t)
     summands = (near[0], *to_t(near, 1, 2))
     far, hot_w, summands = lax.optimization_barrier((far, hot_w, summands))
+    hot_w = (hot_w, shift_x(hot_w, 1), shift_x(hot_w, -1))
+    (far,) = ffn(info, far, *experts, 1)
+    far, hot_w = lax.optimization_barrier((far, hot_w))
     near = total_of(summands + to_t(near, 3))
-    (far,) = ffn(info, far, *experts, 1)
     far = exchange(far)
     half = hot_w[0].shape[0] // 2
     hot_w += (shift_x(hot_w[1][:half], 1), shift_x(hot_w[2][half:], -1))

time: 252 us -> 274 us (1.087)
  waiting for transfers between devices: 91.1 us -> 127 us
  starting transfers between devices: 102 us -> 85.4 us
  Pallas kernels: 37.1 us -> 44.5 us
  local copies, waits for them, and re-layouts: 15.9 us -> 10.2 us
    all_to_all x1, waiting for transfers between devices: 0.01 us -> 17.5 us  [later_turn(): part = lax.all_to_all(part, ('y', 'x'), 0, 0, tiled=True)]
    ppermute x6, waiting for transfers between devices: 27.9 us -> 14 us  [to_t(): lax.ppermute(groups[k], 't', [(i, i ^ k) for i in pairs])]
    all_to_all x4, waiting for transfers between devices: 0.01 us -> 13.7 us  [exchange(): return lax.all_to_all(send, ('y', 'x'), 0, 0, tiled=True)]
    ppermute x4, waiting for transfers between devices: 20.6 us -> 30.4 us  [shift_x(): return lax.ppermute(array, 'x', [(i, (i + step) % n_x) for i in range(n_x)])]
    ppermute x6, starting transfers between devices: 22.2 us -> 13.1 us  [to_t(): lax.ppermute(groups[k], 't', [(i, i ^ k) for i in pairs])]
    ppermute x3 -> x4, starting transfers between devices: 15 us -> 7.48 us  [the longest x1 7.2 us: own_span(): got = lax.ppermute(chunks[2:], 'zh', SWAP)]
    ppermute x1, waiting for transfers between devices: 8.72 us -> 14.9 us  [per_device(): own_z = lax.ppermute(own, 'zh', SWAP)]
    unnamed x57 -> x53, local copies, waits for them, and re-layouts: 12.3 us -> 6.82 us
  transfers between devices with their start and end apart: 30 -> 31, of which waited for: 15 -> 20; matrix products, arithmetic and copies ran while one was open for 2% -> 2% of each run, Pallas kernels for 8% -> 9%
where the time goes in v5:
time: 274 us; the launch traced here: 272 us
  waiting for transfers between devices  127 us (46%)
  starting transfers between devices  85.4 us (31%)
  Pallas kernels  44.5 us (16%)
  local copies, waits for them, and re-layouts  10.2 us (4%)
  other arithmetic  4.2 us (2%)
    ppermute x4, waiting for transfers between devices, shift_x(): return lax.ppermute(array, 'x', [(i, (i + step) % n_x) for i in range(n_x)])  30.4 us
    all_to_all x4, starting transfers between devices, exchange(): return lax.all_to_all(send, ('y', 'x'), 0, 0, tiled=True)  29 us
    all_to_all x1, waiting for transfers between devices, later_turn(): part = lax.all_to_all(part, ('y', 'x'), 0, 0, tiled=True)  17.5 us
    ppermute x4, waiting for transfers between devices, per_device(): total += lax.ppermute(piece, ('zh', 't'), there).astype(jnp.float32)  17.2 us
    ppermute x1, waiting for transfers between devices, per_device(): own_z = lax.ppermute(own, 'zh', SWAP)  14.9 us
    pallas_call x2, Pallas kernels, ffn(): pl.pallas_call(ffn_kernel, out_shape=[jax.ShapeDtypeStruct((n_src, rows,...  14.1 us
    ppermute x6, waiting for transfers between devices, to_t(): lax.ppermute(groups[k], 't', [(i, i ^ k) for i in pairs])  14 us
    all_to_all x4, waiting for transfers between devices, exchange(): return lax.all_to_all(send, ('y', 'x'), 0, 0, tiled=True)  13.7 us
  transfers between devices with their start and end apart: 31, of which 20 were waited for; matrix products, arithmetic and copies ran while one was open for 2% of the time, Pallas kernels for 9%

profile of v5, /device:TPU:2, one launch (start us, length us, event | category | flops | bytes accessed | tf_op | source)
XLA Modules:
  0.0 272.1 jit_solution(12617594397724482537)
XLA Ops:
  7.8 4.3 %shard_map.74 = (bf16[16,800,128]{2,1,0:T(8,128)(2,1)S(1)}, bf16[512,256]{1,0:T(8,128)(2,1)S(1)}, bf16[64,256]{1,0:T(8,128)(2,1)S(1)}) custom-call(s32[9]{0:T(128)S(1)} %concatenate.14.info, bf16[136,2048]{1,0:T(8,128)(2,1)S(1)} %fusion.1.a_ref.refs_0_, bf16[136,2048]{1,0:T(8,128)(2,1)S(1)} %collective-permute-done.1.b_ref.refs_1_, ...), custom_call_target="tpu_custom_call" | custom-call | flops 536870912 | bytes 3145728 | tf_op jit(solution)/shard_map/pallas_call | solution.py:390
  14.6 7.6 %all-to-all-start.1 = ((bf16[16,800,128]{2,1,0:T(8,128)(2,1)}), bf16[16,800,128]{2,1,0:T(8,128)(2,1)S(1)}, u32[]{:S(2)}, u32[]{:S(2)}) async-start(bf16[16,800,128]{2,1,0:T(8,128)(2,1)} %copy-done.4), calls=%async_computation.1 | async-start | bytes 6553600 | tf_op jit(solution)/shard_map/all_to_all | solution.py:516
  22.2 7.2 %collective-permute-start.3 = (bf16[136,2048]{1,0:T(8,128)(2,1)}, bf16[136,2048]{1,0:T(8,128)(2,1)}, u32[]{:S(2)}, u32[]{:S(2)}) collective-permute-start(bf16[136,2048]{1,0:T(8,128)(2,1)} %copy-done.2), channel_id=1, source_target_pairs={{0,32},{32,0},{1,33},{33,1},{2,34},{34,2},{3,35},{35,3},{4,36},{36... | collective-permute-start | bytes 1671176 | tf_op jit(solution)/shard_map/ppermute | solution.py:537
  29.3 14.9 %collective-permute-done.3.a_ref.refs_2_ = bf16[136,2048]{1,0:T(8,128)(2,1)} collective-permute-done((bf16[136,2048]{1,0:T(8,128)(2,1)}, bf16[136,2048]{1,0:T(8,128)(2,1)}, u32[]{:S(2)}, u32[]{:S(2)}) %collective-permute-start.3) | collective-permute-done | bytes 557088 | tf_op jit(solution)/shard_map/ppermute | solution.py:537
  46.6 5.3 %shard_map.76 = (bf16[16,512,128]{2,1,0:T(8,128)(2,1)S(1)}, bf16[512,256]{1,0:T(8,128)(2,1)S(1)}, bf16[64,256]{1,0:T(8,128)(2,1)S(1)}) custom-call(s32[9]{0:T(128)S(1)} %concatenate.14.info, bf16[136,2048]{1,0:T(8,128)(2,1)} %collective-permute-done.3.a_ref.refs_2_, bf16[136,2048]{1,0:T(8,128)(2,1)} %collective-permute-done.4.b_ref.refs_3_), custom_call_target="tpu_custom_call" | custom-call | flops 536870912 | bytes 3145728 | tf_op jit(solution)/shard_map/pallas_call | solution.py:390
  54.5 13.7 %all-to-all-done.1.refs_0_.refs_1_.x_ref = bf16[16,800,128]{2,1,0:T(8,128)(2,1)S(1)} async-done(((bf16[16,800,128]{2,1,0:T(8,128)(2,1)}), bf16[16,800,128]{2,1,0:T(8,128)(2,1)S(1)}, u32[]{:S(2)}, u32[]{:S(2)}) %all-to-all-start.1) | async-done | bytes 3276832 | tf_op jit(solution)/shard_map/all_to_all | solution.py:516
  70.6 36.2 %while.13 = (s32[]{:T(128)}, bf16[4,288,128]{2,1,0:T(8,128)(2,1)}, s32[]{:T(128)}, s32[9]{0:T(128)S(1)}, bf16[2,192,2048]{2,1,0:T(8,128)(2,1)}, /*index=5*/bf16[...) while((s32[]{:T(128)}, bf16[4,288,128]{2,1,0:T(8,128)(2,1)}, s32[]{:T(128)}, s32[9]{0:T(128)S(1)}, ...), condition=%wide.region_3.0_spmd, body=%wide.region_2.3_spmd.sunk | while | flops 2 | bytes 19169576 | solution.py:225
  78.5 8.8 %all-to-all-start = ((bf16[16,288,128]{2,1,0:T(8,128)(2,1)}), bf16[16,288,128]{2,1,0:T(8,128)(2,1)S(1)}, u32[]{:S(2)}, u32[]{:S(2)}) async-start(bf16[16,288,128]{2,1,0:T(8,128)(2,1)} %body.13), calls=%async_computation | async-start | bytes 2359296 | tf_op jit(solution)/shard_map/while/body/all_to_all | solution.py:195
  87.4 17.5 %all-to-all-done.part_ref = bf16[16,288,128]{2,1,0:T(8,128)(2,1)S(1)} async-done(((bf16[16,288,128]{2,1,0:T(8,128)(2,1)}), bf16[16,288,128]{2,1,0:T(8,128)(2,1)S(1)}, u32[]{:S(2)}, u32[]{:S(2)}) %all-to-all-start) | async-done | bytes 1179680 | tf_op jit(solution)/shard_map/while/body/all_to_all | solution.py:195
  106.8 6.7 %all-to-all-start.2 = ((bf16[16,512,128]{2,1,0:T(8,128)(2,1)}), bf16[16,512,128]{2,1,0:T(8,128)(2,1)}, u32[]{:S(2)}, u32[]{:S(2)}) async-start(bf16[16,512,128]{2,1,0:T(8,128)(2,1)} %copy-done.7), calls=%async_computation.2 | async-start | bytes 4194304 | tf_op jit(solution)/shard_map/all_to_all | solution.py:516
  115.0 7.2 %collective-permute-start.5 = (bf16[2,288,128]{2,1,0:T(8,128)(2,1)}, bf16[2,288,128]{2,1,0:T(8,128)(2,1)}, u32[]{:S(2)}, u32[]{:S(2)}) collective-permute-start(bf16[2,288,128]{2,1,0:T(8,128)(2,1)} %slice.43), channel_id=1, source_target_pairs={{0,32},{32,0},{1,33},{33,1},{2,34},{34,2},{3,35},{35,3},{4,36},{36... | collective-permute-start | bytes 442376 | tf_op jit(solution)/shard_map/ppermute | solution.py:231
  122.2 4.7 %collective-permute-done.5.got_ref = bf16[2,288,128]{2,1,0:T(8,128)(2,1)} collective-permute-done((bf16[2,288,128]{2,1,0:T(8,128)(2,1)}, bf16[2,288,128]{2,1,0:T(8,128)(2,1)}, u32[]{:S(2)}, u32[]{:S(2)}) %collective-permute-start.5) | collective-permute-done | bytes 147488 | tf_op jit(solution)/shard_map/ppermute | solution.py:231
  128.6 6.9 %shard_map.78 = (bf16[16,32,512]{2,1,0:T(8,128)(2,1)S(1)}, bf16[16,32,512]{2,1,0:T(8,128)(2,1)S(1)}, bf16[16,32,512]{2,1,0:T(8,128)(2,1)S(1)}, bf16[16,32,512]{2,1,0:T(8,128)(2,1)S(1)}) custom-call(s32[9]{0:T(128)S(1)} %get-tuple-element.340, bf16[16,800,128]{2,1,0:T(8,128)(2,1)S(1)} %copy-done.1, bf16[2,192,2048]{2,1,0:T(8,128)(2,1)} %get-tuple-element.311, ...), custom_call_target="tpu_custom_call" | custom-call | flops 1207959552 | bytes 11272192 | tf_op jit(solution)/shard_map/pallas_call | solution.py:447
  144.0 4.1 %collective-permute-done.8 = bf16[576,128]{1,0:T(8,128)(2,1)S(1)} collective-permute-done((bf16[576,128]{1,0:T(8,128)(2,1)S(1)}, bf16[576,128]{1,0:T(8,128)(2,1)S(1)}, u32[]{:S(2)}, u32[]{:S(2)}) %collective-permute-start.8) | collective-permute-done | bytes 147488 | tf_op jit(solution)/shard_map/ppermute | solution.py:242
  150.6 10.6 %collective-permute-done.10 = bf16[16,32,512]{2,1,0:T(8,128)(2,1)S(1)} collective-permute-done((bf16[16,32,512]{2,1,0:T(8,128)(2,1)S(1)}, bf16[16,32,512]{2,1,0:T(8,128)(2,1)S(1)}, u32[]{:S(2)}, u32[]{:S(2)}) %collective-permute-start.10) | collective-permute-done | bytes 524320 | tf_op jit(solution)/shard_map/ppermute | solution.py:521
  164.3 7.3 %shard_map.79 = bf16[16,32,2048]{2,1,0:T(8,128)(2,1)} custom-call(s32[9]{0:T(128)S(1)} %get-tuple-element.340, bf16[16,512,128]{2,1,0:T(8,128)(2,1)} %all-to-all-done.2.x_ref, bf16[2,192,2048]{2,1,0:T(8,128)(2,1)S(1)} %copy-done.19, bf16[2,192,2048]{2,1,0:T(8,128)(2,1)} %get-tuple-element.312, bf16[2,192,2048]{2,1,0:T(8,128)(2,1)} %get-tuple-element.313), custom_call_target="tpu_custom_call" | custom-call | flops 1207959552 | bytes 8912896 | tf_op jit(solution)/shard_map/pallas_call | solution.py:447
  171.6 5.4 %collective-permute-done.13.refs_6_ = bf16[4,576,128]{2,1,0:T(8,128)(2,1)S(1)} collective-permute-done((bf16[4,576,128]{2,1,0:T(8,128)(2,1)S(1)}, bf16[4,576,128]{2,1,0:T(8,128)(2,1)S(1)}, u32[]{:S(2)}, u32[]{:S(2)}) %collective-permute-start.13) | collective-permute-done | bytes 589856 | tf_op jit(solution)/shard_map/ppermute | solution.py:248
  178.2 7.2 %all-to-all-start.3 = ((bf16[16,32,2048]{2,1,0:T(8,128)(2,1)}), bf16[16,32,2048]{2,1,0:T(8,128)(2,1)S(1)}, u32[]{:S(2)}, u32[]{:S(2)}) async-start(bf16[16,32,2048]{2,1,0:T(8,128)(2,1)} %shard_map.79), calls=%async_computation.3 | async-start | bytes 4194304 | tf_op jit(solution)/shard_map/all_to_all | solution.py:516
  185.5 4.2 %collective-permute-start.14 = (bf16[16,32,512]{2,1,0:T(8,128)(2,1)}, bf16[16,32,512]{2,1,0:T(8,128)(2,1)S(1)}, u32[]{:S(2)}, u32[]{:S(2)}) collective-permute-start(bf16[16,32,512]{2,1,0:T(8,128)(2,1)} %copy-done.18), channel_id=1, source_target_pairs={{0,3},{1,2},{2,1},{3,0},{4,7},{5,6},{6,5},{7,4},{8,11},{9,10},{10,... | collective-permute-start | bytes 1572872 | tf_op jit(solution)/shard_map/ppermute | solution.py:521
  192.8 23.7 %collective-permute-done.16.refs_8_ = bf16[2,576,128]{2,1,0:T(8,128)(2,1)S(1)} collective-permute-done((bf16[2,576,128]{2,1,0:T(8,128)(2,1)S(1)}, bf16[2,576,128]{2,1,0:T(8,128)(2,1)S(1)}, u32[]{:S(2)}, u32[]{:S(2)}) %collective-permute-start.16) | collective-permute-done | bytes 294944 | tf_op jit(solution)/shard_map/ppermute | solution.py:248
  234.1 7.4 %all-to-all-start.4 = ((bf16[16,32,512]{2,1,0:T(8,128)(2,1)}), bf16[16,32,512]{2,1,0:T(8,128)(2,1)S(1)}, u32[]{:S(2)}, u32[]{:S(2)}) async-start(bf16[16,32,512]{2,1,0:T(8,128)(2,1)} %add_convert_fusion), calls=%async_computation.4 | async-start | bytes 1048576 | tf_op jit(solution)/shard_map/all_to_all | solution.py:516
  241.7 5.3 %collective-permute-start.21 = (bf16[128,512]{1,0:T(8,128)(2,1)S(1)}, bf16[128,512]{1,0:T(8,128)(2,1)S(1)}, u32[]{:S(2)}, u32[]{:S(2)}) collective-permute-start(bf16[128,512]{1,0:T(8,128)(2,1)S(1)} %get-tuple-element.203), channel_id=1, source_target_pairs={{0,32},{1,33},{2,34},{3,35},{32,0},{33,1},{34,2},{35,3},{4,36},{5,... | collective-permute-start | bytes 393224 | tf_op jit(solution)/shard_map/ppermute | solution.py:572
  247.0 4.9 %collective-permute-start.23 = (bf16[128,512]{1,0:T(8,128)(2,1)S(1)}, bf16[128,512]{1,0:T(8,128)(2,1)S(1)}, u32[]{:S(2)}, u32[]{:S(2)}) collective-permute-start(bf16[128,512]{1,0:T(8,128)(2,1)S(1)} %get-tuple-element.205), channel_id=1, source_target_pairs={{0,34},{1,35},{2,32},{3,33},{32,2},{33,3},{34,0},{35,1},{4,38},{5,... | collective-permute-start | bytes 393224 | tf_op jit(solution)/shard_map/ppermute | solution.py:572
  252.3 12.4 %collective-permute-done.24 = bf16[128,512]{1,0:T(8,128)(2,1)S(1)} collective-permute-done((bf16[128,512]{1,0:T(8,128)(2,1)S(1)}, bf16[128,512]{1,0:T(8,128)(2,1)S(1)}, u32[]{:S(2)}, u32[]{:S(2)}) %collective-permute-start.24) | collective-permute-done | bytes 131104 | tf_op jit(solution)/shard_map/ppermute | solution.py:572
  (129 shorter events, 73.7 us)
Async XLA Ops:
  14.6 53.7 %all-to-all-start.1 = ((bf16[16,800,128]{2,1,0:T(8,128)(2,1)}), bf16[16,800,128]{2,1,0:T(8,128)(2,1)S(1)}, u32[]{:S(2)}, u32[]{:S(2)}) async-start(bf16[16,800,128]{2,1,0:T(8,128)(2,1)} %copy-done.4), calls=%async_computation.1 | async-start | bytes 6553600 | tf_op jit(solution)/shard_map/all_to_all | solution.py:516
  22.2 22.1 %collective-permute-start.3 = (bf16[136,2048]{1,0:T(8,128)(2,1)}, bf16[136,2048]{1,0:T(8,128)(2,1)}, u32[]{:S(2)}, u32[]{:S(2)}) collective-permute-start(bf16[136,2048]{1,0:T(8,128)(2,1)} %copy-done.2), channel_id=1, source_target_pairs={{0,32},{32,0},{1,33},{33,1},{2,34},{34,2},{3,35},{35,3},{4,36},{36... | collective-permute-start | bytes 1671176 | tf_op jit(solution)/shard_map/ppermute | solution.py:537
  78.5 26.3 %all-to-all-start = ((bf16[16,288,128]{2,1,0:T(8,128)(2,1)}), bf16[16,288,128]{2,1,0:T(8,128)(2,1)S(1)}, u32[]{:S(2)}, u32[]{:S(2)}) async-start(bf16[16,288,128]{2,1,0:T(8,128)(2,1)} %body.13), calls=%async_computation | async-start | bytes 2359296 | tf_op jit(solution)/shard_map/while/body/all_to_all | solution.py:195
  106.8 54.5 %all-to-all-start.2 = ((bf16[16,512,128]{2,1,0:T(8,128)(2,1)}), bf16[16,512,128]{2,1,0:T(8,128)(2,1)}, u32[]{:S(2)}, u32[]{:S(2)}) async-start(bf16[16,512,128]{2,1,0:T(8,128)(2,1)} %copy-done.7), calls=%async_computation.2 | async-start | bytes 4194304 | tf_op jit(solution)/shard_map/all_to_all | solution.py:516
  115.0 12.0 %collective-permute-start.5 = (bf16[2,288,128]{2,1,0:T(8,128)(2,1)}, bf16[2,288,128]{2,1,0:T(8,128)(2,1)}, u32[]{:S(2)}, u32[]{:S(2)}) collective-permute-start(bf16[2,288,128]{2,1,0:T(8,128)(2,1)} %slice.43), channel_id=1, source_target_pairs={{0,32},{32,0},{1,33},{33,1},{2,34},{34,2},{3,35},{35,3},{4,36},{36... | collective-permute-start | bytes 442376 | tf_op jit(solution)/shard_map/ppermute | solution.py:231
  128.5 11.1 %collective-permute-start.6 = (bf16[288,128]{1,0:T(8,128)(2,1)S(1)}, bf16[288,128]{1,0:T(8,128)(2,1)S(1)}, u32[]{:S(2)}, u32[]{:S(2)}) collective-permute-start(bf16[288,128]{1,0:T(8,128)(2,1)S(1)} %get-tuple-element.156), channel_id=1, source_target_pairs={{0,4},{4,0},{1,5},{5,1},{2,6},{6,2},{3,7},{7,3},{8,12},{12,8},{9,1... | collective-permute-start | bytes 221192 | tf_op jit(solution)/shard_map/ppermute | solution.py:233
  135.5 25.7 %collective-permute-start.10 = (bf16[16,32,512]{2,1,0:T(8,128)(2,1)S(1)}, bf16[16,32,512]{2,1,0:T(8,128)(2,1)S(1)}, u32[]{:S(2)}, u32[]{:S(2)}) collective-permute-start(bf16[16,32,512]{2,1,0:T(8,128)(2,1)S(1)} %get-tuple-element.158), channel_id=1, source_target_pairs={{0,1},{1,0},{2,3},{3,2},{4,5},{5,4},{6,7},{7,6},{8,9},{9,8},{10,11... | collective-permute-start | bytes 1572872 | tf_op jit(solution)/shard_map/ppermute | solution.py:521
  137.4 23.8 %collective-permute-start.11 = (bf16[16,32,512]{2,1,0:T(8,128)(2,1)S(1)}, bf16[16,32,512]{2,1,0:T(8,128)(2,1)}, u32[]{:S(2)}, u32[]{:S(2)}) collective-permute-start(bf16[16,32,512]{2,1,0:T(8,128)(2,1)S(1)} %get-tuple-element.159), channel_id=1, source_target_pairs={{0,2},{1,3},{2,0},{3,1},{4,6},{5,7},{6,4},{7,5},{8,10},{9,11},{10,... | collective-permute-start | bytes 1572872 | tf_op jit(solution)/shard_map/ppermute | solution.py:521
  139.7 8.3 %collective-permute-start.8 = (bf16[576,128]{1,0:T(8,128)(2,1)S(1)}, bf16[576,128]{1,0:T(8,128)(2,1)S(1)}, u32[]{:S(2)}, u32[]{:S(2)}) collective-permute-start(bf16[576,128]{1,0:T(8,128)(2,1)S(1)} %get-tuple-element.208), channel_id=1, source_target_pairs={{0,128},{64,192},{128,0},{192,64},{1,129},{65,193},{129,1},{193,65... | collective-permute-start | bytes 442376 | tf_op jit(solution)/shard_map/ppermute | solution.py:242
  142.8 7.4 %collective-permute-start.7 = (bf16[576,128]{1,0:T(8,128)(2,1)S(1)}, bf16[576,128]{1,0:T(8,128)(2,1)S(1)}, u32[]{:S(2)}, u32[]{:S(2)}) collective-permute-start(bf16[576,128]{1,0:T(8,128)(2,1)S(1)} %get-tuple-element.208), channel_id=1, source_target_pairs={{0,64},{64,0},{128,192},{192,128},{1,65},{65,1},{129,193},{193,129... | collective-permute-start | bytes 442376 | tf_op jit(solution)/shard_map/ppermute | solution.py:242
  143.4 7.0 %collective-permute-start.9 = (bf16[576,128]{1,0:T(8,128)(2,1)S(1)}, bf16[576,128]{1,0:T(8,128)(2,1)S(1)}, u32[]{:S(2)}, u32[]{:S(2)}) collective-permute-start(bf16[576,128]{1,0:T(8,128)(2,1)S(1)} %get-tuple-element.208), channel_id=1, source_target_pairs={{0,192},{64,128},{128,64},{192,0},{1,193},{65,129},{129,65},{193,1... | collective-permute-start | bytes 442376 | tf_op jit(solution)/shard_map/ppermute | solution.py:242
  162.0 15.0 %collective-permute-start.13 = (bf16[4,576,128]{2,1,0:T(8,128)(2,1)S(1)}, bf16[4,576,128]{2,1,0:T(8,128)(2,1)S(1)}, u32[]{:S(2)}, u32[]{:S(2)}) collective-permute-start(bf16[4,576,128]{2,1,0:T(8,128)(2,1)S(1)} %pad_maximum_fusion.refs_4_), channel_id=1, source_target_pairs={{0,24},{8,0},{16,8},{24,16},{1,25},{9,1},{17,9},{25,17},{2,26},{10... | collective-permute-start | bytes 1769480 | tf_op jit(solution)/shard_map/ppermute | solution.py:248
  164.3 13.9 %collective-permute-start.12 = (bf16[4,576,128]{2,1,0:T(8,128)(2,1)S(1)}, bf16[4,576,128]{2,1,0:T(8,128)(2,1)}, u32[]{:S(2)}, u32[]{:S(2)}) collective-permute-start(bf16[4,576,128]{2,1,0:T(8,128)(2,1)S(1)} %pad_maximum_fusion.refs_4_), channel_id=1, source_target_pairs={{0,8},{8,16},{16,24},{24,0},{1,9},{9,17},{17,25},{25,1},{2,10},{10... | collective-permute-start | bytes 1769480 | tf_op jit(solution)/shard_map/ppermute | solution.py:248
  178.2 51.7 %all-to-all-start.3 = ((bf16[16,32,2048]{2,1,0:T(8,128)(2,1)}), bf16[16,32,2048]{2,1,0:T(8,128)(2,1)S(1)}, u32[]{:S(2)}, u32[]{:S(2)}) async-start(bf16[16,32,2048]{2,1,0:T(8,128)(2,1)} %shard_map.79), calls=%async_computation.3 | async-start | bytes 4194304 | tf_op jit(solution)/shard_map/all_to_all | solution.py:516
  185.5 38.8 %collective-permute-start.14 = (bf16[16,32,512]{2,1,0:T(8,128)(2,1)}, bf16[16,32,512]{2,1,0:T(8,128)(2,1)S(1)}, u32[]{:S(2)}, u32[]{:S(2)}) collective-permute-start(bf16[16,32,512]{2,1,0:T(8,128)(2,1)} %copy-done.18), channel_id=1, source_target_pairs={{0,3},{1,2},{2,1},{3,0},{4,7},{5,6},{6,5},{7,4},{8,11},{9,10},{10,... | collective-permute-start | bytes 1572872 | tf_op jit(solution)/shard_map/ppermute | solution.py:521
  190.7 25.8 %collective-permute-start.16 = (bf16[2,576,128]{2,1,0:T(8,128)(2,1)S(1)}, bf16[2,576,128]{2,1,0:T(8,128)(2,1)S(1)}, u32[]{:S(2)}, u32[]{:S(2)}) collective-permute-start(bf16[2,576,128]{2,1,0:T(8,128)(2,1)S(1)} %slice.45), channel_id=1, source_target_pairs={{0,24},{8,0},{16,8},{24,16},{1,25},{9,1},{17,9},{25,17},{2,26},{10... | collective-permute-start | bytes 884744 | tf_op jit(solution)/shard_map/ppermute | solution.py:248
  190.9 25.7 %collective-permute-start.15 = (bf16[2,576,128]{2,1,0:T(8,128)(2,1)S(1)}, bf16[2,576,128]{2,1,0:T(8,128)(2,1)S(1)}, u32[]{:S(2)}, u32[]{:S(2)}) collective-permute-start(bf16[2,576,128]{2,1,0:T(8,128)(2,1)S(1)} %slice.44), channel_id=1, source_target_pairs={{0,8},{8,16},{16,24},{24,0},{1,9},{9,17},{17,25},{25,1},{2,10},{10... | collective-permute-start | bytes 884744 | tf_op jit(solution)/shard_map/ppermute | solution.py:248
  219.5 7.0 %collective-permute-start.17 = (bf16[64,512]{1,0:T(8,128)(2,1)S(1)}, bf16[64,512]{1,0:T(8,128)(2,1)S(1)}, u32[]{:S(2)}, u32[]{:S(2)}) collective-permute-start(bf16[64,512]{1,0:T(8,128)(2,1)S(1)} %get-tuple-element.171), channel_id=1, source_target_pairs={{0,1},{1,0},{2,3},{3,2},{4,5},{5,4},{6,7},{7,6},{8,9},{9,8},{10,11... | collective-permute-start | bytes 196616 | tf_op jit(solution)/shard_map/ppermute | solution.py:521
  234.1 7.4 %collective-permute-start.20 = (bf16[4,128,512]{2,1,0:T(8,128)(2,1)}, bf16[4,128,512]{2,1,0:T(8,128)(2,1)S(1)}, u32[]{:S(2)}, u32[]{:S(2)}) collective-permute-start(bf16[4,128,512]{2,1,0:T(8,128)(2,1)} %get-tuple-element.181), channel_id=1, source_target_pairs={{0,4},{4,0},{1,5},{5,1},{2,6},{6,2},{3,7},{7,3},{8,12},{12,8},{9,1... | collective-permute-start | bytes 1572872 | tf_op jit(solution)/shard_map/ppermute | solution.py:567
  234.1 35.5 %all-to-all-start.4 = ((bf16[16,32,512]{2,1,0:T(8,128)(2,1)}), bf16[16,32,512]{2,1,0:T(8,128)(2,1)S(1)}, u32[]{:S(2)}, u32[]{:S(2)}) async-start(bf16[16,32,512]{2,1,0:T(8,128)(2,1)} %add_convert_fusion), calls=%async_computation.4 | async-start | bytes 1048576 | tf_op jit(solution)/shard_map/all_to_all | solution.py:516
  241.7 10.6 %collective-permute-start.21 = (bf16[128,512]{1,0:T(8,128)(2,1)S(1)}, bf16[128,512]{1,0:T(8,128)(2,1)S(1)}, u32[]{:S(2)}, u32[]{:S(2)}) collective-permute-start(bf16[128,512]{1,0:T(8,128)(2,1)S(1)} %get-tuple-element.203), channel_id=1, source_target_pairs={{0,32},{1,33},{2,34},{3,35},{32,0},{33,1},{34,2},{35,3},{4,36},{5,... | collective-permute-start | bytes 393224 | tf_op jit(solution)/shard_map/ppermute | solution.py:572
  247.0 17.7 %collective-permute-start.24 = (bf16[128,512]{1,0:T(8,128)(2,1)S(1)}, bf16[128,512]{1,0:T(8,128)(2,1)S(1)}, u32[]{:S(2)}, u32[]{:S(2)}) collective-permute-start(bf16[128,512]{1,0:T(8,128)(2,1)S(1)} %get-tuple-element.204), channel_id=1, source_target_pairs={{0,35},{1,34},{2,33},{3,32},{32,3},{33,2},{34,1},{35,0},{4,39},{5,... | collective-permute-start | bytes 393224 | tf_op jit(solution)/shard_map/ppermute | solution.py:572
  247.0 20.5 %collective-permute-start.23 = (bf16[128,512]{1,0:T(8,128)(2,1)S(1)}, bf16[128,512]{1,0:T(8,128)(2,1)S(1)}, u32[]{:S(2)}, u32[]{:S(2)}) collective-permute-start(bf16[128,512]{1,0:T(8,128)(2,1)S(1)} %get-tuple-element.205), channel_id=1, source_target_pairs={{0,34},{1,35},{2,32},{3,33},{32,2},{33,3},{34,0},{35,1},{4,38},{5,... | collective-permute-start | bytes 393224 | tf_op jit(solution)/shard_map/ppermute | solution.py:572
  251.8 17.7 %collective-permute-start.22 = (bf16[128,512]{1,0:T(8,128)(2,1)S(1)}, bf16[128,512]{1,0:T(8,128)(2,1)S(1)}, u32[]{:S(2)}, u32[]{:S(2)}) collective-permute-start(bf16[128,512]{1,0:T(8,128)(2,1)S(1)} %get-tuple-element.206), channel_id=1, source_target_pairs={{0,33},{1,32},{2,35},{3,34},{32,1},{33,0},{34,3},{35,2},{4,37},{5,... | collective-permute-start | bytes 393224 | tf_op jit(solution)/shard_map/ppermute | solution.py:572
  (34 other events, 354.1 us)

commit v6 on v4

--- a/solution.py
+++ b/solution.py
@@ -192,14 +192,17 @@
     )(info, chunks, got)
 
 
-def fetch_hot(info, hot_ids, held, c):
+def first_chunks(info, hot_ids, held):
     chips = chip_of(hot_ids)
     before = jnp.arange(SPANS)[None, :] < jnp.arange(SPANS)[:, None]
     turns = 1 + jnp.max(jnp.sum((chips[:, None] == chips[None, :]) & before, axis=1))
     chunks = hot_round(info, held)
-    chunks = lax.fori_loop(
+    return lax.fori_loop(
         1, turns, lambda turn, old: hot_round(info.at[TURN].set(turn), held, old), chunks
     )
+
+
+def own_span(info, chunks, c):
     got = lax.ppermute(chunks[2:], "zh", SWAP)
     mine, give = pair(info, chunks, got)
     got = lax.ppermute(give, "c", SWAP)
@@ -221,12 +224,12 @@
 
 
 def hot_kernel(info, *refs):
-    *refs, far_ref, near_rows = refs
-    tok_refs, w_refs, near_refs = refs[:4], refs[4:9], refs[9:]
+    *refs, near_ref, far_rows = refs
+    tok_refs, w_refs, far_refs = refs[:4], refs[4:9], refs[9:]
     n_y, rows, lane = w_refs[0].shape
     units = rows // 3
-    half = far_ref.shape[0]
-    cols = near_refs[0].shape[1]
+    half = near_ref.shape[0]
+    cols = far_refs[0].shape[1]
     pieces = [(0, i, w_refs[0], i) for i in range(n_y)]
     pieces += [(3, i, w_refs[1], i) for i in range(n_y)]
     pieces += [(1, i, w_refs[2], i) for i in range(n_y)]
@@ -243,11 +246,11 @@
     hidden = (jax.nn.silu(proj[:, :units]) * proj[:, units:]).astype(jnp.bfloat16)
     for far, i, w_ref, at in pieces:
         out = dot(hidden, w_ref[at, 2 * units :], 1, 0).astype(jnp.bfloat16)
-        near_rows[:, columns(far, i)] = out[:half]
-        far_ref[:, columns(far, i)] = out[half:]
-    for i, near_ref in enumerate(near_refs):
+        far_rows[:, columns(far, i)] = out[:half]
+        near_ref[:, columns(far, i)] = out[half:]
+    for i, far_ref in enumerate(far_refs):
         start = pl.multiple_of((info[TENSOR] ^ i) * cols, cols)
-        near_ref[...] = near_rows[:, pl.ds(start, cols)]
+        far_ref[...] = far_rows[:, pl.ds(start, cols)]
 
 
 def hot_ffn(info, blocks, hot_w, rows):
@@ -257,7 +260,7 @@
     n_t = lax.axis_size("t")
     shapes = [jax.ShapeDtypeStruct((2 * rows, width // n_t), jnp.bfloat16)] * n_t
     shapes.append(jax.ShapeDtypeStruct((2 * rows, width), jnp.bfloat16))
-    *near, far = pl.pallas_call(
+    *far, near = pl.pallas_call(
         hot_kernel,
         out_shape=shapes,
         grid_spec=pltpu.PrefetchScalarGridSpec(
@@ -378,7 +381,7 @@
 def ffn(info, x, w_gate, w_up, w_down, groups):
     n_src, rows, width = x.shape
     exp_dev, units, _ = w_gate.shape
-    steps = 2
+    steps = 1
 
     def block(cols):
         return pl.BlockSpec((n_src // steps, rows // exp_dev, cols), lambda e, i, info: (i, e, 0))
@@ -481,39 +484,39 @@
     n_slot = near.shape[0]
     slots = (16, n_slot // 16, width)
 
-    hot_w = fetch_hot(info, hot_ids, experts, c)
-    near, own_z = lax.optimization_barrier((near, own_z))
-    near = exchange(near.reshape(slots))
+    chunks = first_chunks(info, hot_ids, experts)
+    near, chunks, own_z = lax.optimization_barrier((near.reshape(slots), chunks, own_z))
+    near = exchange(near)
+    own_zc = lax.ppermute(own_z, "c", SWAP)
+    far, far_mix, far_hot_mix = route(info, own_z, own_zc, tok_dev)
+    hot_w = own_span(info, chunks, c)
+    far, hot_w = lax.optimization_barrier((far.reshape(slots), hot_w))
+    far = exchange(far)
     hot_w = along_y(hot_w)
-    own_zc = lax.ppermute(own_z, "c", SWAP)
-    own_zc, hot_w = lax.optimization_barrier((own_zc, hot_w))
-    far, far_mix, far_hot_mix = route(info, own_z, own_zc, tok_dev)
-    far = exchange(far.reshape(slots))
+    (near,) = ffn(info, near, *experts, 1)
     hot_w = (hot_w, shift_x(hot_w, 1), shift_x(hot_w, -1))
-    near = ffn(info, near, *experts, n_t)
-    summands = (near[0], *to_t(near, 1, 2))
-    far, hot_w, summands = lax.optimization_barrier((far, hot_w, summands))
-    near = total_of(summands + to_t(near, 3))
-    (far,) = ffn(info, far, *experts, 1)
-    far = exchange(far)
+    near, hot_w = lax.optimization_barrier((near, hot_w))
+    near = exchange(near)
+    far = ffn(info, far, *experts, n_t)
+    far = total_of((far[0], *to_t(far, 1, 2, 3)))
     half = hot_w[0].shape[0] // 2
     hot_w += (shift_x(hot_w[1][:half], 1), shift_x(hot_w[2][half:], -1))
-    near_hot, far_hot = hot_ffn(info, (own, own_c, own_z, own_zc), hot_w, tok_dev // SPANS)
-    near_hot = total_of((near_hot[0], *to_t(near_hot, 1, 2, 3)))
-    far, near, near_hot, far_hot = lax.optimization_barrier((far, near, near_hot, far_hot))
-
-    near = exchange(near).reshape(n_slot, width // n_t)
-    mine, other = mix_rows(info, far_mix, far_hot_mix, far.reshape(n_slot, width), far_hot)
+    near_hot, far_hot = hot_ffn(info, (own_z, own_zc, own, own_c), hot_w, tok_dev // SPANS)
+    far_hot = total_of((far_hot[0], *to_t(far_hot, 1, 2, 3)))
+    near, far, near_hot, far_hot = lax.optimization_barrier((near, far, near_hot, far_hot))
+
+    far = exchange(far).reshape(n_slot, width // n_t)
+    mine, other = mix_rows(info, near_mix, near_hot_mix, near.reshape(n_slot, width), near_hot)
     got = lax.ppermute(other, "c", SWAP)
-    total = jnp.zeros((tok_dev, width // n_t), jnp.float32)
-    for k in range(n_t):
-        piece = (mine[k].astype(jnp.float32) + got[k].astype(jnp.float32)).astype(jnp.bfloat16)
-        there = [(z * n_t + i, (1 - z) * n_t + (i ^ k)) for z in (0, 1) for i in range(n_t)]
-        total += lax.ppermute(piece, ("zh", "t"), there).astype(jnp.float32)
-    near, total = lax.optimization_barrier((near, total))
-    mine, other = mix_quarter(near_mix, near_hot_mix, near, near_hot)
-    got = lax.ppermute(other, "c", SWAP)
-    return (total + mine + got.astype(jnp.float32)).astype(jnp.bfloat16)
+    pieces = [mine[k].astype(jnp.float32) + got[k].astype(jnp.float32) for k in range(n_t)]
+    total = pieces[0]
+    for part in to_t([piece.astype(jnp.bfloat16) for piece in pieces], 1, 2, 3):
+        total += part.astype(jnp.float32)
+    far, total = lax.optimization_barrier((far, total))
+    mine, other = mix_quarter(far_mix, far_hot_mix, far, far_hot)
+    mine += lax.ppermute(other, "c", SWAP).astype(jnp.float32)
+    got = lax.ppermute(mine.astype(jnp.bfloat16), "zh", SWAP)
+    return (total + got.astype(jnp.float32)).astype(jnp.bfloat16)
 
 
 def solution(mesh):

time: 252 us -> 251 us (level)
  waiting for transfers between devices: 91.1 us -> 111 us
  starting transfers between devices: 102 us -> 88.7 us
  local copies, waits for them, and re-layouts: 15.9 us -> 10.9 us
  Pallas kernels: 37.1 us -> 33.7 us
  other arithmetic: 3.1 us -> 5.63 us
    ppermute x3, waiting for transfers between devices: 7.48 us -> 27.9 us  [along_y(): column.append(lax.ppermute(chunk, 'y', [(i, i ^ k) for i in range(n_y)]))]
    ppermute x6 -> x4, waiting for transfers between devices: 22.2 us -> 14 us  [the longest x1 6.84 us: per_device(): got = lax.ppermute(mine.astype(jnp.bfloat16), 'zh', SWAP)]
    ppermute x6 -> x9, waiting for transfers between devices: 27.9 us -> 34.6 us  [to_t(): lax.ppermute(groups[k], 't', [(i, i ^ k) for i in pairs])]
    ppermute x6 -> x9, starting transfers between devices: 22.2 us -> 16 us  [to_t(): lax.ppermute(groups[k], 't', [(i, i ^ k) for i in pairs])]
    ppermute x6 -> x4, starting transfers between devices: 25.8 us -> 20.5 us  [the longest x1 14.9 us: own_span(): got = lax.ppermute(chunks[2:], 'zh', SWAP)]
    unnamed x57 -> x43, local copies, waits for them, and re-layouts: 12.3 us -> 7.26 us
    pallas_call x2, Pallas kernels: 14.3 us -> 10.2 us  [ffn(): pl.pallas_call(ffn_kernel, out_shape=[jax.ShapeDtypeStruct((n_src, rows,...]
    ppermute x1, waiting for transfers between devices: 8.72 us -> 4.79 us  [per_device(): own_z = lax.ppermute(own, 'zh', SWAP)]
  transfers between devices with their start and end apart: 30 -> 30, of which waited for: 15 -> 15; matrix products, arithmetic and copies ran while one was open for 2% -> 3% of each run, Pallas kernels for 8% -> 10%
where the time goes in v6:
time: 251 us
  waiting for transfers between devices  111 us (44%)
  starting transfers between devices  88.7 us (35%)
  Pallas kernels  33.7 us (13%)
  local copies, waits for them, and re-layouts  10.9 us (4%)
  other arithmetic  5.63 us (2%)
    ppermute x9, waiting for transfers between devices, to_t(): lax.ppermute(groups[k], 't', [(i, i ^ k) for i in pairs])  34.6 us
    all_to_all x4, starting transfers between devices, exchange(): return lax.all_to_all(send, ('y', 'x'), 0, 0, tiled=True)  28.8 us
    ppermute x3, waiting for transfers between devices, along_y(): column.append(lax.ppermute(chunk, 'y', [(i, i ^ k) for i in range(n_y)]))  27.9 us
    ppermute x4, waiting for transfers between devices, shift_x(): return lax.ppermute(array, 'x', [(i, (i + step) % n_x) for i in range(n_x)])  23.3 us
    ppermute x9, starting transfers between devices, to_t(): lax.ppermute(groups[k], 't', [(i, i ^ k) for i in pairs])  16 us
    ppermute x1, starting transfers between devices, own_span(): got = lax.ppermute(chunks[2:], 'zh', SWAP)  14.9 us
    pallas_call x2, Pallas kernels, ffn(): pl.pallas_call(ffn_kernel, out_shape=[jax.ShapeDtypeStruct((n_src, rows,...  10.2 us
    pallas_call x2, Pallas kernels, route(): pl.pallas_call(route_kernel, out_shape=shapes, grid_spec=pltpu.PrefetchSc...  9.13 us
  transfers between devices with their start and end apart: 30, of which 15 were waited for; matrix products, arithmetic and copies ran while one was open for 3% of the time, Pallas kernels for 10%

profile of v6, /device:TPU:2, one launch (start us, length us, event | category | flops | bytes accessed | tf_op | source)
XLA Modules:
  0.0 250.5 jit_solution(15812723947822930500)
XLA Ops:
  8.7 7.6 %all-to-all-start.1 = ((bf16[16,288,128]{2,1,0:T(8,128)(2,1)}), bf16[16,288,128]{2,1,0:T(8,128)(2,1)S(1)}, u32[]{:S(2)}, u32[]{:S(2)}) async-start(bf16[16,288,128]{2,1,0:T(8,128)(2,1)} %shard_map.75), calls=%async_computation.1 | async-start | bytes 2359296 | tf_op jit(solution)/shard_map/all_to_all | solution.py:169
  16.5 7.3 %collective-permute-start.3 = (bf16[136,2048]{1,0:T(8,128)(2,1)S(1)}, bf16[136,2048]{1,0:T(8,128)(2,1)S(1)}, u32[]{:S(2)}, u32[]{:S(2)}) collective-permute-start(bf16[136,2048]{1,0:T(8,128)(2,1)S(1)} %fusion.1.a_ref.refs_2_), channel_id=1, source_target_pairs={{0,32},{32,0},{1,33},{33,1},{2,34},{34,2},{3,35},{35,3},{4,36},{36... | collective-permute-start | bytes 1671176 | tf_op jit(solution)/shard_map/ppermute | solution.py:481
  25.4 4.0 %shard_map.73 = (bf16[512,2048]{1,0:T(8,128)(2,1)S(1)}, bf16[512,256]{1,0:T(8,128)(2,1)S(1)}, bf16[64,256]{1,0:T(8,128)(2,1)S(1)}) custom-call(s32[9]{0:T(128)S(1)} %concatenate.14.info, bf16[136,2048]{1,0:T(8,128)(2,1)S(1)} %fusion.1.a_ref.refs_2_, bf16[136,2048]{1,0:T(8,128)(2,1)S(1)} %collective-permute-done.1.b_ref.refs_3_), custom_call_target="tpu_custom_call" | custom-call | flops 536870912 | bytes 3145728 | tf_op jit(solution)/shard_map/pallas_call | solution.py:346
  34.5 4.8 %collective-permute-done.3.a_ref.refs_0_ = bf16[136,2048]{1,0:T(8,128)(2,1)S(1)} collective-permute-done((bf16[136,2048]{1,0:T(8,128)(2,1)S(1)}, bf16[136,2048]{1,0:T(8,128)(2,1)S(1)}, u32[]{:S(2)}, u32[]{:S(2)}) %collective-permute-start.3) | collective-permute-done | bytes 557088 | tf_op jit(solution)/shard_map/ppermute | solution.py:481
  40.0 7.2 %all-to-all-start.2 = ((bf16[16,32,2048]{2,1,0:T(8,128)(2,1)}), bf16[16,32,2048]{2,1,0:T(8,128)(2,1)S(1)}, u32[]{:S(2)}, u32[]{:S(2)}) async-start(bf16[16,32,2048]{2,1,0:T(8,128)(2,1)} %bitcast.36), calls=%async_computation.2 | async-start | bytes 4194304 | tf_op jit(solution)/shard_map/all_to_all | solution.py:460
  48.2 14.9 %collective-permute-start.5 = (bf16[2,288,128]{2,1,0:T(8,128)(2,1)S(1)}, bf16[2,288,128]{2,1,0:T(8,128)(2,1)S(1)}, u32[]{:S(2)}, u32[]{:S(2)}) collective-permute-start(bf16[2,288,128]{2,1,0:T(8,128)(2,1)S(1)} %slice.43), channel_id=1, source_target_pairs={{0,32},{32,0},{1,33},{33,1},{2,34},{34,2},{3,35},{35,3},{4,36},{36... | collective-permute-start | bytes 442376 | tf_op jit(solution)/shard_map/ppermute | solution.py:206
  63.0 4.3 %collective-permute-done.5.got_ref = bf16[2,288,128]{2,1,0:T(8,128)(2,1)S(1)} collective-permute-done((bf16[2,288,128]{2,1,0:T(8,128)(2,1)S(1)}, bf16[2,288,128]{2,1,0:T(8,128)(2,1)S(1)}, u32[]{:S(2)}, u32[]{:S(2)}) %collective-permute-start.5) | collective-permute-done | bytes 147488 | tf_op jit(solution)/shard_map/ppermute | solution.py:206
  73.3 5.1 %shard_map.78 = (bf16[512,2048]{1,0:T(8,128)(2,1)S(1)}, bf16[512,256]{1,0:T(8,128)(2,1)S(1)}, bf16[64,256]{1,0:T(8,128)(2,1)S(1)}) custom-call(s32[9]{0:T(128)S(1)} %get-tuple-element.337, bf16[136,2048]{1,0:T(8,128)(2,1)S(1)} %collective-permute-done.3.a_ref.refs_0_, bf16[136,2048]{1,0:T(8,128)(2,1)} %collective-permute-done.4.b_ref.refs_1_), custom_call_target="tpu_custom_call" | custom-call | flops 536870912 | bytes 3145728 | tf_op jit(solution)/shard_map/pallas_call | solution.py:346
  81.0 7.2 %all-to-all-start.4 = ((bf16[16,32,2048]{2,1,0:T(8,128)(2,1)}), bf16[16,32,2048]{2,1,0:T(8,128)(2,1)}, u32[]{:S(2)}, u32[]{:S(2)}) async-start(bf16[16,32,2048]{2,1,0:T(8,128)(2,1)} %bitcast.37), calls=%async_computation.4 | async-start | bytes 4194304 | tf_op jit(solution)/shard_map/all_to_all | solution.py:460
  92.5 27.9 %collective-permute-done.9 = bf16[576,128]{1,0:T(8,128)(2,1)S(1)} collective-permute-done((bf16[576,128]{1,0:T(8,128)(2,1)S(1)}, bf16[576,128]{1,0:T(8,128)(2,1)S(1)}, u32[]{:S(2)}, u32[]{:S(2)}) %collective-permute-start.9) | collective-permute-done | bytes 147488 | tf_op jit(solution)/shard_map/ppermute | solution.py:217
  123.5 5.4 %shard_map.77 = bf16[16,32,2048]{2,1,0:T(8,128)(2,1)} custom-call(s32[9]{0:T(128)S(1)} %get-tuple-element.337, bf16[16,32,2048]{2,1,0:T(8,128)(2,1)S(1)} %all-to-all-done.2.x_ref, bf16[2,192,2048]{2,1,0:T(8,128)(2,1)} %get-tuple-element.307, bf16[2,192,2048]{2,1,0:T(8,128)(2,1)} %get-tuple-element.308, bf16[2,192,2048]{2,1,0:T(8,128)(2,1)} %get-tuple-element.309), custom_call_target="tpu_custom_call" | custom-call | flops 1207959552 | bytes 8912896 | tf_op jit(solution)/shard_map/pallas_call | solution.py:391
  128.9 7.5 %collective-permute-done.11.refs_6_ = bf16[4,576,128]{2,1,0:T(8,128)(2,1)S(1)} collective-permute-done((bf16[4,576,128]{2,1,0:T(8,128)(2,1)S(1)}, bf16[4,576,128]{2,1,0:T(8,128)(2,1)S(1)}, u32[]{:S(2)}, u32[]{:S(2)}) %collective-permute-start.11) | collective-permute-done | bytes 589856 | tf_op jit(solution)/shard_map/ppermute | solution.py:223
  137.3 6.3 %all-to-all-start.3 = ((bf16[16,32,2048]{2,1,0:T(8,128)(2,1)}), bf16[16,32,2048]{2,1,0:T(8,128)(2,1)S(1)}, u32[]{:S(2)}, u32[]{:S(2)}) async-start(bf16[16,32,2048]{2,1,0:T(8,128)(2,1)} %shard_map.77), calls=%async_computation.3 | async-start | bytes 4194304 | tf_op jit(solution)/shard_map/all_to_all | solution.py:460
  147.7 4.8 %shard_map.80 = (bf16[16,32,512]{2,1,0:T(8,128)(2,1)S(1)}, bf16[16,32,512]{2,1,0:T(8,128)(2,1)S(1)}, bf16[16,32,512]{2,1,0:T(8,128)(2,1)S(1)}, bf16[16,32,512]{2,1,0:T(8,128)(2,1)S(1)}) custom-call(s32[9]{0:T(128)S(1)} %get-tuple-element.337, bf16[16,32,2048]{2,1,0:T(8,128)(2,1)} %all-to-all-done.4.x_ref, bf16[2,192,2048]{2,1,0:T(8,128)(2,1)} %get-tuple-element.307, ...), custom_call_target="tpu_custom_call" | custom-call | flops 1207959552 | bytes 8912896 | tf_op jit(solution)/shard_map/pallas_call | solution.py:391
  152.5 3.7 %collective-permute-start.12 = (bf16[16,32,512]{2,1,0:T(8,128)(2,1)S(1)}, bf16[16,32,512]{2,1,0:T(8,128)(2,1)S(1)}, u32[]{:S(2)}, u32[]{:S(2)}) collective-permute-start(bf16[16,32,512]{2,1,0:T(8,128)(2,1)S(1)} %get-tuple-element.160), channel_id=1, source_target_pairs={{0,1},{1,0},{2,3},{3,2},{4,5},{5,4},{6,7},{7,6},{8,9},{9,8},{10,11... | collective-permute-start | bytes 1572872 | tf_op jit(solution)/shard_map/ppermute | solution.py:465
  158.7 15.8 %collective-permute-done.16.refs_8_ = bf16[2,576,128]{2,1,0:T(8,128)(2,1)S(1)} collective-permute-done((bf16[2,576,128]{2,1,0:T(8,128)(2,1)S(1)}, bf16[2,576,128]{2,1,0:T(8,128)(2,1)S(1)}, u32[]{:S(2)}, u32[]{:S(2)}) %collective-permute-start.16) | collective-permute-done | bytes 294944 | tf_op jit(solution)/shard_map/ppermute | solution.py:223
  177.5 4.0 %collective-permute-start.17 = (bf16[64,512]{1,0:T(8,128)(2,1)S(1)}, bf16[64,512]{1,0:T(8,128)(2,1)S(1)}, u32[]{:S(2)}, u32[]{:S(2)}) collective-permute-start(bf16[64,512]{1,0:T(8,128)(2,1)S(1)} %get-tuple-element.168), channel_id=1, source_target_pairs={{0,1},{1,0},{2,3},{3,2},{4,5},{5,4},{6,7},{7,6},{8,9},{9,8},{10,11... | collective-permute-start | bytes 196616 | tf_op jit(solution)/shard_map/ppermute | solution.py:465
  181.8 7.9 %collective-permute-done.17 = bf16[64,512]{1,0:T(8,128)(2,1)S(1)} collective-permute-done((bf16[64,512]{1,0:T(8,128)(2,1)S(1)}, bf16[64,512]{1,0:T(8,128)(2,1)S(1)}, u32[]{:S(2)}, u32[]{:S(2)}) %collective-permute-start.17) | collective-permute-done | bytes 65568 | tf_op jit(solution)/shard_map/ppermute | solution.py:465
  191.5 15.3 %collective-permute-done.18 = bf16[64,512]{1,0:T(8,128)(2,1)S(1)} collective-permute-done((bf16[64,512]{1,0:T(8,128)(2,1)S(1)}, bf16[64,512]{1,0:T(8,128)(2,1)S(1)}, u32[]{:S(2)}, u32[]{:S(2)}) %collective-permute-start.18) | collective-permute-done | bytes 65568 | tf_op jit(solution)/shard_map/ppermute | solution.py:465
  212.2 8.1 %all-to-all-start.5 = ((bf16[16,32,512]{2,1,0:T(8,128)(2,1)}), bf16[16,32,512]{2,1,0:T(8,128)(2,1)S(1)}, u32[]{:S(2)}, u32[]{:S(2)}) async-start(bf16[16,32,512]{2,1,0:T(8,128)(2,1)} %add_convert_fusion), calls=%async_computation.5 | async-start | bytes 1048576 | tf_op jit(solution)/shard_map/all_to_all | solution.py:460
  225.9 5.0 %collective-permute-done.23 = bf16[128,512]{1,0:T(8,128)(2,1)S(1)} collective-permute-done((bf16[128,512]{1,0:T(8,128)(2,1)S(1)}, bf16[128,512]{1,0:T(8,128)(2,1)S(1)}, u32[]{:S(2)}, u32[]{:S(2)}) %collective-permute-start.23) | collective-permute-done | bytes 131104 | tf_op jit(solution)/shard_map/ppermute | solution.py:465
  230.9 4.6 %collective-permute-done.22 = bf16[128,512]{1,0:T(8,128)(2,1)S(1)} collective-permute-done((bf16[128,512]{1,0:T(8,128)(2,1)S(1)}, bf16[128,512]{1,0:T(8,128)(2,1)S(1)}, u32[]{:S(2)}, u32[]{:S(2)}) %collective-permute-start.22) | collective-permute-done | bytes 131104 | tf_op jit(solution)/shard_map/ppermute | solution.py:465
  237.5 5.5 %collective-permute-start.25 = (bf16[128,512]{1,0:T(8,128)(2,1)S(1)}, bf16[128,512]{1,0:T(8,128)(2,1)S(1)}, u32[]{:S(2)}, u32[]{:S(2)}) collective-permute-start(bf16[128,512]{1,0:T(8,128)(2,1)S(1)} %add_convert_fusion.2), channel_id=1, source_target_pairs={{0,32},{32,0},{1,33},{33,1},{2,34},{34,2},{3,35},{35,3},{4,36},{36... | collective-permute-start | bytes 393224 | tf_op jit(solution)/shard_map/ppermute | solution.py:518
  243.0 6.8 %collective-permute-done.25 = bf16[128,512]{1,0:T(8,128)(2,1)S(1)} collective-permute-done((bf16[128,512]{1,0:T(8,128)(2,1)S(1)}, bf16[128,512]{1,0:T(8,128)(2,1)S(1)}, u32[]{:S(2)}, u32[]{:S(2)}) %collective-permute-start.25) | collective-permute-done | bytes 131104 | tf_op jit(solution)/shard_map/ppermute | solution.py:518
  (111 shorter events, 58.4 us)
Async XLA Ops:
  8.7 25.1 %all-to-all-start.1 = ((bf16[16,288,128]{2,1,0:T(8,128)(2,1)}), bf16[16,288,128]{2,1,0:T(8,128)(2,1)S(1)}, u32[]{:S(2)}, u32[]{:S(2)}) async-start(bf16[16,288,128]{2,1,0:T(8,128)(2,1)} %shard_map.75), calls=%async_computation.1 | async-start | bytes 2359296 | tf_op jit(solution)/shard_map/all_to_all | solution.py:169
  16.5 22.7 %collective-permute-start.3 = (bf16[136,2048]{1,0:T(8,128)(2,1)S(1)}, bf16[136,2048]{1,0:T(8,128)(2,1)S(1)}, u32[]{:S(2)}, u32[]{:S(2)}) collective-permute-start(bf16[136,2048]{1,0:T(8,128)(2,1)S(1)} %fusion.1.a_ref.refs_2_), channel_id=1, source_target_pairs={{0,32},{32,0},{1,33},{33,1},{2,34},{34,2},{3,35},{35,3},{4,36},{36... | collective-permute-start | bytes 1671176 | tf_op jit(solution)/shard_map/ppermute | solution.py:481
  40.0 40.4 %all-to-all-start.2 = ((bf16[16,32,2048]{2,1,0:T(8,128)(2,1)}), bf16[16,32,2048]{2,1,0:T(8,128)(2,1)S(1)}, u32[]{:S(2)}, u32[]{:S(2)}) async-start(bf16[16,32,2048]{2,1,0:T(8,128)(2,1)} %bitcast.36), calls=%async_computation.2 | async-start | bytes 4194304 | tf_op jit(solution)/shard_map/all_to_all | solution.py:460
  48.2 19.1 %collective-permute-start.5 = (bf16[2,288,128]{2,1,0:T(8,128)(2,1)S(1)}, bf16[2,288,128]{2,1,0:T(8,128)(2,1)S(1)}, u32[]{:S(2)}, u32[]{:S(2)}) collective-permute-start(bf16[2,288,128]{2,1,0:T(8,128)(2,1)S(1)} %slice.43), channel_id=1, source_target_pairs={{0,32},{32,0},{1,33},{33,1},{2,34},{34,2},{3,35},{35,3},{4,36},{36... | collective-permute-start | bytes 442376 | tf_op jit(solution)/shard_map/ppermute | solution.py:206
  63.0 10.2 %collective-permute-start.4 = (bf16[136,2048]{1,0:T(8,128)(2,1)S(1)}, bf16[136,2048]{1,0:T(8,128)(2,1)}, u32[]{:S(2)}, u32[]{:S(2)}) collective-permute-start(bf16[136,2048]{1,0:T(8,128)(2,1)S(1)} %collective-permute-done.3.a_ref.refs_0_), channel_id=1, source_target_pairs={{0,4},{4,0},{1,5},{5,1},{2,6},{6,2},{3,7},{7,3},{8,12},{12,8},{9,1... | collective-permute-start | bytes 1671176 | tf_op jit(solution)/shard_map/ppermute | solution.py:490
  81.0 56.3 %all-to-all-start.4 = ((bf16[16,32,2048]{2,1,0:T(8,128)(2,1)}), bf16[16,32,2048]{2,1,0:T(8,128)(2,1)}, u32[]{:S(2)}, u32[]{:S(2)}) async-start(bf16[16,32,2048]{2,1,0:T(8,128)(2,1)} %bitcast.37), calls=%async_computation.4 | async-start | bytes 4194304 | tf_op jit(solution)/shard_map/all_to_all | solution.py:460
  88.3 32.1 %collective-permute-start.9 = (bf16[576,128]{1,0:T(8,128)(2,1)S(1)}, bf16[576,128]{1,0:T(8,128)(2,1)S(1)}, u32[]{:S(2)}, u32[]{:S(2)}) collective-permute-start(bf16[576,128]{1,0:T(8,128)(2,1)S(1)} %copy-done.16), channel_id=1, source_target_pairs={{0,192},{64,128},{128,64},{192,0},{1,193},{65,129},{129,65},{193,1... | collective-permute-start | bytes 442376 | tf_op jit(solution)/shard_map/ppermute | solution.py:217
  91.0 29.3 %collective-permute-start.8 = (bf16[576,128]{1,0:T(8,128)(2,1)S(1)}, bf16[576,128]{1,0:T(8,128)(2,1)S(1)}, u32[]{:S(2)}, u32[]{:S(2)}) collective-permute-start(bf16[576,128]{1,0:T(8,128)(2,1)S(1)} %copy-done.16), channel_id=1, source_target_pairs={{0,128},{64,192},{128,0},{192,64},{1,129},{65,193},{129,1},{193,65... | collective-permute-start | bytes 442376 | tf_op jit(solution)/shard_map/ppermute | solution.py:217
  91.9 28.5 %collective-permute-start.7 = (bf16[576,128]{1,0:T(8,128)(2,1)S(1)}, bf16[576,128]{1,0:T(8,128)(2,1)S(1)}, u32[]{:S(2)}, u32[]{:S(2)}) collective-permute-start(bf16[576,128]{1,0:T(8,128)(2,1)S(1)} %copy-done.16), channel_id=1, source_target_pairs={{0,64},{64,0},{128,192},{192,128},{1,65},{65,1},{129,193},{193,129... | collective-permute-start | bytes 442376 | tf_op jit(solution)/shard_map/ppermute | solution.py:217
  121.4 15.0 %collective-permute-start.11 = (bf16[4,576,128]{2,1,0:T(8,128)(2,1)S(1)}, bf16[4,576,128]{2,1,0:T(8,128)(2,1)S(1)}, u32[]{:S(2)}, u32[]{:S(2)}) collective-permute-start(bf16[4,576,128]{2,1,0:T(8,128)(2,1)S(1)} %pad_maximum_fusion.refs_4_), channel_id=1, source_target_pairs={{0,24},{8,0},{16,8},{24,16},{1,25},{9,1},{17,9},{25,17},{2,26},{10... | collective-permute-start | bytes 1769480 | tf_op jit(solution)/shard_map/ppermute | solution.py:223
  121.5 15.8 %collective-permute-start.10 = (bf16[4,576,128]{2,1,0:T(8,128)(2,1)S(1)}, bf16[4,576,128]{2,1,0:T(8,128)(2,1)}, u32[]{:S(2)}, u32[]{:S(2)}) collective-permute-start(bf16[4,576,128]{2,1,0:T(8,128)(2,1)S(1)} %pad_maximum_fusion.refs_4_), channel_id=1, source_target_pairs={{0,8},{8,16},{16,24},{24,0},{1,9},{9,17},{17,25},{25,1},{2,10},{10... | collective-permute-start | bytes 1769480 | tf_op jit(solution)/shard_map/ppermute | solution.py:223
  137.3 70.7 %all-to-all-start.3 = ((bf16[16,32,2048]{2,1,0:T(8,128)(2,1)}), bf16[16,32,2048]{2,1,0:T(8,128)(2,1)S(1)}, u32[]{:S(2)}, u32[]{:S(2)}) async-start(bf16[16,32,2048]{2,1,0:T(8,128)(2,1)} %shard_map.77), calls=%async_computation.3 | async-start | bytes 4194304 | tf_op jit(solution)/shard_map/all_to_all | solution.py:460
  145.6 28.9 %collective-permute-start.16 = (bf16[2,576,128]{2,1,0:T(8,128)(2,1)S(1)}, bf16[2,576,128]{2,1,0:T(8,128)(2,1)S(1)}, u32[]{:S(2)}, u32[]{:S(2)}) collective-permute-start(bf16[2,576,128]{2,1,0:T(8,128)(2,1)S(1)} %slice.45), channel_id=1, source_target_pairs={{0,24},{8,0},{16,8},{24,16},{1,25},{9,1},{17,9},{25,17},{2,26},{10... | collective-permute-start | bytes 884744 | tf_op jit(solution)/shard_map/ppermute | solution.py:223
  145.9 28.6 %collective-permute-start.15 = (bf16[2,576,128]{2,1,0:T(8,128)(2,1)S(1)}, bf16[2,576,128]{2,1,0:T(8,128)(2,1)S(1)}, u32[]{:S(2)}, u32[]{:S(2)}) collective-permute-start(bf16[2,576,128]{2,1,0:T(8,128)(2,1)S(1)} %slice.44), channel_id=1, source_target_pairs={{0,8},{8,16},{16,24},{24,0},{1,9},{9,17},{17,25},{25,1},{2,10},{10... | collective-permute-start | bytes 884744 | tf_op jit(solution)/shard_map/ppermute | solution.py:223
  152.5 54.4 %collective-permute-start.12 = (bf16[16,32,512]{2,1,0:T(8,128)(2,1)S(1)}, bf16[16,32,512]{2,1,0:T(8,128)(2,1)S(1)}, u32[]{:S(2)}, u32[]{:S(2)}) collective-permute-start(bf16[16,32,512]{2,1,0:T(8,128)(2,1)S(1)} %get-tuple-element.160), channel_id=1, source_target_pairs={{0,1},{1,0},{2,3},{3,2},{4,5},{5,4},{6,7},{7,6},{8,9},{9,8},{10,11... | collective-permute-start | bytes 1572872 | tf_op jit(solution)/shard_map/ppermute | solution.py:465
  156.3 50.6 %collective-permute-start.13 = (bf16[16,32,512]{2,1,0:T(8,128)(2,1)S(1)}, bf16[16,32,512]{2,1,0:T(8,128)(2,1)S(1)}, u32[]{:S(2)}, u32[]{:S(2)}) collective-permute-start(bf16[16,32,512]{2,1,0:T(8,128)(2,1)S(1)} %get-tuple-element.161), channel_id=1, source_target_pairs={{0,2},{1,3},{2,0},{3,1},{4,6},{5,7},{6,4},{7,5},{8,10},{9,11},{10,... | collective-permute-start | bytes 1572872 | tf_op jit(solution)/shard_map/ppermute | solution.py:465
  156.9 50.0 %collective-permute-start.14 = (bf16[16,32,512]{2,1,0:T(8,128)(2,1)S(1)}, bf16[16,32,512]{2,1,0:T(8,128)(2,1)S(1)}, u32[]{:S(2)}, u32[]{:S(2)}) collective-permute-start(bf16[16,32,512]{2,1,0:T(8,128)(2,1)S(1)} %get-tuple-element.162), channel_id=1, source_target_pairs={{0,3},{1,2},{2,1},{3,0},{4,7},{5,6},{6,5},{7,4},{8,11},{9,10},{10,... | collective-permute-start | bytes 1572872 | tf_op jit(solution)/shard_map/ppermute | solution.py:465
  177.5 12.2 %collective-permute-start.17 = (bf16[64,512]{1,0:T(8,128)(2,1)S(1)}, bf16[64,512]{1,0:T(8,128)(2,1)S(1)}, u32[]{:S(2)}, u32[]{:S(2)}) collective-permute-start(bf16[64,512]{1,0:T(8,128)(2,1)S(1)} %get-tuple-element.168), channel_id=1, source_target_pairs={{0,1},{1,0},{2,3},{3,2},{4,5},{5,4},{6,7},{7,6},{8,9},{9,8},{10,11... | collective-permute-start | bytes 196616 | tf_op jit(solution)/shard_map/ppermute | solution.py:465
  181.4 25.4 %collective-permute-start.18 = (bf16[64,512]{1,0:T(8,128)(2,1)S(1)}, bf16[64,512]{1,0:T(8,128)(2,1)S(1)}, u32[]{:S(2)}, u32[]{:S(2)}) collective-permute-start(bf16[64,512]{1,0:T(8,128)(2,1)S(1)} %get-tuple-element.169), channel_id=1, source_target_pairs={{0,2},{1,3},{2,0},{3,1},{4,6},{5,7},{6,4},{7,5},{8,10},{9,11},{10,... | collective-permute-start | bytes 196616 | tf_op jit(solution)/shard_map/ppermute | solution.py:465
  189.7 17.1 %collective-permute-start.19 = (bf16[64,512]{1,0:T(8,128)(2,1)S(1)}, bf16[64,512]{1,0:T(8,128)(2,1)S(1)}, u32[]{:S(2)}, u32[]{:S(2)}) collective-permute-start(bf16[64,512]{1,0:T(8,128)(2,1)S(1)} %get-tuple-element.170), channel_id=1, source_target_pairs={{0,3},{1,2},{2,1},{3,0},{4,7},{5,6},{6,5},{7,4},{8,11},{9,10},{10,... | collective-permute-start | bytes 196616 | tf_op jit(solution)/shard_map/ppermute | solution.py:465
  212.2 23.4 %all-to-all-start.5 = ((bf16[16,32,512]{2,1,0:T(8,128)(2,1)}), bf16[16,32,512]{2,1,0:T(8,128)(2,1)S(1)}, u32[]{:S(2)}, u32[]{:S(2)}) async-start(bf16[16,32,512]{2,1,0:T(8,128)(2,1)} %add_convert_fusion), calls=%async_computation.5 | async-start | bytes 1048576 | tf_op jit(solution)/shard_map/all_to_all | solution.py:460
  221.8 9.1 %collective-permute-start.23 = (bf16[128,512]{1,0:T(8,128)(2,1)S(1)}, bf16[128,512]{1,0:T(8,128)(2,1)S(1)}, u32[]{:S(2)}, u32[]{:S(2)}) collective-permute-start(bf16[128,512]{1,0:T(8,128)(2,1)S(1)} %get-tuple-element.200), channel_id=1, source_target_pairs={{0,3},{1,2},{2,1},{3,0},{4,7},{5,6},{6,5},{7,4},{8,11},{9,10},{10,... | collective-permute-start | bytes 393224 | tf_op jit(solution)/shard_map/ppermute | solution.py:465
  223.7 11.8 %collective-permute-start.22 = (bf16[128,512]{1,0:T(8,128)(2,1)S(1)}, bf16[128,512]{1,0:T(8,128)(2,1)S(1)}, u32[]{:S(2)}, u32[]{:S(2)}) collective-permute-start(bf16[128,512]{1,0:T(8,128)(2,1)S(1)} %get-tuple-element.201), channel_id=1, source_target_pairs={{0,2},{1,3},{2,0},{3,1},{4,6},{5,7},{6,4},{7,5},{8,10},{9,11},{10,... | collective-permute-start | bytes 393224 | tf_op jit(solution)/shard_map/ppermute | solution.py:465
  237.5 12.4 %collective-permute-start.25 = (bf16[128,512]{1,0:T(8,128)(2,1)S(1)}, bf16[128,512]{1,0:T(8,128)(2,1)S(1)}, u32[]{:S(2)}, u32[]{:S(2)}) collective-permute-start(bf16[128,512]{1,0:T(8,128)(2,1)S(1)} %add_convert_fusion.2), channel_id=1, source_target_pairs={{0,32},{32,0},{1,33},{33,1},{2,34},{34,2},{3,35},{35,3},{4,36},{36... | collective-permute-start | bytes 393224 | tf_op jit(solution)/shard_map/ppermute | solution.py:518
  (27 other events, 271.6 us)

commit v7 on v6

--- a/solution.py
+++ b/solution.py
@@ -210,44 +210,22 @@
     return jnp.concatenate([first, second], axis=0)
 
 
-def along_y(chunk):
-    n_y = lax.axis_size("y")
-    column = [chunk]
-    for k in range(1, n_y):
-        column.append(lax.ppermute(chunk, "y", [(i, i ^ k) for i in range(n_y)]))
-    return jnp.stack(column)
-
-
-def shift_x(array, step):
-    n_x = lax.axis_size("x")
-    return lax.ppermute(array, "x", [(i, (i + step) % n_x) for i in range(n_x)])
-
-
 def hot_kernel(info, *refs):
     *refs, near_ref, far_rows = refs
-    tok_refs, w_refs, far_refs = refs[:4], refs[4:9], refs[9:]
-    n_y, rows, lane = w_refs[0].shape
+    tok_refs, w_ref, far_refs = refs[:4], refs[4], refs[5:]
+    n_chunk, rows, lane = w_ref.shape
     units = rows // 3
     half = near_ref.shape[0]
     cols = far_refs[0].shape[1]
-    pieces = [(0, i, w_refs[0], i) for i in range(n_y)]
-    pieces += [(3, i, w_refs[1], i) for i in range(n_y)]
-    pieces += [(1, i, w_refs[2], i) for i in range(n_y)]
-    pieces += [(2, i, w_refs[3 + i // 2], i % 2) for i in range(n_y)]
-
-    def columns(far, i):
-        start = ((info[CHIP] >> 3 ^ i) * 4 + ((info[CHIP] + far) & 3)) * lane
-        return pl.ds(pl.multiple_of(start, lane), lane)
-
+    tok = jnp.concatenate([r[...] for r in tok_refs], axis=0)
     proj = jnp.zeros((2 * half, 2 * units), jnp.float32)
-    for far, i, w_ref, at in pieces:
-        tok = jnp.concatenate([r[:, columns(far, i)] for r in tok_refs], axis=0)
-        proj += dot(tok, w_ref[at, : 2 * units], 1, 1)
+    for n in range(n_chunk):
+        proj += dot(tok[:, n * lane : (n + 1) * lane], w_ref[n, : 2 * units], 1, 1)
     hidden = (jax.nn.silu(proj[:, :units]) * proj[:, units:]).astype(jnp.bfloat16)
-    for far, i, w_ref, at in pieces:
-        out = dot(hidden, w_ref[at, 2 * units :], 1, 0).astype(jnp.bfloat16)
-        far_rows[:, columns(far, i)] = out[:half]
-        near_ref[:, columns(far, i)] = out[half:]
+    for n in range(n_chunk):
+        out = dot(hidden, w_ref[n, 2 * units :], 1, 0).astype(jnp.bfloat16)
+        far_rows[:, n * lane : (n + 1) * lane] = out[:half]
+        near_ref[:, n * lane : (n + 1) * lane] = out[half:]
     for i, far_ref in enumerate(far_refs):
         start = pl.multiple_of((info[TENSOR] ^ i) * cols, cols)
         far_ref[...] = far_rows[:, pl.ds(start, cols)]
@@ -255,7 +233,7 @@
 
 def hot_ffn(info, blocks, hot_w, rows):
     width = blocks[0].shape[1]
-    w_size = sum(w.size for w in hot_w)
+    w_size = hot_w.size
     spec = pl.BlockSpec((rows, width), lambda i, info: (span_at(info, 0), 0))
     n_t = lax.axis_size("t")
     shapes = [jax.ShapeDtypeStruct((2 * rows, width // n_t), jnp.bfloat16)] * n_t
@@ -266,13 +244,13 @@
         grid_spec=pltpu.PrefetchScalarGridSpec(
             num_scalar_prefetch=1,
             grid=(1,),
-            in_specs=[spec] * 4 + [whole(w.shape) for w in hot_w],
+            in_specs=[spec] * 4 + [whole(hot_w.shape)],
             out_specs=[whole(shape.shape) for shape in shapes],
             scratch_shapes=[pltpu.VMEM((2 * rows, width), jnp.bfloat16)],
         ),
         compiler_params=PARAMS,
         cost_estimate=cost(8 * rows * w_size, 2 * w_size + 16 * rows * width),
-    )(info, *blocks, *hot_w)
+    )(info, *blocks, hot_w)
     return near, far
 
 
@@ -491,19 +469,15 @@
     far, far_mix, far_hot_mix = route(info, own_z, own_zc, tok_dev)
     hot_w = own_span(info, chunks, c)
     far, hot_w = lax.optimization_barrier((far.reshape(slots), hot_w))
+    hot_w = lax.all_gather(hot_w, ("y", "x"), axis=0, tiled=False)
     far = exchange(far)
-    hot_w = along_y(hot_w)
     (near,) = ffn(info, near, *experts, 1)
-    hot_w = (hot_w, shift_x(hot_w, 1), shift_x(hot_w, -1))
-    near, hot_w = lax.optimization_barrier((near, hot_w))
     near = exchange(near)
     far = ffn(info, far, *experts, n_t)
     far = total_of((far[0], *to_t(far, 1, 2, 3)))
-    half = hot_w[0].shape[0] // 2
-    hot_w += (shift_x(hot_w[1][:half], 1), shift_x(hot_w[2][half:], -1))
     near_hot, far_hot = hot_ffn(info, (own_z, own_zc, own, own_c), hot_w, tok_dev // SPANS)
     far_hot = total_of((far_hot[0], *to_t(far_hot, 1, 2, 3)))
-    near, far, near_hot, far_hot = lax.optimization_barrier((near, far, near_hot, far_hot))
+    near, far = lax.optimization_barrier((near, far))
 
     far = exchange(far).reshape(n_slot, width // n_t)
     mine, other = mix_rows(info, near_mix, near_hot_mix, near.reshape(n_slot, width), near_hot)

time: 251 us -> 247 us (0.984)
  between operations: 1.07 us -> 14.3 us
  starting transfers between devices: 88.7 us -> 78.4 us
  waiting for transfers between devices: 111 us -> 104 us
    ppermute x7 -> x0, waiting for transfers between devices: 51.2 us -> none  [the longest x3 27.9 us: along_y(): column.append(lax.ppermute(chunk, 'y', [(i, i ^ k) for i in range(n_y)]))]
    all_to_all x4, waiting for transfers between devices: 0.01 us -> 24 us  [exchange(): return lax.all_to_all(send, ('y', 'x'), 0, 0, tiled=True)]
    ppermute x9, waiting for transfers between devices: 34.6 us -> 54.7 us  [to_t(): lax.ppermute(groups[k], 't', [(i, i ^ k) for i in pairs])]
    ppermute x7 -> x0, starting transfers between devices: 8.38 us -> none  [the longest x4 4.2 us: shift_x(): return lax.ppermute(array, 'x', [(i, (i + step) % n_x) for i in range(n_x)])]
    ppermute x9, starting transfers between devices: 16 us -> 12.3 us  [to_t(): lax.ppermute(groups[k], 't', [(i, i ^ k) for i in pairs])]
    unnamed x43, local copies, waits for them, and re-layouts: 7.26 us -> 10.7 us
  transfers between devices with their start and end apart: 30 -> 24, of which waited for: 15 -> 13; matrix products, arithmetic and copies ran while one was open for 3% -> 2% of each run, Pallas kernels for 10% -> 9%
where the time goes in v7:
time: 247 us; the launch traced here: 246 us
  waiting for transfers between devices  104 us (42%)
  starting transfers between devices  78.4 us (32%)
  Pallas kernels  32.6 us (13%)
  between operations  14.3 us (6%)
  local copies, waits for them, and re-layouts  12.4 us (5%)
  other arithmetic  4.57 us (2%)
    ppermute x9, waiting for transfers between devices, to_t(): lax.ppermute(groups[k], 't', [(i, i ^ k) for i in pairs])  54.7 us
    all_to_all x4, starting transfers between devices, exchange(): return lax.all_to_all(send, ('y', 'x'), 0, 0, tiled=True)  30.3 us
    all_to_all x4, waiting for transfers between devices, exchange(): return lax.all_to_all(send, ('y', 'x'), 0, 0, tiled=True)  24 us
    ppermute x1, starting transfers between devices, own_span(): got = lax.ppermute(chunks[2:], 'zh', SWAP)  14.9 us
    ppermute x9, starting transfers between devices, to_t(): lax.ppermute(groups[k], 't', [(i, i ^ k) for i in pairs])  12.3 us
    unnamed x43, local copies, waits for them, and re-layouts  10.7 us
    pallas_call x2, Pallas kernels, ffn(): pl.pallas_call(ffn_kernel, out_shape=[jax.ShapeDtypeStruct((n_src, rows,...  9.35 us
    pallas_call x2, Pallas kernels, route(): pl.pallas_call(route_kernel, out_shape=shapes, grid_spec=pltpu.PrefetchSc...  9.13 us
  transfers between devices with their start and end apart: 24, of which 13 were waited for; matrix products, arithmetic and copies ran while one was open for 2% of the time, Pallas kernels for 9%

profile of v7, /device:TPU:2, one launch (start us, length us, event | category | flops | bytes accessed | tf_op | source)
XLA Modules:
  0.0 245.7 jit_solution(2662285437084989536)
XLA Ops:
  7.3 3.3 %shard_map.74 = (bf16[16,288,128]{2,1,0:T(8,128)(2,1)S(1)}, bf16[16,288,128]{2,1,0:T(8,128)(2,1)S(1)}) custom-call(s32[9]{0:T(128)S(1)} %concatenate.14.info, bf16[2,192,2048]{2,1,0:T(8,128)(2,1)} %gate_ref.5, bf16[2,192,2048]{2,1,0:T(8,128)(2,1)} %up_ref.5, bf16[2,192,2048]{2,1,0:T(8,128)(2,1)} %down_ref.5), custom_call_target="tpu_custom_call" | custom-call | bytes 4718592 | tf_op jit(solution)/shard_map/pallas_call | solution.py:89
  15.2 7.6 %all-to-all-start.1 = ((bf16[16,288,128]{2,1,0:T(8,128)(2,1)}), bf16[16,288,128]{2,1,0:T(8,128)(2,1)S(1)}, u32[]{:S(2)}, u32[]{:S(2)}) async-start(bf16[16,288,128]{2,1,0:T(8,128)(2,1)} %shard_map.75), calls=%async_computation.1 | async-start | bytes 2359296 | tf_op jit(solution)/shard_map/all_to_all | solution.py:169
  23.1 7.3 %collective-permute-start.3 = (bf16[136,2048]{1,0:T(8,128)(2,1)S(1)}, bf16[136,2048]{1,0:T(8,128)(2,1)S(1)}, u32[]{:S(2)}, u32[]{:S(2)}) collective-permute-start(bf16[136,2048]{1,0:T(8,128)(2,1)S(1)} %fusion.1.a_ref.refs_2_), channel_id=1, source_target_pairs={{0,32},{32,0},{1,33},{33,1},{2,34},{34,2},{3,35},{35,3},{4,36},{36... | collective-permute-start | bytes 1671176 | tf_op jit(solution)/shard_map/ppermute | solution.py:459
  31.8 4.0 %shard_map.73 = (bf16[512,2048]{1,0:T(8,128)(2,1)S(1)}, bf16[512,256]{1,0:T(8,128)(2,1)S(1)}, bf16[64,256]{1,0:T(8,128)(2,1)S(1)}) custom-call(s32[9]{0:T(128)S(1)} %concatenate.14.info, bf16[136,2048]{1,0:T(8,128)(2,1)S(1)} %fusion.1.a_ref.refs_2_, bf16[136,2048]{1,0:T(8,128)(2,1)S(1)} %collective-permute-done.1.b_ref.refs_3_), custom_call_target="tpu_custom_call" | custom-call | flops 536870912 | bytes 3145728 | tf_op jit(solution)/shard_map/pallas_call | solution.py:324
  37.2 3.2 %all-to-all-done.1.part_ref = bf16[16,288,128]{2,1,0:T(8,128)(2,1)S(1)} async-done(((bf16[16,288,128]{2,1,0:T(8,128)(2,1)}), bf16[16,288,128]{2,1,0:T(8,128)(2,1)S(1)}, u32[]{:S(2)}, u32[]{:S(2)}) %all-to-all-start.1) | async-done | bytes 1179680 | tf_op jit(solution)/shard_map/all_to_all | solution.py:169
  41.0 4.8 %collective-permute-done.3.a_ref.refs_0_ = bf16[136,2048]{1,0:T(8,128)(2,1)S(1)} collective-permute-done((bf16[136,2048]{1,0:T(8,128)(2,1)S(1)}, bf16[136,2048]{1,0:T(8,128)(2,1)S(1)}, u32[]{:S(2)}, u32[]{:S(2)}) %collective-permute-start.3) | collective-permute-done | bytes 557088 | tf_op jit(solution)/shard_map/ppermute | solution.py:459
  47.4 7.2 %all-to-all-start.2 = ((bf16[16,32,2048]{2,1,0:T(8,128)(2,1)}), bf16[16,32,2048]{2,1,0:T(8,128)(2,1)S(1)}, u32[]{:S(2)}, u32[]{:S(2)}) async-start(bf16[16,32,2048]{2,1,0:T(8,128)(2,1)} %bitcast.34), calls=%async_computation.2 | async-start | bytes 4194304 | tf_op jit(solution)/shard_map/all_to_all | solution.py:438
  55.6 14.9 %collective-permute-start.5 = (bf16[2,288,128]{2,1,0:T(8,128)(2,1)S(1)}, bf16[2,288,128]{2,1,0:T(8,128)(2,1)S(1)}, u32[]{:S(2)}, u32[]{:S(2)}) collective-permute-start(bf16[2,288,128]{2,1,0:T(8,128)(2,1)S(1)} %slice.37), channel_id=1, source_target_pairs={{0,32},{32,0},{1,33},{33,1},{2,34},{34,2},{3,35},{35,3},{4,36},{36... | collective-permute-start | bytes 442376 | tf_op jit(solution)/shard_map/ppermute | solution.py:206
  70.4 4.3 %collective-permute-done.5.got_ref = bf16[2,288,128]{2,1,0:T(8,128)(2,1)S(1)} collective-permute-done((bf16[2,288,128]{2,1,0:T(8,128)(2,1)S(1)}, bf16[2,288,128]{2,1,0:T(8,128)(2,1)S(1)}, u32[]{:S(2)}, u32[]{:S(2)}) %collective-permute-start.5) | collective-permute-done | bytes 147488 | tf_op jit(solution)/shard_map/ppermute | solution.py:206
  81.1 5.1 %shard_map.78 = (bf16[512,2048]{1,0:T(8,128)(2,1)S(1)}, bf16[512,256]{1,0:T(8,128)(2,1)S(1)}, bf16[64,256]{1,0:T(8,128)(2,1)S(1)}) custom-call(s32[9]{0:T(128)S(1)} %get-tuple-element.318, bf16[136,2048]{1,0:T(8,128)(2,1)S(1)} %copy-done.5, bf16[136,2048]{1,0:T(8,128)(2,1)} %collective-permute-done.4.b_ref.refs_1_), custom_call_target="tpu_custom_call" | custom-call | flops 536870912 | bytes 3145728 | tf_op jit(solution)/shard_map/pallas_call | solution.py:324
  88.9 7.3 %all-to-all-start.4 = ((bf16[16,32,2048]{2,1,0:T(8,128)(2,1)}), bf16[16,32,2048]{2,1,0:T(8,128)(2,1)}, u32[]{:S(2)}, u32[]{:S(2)}) async-start(bf16[16,32,2048]{2,1,0:T(8,128)(2,1)} %bitcast.35), calls=%async_computation.4 | async-start | bytes 4194304 | tf_op jit(solution)/shard_map/all_to_all | solution.py:438
  96.1 4.5 %shard_map.77 = bf16[16,32,2048]{2,1,0:T(8,128)(2,1)S(1)} custom-call(s32[9]{0:T(128)S(1)} %get-tuple-element.318, bf16[16,32,2048]{2,1,0:T(8,128)(2,1)S(1)} %all-to-all-done.2.x_ref, bf16[2,192,2048]{2,1,0:T(8,128)(2,1)} %get-tuple-element.294, bf16[2,192,2048]{2,1,0:T(8,128)(2,1)} %get-tuple-element.295, bf16[2,192,2048]{2,1,0:T(8,128)(2,1)} %get-tuple-element.296), custom_call_target="tpu_custom_call" | custom-call | flops 1207959552 | bytes 8912896 | tf_op jit(solution)/shard_map/pallas_call | solution.py:369
  102.0 24.0 %all-to-all-done.4.x_ref = bf16[16,32,2048]{2,1,0:T(8,128)(2,1)} async-done(((bf16[16,32,2048]{2,1,0:T(8,128)(2,1)}), bf16[16,32,2048]{2,1,0:T(8,128)(2,1)}, u32[]{:S(2)}, u32[]{:S(2)}) %all-to-all-start.4) | async-done | bytes 2097184 | tf_op jit(solution)/shard_map/all_to_all | solution.py:438
  126.0 8.6 %all-to-all-start.3 = ((bf16[16,32,2048]{2,1,0:T(8,128)(2,1)}), bf16[16,32,2048]{2,1,0:T(8,128)(2,1)S(1)}, u32[]{:S(2)}, u32[]{:S(2)}) async-start(bf16[16,32,2048]{2,1,0:T(8,128)(2,1)} %copy-done), calls=%async_computation.3 | async-start | bytes 4194304 | tf_op jit(solution)/shard_map/all_to_all | solution.py:438
  134.6 4.8 %shard_map.80 = (bf16[16,32,512]{2,1,0:T(8,128)(2,1)S(1)}, bf16[16,32,512]{2,1,0:T(8,128)(2,1)S(1)}, bf16[16,32,512]{2,1,0:T(8,128)(2,1)S(1)}, bf16[16,32,512]{2,1,0:T(8,128)(2,1)S(1)}) custom-call(s32[9]{0:T(128)S(1)} %get-tuple-element.318, bf16[16,32,2048]{2,1,0:T(8,128)(2,1)} %all-to-all-done.4.x_ref, bf16[2,192,2048]{2,1,0:T(8,128)(2,1)} %get-tuple-element.294, ...), custom_call_target="tpu_custom_call" | custom-call | flops 1207959552 | bytes 8912896 | tf_op jit(solution)/shard_map/pallas_call | solution.py:369
  139.5 3.1 %collective-permute-start.8 = (bf16[16,32,512]{2,1,0:T(8,128)(2,1)S(1)}, bf16[16,32,512]{2,1,0:T(8,128)(2,1)S(1)}, u32[]{:S(2)}, u32[]{:S(2)}) collective-permute-start(bf16[16,32,512]{2,1,0:T(8,128)(2,1)S(1)} %get-tuple-element.153), channel_id=1, source_target_pairs={{0,2},{1,3},{2,0},{3,1},{4,6},{5,7},{6,4},{7,5},{8,10},{9,11},{10,... | collective-permute-start | bytes 1572872 | tf_op jit(solution)/shard_map/ppermute | solution.py:443
  143.9 12.4 %collective-permute-done.9 = bf16[16,32,512]{2,1,0:T(8,128)(2,1)S(1)} collective-permute-done((bf16[16,32,512]{2,1,0:T(8,128)(2,1)S(1)}, bf16[16,32,512]{2,1,0:T(8,128)(2,1)S(1)}, u32[]{:S(2)}, u32[]{:S(2)}) %collective-permute-start.9) | collective-permute-done | bytes 524320 | tf_op jit(solution)/shard_map/ppermute | solution.py:443
  156.3 30.4 %collective-permute-done.8 = bf16[16,32,512]{2,1,0:T(8,128)(2,1)S(1)} collective-permute-done((bf16[16,32,512]{2,1,0:T(8,128)(2,1)S(1)}, bf16[16,32,512]{2,1,0:T(8,128)(2,1)S(1)}, u32[]{:S(2)}, u32[]{:S(2)}) %collective-permute-start.8) | collective-permute-done | bytes 524320 | tf_op jit(solution)/shard_map/ppermute | solution.py:443
  193.3 3.2 %shard_map.82 = (bf16[4,128,512]{2,1,0:T(8,128)(2,1)S(1)}, bf16[4,128,512]{2,1,0:T(8,128)(2,1)}) custom-call(s32[9]{0:T(128)S(1)} %get-tuple-element.318, bf16[512,256]{1,0:T(8,128)(2,1)S(1)} %get-tuple-element.156.mix_ref, bf16[64,256]{1,0:T(8,128)(2,1)S(1)} %copy-done.10, bf16[512,2048]{1,0:T(8,128)(2,1)S(1)} %bitcast.31, ...), custom_call_target="tpu_custom_call" | custom-call | flops 536870912 | bytes 3145728 | tf_op jit(solution)/shard_map/pallas_call | solution.py:398
  196.7 7.2 %all-to-all-start.5 = ((bf16[16,32,512]{2,1,0:T(8,128)(2,1)}), bf16[16,32,512]{2,1,0:T(8,128)(2,1)S(1)}, u32[]{:S(2)}, u32[]{:S(2)}) async-start(bf16[16,32,512]{2,1,0:T(8,128)(2,1)} %add_convert_fusion), calls=%async_computation.5 | async-start | bytes 1048576 | tf_op jit(solution)/shard_map/all_to_all | solution.py:438
  212.9 4.3 %collective-permute-done.15 = bf16[64,512]{1,0:T(8,128)(2,1)S(1)} collective-permute-done((bf16[64,512]{1,0:T(8,128)(2,1)}, bf16[64,512]{1,0:T(8,128)(2,1)S(1)}, u32[]{:S(2)}, u32[]{:S(2)}) %collective-permute-start.15) | collective-permute-done | bytes 65568 | tf_op jit(solution)/shard_map/ppermute | solution.py:443
  217.2 6.7 %collective-permute-done.12 = bf16[128,512]{1,0:T(8,128)(2,1)S(1)} collective-permute-done((bf16[128,512]{1,0:T(8,128)(2,1)S(1)}, bf16[128,512]{1,0:T(8,128)(2,1)S(1)}, u32[]{:S(2)}, u32[]{:S(2)}) %collective-permute-start.12) | collective-permute-done | bytes 131104 | tf_op jit(solution)/shard_map/ppermute | solution.py:443
  225.9 5.5 %collective-permute-start.18 = (bf16[128,512]{1,0:T(8,128)(2,1)S(1)}, bf16[128,512]{1,0:T(8,128)(2,1)S(1)}, u32[]{:S(2)}, u32[]{:S(2)}) collective-permute-start(bf16[128,512]{1,0:T(8,128)(2,1)S(1)} %add_convert_fusion.2), channel_id=1, source_target_pairs={{0,32},{32,0},{1,33},{33,1},{2,34},{34,2},{3,35},{35,3},{4,36},{36... | collective-permute-start | bytes 393224 | tf_op jit(solution)/shard_map/ppermute | solution.py:492
  231.4 6.8 %collective-permute-done.18 = bf16[128,512]{1,0:T(8,128)(2,1)S(1)} collective-permute-done((bf16[128,512]{1,0:T(8,128)(2,1)S(1)}, bf16[128,512]{1,0:T(8,128)(2,1)S(1)}, u32[]{:S(2)}, u32[]{:S(2)}) %collective-permute-start.18) | collective-permute-done | bytes 131104 | tf_op jit(solution)/shard_map/ppermute | solution.py:492
  (97 shorter events, 40.9 us)
Async XLA Ops:
  10.6 2.9 %collective-permute-start.2 = (bf16[16,288,128]{2,1,0:T(8,128)(2,1)S(1)}, bf16[16,288,128]{2,1,0:T(8,128)(2,1)S(1)}, u32[]{:S(2)}, u32[]{:S(2)}) collective-permute-start(bf16[16,288,128]{2,1,0:T(8,128)(2,1)S(1)} %get-tuple-element.142), channel_id=1, source_target_pairs={{0,4},{4,0},{1,5},{5,1},{2,6},{6,2},{3,7},{7,3},{8,12},{12,8},{9,1... | collective-permute-start | bytes 3538952 | tf_op jit(solution)/shard_map/ppermute | solution.py:168
  15.2 25.1 %all-to-all-start.1 = ((bf16[16,288,128]{2,1,0:T(8,128)(2,1)}), bf16[16,288,128]{2,1,0:T(8,128)(2,1)S(1)}, u32[]{:S(2)}, u32[]{:S(2)}) async-start(bf16[16,288,128]{2,1,0:T(8,128)(2,1)} %shard_map.75), calls=%async_computation.1 | async-start | bytes 2359296 | tf_op jit(solution)/shard_map/all_to_all | solution.py:169
  23.0 8.8 %collective-permute-start.1 = (bf16[136,2048]{1,0:T(8,128)(2,1)S(1)}, bf16[136,2048]{1,0:T(8,128)(2,1)S(1)}, u32[]{:S(2)}, u32[]{:S(2)}) collective-permute-start(bf16[136,2048]{1,0:T(8,128)(2,1)S(1)} %fusion.1.a_ref.refs_2_), channel_id=1, source_target_pairs={{0,4},{4,0},{1,5},{5,1},{2,6},{6,2},{3,7},{7,3},{8,12},{12,8},{9,1... | collective-permute-start | bytes 1671176 | tf_op jit(solution)/shard_map/ppermute | solution.py:460
  23.1 22.7 %collective-permute-start.3 = (bf16[136,2048]{1,0:T(8,128)(2,1)S(1)}, bf16[136,2048]{1,0:T(8,128)(2,1)S(1)}, u32[]{:S(2)}, u32[]{:S(2)}) collective-permute-start(bf16[136,2048]{1,0:T(8,128)(2,1)S(1)} %fusion.1.a_ref.refs_2_), channel_id=1, source_target_pairs={{0,32},{32,0},{1,33},{33,1},{2,34},{34,2},{3,35},{35,3},{4,36},{36... | collective-permute-start | bytes 1671176 | tf_op jit(solution)/shard_map/ppermute | solution.py:459
  47.4 41.5 %all-to-all-start.2 = ((bf16[16,32,2048]{2,1,0:T(8,128)(2,1)}), bf16[16,32,2048]{2,1,0:T(8,128)(2,1)S(1)}, u32[]{:S(2)}, u32[]{:S(2)}) async-start(bf16[16,32,2048]{2,1,0:T(8,128)(2,1)} %bitcast.34), calls=%async_computation.2 | async-start | bytes 4194304 | tf_op jit(solution)/shard_map/all_to_all | solution.py:438
  54.6 133.3 %all-gather.3.cloned.1.call-start = ((), (), s32[]{:S(2)}) async-start(), calls=%async_computation.6 | async-start | bytes 2506752 | tf_op jit(solution)/shard_map/all_gather | solution.py:472
  55.6 19.1 %collective-permute-start.5 = (bf16[2,288,128]{2,1,0:T(8,128)(2,1)S(1)}, bf16[2,288,128]{2,1,0:T(8,128)(2,1)S(1)}, u32[]{:S(2)}, u32[]{:S(2)}) collective-permute-start(bf16[2,288,128]{2,1,0:T(8,128)(2,1)S(1)} %slice.37), channel_id=1, source_target_pairs={{0,32},{32,0},{1,33},{33,1},{2,34},{34,2},{3,35},{35,3},{4,36},{36... | collective-permute-start | bytes 442376 | tf_op jit(solution)/shard_map/ppermute | solution.py:206
  70.4 9.6 %collective-permute-start.4 = (bf16[136,2048]{1,0:T(8,128)(2,1)}, bf16[136,2048]{1,0:T(8,128)(2,1)}, u32[]{:S(2)}, u32[]{:S(2)}) collective-permute-start(bf16[136,2048]{1,0:T(8,128)(2,1)} %copy-done.4), channel_id=1, source_target_pairs={{0,4},{4,0},{1,5},{5,1},{2,6},{6,2},{3,7},{7,3},{8,12},{12,8},{9,1... | collective-permute-start | bytes 1671176 | tf_op jit(solution)/shard_map/ppermute | solution.py:468
  76.8 1.6 collective-permute-start.6
  88.9 37.2 %all-to-all-start.4 = ((bf16[16,32,2048]{2,1,0:T(8,128)(2,1)}), bf16[16,32,2048]{2,1,0:T(8,128)(2,1)}, u32[]{:S(2)}, u32[]{:S(2)}) async-start(bf16[16,32,2048]{2,1,0:T(8,128)(2,1)} %bitcast.35), calls=%async_computation.4 | async-start | bytes 4194304 | tf_op jit(solution)/shard_map/all_to_all | solution.py:438
  126.0 61.9 %all-to-all-start.3 = ((bf16[16,32,2048]{2,1,0:T(8,128)(2,1)}), bf16[16,32,2048]{2,1,0:T(8,128)(2,1)S(1)}, u32[]{:S(2)}, u32[]{:S(2)}) async-start(bf16[16,32,2048]{2,1,0:T(8,128)(2,1)} %copy-done), calls=%async_computation.3 | async-start | bytes 4194304 | tf_op jit(solution)/shard_map/all_to_all | solution.py:438
  139.4 16.8 %collective-permute-start.9 = (bf16[16,32,512]{2,1,0:T(8,128)(2,1)S(1)}, bf16[16,32,512]{2,1,0:T(8,128)(2,1)S(1)}, u32[]{:S(2)}, u32[]{:S(2)}) collective-permute-start(bf16[16,32,512]{2,1,0:T(8,128)(2,1)S(1)} %get-tuple-element.154), channel_id=1, source_target_pairs={{0,3},{1,2},{2,1},{3,0},{4,7},{5,6},{6,5},{7,4},{8,11},{9,10},{10,... | collective-permute-start | bytes 1572872 | tf_op jit(solution)/shard_map/ppermute | solution.py:443
  139.5 47.2 %collective-permute-start.8 = (bf16[16,32,512]{2,1,0:T(8,128)(2,1)S(1)}, bf16[16,32,512]{2,1,0:T(8,128)(2,1)S(1)}, u32[]{:S(2)}, u32[]{:S(2)}) collective-permute-start(bf16[16,32,512]{2,1,0:T(8,128)(2,1)S(1)} %get-tuple-element.153), channel_id=1, source_target_pairs={{0,2},{1,3},{2,0},{3,1},{4,6},{5,7},{6,4},{7,5},{8,10},{9,11},{10,... | collective-permute-start | bytes 1572872 | tf_op jit(solution)/shard_map/ppermute | solution.py:443
  142.7 44.0 %collective-permute-start.7 = (bf16[16,32,512]{2,1,0:T(8,128)(2,1)S(1)}, bf16[16,32,512]{2,1,0:T(8,128)(2,1)S(1)}, u32[]{:S(2)}, u32[]{:S(2)}) collective-permute-start(bf16[16,32,512]{2,1,0:T(8,128)(2,1)S(1)} %get-tuple-element.152), channel_id=1, source_target_pairs={{0,1},{1,0},{2,3},{3,2},{4,5},{5,4},{6,7},{7,6},{8,9},{9,8},{10,11... | collective-permute-start | bytes 1572872 | tf_op jit(solution)/shard_map/ppermute | solution.py:443
  196.6 11.7 %collective-permute-start.10 = (bf16[4,128,512]{2,1,0:T(8,128)(2,1)}, bf16[4,128,512]{2,1,0:T(8,128)(2,1)S(1)}, u32[]{:S(2)}, u32[]{:S(2)}) collective-permute-start(bf16[4,128,512]{2,1,0:T(8,128)(2,1)} %get-tuple-element.162), channel_id=1, source_target_pairs={{0,4},{4,0},{1,5},{5,1},{2,6},{6,2},{3,7},{7,3},{8,12},{12,8},{9,1... | collective-permute-start | bytes 1572872 | tf_op jit(solution)/shard_map/ppermute | solution.py:484
  196.7 27.3 %all-to-all-start.5 = ((bf16[16,32,512]{2,1,0:T(8,128)(2,1)}), bf16[16,32,512]{2,1,0:T(8,128)(2,1)S(1)}, u32[]{:S(2)}, u32[]{:S(2)}) async-start(bf16[16,32,512]{2,1,0:T(8,128)(2,1)} %add_convert_fusion), calls=%async_computation.5 | async-start | bytes 1048576 | tf_op jit(solution)/shard_map/all_to_all | solution.py:438
  203.9 7.1 %collective-permute-start.16 = (bf16[64,512]{1,0:T(8,128)(2,1)}, bf16[64,512]{1,0:T(8,128)(2,1)S(1)}, u32[]{:S(2)}, u32[]{:S(2)}) collective-permute-start(bf16[64,512]{1,0:T(8,128)(2,1)} %copy-done.15), channel_id=1, source_target_pairs={{0,3},{1,2},{2,1},{3,0},{4,7},{5,6},{6,5},{7,4},{8,11},{9,10},{10,... | collective-permute-start | bytes 196616 | tf_op jit(solution)/shard_map/ppermute | solution.py:443
  205.2 12.0 %collective-permute-start.15 = (bf16[64,512]{1,0:T(8,128)(2,1)}, bf16[64,512]{1,0:T(8,128)(2,1)S(1)}, u32[]{:S(2)}, u32[]{:S(2)}) collective-permute-start(bf16[64,512]{1,0:T(8,128)(2,1)} %copy-done.14), channel_id=1, source_target_pairs={{0,2},{1,3},{2,0},{3,1},{4,6},{5,7},{6,4},{7,5},{8,10},{9,11},{10,... | collective-permute-start | bytes 196616 | tf_op jit(solution)/shard_map/ppermute | solution.py:443
  205.2 12.0 %collective-permute-start.14 = (bf16[64,512]{1,0:T(8,128)(2,1)}, bf16[64,512]{1,0:T(8,128)(2,1)S(1)}, u32[]{:S(2)}, u32[]{:S(2)}) collective-permute-start(bf16[64,512]{1,0:T(8,128)(2,1)} %copy-done.13), channel_id=1, source_target_pairs={{0,1},{1,0},{2,3},{3,2},{4,5},{5,4},{6,7},{7,6},{8,9},{9,8},{10,11... | collective-permute-start | bytes 196616 | tf_op jit(solution)/shard_map/ppermute | solution.py:443
  208.4 8.8 %collective-permute-start.13 = (bf16[128,512]{1,0:T(8,128)(2,1)S(1)}, bf16[128,512]{1,0:T(8,128)(2,1)S(1)}, u32[]{:S(2)}, u32[]{:S(2)}) collective-permute-start(bf16[128,512]{1,0:T(8,128)(2,1)S(1)} %get-tuple-element.188), channel_id=1, source_target_pairs={{0,3},{1,2},{2,1},{3,0},{4,7},{5,6},{6,5},{7,4},{8,11},{9,10},{10,... | collective-permute-start | bytes 393224 | tf_op jit(solution)/shard_map/ppermute | solution.py:443
  209.8 14.1 %collective-permute-start.12 = (bf16[128,512]{1,0:T(8,128)(2,1)S(1)}, bf16[128,512]{1,0:T(8,128)(2,1)S(1)}, u32[]{:S(2)}, u32[]{:S(2)}) collective-permute-start(bf16[128,512]{1,0:T(8,128)(2,1)S(1)} %get-tuple-element.189), channel_id=1, source_target_pairs={{0,2},{1,3},{2,0},{3,1},{4,6},{5,7},{6,4},{7,5},{8,10},{9,11},{10,... | collective-permute-start | bytes 393224 | tf_op jit(solution)/shard_map/ppermute | solution.py:443
  211.0 12.9 %collective-permute-start.11 = (bf16[128,512]{1,0:T(8,128)(2,1)S(1)}, bf16[128,512]{1,0:T(8,128)(2,1)S(1)}, u32[]{:S(2)}, u32[]{:S(2)}) collective-permute-start(bf16[128,512]{1,0:T(8,128)(2,1)S(1)} %get-tuple-element.187), channel_id=1, source_target_pairs={{0,1},{1,0},{2,3},{3,2},{4,5},{5,4},{6,7},{7,6},{8,9},{9,8},{10,11... | collective-permute-start | bytes 393224 | tf_op jit(solution)/shard_map/ppermute | solution.py:443
  224.4 1.4 collective-permute-start.17
  225.9 12.4 %collective-permute-start.18 = (bf16[128,512]{1,0:T(8,128)(2,1)S(1)}, bf16[128,512]{1,0:T(8,128)(2,1)S(1)}, u32[]{:S(2)}, u32[]{:S(2)}) collective-permute-start(bf16[128,512]{1,0:T(8,128)(2,1)S(1)} %add_convert_fusion.2), channel_id=1, source_target_pairs={{0,32},{32,0},{1,33},{33,1},{2,34},{34,2},{3,35},{35,3},{4,36},{36... | collective-permute-start | bytes 393224 | tf_op jit(solution)/shard_map/ppermute | solution.py:492
  (21 other events, 101.4 us)
Sparse Core Ops, SparseCore 0:
  89.0 81.2 all-gather.2

commit v8 on v6

--- a/solution.py
+++ b/solution.py
@@ -489,25 +489,25 @@
     near = exchange(near)
     own_zc = lax.ppermute(own_z, "c", SWAP)
     far, far_mix, far_hot_mix = route(info, own_z, own_zc, tok_dev)
-    hot_w = own_span(info, chunks, c)
+    hot_w = along_y(own_span(info, chunks, c))
     far, hot_w = lax.optimization_barrier((far.reshape(slots), hot_w))
     far = exchange(far)
-    hot_w = along_y(hot_w)
+    hot_w = (hot_w, shift_x(hot_w, 1), shift_x(hot_w, -1))
     (near,) = ffn(info, near, *experts, 1)
-    hot_w = (hot_w, shift_x(hot_w, 1), shift_x(hot_w, -1))
     near, hot_w = lax.optimization_barrier((near, hot_w))
     near = exchange(near)
     far = ffn(info, far, *experts, n_t)
-    far = total_of((far[0], *to_t(far, 1, 2, 3)))
+    far, hot_w = lax.optimization_barrier((tuple(far), hot_w))
     half = hot_w[0].shape[0] // 2
     hot_w += (shift_x(hot_w[1][:half], 1), shift_x(hot_w[2][half:], -1))
+    far = total_of((far[0], *to_t(far, 1, 2, 3)))
     near_hot, far_hot = hot_ffn(info, (own_z, own_zc, own, own_c), hot_w, tok_dev // SPANS)
-    far_hot = total_of((far_hot[0], *to_t(far_hot, 1, 2, 3)))
-    near, far, near_hot, far_hot = lax.optimization_barrier((near, far, near_hot, far_hot))
-
-    far = exchange(far).reshape(n_slot, width // n_t)
     mine, other = mix_rows(info, near_mix, near_hot_mix, near.reshape(n_slot, width), near_hot)
     got = lax.ppermute(other, "c", SWAP)
+    mine, got, far, far_hot = lax.optimization_barrier((mine, got, far, far_hot))
+
+    far_hot = total_of((far_hot[0], *to_t(far_hot, 1, 2, 3)))
+    far = exchange(far).reshape(n_slot, width // n_t)
     pieces = [mine[k].astype(jnp.float32) + got[k].astype(jnp.float32) for k in range(n_t)]
     total = pieces[0]
     for part in to_t([piece.astype(jnp.bfloat16) for piece in pieces], 1, 2, 3):

time: 251 us -> 253 us (level)
  starting transfers between devices: 88.7 us -> 101 us
  waiting for transfers between devices: 111 us -> 101 us
    ppermute x3, waiting for transfers between devices: 27.9 us -> 8.26 us  [along_y(): column.append(lax.ppermute(chunk, 'y', [(i, i ^ k) for i in range(n_y)]))]
    ppermute x4, waiting for transfers between devices: 23.3 us -> 41.4 us  [shift_x(): return lax.ppermute(array, 'x', [(i, (i + step) % n_x) for i in range(n_x)])]
    ppermute x9, starting transfers between devices: 16 us -> 28 us  [to_t(): lax.ppermute(groups[k], 't', [(i, i ^ k) for i in pairs])]
    ppermute x9, waiting for transfers between devices: 34.6 us -> 27.2 us  [to_t(): lax.ppermute(groups[k], 't', [(i, i ^ k) for i in pairs])]
    unnamed x43 -> x59, local copies, waits for them, and re-layouts: 7.26 us -> 11.1 us
  transfers between devices with their start and end apart: 30 -> 30, of which waited for: 15 -> 16; matrix products, arithmetic and copies ran while one was open for 3% -> 2% of each run, Pallas kernels for 10% -> 10%
where the time goes in v8:
time: 253 us; the launch traced here: 252 us
  starting transfers between devices  101 us (40%)
  waiting for transfers between devices  101 us (40%)
  Pallas kernels  31.2 us (12%)
  local copies, waits for them, and re-layouts  13 us (5%)
  other arithmetic  4.45 us (2%)
    ppermute x4, waiting for transfers between devices, shift_x(): return lax.ppermute(array, 'x', [(i, (i + step) % n_x) for i in range(n_x)])  41.4 us
    all_to_all x4, starting transfers between devices, exchange(): return lax.all_to_all(send, ('y', 'x'), 0, 0, tiled=True)  28.7 us
    ppermute x9, starting transfers between devices, to_t(): lax.ppermute(groups[k], 't', [(i, i ^ k) for i in pairs])  28 us
    ppermute x9, waiting for transfers between devices, to_t(): lax.ppermute(groups[k], 't', [(i, i ^ k) for i in pairs])  27.2 us
    ppermute x1, starting transfers between devices, own_span(): got = lax.ppermute(chunks[2:], 'zh', SWAP)  14.9 us
    unnamed x59, local copies, waits for them, and re-layouts  11.1 us
    pallas_call x2, Pallas kernels, ffn(): pl.pallas_call(ffn_kernel, out_shape=[jax.ShapeDtypeStruct((n_src, rows,...  10.2 us
    pallas_call x2, Pallas kernels, route(): pl.pallas_call(route_kernel, out_shape=shapes, grid_spec=pltpu.PrefetchSc...  9.13 us
  transfers between devices with their start and end apart: 30, of which 16 were waited for; matrix products, arithmetic and copies ran while one was open for 2% of the time, Pallas kernels for 10%

profile of v8, /device:TPU:2, one launch (start us, length us, event | category | flops | bytes accessed | tf_op | source)
XLA Modules:
  0.0 251.9 jit_solution(6736807993488572359)
XLA Ops:
  0.7 3.3 %shard_map.74 = (bf16[16,288,128]{2,1,0:T(8,128)(2,1)S(1)}, bf16[16,288,128]{2,1,0:T(8,128)(2,1)S(1)}) custom-call(s32[9]{0:T(128)S(1)} %concatenate.14.info, bf16[2,192,2048]{2,1,0:T(8,128)(2,1)} %gate_ref.5, bf16[2,192,2048]{2,1,0:T(8,128)(2,1)} %up_ref.5, bf16[2,192,2048]{2,1,0:T(8,128)(2,1)} %down_ref.5), custom_call_target="tpu_custom_call" | custom-call | bytes 4718592 | tf_op jit(solution)/shard_map/pallas_call | solution.py:89
  8.7 7.6 %all-to-all-start.1 = ((bf16[16,288,128]{2,1,0:T(8,128)(2,1)}), bf16[16,288,128]{2,1,0:T(8,128)(2,1)S(1)}, u32[]{:S(2)}, u32[]{:S(2)}) async-start(bf16[16,288,128]{2,1,0:T(8,128)(2,1)} %shard_map.75), calls=%async_computation.1 | async-start | bytes 2359296 | tf_op jit(solution)/shard_map/all_to_all | solution.py:169
  16.5 7.3 %collective-permute-start.3 = (bf16[136,2048]{1,0:T(8,128)(2,1)S(1)}, bf16[136,2048]{1,0:T(8,128)(2,1)}, u32[]{:S(2)}, u32[]{:S(2)}) collective-permute-start(bf16[136,2048]{1,0:T(8,128)(2,1)S(1)} %fusion.1.a_ref.refs_2_), channel_id=1, source_target_pairs={{0,32},{32,0},{1,33},{33,1},{2,34},{34,2},{3,35},{35,3},{4,36},{36... | collective-permute-start | bytes 1671176 | tf_op jit(solution)/shard_map/ppermute | solution.py:481
  25.3 4.0 %shard_map.73 = (bf16[512,2048]{1,0:T(8,128)(2,1)S(1)}, bf16[512,256]{1,0:T(8,128)(2,1)S(1)}, bf16[64,256]{1,0:T(8,128)(2,1)S(1)}) custom-call(s32[9]{0:T(128)S(1)} %concatenate.14.info, bf16[136,2048]{1,0:T(8,128)(2,1)S(1)} %fusion.1.a_ref.refs_2_, bf16[136,2048]{1,0:T(8,128)(2,1)S(1)} %collective-permute-done.1.b_ref.refs_3_), custom_call_target="tpu_custom_call" | custom-call | flops 536870912 | bytes 3145728 | tf_op jit(solution)/shard_map/pallas_call | solution.py:346
  34.5 4.9 %collective-permute-done.3.a_ref.refs_0_ = bf16[136,2048]{1,0:T(8,128)(2,1)} collective-permute-done((bf16[136,2048]{1,0:T(8,128)(2,1)S(1)}, bf16[136,2048]{1,0:T(8,128)(2,1)}, u32[]{:S(2)}, u32[]{:S(2)}) %collective-permute-start.3) | collective-permute-done | bytes 557088 | tf_op jit(solution)/shard_map/ppermute | solution.py:481
  39.4 7.2 %all-to-all-start.2 = ((bf16[16,32,2048]{2,1,0:T(8,128)(2,1)}), bf16[16,32,2048]{2,1,0:T(8,128)(2,1)S(1)}, u32[]{:S(2)}, u32[]{:S(2)}) async-start(bf16[16,32,2048]{2,1,0:T(8,128)(2,1)} %bitcast.37), calls=%async_computation.2 | async-start | bytes 4194304 | tf_op jit(solution)/shard_map/all_to_all | solution.py:460
  46.6 14.9 %collective-permute-start.5 = (bf16[2,288,128]{2,1,0:T(8,128)(2,1)S(1)}, bf16[2,288,128]{2,1,0:T(8,128)(2,1)S(1)}, u32[]{:S(2)}, u32[]{:S(2)}) collective-permute-start(bf16[2,288,128]{2,1,0:T(8,128)(2,1)S(1)} %slice.43), channel_id=1, source_target_pairs={{0,32},{32,0},{1,33},{33,1},{2,34},{34,2},{3,35},{35,3},{4,36},{36... | collective-permute-start | bytes 442376 | tf_op jit(solution)/shard_map/ppermute | solution.py:206
  61.5 4.3 %collective-permute-done.5.got_ref = bf16[2,288,128]{2,1,0:T(8,128)(2,1)S(1)} collective-permute-done((bf16[2,288,128]{2,1,0:T(8,128)(2,1)S(1)}, bf16[2,288,128]{2,1,0:T(8,128)(2,1)S(1)}, u32[]{:S(2)}, u32[]{:S(2)}) %collective-permute-start.5) | collective-permute-done | bytes 147488 | tf_op jit(solution)/shard_map/ppermute | solution.py:206
  72.0 5.7 %collective-permute-done.8 = bf16[576,128]{1,0:T(8,128)(2,1)S(1)} collective-permute-done((bf16[576,128]{1,0:T(8,128)(2,1)S(1)}, bf16[576,128]{1,0:T(8,128)(2,1)S(1)}, u32[]{:S(2)}, u32[]{:S(2)}) %collective-permute-start.8) | collective-permute-done | bytes 147488 | tf_op jit(solution)/shard_map/ppermute | solution.py:217
  80.3 5.1 %shard_map.78 = (bf16[512,2048]{1,0:T(8,128)(2,1)S(1)}, bf16[512,256]{1,0:T(8,128)(2,1)S(1)}, bf16[64,256]{1,0:T(8,128)(2,1)S(1)}) custom-call(s32[9]{0:T(128)S(1)} %get-tuple-element.355, bf16[136,2048]{1,0:T(8,128)(2,1)} %collective-permute-done.3.a_ref.refs_0_, bf16[136,2048]{1,0:T(8,128)(2,1)S(1)} %collective-permute-done.4.b_ref.refs_1_), custom_call_target="tpu_custom_call" | custom-call | flops 536870912 | bytes 3145728 | tf_op jit(solution)/shard_map/pallas_call | solution.py:346
  88.1 5.9 %all-to-all-start.4 = ((bf16[16,32,2048]{2,1,0:T(8,128)(2,1)}), bf16[16,32,2048]{2,1,0:T(8,128)(2,1)}, u32[]{:S(2)}, u32[]{:S(2)}) async-start(bf16[16,32,2048]{2,1,0:T(8,128)(2,1)} %bitcast.38), calls=%async_computation.4 | async-start | bytes 4194304 | tf_op jit(solution)/shard_map/all_to_all | solution.py:460
  96.0 4.5 %shard_map.77 = bf16[16,32,2048]{2,1,0:T(8,128)(2,1)S(1)} custom-call(s32[9]{0:T(128)S(1)} %get-tuple-element.355, bf16[16,32,2048]{2,1,0:T(8,128)(2,1)S(1)} %all-to-all-done.2.x_ref, bf16[2,192,2048]{2,1,0:T(8,128)(2,1)} %get-tuple-element.329, bf16[2,192,2048]{2,1,0:T(8,128)(2,1)} %get-tuple-element.330, bf16[2,192,2048]{2,1,0:T(8,128)(2,1)} %get-tuple-element.331), custom_call_target="tpu_custom_call" | custom-call | flops 1207959552 | bytes 8912896 | tf_op jit(solution)/shard_map/pallas_call | solution.py:391
  101.9 31.6 %collective-permute-done.11.refs_6_ = bf16[4,576,128]{2,1,0:T(8,128)(2,1)S(1)} collective-permute-done((bf16[4,576,128]{2,1,0:T(8,128)(2,1)S(1)}, bf16[4,576,128]{2,1,0:T(8,128)(2,1)S(1)}, u32[]{:S(2)}, u32[]{:S(2)}) %collective-permute-start.11) | collective-permute-done | bytes 589856 | tf_op jit(solution)/shard_map/ppermute | solution.py:223
  134.3 7.3 %all-to-all-start.3 = ((bf16[16,32,2048]{2,1,0:T(8,128)(2,1)}), bf16[16,32,2048]{2,1,0:T(8,128)(2,1)S(1)}, u32[]{:S(2)}, u32[]{:S(2)}) async-start(bf16[16,32,2048]{2,1,0:T(8,128)(2,1)} %copy-done), calls=%async_computation.3 | async-start | bytes 4194304 | tf_op jit(solution)/shard_map/all_to_all | solution.py:460
  141.6 5.6 %shard_map.80 = (bf16[16,32,512]{2,1,0:T(8,128)(2,1)S(1)}, bf16[16,32,512]{2,1,0:T(8,128)(2,1)}, bf16[16,32,512]{2,1,0:T(8,128)(2,1)}, bf16[16,32,512]{2,1,0:T(8,128)(2,1)}) custom-call(s32[9]{0:T(128)S(1)} %get-tuple-element.355, bf16[16,32,2048]{2,1,0:T(8,128)(2,1)} %all-to-all-done.4.x_ref, bf16[2,192,2048]{2,1,0:T(8,128)(2,1)} %get-tuple-element.329, ...), custom_call_target="tpu_custom_call" | custom-call | flops 1207959552 | bytes 8912896 | tf_op jit(solution)/shard_map/pallas_call | solution.py:391
  151.3 10.6 %collective-permute-start.15 = (bf16[16,32,512]{2,1,0:T(8,128)(2,1)}, bf16[16,32,512]{2,1,0:T(8,128)(2,1)}, u32[]{:S(2)}, u32[]{:S(2)}) collective-permute-start(bf16[16,32,512]{2,1,0:T(8,128)(2,1)} %get-tuple-element.185), channel_id=1, source_target_pairs={{0,1},{1,0},{2,3},{3,2},{4,5},{5,4},{6,7},{7,6},{8,9},{9,8},{10,11... | collective-permute-start | bytes 1572872 | tf_op jit(solution)/shard_map/ppermute | solution.py:465
  164.3 9.8 %collective-permute-done.13.refs_8_ = bf16[2,576,128]{2,1,0:T(8,128)(2,1)S(1)} collective-permute-done((bf16[2,576,128]{2,1,0:T(8,128)(2,1)S(1)}, bf16[2,576,128]{2,1,0:T(8,128)(2,1)S(1)}, u32[]{:S(2)}, u32[]{:S(2)}) %collective-permute-start.13) | collective-permute-done | bytes 294944 | tf_op jit(solution)/shard_map/ppermute | solution.py:223
  183.7 16.7 %collective-permute-done.16 = bf16[16,32,512]{2,1,0:T(8,128)(2,1)} collective-permute-done((bf16[16,32,512]{2,1,0:T(8,128)(2,1)}, bf16[16,32,512]{2,1,0:T(8,128)(2,1)}, u32[]{:S(2)}, u32[]{:S(2)}) %collective-permute-start.16) | collective-permute-done | bytes 524320 | tf_op jit(solution)/shard_map/ppermute | solution.py:465
  203.0 8.3 %all-to-all-start.5 = ((bf16[16,32,512]{2,1,0:T(8,128)(2,1)}), bf16[16,32,512]{2,1,0:T(8,128)(2,1)S(1)}, u32[]{:S(2)}, u32[]{:S(2)}) async-start(bf16[16,32,512]{2,1,0:T(8,128)(2,1)} %add_convert_fusion), calls=%async_computation.5 | async-start | bytes 1048576 | tf_op jit(solution)/shard_map/all_to_all | solution.py:460
  211.3 8.9 %collective-permute-start.21 = (bf16[64,512]{1,0:T(8,128)(2,1)S(1)}, bf16[64,512]{1,0:T(8,128)(2,1)S(1)}, u32[]{:S(2)}, u32[]{:S(2)}) collective-permute-start(bf16[64,512]{1,0:T(8,128)(2,1)S(1)} %copy-done.24), channel_id=1, source_target_pairs={{0,1},{1,0},{2,3},{3,2},{4,5},{5,4},{6,7},{7,6},{8,9},{9,8},{10,11... | collective-permute-start | bytes 196616 | tf_op jit(solution)/shard_map/ppermute | solution.py:465
  226.4 3.5 %collective-permute-done.22 = bf16[64,512]{1,0:T(8,128)(2,1)S(1)} collective-permute-done((bf16[64,512]{1,0:T(8,128)(2,1)S(1)}, bf16[64,512]{1,0:T(8,128)(2,1)S(1)}, u32[]{:S(2)}, u32[]{:S(2)}) %collective-permute-start.22) | collective-permute-done | bytes 65568 | tf_op jit(solution)/shard_map/ppermute | solution.py:465
  231.6 5.3 %collective-permute-done.19 = bf16[128,512]{1,0:T(8,128)(2,1)S(1)} collective-permute-done((bf16[128,512]{1,0:T(8,128)(2,1)S(1)}, bf16[128,512]{1,0:T(8,128)(2,1)S(1)}, u32[]{:S(2)}, u32[]{:S(2)}) %collective-permute-start.19) | collective-permute-done | bytes 131104 | tf_op jit(solution)/shard_map/ppermute | solution.py:465
  238.9 5.4 %collective-permute-start.25 = (bf16[128,512]{1,0:T(8,128)(2,1)S(1)}, bf16[128,512]{1,0:T(8,128)(2,1)S(1)}, u32[]{:S(2)}, u32[]{:S(2)}) collective-permute-start(bf16[128,512]{1,0:T(8,128)(2,1)S(1)} %add_convert_fusion.2), channel_id=1, source_target_pairs={{0,32},{32,0},{1,33},{33,1},{2,34},{34,2},{3,35},{35,3},{4,36},{36... | collective-permute-start | bytes 393224 | tf_op jit(solution)/shard_map/ppermute | solution.py:518
  244.3 6.9 %collective-permute-done.25 = bf16[128,512]{1,0:T(8,128)(2,1)S(1)} collective-permute-done((bf16[128,512]{1,0:T(8,128)(2,1)S(1)}, bf16[128,512]{1,0:T(8,128)(2,1)S(1)}, u32[]{:S(2)}, u32[]{:S(2)}) %collective-permute-start.25) | collective-permute-done | bytes 131104 | tf_op jit(solution)/shard_map/ppermute | solution.py:518
  (127 shorter events, 56.1 us)
Async XLA Ops:
  8.7 25.1 %all-to-all-start.1 = ((bf16[16,288,128]{2,1,0:T(8,128)(2,1)}), bf16[16,288,128]{2,1,0:T(8,128)(2,1)S(1)}, u32[]{:S(2)}, u32[]{:S(2)}) async-start(bf16[16,288,128]{2,1,0:T(8,128)(2,1)} %shard_map.75), calls=%async_computation.1 | async-start | bytes 2359296 | tf_op jit(solution)/shard_map/all_to_all | solution.py:169
  16.4 8.9 %collective-permute-start.1 = (bf16[136,2048]{1,0:T(8,128)(2,1)S(1)}, bf16[136,2048]{1,0:T(8,128)(2,1)S(1)}, u32[]{:S(2)}, u32[]{:S(2)}) collective-permute-start(bf16[136,2048]{1,0:T(8,128)(2,1)S(1)} %fusion.1.a_ref.refs_2_), channel_id=1, source_target_pairs={{0,4},{4,0},{1,5},{5,1},{2,6},{6,2},{3,7},{7,3},{8,12},{12,8},{9,1... | collective-permute-start | bytes 1671176 | tf_op jit(solution)/shard_map/ppermute | solution.py:482
  16.5 22.8 %collective-permute-start.3 = (bf16[136,2048]{1,0:T(8,128)(2,1)S(1)}, bf16[136,2048]{1,0:T(8,128)(2,1)}, u32[]{:S(2)}, u32[]{:S(2)}) collective-permute-start(bf16[136,2048]{1,0:T(8,128)(2,1)S(1)} %fusion.1.a_ref.refs_2_), channel_id=1, source_target_pairs={{0,32},{32,0},{1,33},{33,1},{2,34},{34,2},{3,35},{35,3},{4,36},{36... | collective-permute-start | bytes 1671176 | tf_op jit(solution)/shard_map/ppermute | solution.py:481
  39.4 48.7 %all-to-all-start.2 = ((bf16[16,32,2048]{2,1,0:T(8,128)(2,1)}), bf16[16,32,2048]{2,1,0:T(8,128)(2,1)S(1)}, u32[]{:S(2)}, u32[]{:S(2)}) async-start(bf16[16,32,2048]{2,1,0:T(8,128)(2,1)} %bitcast.37), calls=%async_computation.2 | async-start | bytes 4194304 | tf_op jit(solution)/shard_map/all_to_all | solution.py:460
  46.6 19.1 %collective-permute-start.5 = (bf16[2,288,128]{2,1,0:T(8,128)(2,1)S(1)}, bf16[2,288,128]{2,1,0:T(8,128)(2,1)S(1)}, u32[]{:S(2)}, u32[]{:S(2)}) collective-permute-start(bf16[2,288,128]{2,1,0:T(8,128)(2,1)S(1)} %slice.43), channel_id=1, source_target_pairs={{0,32},{32,0},{1,33},{33,1},{2,34},{34,2},{3,35},{35,3},{4,36},{36... | collective-permute-start | bytes 442376 | tf_op jit(solution)/shard_map/ppermute | solution.py:206
  66.4 13.9 %collective-permute-start.4 = (bf16[136,2048]{1,0:T(8,128)(2,1)}, bf16[136,2048]{1,0:T(8,128)(2,1)S(1)}, u32[]{:S(2)}, u32[]{:S(2)}) collective-permute-start(bf16[136,2048]{1,0:T(8,128)(2,1)} %collective-permute-done.3.a_ref.refs_0_), channel_id=1, source_target_pairs={{0,4},{4,0},{1,5},{5,1},{2,6},{6,2},{3,7},{7,3},{8,12},{12,8},{9,1... | collective-permute-start | bytes 1671176 | tf_op jit(solution)/shard_map/ppermute | solution.py:490
  67.7 9.9 %collective-permute-start.8 = (bf16[576,128]{1,0:T(8,128)(2,1)S(1)}, bf16[576,128]{1,0:T(8,128)(2,1)S(1)}, u32[]{:S(2)}, u32[]{:S(2)}) collective-permute-start(bf16[576,128]{1,0:T(8,128)(2,1)S(1)} %get-tuple-element.223), channel_id=1, source_target_pairs={{0,128},{64,192},{128,0},{192,64},{1,129},{65,193},{129,1},{193,65... | collective-permute-start | bytes 442376 | tf_op jit(solution)/shard_map/ppermute | solution.py:217
  71.4 8.9 %collective-permute-start.9 = (bf16[576,128]{1,0:T(8,128)(2,1)S(1)}, bf16[576,128]{1,0:T(8,128)(2,1)S(1)}, u32[]{:S(2)}, u32[]{:S(2)}) collective-permute-start(bf16[576,128]{1,0:T(8,128)(2,1)S(1)} %get-tuple-element.223), channel_id=1, source_target_pairs={{0,192},{64,128},{128,64},{192,0},{1,193},{65,129},{129,65},{193,1... | collective-permute-start | bytes 442376 | tf_op jit(solution)/shard_map/ppermute | solution.py:217
  88.1 46.2 %all-to-all-start.4 = ((bf16[16,32,2048]{2,1,0:T(8,128)(2,1)}), bf16[16,32,2048]{2,1,0:T(8,128)(2,1)}, u32[]{:S(2)}, u32[]{:S(2)}) async-start(bf16[16,32,2048]{2,1,0:T(8,128)(2,1)} %bitcast.38), calls=%async_computation.4 | async-start | bytes 4194304 | tf_op jit(solution)/shard_map/all_to_all | solution.py:460
  94.0 39.5 %collective-permute-start.11 = (bf16[4,576,128]{2,1,0:T(8,128)(2,1)S(1)}, bf16[4,576,128]{2,1,0:T(8,128)(2,1)S(1)}, u32[]{:S(2)}, u32[]{:S(2)}) collective-permute-start(bf16[4,576,128]{2,1,0:T(8,128)(2,1)S(1)} %pad_maximum_fusion.refs_4_), channel_id=1, source_target_pairs={{0,24},{8,0},{16,8},{24,16},{1,25},{9,1},{17,9},{25,17},{2,26},{10... | collective-permute-start | bytes 1769480 | tf_op jit(solution)/shard_map/ppermute | solution.py:223
  94.2 40.1 %collective-permute-start.10 = (bf16[4,576,128]{2,1,0:T(8,128)(2,1)S(1)}, bf16[4,576,128]{2,1,0:T(8,128)(2,1)}, u32[]{:S(2)}, u32[]{:S(2)}) collective-permute-start(bf16[4,576,128]{2,1,0:T(8,128)(2,1)S(1)} %pad_maximum_fusion.refs_4_), channel_id=1, source_target_pairs={{0,8},{8,16},{16,24},{24,0},{1,9},{9,17},{17,25},{25,1},{2,10},{10... | collective-permute-start | bytes 1769480 | tf_op jit(solution)/shard_map/ppermute | solution.py:223
  134.3 46.0 %all-to-all-start.3 = ((bf16[16,32,2048]{2,1,0:T(8,128)(2,1)}), bf16[16,32,2048]{2,1,0:T(8,128)(2,1)S(1)}, u32[]{:S(2)}, u32[]{:S(2)}) async-start(bf16[16,32,2048]{2,1,0:T(8,128)(2,1)} %copy-done), calls=%async_computation.3 | async-start | bytes 4194304 | tf_op jit(solution)/shard_map/all_to_all | solution.py:460
  149.2 25.0 %collective-permute-start.13 = (bf16[2,576,128]{2,1,0:T(8,128)(2,1)S(1)}, bf16[2,576,128]{2,1,0:T(8,128)(2,1)S(1)}, u32[]{:S(2)}, u32[]{:S(2)}) collective-permute-start(bf16[2,576,128]{2,1,0:T(8,128)(2,1)S(1)} %slice.45), channel_id=1, source_target_pairs={{0,24},{8,0},{16,8},{24,16},{1,25},{9,1},{17,9},{25,17},{2,26},{10... | collective-permute-start | bytes 884744 | tf_op jit(solution)/shard_map/ppermute | solution.py:223
  149.4 24.8 %collective-permute-start.12 = (bf16[2,576,128]{2,1,0:T(8,128)(2,1)S(1)}, bf16[2,576,128]{2,1,0:T(8,128)(2,1)S(1)}, u32[]{:S(2)}, u32[]{:S(2)}) collective-permute-start(bf16[2,576,128]{2,1,0:T(8,128)(2,1)S(1)} %slice.44), channel_id=1, source_target_pairs={{0,8},{8,16},{16,24},{24,0},{1,9},{9,17},{17,25},{25,1},{2,10},{10... | collective-permute-start | bytes 884744 | tf_op jit(solution)/shard_map/ppermute | solution.py:223
  151.3 32.4 %collective-permute-start.15 = (bf16[16,32,512]{2,1,0:T(8,128)(2,1)}, bf16[16,32,512]{2,1,0:T(8,128)(2,1)}, u32[]{:S(2)}, u32[]{:S(2)}) collective-permute-start(bf16[16,32,512]{2,1,0:T(8,128)(2,1)} %get-tuple-element.185), channel_id=1, source_target_pairs={{0,1},{1,0},{2,3},{3,2},{4,5},{5,4},{6,7},{7,6},{8,9},{9,8},{10,11... | collective-permute-start | bytes 1572872 | tf_op jit(solution)/shard_map/ppermute | solution.py:465
  161.9 38.5 %collective-permute-start.16 = (bf16[16,32,512]{2,1,0:T(8,128)(2,1)}, bf16[16,32,512]{2,1,0:T(8,128)(2,1)}, u32[]{:S(2)}, u32[]{:S(2)}) collective-permute-start(bf16[16,32,512]{2,1,0:T(8,128)(2,1)} %get-tuple-element.186), channel_id=1, source_target_pairs={{0,2},{1,3},{2,0},{3,1},{4,6},{5,7},{6,4},{7,5},{8,10},{9,11},{10,... | collective-permute-start | bytes 1572872 | tf_op jit(solution)/shard_map/ppermute | solution.py:465
  162.5 38.0 %collective-permute-start.17 = (bf16[16,32,512]{2,1,0:T(8,128)(2,1)}, bf16[16,32,512]{2,1,0:T(8,128)(2,1)}, u32[]{:S(2)}, u32[]{:S(2)}) collective-permute-start(bf16[16,32,512]{2,1,0:T(8,128)(2,1)} %get-tuple-element.187), channel_id=1, source_target_pairs={{0,3},{1,2},{2,1},{3,0},{4,7},{5,6},{6,5},{7,4},{8,11},{9,10},{10,... | collective-permute-start | bytes 1572872 | tf_op jit(solution)/shard_map/ppermute | solution.py:465
  183.6 19.4 %collective-permute-start.14 = (bf16[4,128,512]{2,1,0:T(8,128)(2,1)S(1)}, bf16[4,128,512]{2,1,0:T(8,128)(2,1)S(1)}, u32[]{:S(2)}, u32[]{:S(2)}) collective-permute-start(bf16[4,128,512]{2,1,0:T(8,128)(2,1)S(1)} %get-tuple-element.183), channel_id=1, source_target_pairs={{0,4},{4,0},{1,5},{5,1},{2,6},{6,2},{3,7},{7,3},{8,12},{12,8},{9,1... | collective-permute-start | bytes 1572872 | tf_op jit(solution)/shard_map/ppermute | solution.py:506
  203.0 34.0 %all-to-all-start.5 = ((bf16[16,32,512]{2,1,0:T(8,128)(2,1)}), bf16[16,32,512]{2,1,0:T(8,128)(2,1)S(1)}, u32[]{:S(2)}, u32[]{:S(2)}) async-start(bf16[16,32,512]{2,1,0:T(8,128)(2,1)} %add_convert_fusion), calls=%async_computation.5 | async-start | bytes 1048576 | tf_op jit(solution)/shard_map/all_to_all | solution.py:460
  211.3 14.6 %collective-permute-start.21 = (bf16[64,512]{1,0:T(8,128)(2,1)S(1)}, bf16[64,512]{1,0:T(8,128)(2,1)S(1)}, u32[]{:S(2)}, u32[]{:S(2)}) collective-permute-start(bf16[64,512]{1,0:T(8,128)(2,1)S(1)} %copy-done.24), channel_id=1, source_target_pairs={{0,1},{1,0},{2,3},{3,2},{4,5},{5,4},{6,7},{7,6},{8,9},{9,8},{10,11... | collective-permute-start | bytes 196616 | tf_op jit(solution)/shard_map/ppermute | solution.py:465
  220.2 9.7 %collective-permute-start.22 = (bf16[64,512]{1,0:T(8,128)(2,1)S(1)}, bf16[64,512]{1,0:T(8,128)(2,1)S(1)}, u32[]{:S(2)}, u32[]{:S(2)}) collective-permute-start(bf16[64,512]{1,0:T(8,128)(2,1)S(1)} %copy-done.22), channel_id=1, source_target_pairs={{0,2},{1,3},{2,0},{3,1},{4,6},{5,7},{6,4},{7,5},{8,10},{9,11},{10,... | collective-permute-start | bytes 196616 | tf_op jit(solution)/shard_map/ppermute | solution.py:465
  220.9 9.0 %collective-permute-start.23 = (bf16[64,512]{1,0:T(8,128)(2,1)S(1)}, bf16[64,512]{1,0:T(8,128)(2,1)S(1)}, u32[]{:S(2)}, u32[]{:S(2)}) collective-permute-start(bf16[64,512]{1,0:T(8,128)(2,1)S(1)} %copy-done.20), channel_id=1, source_target_pairs={{0,3},{1,2},{2,1},{3,0},{4,7},{5,6},{6,5},{7,4},{8,11},{9,10},{10,... | collective-permute-start | bytes 196616 | tf_op jit(solution)/shard_map/ppermute | solution.py:465
  225.9 11.0 %collective-permute-start.19 = (bf16[128,512]{1,0:T(8,128)(2,1)S(1)}, bf16[128,512]{1,0:T(8,128)(2,1)S(1)}, u32[]{:S(2)}, u32[]{:S(2)}) collective-permute-start(bf16[128,512]{1,0:T(8,128)(2,1)S(1)} %get-tuple-element.221), channel_id=1, source_target_pairs={{0,2},{1,3},{2,0},{3,1},{4,6},{5,7},{6,4},{7,5},{8,10},{9,11},{10,... | collective-permute-start | bytes 393224 | tf_op jit(solution)/shard_map/ppermute | solution.py:465
  238.9 12.4 %collective-permute-start.25 = (bf16[128,512]{1,0:T(8,128)(2,1)S(1)}, bf16[128,512]{1,0:T(8,128)(2,1)S(1)}, u32[]{:S(2)}, u32[]{:S(2)}) collective-permute-start(bf16[128,512]{1,0:T(8,128)(2,1)S(1)} %add_convert_fusion.2), channel_id=1, source_target_pairs={{0,32},{32,0},{1,33},{33,1},{2,34},{34,2},{3,35},{35,3},{4,36},{36... | collective-permute-start | bytes 393224 | tf_op jit(solution)/shard_map/ppermute | solution.py:518
  (35 other events, 353.1 us)

commit v9 on v8

--- a/solution.py
+++ b/solution.py
@@ -284,10 +284,10 @@
     return jnp.concatenate([tokens, meta], axis=0)
 
 
-def route_kernel(info, a_ref, b_ref, send_ref, mix_ref, hot_mix_ref):
+def route_kernel(info, a_ref, b_ref, *refs):
+    send_ref, mix_ref, hot_mix_ref = refs[-3:]
     zh, c = info[Z_HI], info[CORE]
-    n_tok = mix_ref.shape[1]
-    n_slot = send_ref.shape[0]
+    n_slot, n_tok = mix_ref.shape
     tok_dev = n_tok // 2
     span_rows = tok_dev // SPANS
 
@@ -326,20 +326,22 @@
     pick = jnp.where(chosen, 1.0, 0.0).astype(jnp.bfloat16)
     sent = dot(pick[:, :tok_dev], a_ref[:tok_dev], 1, 0)
     sent += dot(pick[:, tok_dev:], b_ref[:tok_dev], 1, 0)
-    send_ref[...] = sent.astype(jnp.bfloat16)
+    send_ref[...] = sent.astype(jnp.bfloat16).reshape(send_ref.shape)
     mix_ref[...] = jnp.where(chosen, gate, 0.0).astype(jnp.bfloat16)
     hot_row = iota((2 * span_rows, 1), 0)
     hot_row = hot_row // span_rows * tok_dev + (2 * zh + c) * span_rows + hot_row % span_rows
     hot_mix_ref[...] = jnp.where(hot_row == row, hot_gate, 0.0).astype(jnp.bfloat16)
 
 
-def route(info, a, b, tok_dev):
+def route(info, a, b, tok_dev, half, base=()):
     width = a.shape[1]
     n_slot = 32 * 2 * SPANS * CAPACITY
+    n_dest = 16
     steps = 4
     span_rows = tok_dev // SPANS
+    rows = n_slot // n_dest
     shapes = (
-        jax.ShapeDtypeStruct((n_slot, width), jnp.bfloat16),
+        jax.ShapeDtypeStruct((n_dest, 2 * rows, width), jnp.bfloat16),
         jax.ShapeDtypeStruct((n_slot, 2 * tok_dev), jnp.bfloat16),
         jax.ShapeDtypeStruct((2 * span_rows, 2 * tok_dev), jnp.bfloat16),
     )
@@ -349,16 +351,18 @@
         grid_spec=pltpu.PrefetchScalarGridSpec(
             num_scalar_prefetch=1,
             grid=(steps,),
-            in_specs=[whole(a.shape), whole(b.shape)],
+            in_specs=[whole(a.shape), whole(b.shape)]
+            + [pl.BlockSpec(memory_space=pl.ANY)] * len(base),
             out_specs=(
-                pl.BlockSpec((n_slot // steps, width), lambda i, info: (i, 0)),
+                pl.BlockSpec((n_dest // steps, rows, width), lambda i, info: (i, half, 0)),
                 pl.BlockSpec((n_slot // steps, 2 * tok_dev), lambda i, info: (i, 0)),
                 whole(shapes[2].shape),
             ),
         ),
+        input_output_aliases={3: 0} if base else {},
         compiler_params=PARAMS,
         cost_estimate=cost(4 * n_slot * tok_dev * width, 2 * width * (n_slot + 2 * tok_dev)),
-    )(info, a, b)
+    )(info, a, b, *base)
 
 
 def ffn_kernel(info, x_ref, gate_ref, up_ref, down_ref, *out_refs):
@@ -378,27 +382,29 @@
         out_ref[...] = out.reshape(n_src, rows, cols)
 
 
-def ffn(info, x, w_gate, w_up, w_down, groups):
+def ffn(info, x, w_gate, w_up, w_down, half, groups):
     n_src, rows, width = x.shape
     exp_dev, units, _ = w_gate.shape
-    steps = 1
-
-    def block(cols):
-        return pl.BlockSpec((n_src // steps, rows // exp_dev, cols), lambda e, i, info: (i, e, 0))
-
-    w_spec = pl.BlockSpec((1, units, width), lambda e, i, info: (e, 0, 0))
+    rows //= 2
     cols = width // groups
+    block = (n_src, rows // exp_dev)
+    w_spec = pl.BlockSpec((1, units, width), lambda e, info: (e, 0, 0))
     return pl.pallas_call(
         ffn_kernel,
         out_shape=[jax.ShapeDtypeStruct((n_src, rows, cols), jnp.bfloat16)] * groups,
         grid_spec=pltpu.PrefetchScalarGridSpec(
             num_scalar_prefetch=1,
-            grid=(exp_dev, steps),
-            in_specs=[block(width), w_spec, w_spec, w_spec],
-            out_specs=[block(cols)] * groups,
-        ),
-        compiler_params=PARAMS,
-        cost_estimate=cost(6 * n_src * rows * units * width, 4 * x.size + 6 * w_gate.size),
+            grid=(exp_dev,),
+            in_specs=[
+                pl.BlockSpec((*block, width), lambda e, info: (0, half * exp_dev + e, 0)),
+                w_spec,
+                w_spec,
+                w_spec,
+            ],
+            out_specs=[pl.BlockSpec((*block, cols), lambda e, info: (0, e, 0))] * groups,
+        ),
+        compiler_params=PARAMS,
+        cost_estimate=cost(6 * n_src * rows * units * width, 2 * x.size + 6 * w_gate.size),
     )(info, x, w_gate, w_up, w_down)
 
 
@@ -480,24 +486,22 @@
     own = pack(tokens, expert_ids, gate_values)
     own_z = lax.ppermute(own, "zh", SWAP)
     own_c = lax.ppermute(own, "c", SWAP)
-    near, near_mix, near_hot_mix = route(info, own, own_c, tok_dev)
-    n_slot = near.shape[0]
-    slots = (16, n_slot // 16, width)
+    rows, near_mix, near_hot_mix = route(info, own, own_c, tok_dev, 0)
+    n_slot = near_mix.shape[0]
 
     chunks = first_chunks(info, hot_ids, experts)
-    near, chunks, own_z = lax.optimization_barrier((near.reshape(slots), chunks, own_z))
+    own_zc = lax.ppermute(own_z, "c", SWAP)
+    rows, far_mix, far_hot_mix = route(info, own_z, own_zc, tok_dev, 1, (rows,))
+    rows, chunks = lax.optimization_barrier((rows, chunks))
+    rows = exchange(rows)
+    hot_w = along_y(own_span(info, chunks, c))
+    hot_w = (hot_w, shift_x(hot_w, 1), shift_x(hot_w, -1))
+    rows, hot_w = lax.optimization_barrier((rows, hot_w))
+    far = ffn(info, rows, *experts, 1, n_t)
+    far, rows = lax.optimization_barrier((tuple(far), rows))
+    (near,) = ffn(info, rows, *experts, 0, 1)
     near = exchange(near)
-    own_zc = lax.ppermute(own_z, "c", SWAP)
-    far, far_mix, far_hot_mix = route(info, own_z, own_zc, tok_dev)
-    hot_w = along_y(own_span(info, chunks, c))
-    far, hot_w = lax.optimization_barrier((far.reshape(slots), hot_w))
-    far = exchange(far)
-    hot_w = (hot_w, shift_x(hot_w, 1), shift_x(hot_w, -1))
-    (near,) = ffn(info, near, *experts, 1)
-    near, hot_w = lax.optimization_barrier((near, hot_w))
-    near = exchange(near)
-    far = ffn(info, far, *experts, n_t)
-    far, hot_w = lax.optimization_barrier((tuple(far), hot_w))
+    far, hot_w = lax.optimization_barrier((far, hot_w))
     half = hot_w[0].shape[0] // 2
     hot_w += (shift_x(hot_w[1][:half], 1), shift_x(hot_w[2][half:], -1))
     far = total_of((far[0], *to_t(far, 1, 2, 3)))

time: 253 us -> 251 us (level)
  local copies, waits for them, and re-layouts: 13 us -> 17.9 us
  starting transfers between devices: 101 us -> 97.2 us
    ppermute x3, waiting for transfers between devices: 8.26 us -> 31.7 us  [along_y(): column.append(lax.ppermute(chunk, 'y', [(i, i ^ k) for i in range(n_y)]))]
    ppermute x4, waiting for transfers between devices: 41.4 us -> 29.4 us  [shift_x(): return lax.ppermute(array, 'x', [(i, (i + step) % n_x) for i in range(n_x)])]
    ppermute x9, waiting for transfers between devices: 27.2 us -> 19.6 us  [to_t(): lax.ppermute(groups[k], 't', [(i, i ^ k) for i in pairs])]
    all_to_all x4 -> x3, starting transfers between devices: 28.7 us -> 24.4 us  [exchange(): return lax.all_to_all(send, ('y', 'x'), 0, 0, tiled=True)]
    unnamed x59 -> x77, local copies, waits for them, and re-layouts: 11.1 us -> 15.1 us
    all_to_all x1, waiting for transfers between devices: 3.11 us -> 0.01 us  [hot_round(): part = lax.all_to_all(part, ('y', 'x'), 0, 0, tiled=True)]
    ppermute x1, waiting for transfers between devices: 2.83 us -> 0.01 us  [hot_round(): part = choose(info, keep, lax.ppermute(give, 'c', SWAP))]
  transfers between devices with their start and end apart: 30 -> 29, of which waited for: 16 -> 14; matrix products, arithmetic and copies ran while one was open for 2% -> 2% of each run, Pallas kernels for 10% -> 6%
where the time goes in v9:
time: 251 us
  waiting for transfers between devices  101 us (40%)
  starting transfers between devices  97.2 us (39%)
  Pallas kernels  29.3 us (12%)
  local copies, waits for them, and re-layouts  17.9 us (7%)
  other arithmetic  4.51 us (2%)
    ppermute x3, waiting for transfers between devices, along_y(): column.append(lax.ppermute(chunk, 'y', [(i, i ^ k) for i in range(n_y)]))  31.7 us
    ppermute x4, waiting for transfers between devices, shift_x(): return lax.ppermute(array, 'x', [(i, (i + step) % n_x) for i in range(n_x)])  29.4 us
    ppermute x9, starting transfers between devices, to_t(): lax.ppermute(groups[k], 't', [(i, i ^ k) for i in pairs])  28.9 us
    all_to_all x3, starting transfers between devices, exchange(): return lax.all_to_all(send, ('y', 'x'), 0, 0, tiled=True)  24.4 us
    ppermute x9, waiting for transfers between devices, to_t(): lax.ppermute(groups[k], 't', [(i, i ^ k) for i in pairs])  19.6 us
    unnamed x77, local copies, waits for them, and re-layouts  15.1 us
    ppermute x1, starting transfers between devices, own_span(): got = lax.ppermute(chunks[2:], 'zh', SWAP)  14.8 us
    pallas_call x2, Pallas kernels, ffn(): pl.pallas_call(ffn_kernel, out_shape=[jax.ShapeDtypeStruct((n_src, rows,...  9.3 us
  transfers between devices with their start and end apart: 29, of which 14 were waited for; matrix products, arithmetic and copies ran while one was open for 2% of the time, Pallas kernels for 6%

profile of v9, /device:TPU:2, one launch (start us, length us, event | category | flops | bytes accessed | tf_op | source)
XLA Modules:
  0.0 250.7 jit_solution(5777063187362430413)
XLA Ops:
  0.7 3.3 %shard_map.75 = (bf16[16,288,128]{2,1,0:T(8,128)(2,1)S(1)}, bf16[16,288,128]{2,1,0:T(8,128)(2,1)S(1)}) custom-call(s32[9]{0:T(128)S(1)} %concatenate.14.info, bf16[2,192,2048]{2,1,0:T(8,128)(2,1)} %gate_ref.5, bf16[2,192,2048]{2,1,0:T(8,128)(2,1)} %up_ref.5, bf16[2,192,2048]{2,1,0:T(8,128)(2,1)} %down_ref.5), custom_call_target="tpu_custom_call" | custom-call | bytes 4718592 | tf_op jit(solution)/shard_map/pallas_call | solution.py:89
  4.3 7.3 %collective-permute-start.2 = (bf16[136,2048]{1,0:T(8,128)(2,1)S(1)}, bf16[136,2048]{1,0:T(8,128)(2,1)S(1)}, u32[]{:S(2)}, u32[]{:S(2)}) collective-permute-start(bf16[136,2048]{1,0:T(8,128)(2,1)S(1)} %fusion.1.a_ref.refs_2_), channel_id=1, source_target_pairs={{0,32},{32,0},{1,33},{33,1},{2,34},{34,2},{3,35},{35,3},{4,36},{36... | collective-permute-start | bytes 1671176 | tf_op jit(solution)/shard_map/ppermute | solution.py:487
  13.3 7.6 %all-to-all-start.1 = ((bf16[16,288,128]{2,1,0:T(8,128)(2,1)}), bf16[16,288,128]{2,1,0:T(8,128)(2,1)S(1)}, u32[]{:S(2)}, u32[]{:S(2)}) async-start(bf16[16,288,128]{2,1,0:T(8,128)(2,1)} %shard_map.76), calls=%async_computation.1 | async-start | bytes 2359296 | tf_op jit(solution)/shard_map/all_to_all | solution.py:169
  20.9 6.2 %collective-permute-done.2.a_ref.refs_0_ = bf16[136,2048]{1,0:T(8,128)(2,1)S(1)} collective-permute-done((bf16[136,2048]{1,0:T(8,128)(2,1)S(1)}, bf16[136,2048]{1,0:T(8,128)(2,1)S(1)}, u32[]{:S(2)}, u32[]{:S(2)}) %collective-permute-start.2) | collective-permute-done | bytes 557088 | tf_op jit(solution)/shard_map/ppermute | solution.py:487
  28.7 4.1 %shard_map.73 = (bf16[16,64,2048]{2,1,0:T(8,128)(2,1)S(1)}, bf16[512,256]{1,0:T(8,128)(2,1)S(1)}, bf16[64,256]{1,0:T(8,128)(2,1)S(1)}) custom-call(s32[9]{0:T(128)S(1)} %concatenate.14.info, bf16[136,2048]{1,0:T(8,128)(2,1)S(1)} %fusion.1.a_ref.refs_2_, bf16[136,2048]{1,0:T(8,128)(2,1)S(1)} %collective-permute-done.1.b_ref.refs_3_), custom_call_target="tpu_custom_call" | custom-call | flops 536870912 | bytes 3145728 | tf_op jit(solution)/shard_map/pallas_call | solution.py:348
  33.5 4.1 %shard_map.74 = (bf16[16,64,2048]{2,1,0:T(8,128)(2,1)S(1)}, bf16[512,256]{1,0:T(8,128)(2,1)S(1)}, bf16[64,256]{1,0:T(8,128)(2,1)S(1)}) custom-call(s32[9]{0:T(128)S(1)} %concatenate.14.info, bf16[136,2048]{1,0:T(8,128)(2,1)S(1)} %collective-permute-done.2.a_ref.refs_0_, ...), custom_call_target="tpu_custom_call", output_to_operand_aliasing={{0}: (3, {})} | custom-call | flops 536870912 | bytes 3145728 | tf_op jit(solution)/shard_map/pallas_call | solution.py:348
  41.0 7.5 %all-to-all-start.2 = ((bf16[16,64,2048]{2,1,0:T(8,128)(2,1)}), bf16[16,64,2048]{2,1,0:T(8,128)(2,1)}, u32[]{:S(2)}, u32[]{:S(2)}) async-start(bf16[16,64,2048]{2,1,0:T(8,128)(2,1)} %copy-done), calls=%async_computation.2 | async-start | bytes 8388608 | tf_op jit(solution)/shard_map/all_to_all | solution.py:466
  48.5 14.8 %collective-permute-start.5 = (bf16[2,288,128]{2,1,0:T(8,128)(2,1)S(1)}, bf16[2,288,128]{2,1,0:T(8,128)(2,1)S(1)}, u32[]{:S(2)}, u32[]{:S(2)}) collective-permute-start(bf16[2,288,128]{2,1,0:T(8,128)(2,1)S(1)} %slice.43), channel_id=1, source_target_pairs={{0,32},{32,0},{1,33},{33,1},{2,34},{34,2},{3,35},{35,3},{4,36},{36... | collective-permute-start | bytes 442376 | tf_op jit(solution)/shard_map/ppermute | solution.py:206
  63.4 4.1 %collective-permute-done.5.got_ref = bf16[2,288,128]{2,1,0:T(8,128)(2,1)S(1)} collective-permute-done((bf16[2,288,128]{2,1,0:T(8,128)(2,1)S(1)}, bf16[2,288,128]{2,1,0:T(8,128)(2,1)S(1)}, u32[]{:S(2)}, u32[]{:S(2)}) %collective-permute-start.5) | collective-permute-done | bytes 147488 | tf_op jit(solution)/shard_map/ppermute | solution.py:206
  69.4 3.1 %collective-permute-start.8 = (bf16[576,128]{1,0:T(8,128)(2,1)S(1)}, bf16[576,128]{1,0:T(8,128)(2,1)S(1)}, u32[]{:S(2)}, u32[]{:S(2)}) collective-permute-start(bf16[576,128]{1,0:T(8,128)(2,1)S(1)} %get-tuple-element.227), channel_id=1, source_target_pairs={{0,128},{64,192},{128,0},{192,64},{1,129},{65,193},{129,1},{193,65... | collective-permute-start | bytes 442376 | tf_op jit(solution)/shard_map/ppermute | solution.py:217
  73.6 23.6 %collective-permute-done.8 = bf16[576,128]{1,0:T(8,128)(2,1)S(1)} collective-permute-done((bf16[576,128]{1,0:T(8,128)(2,1)S(1)}, bf16[576,128]{1,0:T(8,128)(2,1)S(1)}, u32[]{:S(2)}, u32[]{:S(2)}) %collective-permute-start.8) | collective-permute-done | bytes 147488 | tf_op jit(solution)/shard_map/ppermute | solution.py:217
  97.3 8.0 %collective-permute-done.7 = bf16[576,128]{1,0:T(8,128)(2,1)S(1)} collective-permute-done((bf16[576,128]{1,0:T(8,128)(2,1)S(1)}, bf16[576,128]{1,0:T(8,128)(2,1)S(1)}, u32[]{:S(2)}, u32[]{:S(2)}) %collective-permute-start.7) | collective-permute-done | bytes 147488 | tf_op jit(solution)/shard_map/ppermute | solution.py:217
  107.5 14.3 %collective-permute-done.11.refs_6_ = bf16[4,576,128]{2,1,0:T(8,128)(2,1)S(1)} collective-permute-done((bf16[4,576,128]{2,1,0:T(8,128)(2,1)S(1)}, bf16[4,576,128]{2,1,0:T(8,128)(2,1)S(1)}, u32[]{:S(2)}, u32[]{:S(2)}) %collective-permute-start.11) | collective-permute-done | bytes 589856 | tf_op jit(solution)/shard_map/ppermute | solution.py:223
  122.6 5.2 %shard_map.79 = (bf16[16,32,512]{2,1,0:T(8,128)(2,1)S(1)}, bf16[16,32,512]{2,1,0:T(8,128)(2,1)S(1)}, bf16[16,32,512]{2,1,0:T(8,128)(2,1)S(1)}, bf16[16,32,512]{2,1,0:T(8,128)(2,1)S(1)}) custom-call(s32[9]{0:T(128)S(1)} %get-tuple-element.361, bf16[16,64,2048]{2,1,0:T(8,128)(2,1)} %all-to-all-done.2.x_ref, bf16[2,192,2048]{2,1,0:T(8,128)(2,1)S(1)} %copy-done.31, ...), custom_call_target="tpu_custom_call" | custom-call | flops 1207959552 | bytes 8912896 | tf_op jit(solution)/shard_map/pallas_call | solution.py:392
  131.1 4.1 %shard_map.80 = bf16[16,32,2048]{2,1,0:T(8,128)(2,1)S(1)} custom-call(s32[9]{0:T(128)S(1)} %get-tuple-element.361, bf16[16,64,2048]{2,1,0:T(8,128)(2,1)} %all-to-all-done.2.x_ref, bf16[2,192,2048]{2,1,0:T(8,128)(2,1)S(1)} %copy-done.31, bf16[2,192,2048]{2,1,0:T(8,128)(2,1)S(1)} %copy-done.32, bf16[2,192,2048]{2,1,0:T(8,128)(2,1)S(1)} %copy-done.33), custom_call_target="tpu_custom_call" | custom-call | flops 1207959552 | bytes 8912896 | tf_op jit(solution)/shard_map/pallas_call | solution.py:392
  136.5 8.7 %all-to-all-start.3 = ((bf16[16,32,2048]{2,1,0:T(8,128)(2,1)}), bf16[16,32,2048]{2,1,0:T(8,128)(2,1)S(1)}, u32[]{:S(2)}, u32[]{:S(2)}) async-start(bf16[16,32,2048]{2,1,0:T(8,128)(2,1)} %copy-done.1), calls=%async_computation.3 | async-start | bytes 4194304 | tf_op jit(solution)/shard_map/all_to_all | solution.py:466
  149.3 10.5 %collective-permute-start.15 = (bf16[16,32,512]{2,1,0:T(8,128)(2,1)}, bf16[16,32,512]{2,1,0:T(8,128)(2,1)}, u32[]{:S(2)}, u32[]{:S(2)}) collective-permute-start(bf16[16,32,512]{2,1,0:T(8,128)(2,1)} %copy-done.24), channel_id=1, source_target_pairs={{0,1},{1,0},{2,3},{3,2},{4,5},{5,4},{6,7},{7,6},{8,9},{9,8},{10,11... | collective-permute-start | bytes 1572872 | tf_op jit(solution)/shard_map/ppermute | solution.py:471
  162.6 15.1 %collective-permute-done.13.refs_8_ = bf16[2,576,128]{2,1,0:T(8,128)(2,1)S(1)} collective-permute-done((bf16[2,576,128]{2,1,0:T(8,128)(2,1)S(1)}, bf16[2,576,128]{2,1,0:T(8,128)(2,1)S(1)}, u32[]{:S(2)}, u32[]{:S(2)}) %collective-permute-start.13) | collective-permute-done | bytes 294944 | tf_op jit(solution)/shard_map/ppermute | solution.py:223
  189.4 9.0 %collective-permute-done.16 = bf16[16,32,512]{2,1,0:T(8,128)(2,1)} collective-permute-done((bf16[16,32,512]{2,1,0:T(8,128)(2,1)}, bf16[16,32,512]{2,1,0:T(8,128)(2,1)}, u32[]{:S(2)}, u32[]{:S(2)}) %collective-permute-start.16) | collective-permute-done | bytes 524320 | tf_op jit(solution)/shard_map/ppermute | solution.py:471
  201.0 8.3 %all-to-all-start.4 = ((bf16[16,32,512]{2,1,0:T(8,128)(2,1)}), bf16[16,32,512]{2,1,0:T(8,128)(2,1)S(1)}, u32[]{:S(2)}, u32[]{:S(2)}) async-start(bf16[16,32,512]{2,1,0:T(8,128)(2,1)} %add_convert_fusion), calls=%async_computation.4 | async-start | bytes 1048576 | tf_op jit(solution)/shard_map/all_to_all | solution.py:466
  209.3 9.2 %collective-permute-start.21 = (bf16[64,512]{1,0:T(8,128)(2,1)S(1)}, bf16[64,512]{1,0:T(8,128)(2,1)S(1)}, u32[]{:S(2)}, u32[]{:S(2)}) collective-permute-start(bf16[64,512]{1,0:T(8,128)(2,1)S(1)} %copy-done.30), channel_id=1, source_target_pairs={{0,1},{1,0},{2,3},{3,2},{4,5},{5,4},{6,7},{7,6},{8,9},{9,8},{10,11... | collective-permute-start | bytes 196616 | tf_op jit(solution)/shard_map/ppermute | solution.py:471
  230.8 4.8 %collective-permute-done.19 = bf16[128,512]{1,0:T(8,128)(2,1)S(1)} collective-permute-done((bf16[128,512]{1,0:T(8,128)(2,1)S(1)}, bf16[128,512]{1,0:T(8,128)(2,1)S(1)}, u32[]{:S(2)}, u32[]{:S(2)}) %collective-permute-start.19) | collective-permute-done | bytes 131104 | tf_op jit(solution)/shard_map/ppermute | solution.py:471
  237.6 5.4 %collective-permute-start.25 = (bf16[128,512]{1,0:T(8,128)(2,1)S(1)}, bf16[128,512]{1,0:T(8,128)(2,1)S(1)}, u32[]{:S(2)}, u32[]{:S(2)}) collective-permute-start(bf16[128,512]{1,0:T(8,128)(2,1)S(1)} %add_convert_fusion.2), channel_id=1, source_target_pairs={{0,32},{32,0},{1,33},{33,1},{2,34},{34,2},{3,35},{35,3},{4,36},{36... | collective-permute-start | bytes 393224 | tf_op jit(solution)/shard_map/ppermute | solution.py:522
  243.0 7.0 %collective-permute-done.25 = bf16[128,512]{1,0:T(8,128)(2,1)S(1)} collective-permute-done((bf16[128,512]{1,0:T(8,128)(2,1)S(1)}, bf16[128,512]{1,0:T(8,128)(2,1)S(1)}, u32[]{:S(2)}, u32[]{:S(2)}) %collective-permute-start.25) | collective-permute-done | bytes 131104 | tf_op jit(solution)/shard_map/ppermute | solution.py:522
  (143 shorter events, 54.3 us)
Async XLA Ops:
  4.3 22.8 %collective-permute-start.2 = (bf16[136,2048]{1,0:T(8,128)(2,1)S(1)}, bf16[136,2048]{1,0:T(8,128)(2,1)S(1)}, u32[]{:S(2)}, u32[]{:S(2)}) collective-permute-start(bf16[136,2048]{1,0:T(8,128)(2,1)S(1)} %fusion.1.a_ref.refs_2_), channel_id=1, source_target_pairs={{0,32},{32,0},{1,33},{33,1},{2,34},{34,2},{3,35},{35,3},{4,36},{36... | collective-permute-start | bytes 1671176 | tf_op jit(solution)/shard_map/ppermute | solution.py:487
  13.3 27.0 %all-to-all-start.1 = ((bf16[16,288,128]{2,1,0:T(8,128)(2,1)}), bf16[16,288,128]{2,1,0:T(8,128)(2,1)S(1)}, u32[]{:S(2)}, u32[]{:S(2)}) async-start(bf16[16,288,128]{2,1,0:T(8,128)(2,1)} %shard_map.76), calls=%async_computation.1 | async-start | bytes 2359296 | tf_op jit(solution)/shard_map/all_to_all | solution.py:169
  20.9 7.8 %collective-permute-start.1 = (bf16[136,2048]{1,0:T(8,128)(2,1)S(1)}, bf16[136,2048]{1,0:T(8,128)(2,1)S(1)}, u32[]{:S(2)}, u32[]{:S(2)}) collective-permute-start(bf16[136,2048]{1,0:T(8,128)(2,1)S(1)} %fusion.1.a_ref.refs_2_), channel_id=1, source_target_pairs={{0,4},{4,0},{1,5},{5,1},{2,6},{6,2},{3,7},{7,3},{8,12},{12,8},{9,1... | collective-permute-start | bytes 1671176 | tf_op jit(solution)/shard_map/ppermute | solution.py:488
  41.0 81.6 %all-to-all-start.2 = ((bf16[16,64,2048]{2,1,0:T(8,128)(2,1)}), bf16[16,64,2048]{2,1,0:T(8,128)(2,1)}, u32[]{:S(2)}, u32[]{:S(2)}) async-start(bf16[16,64,2048]{2,1,0:T(8,128)(2,1)} %copy-done), calls=%async_computation.2 | async-start | bytes 8388608 | tf_op jit(solution)/shard_map/all_to_all | solution.py:466
  48.5 18.9 %collective-permute-start.5 = (bf16[2,288,128]{2,1,0:T(8,128)(2,1)S(1)}, bf16[2,288,128]{2,1,0:T(8,128)(2,1)S(1)}, u32[]{:S(2)}, u32[]{:S(2)}) collective-permute-start(bf16[2,288,128]{2,1,0:T(8,128)(2,1)S(1)} %slice.43), channel_id=1, source_target_pairs={{0,32},{32,0},{1,33},{33,1},{2,34},{34,2},{3,35},{35,3},{4,36},{36... | collective-permute-start | bytes 442376 | tf_op jit(solution)/shard_map/ppermute | solution.py:206
  69.4 27.9 %collective-permute-start.8 = (bf16[576,128]{1,0:T(8,128)(2,1)S(1)}, bf16[576,128]{1,0:T(8,128)(2,1)S(1)}, u32[]{:S(2)}, u32[]{:S(2)}) collective-permute-start(bf16[576,128]{1,0:T(8,128)(2,1)S(1)} %get-tuple-element.227), channel_id=1, source_target_pairs={{0,128},{64,192},{128,0},{192,64},{1,129},{65,193},{129,1},{193,65... | collective-permute-start | bytes 442376 | tf_op jit(solution)/shard_map/ppermute | solution.py:217
  72.5 32.8 %collective-permute-start.7 = (bf16[576,128]{1,0:T(8,128)(2,1)S(1)}, bf16[576,128]{1,0:T(8,128)(2,1)S(1)}, u32[]{:S(2)}, u32[]{:S(2)}) collective-permute-start(bf16[576,128]{1,0:T(8,128)(2,1)S(1)} %get-tuple-element.227), channel_id=1, source_target_pairs={{0,64},{64,0},{128,192},{192,128},{1,65},{65,1},{129,193},{193,129... | collective-permute-start | bytes 442376 | tf_op jit(solution)/shard_map/ppermute | solution.py:217
  73.0 32.3 %collective-permute-start.9 = (bf16[576,128]{1,0:T(8,128)(2,1)S(1)}, bf16[576,128]{1,0:T(8,128)(2,1)S(1)}, u32[]{:S(2)}, u32[]{:S(2)}) collective-permute-start(bf16[576,128]{1,0:T(8,128)(2,1)S(1)} %get-tuple-element.227), channel_id=1, source_target_pairs={{0,192},{64,128},{128,64},{192,0},{1,193},{65,129},{129,65},{193,1... | collective-permute-start | bytes 442376 | tf_op jit(solution)/shard_map/ppermute | solution.py:217
  105.4 16.4 %collective-permute-start.11 = (bf16[4,576,128]{2,1,0:T(8,128)(2,1)S(1)}, bf16[4,576,128]{2,1,0:T(8,128)(2,1)S(1)}, u32[]{:S(2)}, u32[]{:S(2)}) collective-permute-start(bf16[4,576,128]{2,1,0:T(8,128)(2,1)S(1)} %pad_maximum_fusion.refs_4_), channel_id=1, source_target_pairs={{0,24},{8,0},{16,8},{24,16},{1,25},{9,1},{17,9},{25,17},{2,26},{10... | collective-permute-start | bytes 1769480 | tf_op jit(solution)/shard_map/ppermute | solution.py:223
  105.5 17.1 %collective-permute-start.10 = (bf16[4,576,128]{2,1,0:T(8,128)(2,1)S(1)}, bf16[4,576,128]{2,1,0:T(8,128)(2,1)}, u32[]{:S(2)}, u32[]{:S(2)}) collective-permute-start(bf16[4,576,128]{2,1,0:T(8,128)(2,1)S(1)} %pad_maximum_fusion.refs_4_), channel_id=1, source_target_pairs={{0,8},{8,16},{16,24},{24,0},{1,9},{9,17},{17,25},{25,1},{2,10},{10... | collective-permute-start | bytes 1769480 | tf_op jit(solution)/shard_map/ppermute | solution.py:223
  136.5 49.4 %all-to-all-start.3 = ((bf16[16,32,2048]{2,1,0:T(8,128)(2,1)}), bf16[16,32,2048]{2,1,0:T(8,128)(2,1)S(1)}, u32[]{:S(2)}, u32[]{:S(2)}) async-start(bf16[16,32,2048]{2,1,0:T(8,128)(2,1)} %copy-done.1), calls=%async_computation.3 | async-start | bytes 4194304 | tf_op jit(solution)/shard_map/all_to_all | solution.py:466
  147.2 30.5 %collective-permute-start.13 = (bf16[2,576,128]{2,1,0:T(8,128)(2,1)S(1)}, bf16[2,576,128]{2,1,0:T(8,128)(2,1)S(1)}, u32[]{:S(2)}, u32[]{:S(2)}) collective-permute-start(bf16[2,576,128]{2,1,0:T(8,128)(2,1)S(1)} %slice.45), channel_id=1, source_target_pairs={{0,24},{8,0},{16,8},{24,16},{1,25},{9,1},{17,9},{25,17},{2,26},{10... | collective-permute-start | bytes 884744 | tf_op jit(solution)/shard_map/ppermute | solution.py:223
  147.4 30.3 %collective-permute-start.12 = (bf16[2,576,128]{2,1,0:T(8,128)(2,1)S(1)}, bf16[2,576,128]{2,1,0:T(8,128)(2,1)S(1)}, u32[]{:S(2)}, u32[]{:S(2)}) collective-permute-start(bf16[2,576,128]{2,1,0:T(8,128)(2,1)S(1)} %slice.44), channel_id=1, source_target_pairs={{0,8},{8,16},{16,24},{24,0},{1,9},{9,17},{17,25},{25,1},{2,10},{10... | collective-permute-start | bytes 884744 | tf_op jit(solution)/shard_map/ppermute | solution.py:223
  149.3 40.1 %collective-permute-start.15 = (bf16[16,32,512]{2,1,0:T(8,128)(2,1)}, bf16[16,32,512]{2,1,0:T(8,128)(2,1)}, u32[]{:S(2)}, u32[]{:S(2)}) collective-permute-start(bf16[16,32,512]{2,1,0:T(8,128)(2,1)} %copy-done.24), channel_id=1, source_target_pairs={{0,1},{1,0},{2,3},{3,2},{4,5},{5,4},{6,7},{7,6},{8,9},{9,8},{10,11... | collective-permute-start | bytes 1572872 | tf_op jit(solution)/shard_map/ppermute | solution.py:471
  159.9 38.5 %collective-permute-start.16 = (bf16[16,32,512]{2,1,0:T(8,128)(2,1)}, bf16[16,32,512]{2,1,0:T(8,128)(2,1)}, u32[]{:S(2)}, u32[]{:S(2)}) collective-permute-start(bf16[16,32,512]{2,1,0:T(8,128)(2,1)} %copy-done.23), channel_id=1, source_target_pairs={{0,2},{1,3},{2,0},{3,1},{4,6},{5,7},{6,4},{7,5},{8,10},{9,11},{10,... | collective-permute-start | bytes 1572872 | tf_op jit(solution)/shard_map/ppermute | solution.py:471
  161.2 37.3 %collective-permute-start.17 = (bf16[16,32,512]{2,1,0:T(8,128)(2,1)}, bf16[16,32,512]{2,1,0:T(8,128)(2,1)}, u32[]{:S(2)}, u32[]{:S(2)}) collective-permute-start(bf16[16,32,512]{2,1,0:T(8,128)(2,1)} %copy-done.22), channel_id=1, source_target_pairs={{0,3},{1,2},{2,1},{3,0},{4,7},{5,6},{6,5},{7,4},{8,11},{9,10},{10,... | collective-permute-start | bytes 1572872 | tf_op jit(solution)/shard_map/ppermute | solution.py:471
  189.3 11.7 %collective-permute-start.14 = (bf16[4,128,512]{2,1,0:T(8,128)(2,1)S(1)}, bf16[4,128,512]{2,1,0:T(8,128)(2,1)S(1)}, u32[]{:S(2)}, u32[]{:S(2)}) collective-permute-start(bf16[4,128,512]{2,1,0:T(8,128)(2,1)S(1)} %get-tuple-element.187), channel_id=1, source_target_pairs={{0,4},{4,0},{1,5},{5,1},{2,6},{6,2},{3,7},{7,3},{8,12},{12,8},{9,1... | collective-permute-start | bytes 1572872 | tf_op jit(solution)/shard_map/ppermute | solution.py:510
  201.0 34.8 %all-to-all-start.4 = ((bf16[16,32,512]{2,1,0:T(8,128)(2,1)}), bf16[16,32,512]{2,1,0:T(8,128)(2,1)S(1)}, u32[]{:S(2)}, u32[]{:S(2)}) async-start(bf16[16,32,512]{2,1,0:T(8,128)(2,1)} %add_convert_fusion), calls=%async_computation.4 | async-start | bytes 1048576 | tf_op jit(solution)/shard_map/all_to_all | solution.py:466
  209.3 15.6 %collective-permute-start.21 = (bf16[64,512]{1,0:T(8,128)(2,1)S(1)}, bf16[64,512]{1,0:T(8,128)(2,1)S(1)}, u32[]{:S(2)}, u32[]{:S(2)}) collective-permute-start(bf16[64,512]{1,0:T(8,128)(2,1)S(1)} %copy-done.30), channel_id=1, source_target_pairs={{0,1},{1,0},{2,3},{3,2},{4,5},{5,4},{6,7},{7,6},{8,9},{9,8},{10,11... | collective-permute-start | bytes 196616 | tf_op jit(solution)/shard_map/ppermute | solution.py:471
  218.4 9.1 %collective-permute-start.22 = (bf16[64,512]{1,0:T(8,128)(2,1)S(1)}, bf16[64,512]{1,0:T(8,128)(2,1)S(1)}, u32[]{:S(2)}, u32[]{:S(2)}) collective-permute-start(bf16[64,512]{1,0:T(8,128)(2,1)S(1)} %copy-done.28), channel_id=1, source_target_pairs={{0,2},{1,3},{2,0},{3,1},{4,6},{5,7},{6,4},{7,5},{8,10},{9,11},{10,... | collective-permute-start | bytes 196616 | tf_op jit(solution)/shard_map/ppermute | solution.py:471
  219.9 7.6 %collective-permute-start.23 = (bf16[64,512]{1,0:T(8,128)(2,1)S(1)}, bf16[64,512]{1,0:T(8,128)(2,1)S(1)}, u32[]{:S(2)}, u32[]{:S(2)}) collective-permute-start(bf16[64,512]{1,0:T(8,128)(2,1)S(1)} %copy-done.26), channel_id=1, source_target_pairs={{0,3},{1,2},{2,1},{3,0},{4,7},{5,6},{6,5},{7,4},{8,11},{9,10},{10,... | collective-permute-start | bytes 196616 | tf_op jit(solution)/shard_map/ppermute | solution.py:471
  222.1 8.7 %collective-permute-start.20 = (bf16[128,512]{1,0:T(8,128)(2,1)S(1)}, bf16[128,512]{1,0:T(8,128)(2,1)S(1)}, u32[]{:S(2)}, u32[]{:S(2)}) collective-permute-start(bf16[128,512]{1,0:T(8,128)(2,1)S(1)} %get-tuple-element.224), channel_id=1, source_target_pairs={{0,3},{1,2},{2,1},{3,0},{4,7},{5,6},{6,5},{7,4},{8,11},{9,10},{10,... | collective-permute-start | bytes 393224 | tf_op jit(solution)/shard_map/ppermute | solution.py:471
  224.9 10.7 %collective-permute-start.19 = (bf16[128,512]{1,0:T(8,128)(2,1)S(1)}, bf16[128,512]{1,0:T(8,128)(2,1)S(1)}, u32[]{:S(2)}, u32[]{:S(2)}) collective-permute-start(bf16[128,512]{1,0:T(8,128)(2,1)S(1)} %get-tuple-element.225), channel_id=1, source_target_pairs={{0,2},{1,3},{2,0},{3,1},{4,6},{5,7},{6,4},{7,5},{8,10},{9,11},{10,... | collective-permute-start | bytes 393224 | tf_op jit(solution)/shard_map/ppermute | solution.py:471
  237.6 12.4 %collective-permute-start.25 = (bf16[128,512]{1,0:T(8,128)(2,1)S(1)}, bf16[128,512]{1,0:T(8,128)(2,1)S(1)}, u32[]{:S(2)}, u32[]{:S(2)}) collective-permute-start(bf16[128,512]{1,0:T(8,128)(2,1)S(1)} %add_convert_fusion.2), channel_id=1, source_target_pairs={{0,32},{32,0},{1,33},{33,1},{2,34},{34,2},{3,35},{35,3},{4,36},{36... | collective-permute-start | bytes 393224 | tf_op jit(solution)/shard_map/ppermute | solution.py:522
  (43 other events, 463.2 us)

commit v10 on v9

--- a/solution.py
+++ b/solution.py
@@ -495,27 +495,29 @@
     rows, chunks = lax.optimization_barrier((rows, chunks))
     rows = exchange(rows)
     hot_w = along_y(own_span(info, chunks, c))
+    rows, hot_w = lax.optimization_barrier((rows, hot_w))
     hot_w = (hot_w, shift_x(hot_w, 1), shift_x(hot_w, -1))
-    rows, hot_w = lax.optimization_barrier((rows, hot_w))
     far = ffn(info, rows, *experts, 1, n_t)
     far, rows = lax.optimization_barrier((tuple(far), rows))
     (near,) = ffn(info, rows, *experts, 0, 1)
+    summands = (far[0], *to_t(far, 1))
+    near, hot_w, summands = lax.optimization_barrier((near, hot_w, summands))
     near = exchange(near)
-    far, hot_w = lax.optimization_barrier((far, hot_w))
     half = hot_w[0].shape[0] // 2
     hot_w += (shift_x(hot_w[1][:half], 1), shift_x(hot_w[2][half:], -1))
-    far = total_of((far[0], *to_t(far, 1, 2, 3)))
+    far = total_of(summands + to_t(far, 2, 3))
     near_hot, far_hot = hot_ffn(info, (own_z, own_zc, own, own_c), hot_w, tok_dev // SPANS)
     mine, other = mix_rows(info, near_mix, near_hot_mix, near.reshape(n_slot, width), near_hot)
     got = lax.ppermute(other, "c", SWAP)
     mine, got, far, far_hot = lax.optimization_barrier((mine, got, far, far_hot))
 
-    far_hot = total_of((far_hot[0], *to_t(far_hot, 1, 2, 3)))
     far = exchange(far).reshape(n_slot, width // n_t)
     pieces = [mine[k].astype(jnp.float32) + got[k].astype(jnp.float32) for k in range(n_t)]
-    total = pieces[0]
-    for part in to_t([piece.astype(jnp.bfloat16) for piece in pieces], 1, 2, 3):
-        total += part.astype(jnp.float32)
+    parts = to_t(
+        [jnp.concatenate([p.astype(jnp.bfloat16), h]) for p, h in zip(pieces, far_hot)], 1, 2, 3
+    )
+    total = pieces[0] + sum(part[:tok_dev].astype(jnp.float32) for part in parts)
+    far_hot = total_of((far_hot[0], *(part[tok_dev:] for part in parts)))
     far, total = lax.optimization_barrier((far, total))
     mine, other = mix_quarter(far_mix, far_hot_mix, far, far_hot)
     mine += lax.ppermute(other, "c", SWAP).astype(jnp.float32)

time: 251 us -> 240 us (0.956)
  starting transfers between devices: 97.2 us -> 86.7 us
  waiting for transfers between devices: 101 us -> 97.9 us
    ppermute x9 -> x6, starting transfers between devices: 28.9 us -> 18.6 us  [to_t(): lax.ppermute(groups[k], 't', [(i, i ^ k) for i in pairs])]
    all_to_all x3, waiting for transfers between devices: 0.01 us -> 6.91 us  [exchange(): return lax.all_to_all(send, ('y', 'x'), 0, 0, tiled=True)]
    ppermute x4, waiting for transfers between devices: 29.4 us -> 23.2 us  [shift_x(): return lax.ppermute(array, 'x', [(i, (i + step) % n_x) for i in range(n_x)])]
    ppermute x1, waiting for transfers between devices: 6.99 us -> 4.04 us  [per_device(): got = lax.ppermute(mine.astype(jnp.bfloat16), 'zh', SWAP)]
    unnamed x77 -> x79, local copies, waits for them, and re-layouts: 15.1 us -> 15.7 us
    ppermute x9 -> x6, waiting for transfers between devices: 19.6 us -> 19 us  [to_t(): lax.ppermute(groups[k], 't', [(i, i ^ k) for i in pairs])]
  transfers between devices with their start and end apart: 29 -> 26, of which waited for: 14 -> 14; matrix products, arithmetic and copies ran while one was open for 2% -> 2% of each run, Pallas kernels for 6% -> 10%
where the time goes in v10:
time: 240 us; the launch traced here: 237 us
  waiting for transfers between devices  97.9 us (41%)
  starting transfers between devices  86.7 us (36%)
  Pallas kernels  28.7 us (12%)
  local copies, waits for them, and re-layouts  18.5 us (8%)
  other arithmetic  4.42 us (2%)
    ppermute x3, waiting for transfers between devices, along_y(): column.append(lax.ppermute(chunk, 'y', [(i, i ^ k) for i in range(n_y)]))  31.8 us
    ppermute x4, waiting for transfers between devices, shift_x(): return lax.ppermute(array, 'x', [(i, (i + step) % n_x) for i in range(n_x)])  23.2 us
    all_to_all x3, starting transfers between devices, exchange(): return lax.all_to_all(send, ('y', 'x'), 0, 0, tiled=True)  22 us
    ppermute x6, waiting for transfers between devices, to_t(): lax.ppermute(groups[k], 't', [(i, i ^ k) for i in pairs])  19 us
    ppermute x6, starting transfers between devices, to_t(): lax.ppermute(groups[k], 't', [(i, i ^ k) for i in pairs])  18.6 us
    unnamed x79, local copies, waits for them, and re-layouts  15.7 us
    ppermute x1, starting transfers between devices, own_span(): got = lax.ppermute(chunks[2:], 'zh', SWAP)  14.8 us
    pallas_call x2, Pallas kernels, ffn(): pl.pallas_call(ffn_kernel, out_shape=[jax.ShapeDtypeStruct((n_src, rows,...  8.7 us
  transfers between devices with their start and end apart: 26, of which 14 were waited for; matrix products, arithmetic and copies ran while one was open for 2% of the time, Pallas kernels for 10%

profile of v10, /device:TPU:2, one launch (start us, length us, event | category | flops | bytes accessed | tf_op | source)
XLA Modules:
  0.0 237.5 jit_solution(18170709995053019317)
XLA Ops:
  0.7 3.3 %shard_map.75 = (bf16[16,288,128]{2,1,0:T(8,128)(2,1)S(1)}, bf16[16,288,128]{2,1,0:T(8,128)(2,1)S(1)}) custom-call(s32[9]{0:T(128)S(1)} %concatenate.23.info, bf16[2,192,2048]{2,1,0:T(8,128)(2,1)} %gate_ref.5, bf16[2,192,2048]{2,1,0:T(8,128)(2,1)} %up_ref.5, bf16[2,192,2048]{2,1,0:T(8,128)(2,1)} %down_ref.5), custom_call_target="tpu_custom_call" | custom-call | bytes 4718592 | tf_op jit(solution)/shard_map/pallas_call | solution.py:89
  4.3 7.3 %collective-permute-start.2 = (bf16[136,2048]{1,0:T(8,128)(2,1)S(1)}, bf16[136,2048]{1,0:T(8,128)(2,1)S(1)}, u32[]{:S(2)}, u32[]{:S(2)}) collective-permute-start(bf16[136,2048]{1,0:T(8,128)(2,1)S(1)} %fusion.1.a_ref.refs_2_), channel_id=1, source_target_pairs={{0,32},{32,0},{1,33},{33,1},{2,34},{34,2},{3,35},{35,3},{4,36},{36... | collective-permute-start | bytes 1671176 | tf_op jit(solution)/shard_map/ppermute | solution.py:487
  13.3 7.6 %all-to-all-start.1 = ((bf16[16,288,128]{2,1,0:T(8,128)(2,1)}), bf16[16,288,128]{2,1,0:T(8,128)(2,1)S(1)}, u32[]{:S(2)}, u32[]{:S(2)}) async-start(bf16[16,288,128]{2,1,0:T(8,128)(2,1)} %shard_map.76), calls=%async_computation.1 | async-start | bytes 2359296 | tf_op jit(solution)/shard_map/all_to_all | solution.py:169
  20.9 6.2 %collective-permute-done.2.a_ref.refs_0_ = bf16[136,2048]{1,0:T(8,128)(2,1)S(1)} collective-permute-done((bf16[136,2048]{1,0:T(8,128)(2,1)S(1)}, bf16[136,2048]{1,0:T(8,128)(2,1)S(1)}, u32[]{:S(2)}, u32[]{:S(2)}) %collective-permute-start.2) | collective-permute-done | bytes 557088 | tf_op jit(solution)/shard_map/ppermute | solution.py:487
  28.7 4.1 %shard_map.73 = (bf16[16,64,2048]{2,1,0:T(8,128)(2,1)S(1)}, bf16[512,256]{1,0:T(8,128)(2,1)S(1)}, bf16[64,256]{1,0:T(8,128)(2,1)S(1)}) custom-call(s32[9]{0:T(128)S(1)} %concatenate.23.info, bf16[136,2048]{1,0:T(8,128)(2,1)S(1)} %fusion.1.a_ref.refs_2_, bf16[136,2048]{1,0:T(8,128)(2,1)S(1)} %collective-permute-done.1.b_ref.refs_3_), custom_call_target="tpu_custom_call" | custom-call | flops 536870912 | bytes 3145728 | tf_op jit(solution)/shard_map/pallas_call | solution.py:348
  33.6 4.1 %shard_map.74 = (bf16[16,64,2048]{2,1,0:T(8,128)(2,1)S(1)}, bf16[512,256]{1,0:T(8,128)(2,1)S(1)}, bf16[64,256]{1,0:T(8,128)(2,1)S(1)}) custom-call(s32[9]{0:T(128)S(1)} %concatenate.23.info, bf16[136,2048]{1,0:T(8,128)(2,1)S(1)} %collective-permute-done.2.a_ref.refs_0_, ...), custom_call_target="tpu_custom_call", output_to_operand_aliasing={{0}: (3, {})} | custom-call | flops 536870912 | bytes 3145728 | tf_op jit(solution)/shard_map/pallas_call | solution.py:348
  41.1 7.5 %all-to-all-start.2 = ((bf16[16,64,2048]{2,1,0:T(8,128)(2,1)}), bf16[16,64,2048]{2,1,0:T(8,128)(2,1)}, u32[]{:S(2)}, u32[]{:S(2)}) async-start(bf16[16,64,2048]{2,1,0:T(8,128)(2,1)} %copy-done), calls=%async_computation.2 | async-start | bytes 8388608 | tf_op jit(solution)/shard_map/all_to_all | solution.py:466
  48.6 14.8 %collective-permute-start.5 = (bf16[2,288,128]{2,1,0:T(8,128)(2,1)S(1)}, bf16[2,288,128]{2,1,0:T(8,128)(2,1)S(1)}, u32[]{:S(2)}, u32[]{:S(2)}) collective-permute-start(bf16[2,288,128]{2,1,0:T(8,128)(2,1)S(1)} %slice.61), channel_id=1, source_target_pairs={{0,32},{32,0},{1,33},{33,1},{2,34},{34,2},{3,35},{35,3},{4,36},{36... | collective-permute-start | bytes 442376 | tf_op jit(solution)/shard_map/ppermute | solution.py:206
  63.4 4.1 %collective-permute-done.5.got_ref = bf16[2,288,128]{2,1,0:T(8,128)(2,1)S(1)} collective-permute-done((bf16[2,288,128]{2,1,0:T(8,128)(2,1)S(1)}, bf16[2,288,128]{2,1,0:T(8,128)(2,1)S(1)}, u32[]{:S(2)}, u32[]{:S(2)}) %collective-permute-start.5) | collective-permute-done | bytes 147488 | tf_op jit(solution)/shard_map/ppermute | solution.py:206
  73.6 30.8 %collective-permute-done.9 = bf16[576,128]{1,0:T(8,128)(2,1)S(1)} collective-permute-done((bf16[576,128]{1,0:T(8,128)(2,1)S(1)}, bf16[576,128]{1,0:T(8,128)(2,1)S(1)}, u32[]{:S(2)}, u32[]{:S(2)}) %collective-permute-start.9) | collective-permute-done | bytes 147488 | tf_op jit(solution)/shard_map/ppermute | solution.py:217
  105.6 3.8 %all-to-all-done.2.x_ref = bf16[16,64,2048]{2,1,0:T(8,128)(2,1)} async-done(((bf16[16,64,2048]{2,1,0:T(8,128)(2,1)}), bf16[16,64,2048]{2,1,0:T(8,128)(2,1)}, u32[]{:S(2)}, u32[]{:S(2)}) %all-to-all-start.2) | async-done | bytes 4194336 | tf_op jit(solution)/shard_map/all_to_all | solution.py:466
  110.0 3.3 %collective-permute-start.11 = (bf16[4,576,128]{2,1,0:T(8,128)(2,1)S(1)}, bf16[4,576,128]{2,1,0:T(8,128)(2,1)}, u32[]{:S(2)}, u32[]{:S(2)}) collective-permute-start(bf16[4,576,128]{2,1,0:T(8,128)(2,1)S(1)} %pad_maximum_fusion.refs_4_), channel_id=1, source_target_pairs={{0,24},{8,0},{16,8},{24,16},{1,25},{9,1},{17,9},{25,17},{2,26},{10... | collective-permute-start | bytes 1769480 | tf_op jit(solution)/shard_map/ppermute | solution.py:223
  113.3 4.6 %shard_map.79 = (bf16[16,32,512]{2,1,0:T(8,128)(2,1)S(1)}, bf16[16,32,512]{2,1,0:T(8,128)(2,1)S(1)}, bf16[16,32,512]{2,1,0:T(8,128)(2,1)S(1)}, bf16[16,32,512]{2,1,0:T(8,128)(2,1)S(1)}) custom-call(s32[9]{0:T(128)S(1)} %get-tuple-element.350, bf16[16,64,2048]{2,1,0:T(8,128)(2,1)} %all-to-all-done.2.x_ref, bf16[2,192,2048]{2,1,0:T(8,128)(2,1)S(1)} %copy-done.30, ...), custom_call_target="tpu_custom_call" | custom-call | flops 1207959552 | bytes 8912896 | tf_op jit(solution)/shard_map/pallas_call | solution.py:392
  120.3 10.8 %collective-permute-start.12 = (bf16[16,32,512]{2,1,0:T(8,128)(2,1)S(1)}, bf16[16,32,512]{2,1,0:T(8,128)(2,1)S(1)}, u32[]{:S(2)}, u32[]{:S(2)}) collective-permute-start(bf16[16,32,512]{2,1,0:T(8,128)(2,1)S(1)} %get-tuple-element.174), channel_id=1, source_target_pairs={{0,1},{1,0},{2,3},{3,2},{4,5},{5,4},{6,7},{7,6},{8,9},{9,8},{10,11... | collective-permute-start | bytes 1572872 | tf_op jit(solution)/shard_map/ppermute | solution.py:471
  131.1 4.1 %shard_map.80 = bf16[16,32,2048]{2,1,0:T(8,128)(2,1)S(1)} custom-call(s32[9]{0:T(128)S(1)} %get-tuple-element.350, bf16[16,64,2048]{2,1,0:T(8,128)(2,1)} %all-to-all-done.2.x_ref, bf16[2,192,2048]{2,1,0:T(8,128)(2,1)S(1)} %copy-done.30, bf16[2,192,2048]{2,1,0:T(8,128)(2,1)S(1)} %copy-done.31, bf16[2,192,2048]{2,1,0:T(8,128)(2,1)S(1)} %copy-done.32), custom_call_target="tpu_custom_call" | custom-call | flops 1207959552 | bytes 8912896 | tf_op jit(solution)/shard_map/pallas_call | solution.py:392
  136.5 5.8 %collective-permute-done.12 = bf16[16,32,512]{2,1,0:T(8,128)(2,1)S(1)} collective-permute-done((bf16[16,32,512]{2,1,0:T(8,128)(2,1)S(1)}, bf16[16,32,512]{2,1,0:T(8,128)(2,1)S(1)}, u32[]{:S(2)}, u32[]{:S(2)}) %collective-permute-start.12) | collective-permute-done | bytes 524320 | tf_op jit(solution)/shard_map/ppermute | solution.py:471
  143.9 7.3 %all-to-all-start.3 = ((bf16[16,32,2048]{2,1,0:T(8,128)(2,1)}), bf16[16,32,2048]{2,1,0:T(8,128)(2,1)S(1)}, u32[]{:S(2)}, u32[]{:S(2)}) async-start(bf16[16,32,2048]{2,1,0:T(8,128)(2,1)} %copy-done.1), calls=%async_computation.3 | async-start | bytes 4194304 | tf_op jit(solution)/shard_map/all_to_all | solution.py:466
  158.7 22.2 %collective-permute-done.13.refs_7_ = bf16[2,576,128]{2,1,0:T(8,128)(2,1)S(1)} collective-permute-done((bf16[2,576,128]{2,1,0:T(8,128)(2,1)S(1)}, bf16[2,576,128]{2,1,0:T(8,128)(2,1)S(1)}, u32[]{:S(2)}, u32[]{:S(2)}) %collective-permute-start.13) | collective-permute-done | bytes 294944 | tf_op jit(solution)/shard_map/ppermute | solution.py:223
  193.5 7.8 %collective-permute-done.16 = bf16[16,32,512]{2,1,0:T(8,128)(2,1)} collective-permute-done((bf16[16,32,512]{2,1,0:T(8,128)(2,1)}, bf16[16,32,512]{2,1,0:T(8,128)(2,1)}, u32[]{:S(2)}, u32[]{:S(2)}) %collective-permute-start.16) | collective-permute-done | bytes 524320 | tf_op jit(solution)/shard_map/ppermute | solution.py:471
  209.3 7.2 %all-to-all-start.4 = ((bf16[16,32,512]{2,1,0:T(8,128)(2,1)}), bf16[16,32,512]{2,1,0:T(8,128)(2,1)S(1)}, u32[]{:S(2)}, u32[]{:S(2)}) async-start(bf16[16,32,512]{2,1,0:T(8,128)(2,1)} %add_convert_fusion), calls=%async_computation.4 | async-start | bytes 1048576 | tf_op jit(solution)/shard_map/all_to_all | solution.py:466
  216.5 5.4 %collective-permute-done.19 = bf16[192,512]{1,0:T(8,128)(2,1)S(1)} collective-permute-done((bf16[192,512]{1,0:T(8,128)(2,1)S(1)}, bf16[192,512]{1,0:T(8,128)(2,1)S(1)}, u32[]{:S(2)}, u32[]{:S(2)}) %collective-permute-start.19) | collective-permute-done | bytes 196640 | tf_op jit(solution)/shard_map/ppermute | solution.py:471
  222.1 3.2 %all-to-all-done.4 = bf16[16,32,512]{2,1,0:T(8,128)(2,1)S(1)} async-done(((bf16[16,32,512]{2,1,0:T(8,128)(2,1)}), bf16[16,32,512]{2,1,0:T(8,128)(2,1)S(1)}, u32[]{:S(2)}, u32[]{:S(2)}) %all-to-all-start.4) | async-done | bytes 524320 | tf_op jit(solution)/shard_map/all_to_all | solution.py:466
  227.1 5.6 %collective-permute-start.22 = (bf16[128,512]{1,0:T(8,128)(2,1)S(1)}, bf16[128,512]{1,0:T(8,128)(2,1)S(1)}, u32[]{:S(2)}, u32[]{:S(2)}) collective-permute-start(bf16[128,512]{1,0:T(8,128)(2,1)S(1)} %add_convert_fusion.2), channel_id=1, source_target_pairs={{0,32},{32,0},{1,33},{33,1},{2,34},{34,2},{3,35},{35,3},{4,36},{36... | collective-permute-start | bytes 393224 | tf_op jit(solution)/shard_map/ppermute | solution.py:524
  232.7 4.0 %collective-permute-done.22 = bf16[128,512]{1,0:T(8,128)(2,1)S(1)} collective-permute-done((bf16[128,512]{1,0:T(8,128)(2,1)S(1)}, bf16[128,512]{1,0:T(8,128)(2,1)S(1)}, u32[]{:S(2)}, u32[]{:S(2)}) %collective-permute-start.22) | collective-permute-done | bytes 131104 | tf_op jit(solution)/shard_map/ppermute | solution.py:524
  (142 shorter events, 51.4 us)
Async XLA Ops:
  4.1 7.5 %collective-permute-start.4 = (bf16[16,288,128]{2,1,0:T(8,128)(2,1)S(1)}, bf16[16,288,128]{2,1,0:T(8,128)(2,1)S(1)}, u32[]{:S(2)}, u32[]{:S(2)}) collective-permute-start(bf16[16,288,128]{2,1,0:T(8,128)(2,1)S(1)} %get-tuple-element.160), channel_id=1, source_target_pairs={{0,4},{4,0},{1,5},{5,1},{2,6},{6,2},{3,7},{7,3},{8,12},{12,8},{9,1... | collective-permute-start | bytes 3538952 | tf_op jit(solution)/shard_map/ppermute | solution.py:168
  4.3 22.8 %collective-permute-start.2 = (bf16[136,2048]{1,0:T(8,128)(2,1)S(1)}, bf16[136,2048]{1,0:T(8,128)(2,1)S(1)}, u32[]{:S(2)}, u32[]{:S(2)}) collective-permute-start(bf16[136,2048]{1,0:T(8,128)(2,1)S(1)} %fusion.1.a_ref.refs_2_), channel_id=1, source_target_pairs={{0,32},{32,0},{1,33},{33,1},{2,34},{34,2},{3,35},{35,3},{4,36},{36... | collective-permute-start | bytes 1671176 | tf_op jit(solution)/shard_map/ppermute | solution.py:487
  13.3 27.1 %all-to-all-start.1 = ((bf16[16,288,128]{2,1,0:T(8,128)(2,1)}), bf16[16,288,128]{2,1,0:T(8,128)(2,1)S(1)}, u32[]{:S(2)}, u32[]{:S(2)}) async-start(bf16[16,288,128]{2,1,0:T(8,128)(2,1)} %shard_map.76), calls=%async_computation.1 | async-start | bytes 2359296 | tf_op jit(solution)/shard_map/all_to_all | solution.py:169
  20.9 7.8 %collective-permute-start.1 = (bf16[136,2048]{1,0:T(8,128)(2,1)S(1)}, bf16[136,2048]{1,0:T(8,128)(2,1)S(1)}, u32[]{:S(2)}, u32[]{:S(2)}) collective-permute-start(bf16[136,2048]{1,0:T(8,128)(2,1)S(1)} %fusion.1.a_ref.refs_2_), channel_id=1, source_target_pairs={{0,4},{4,0},{1,5},{5,1},{2,6},{6,2},{3,7},{7,3},{8,12},{12,8},{9,1... | collective-permute-start | bytes 1671176 | tf_op jit(solution)/shard_map/ppermute | solution.py:488
  27.1 6.4 %collective-permute-start.3 = (bf16[136,2048]{1,0:T(8,128)(2,1)S(1)}, bf16[136,2048]{1,0:T(8,128)(2,1)S(1)}, u32[]{:S(2)}, u32[]{:S(2)}) collective-permute-start(bf16[136,2048]{1,0:T(8,128)(2,1)S(1)} %collective-permute-done.2.a_ref.refs_0_), channel_id=1, source_target_pairs={{0,4},{4,0},{1,5},{5,1},{2,6},{6,2},{3,7},{7,3},{8,12},{12,8},{9,1... | collective-permute-start | bytes 1671176 | tf_op jit(solution)/shard_map/ppermute | solution.py:493
  41.1 68.2 %all-to-all-start.2 = ((bf16[16,64,2048]{2,1,0:T(8,128)(2,1)}), bf16[16,64,2048]{2,1,0:T(8,128)(2,1)}, u32[]{:S(2)}, u32[]{:S(2)}) async-start(bf16[16,64,2048]{2,1,0:T(8,128)(2,1)} %copy-done), calls=%async_computation.2 | async-start | bytes 8388608 | tf_op jit(solution)/shard_map/all_to_all | solution.py:466
  48.6 18.9 %collective-permute-start.5 = (bf16[2,288,128]{2,1,0:T(8,128)(2,1)S(1)}, bf16[2,288,128]{2,1,0:T(8,128)(2,1)S(1)}, u32[]{:S(2)}, u32[]{:S(2)}) collective-permute-start(bf16[2,288,128]{2,1,0:T(8,128)(2,1)S(1)} %slice.61), channel_id=1, source_target_pairs={{0,32},{32,0},{1,33},{33,1},{2,34},{34,2},{3,35},{35,3},{4,36},{36... | collective-permute-start | bytes 442376 | tf_op jit(solution)/shard_map/ppermute | solution.py:206
  69.5 35.0 %collective-permute-start.9 = (bf16[576,128]{1,0:T(8,128)(2,1)S(1)}, bf16[576,128]{1,0:T(8,128)(2,1)S(1)}, u32[]{:S(2)}, u32[]{:S(2)}) collective-permute-start(bf16[576,128]{1,0:T(8,128)(2,1)S(1)} %get-tuple-element.221), channel_id=1, source_target_pairs={{0,192},{64,128},{128,64},{192,0},{1,193},{65,129},{129,65},{193,1... | collective-permute-start | bytes 442376 | tf_op jit(solution)/shard_map/ppermute | solution.py:217
  72.2 32.2 %collective-permute-start.8 = (bf16[576,128]{1,0:T(8,128)(2,1)S(1)}, bf16[576,128]{1,0:T(8,128)(2,1)S(1)}, u32[]{:S(2)}, u32[]{:S(2)}) collective-permute-start(bf16[576,128]{1,0:T(8,128)(2,1)S(1)} %get-tuple-element.221), channel_id=1, source_target_pairs={{0,128},{64,192},{128,0},{192,64},{1,129},{65,193},{129,1},{193,65... | collective-permute-start | bytes 442376 | tf_op jit(solution)/shard_map/ppermute | solution.py:217
  73.1 32.4 %collective-permute-start.7 = (bf16[576,128]{1,0:T(8,128)(2,1)S(1)}, bf16[576,128]{1,0:T(8,128)(2,1)S(1)}, u32[]{:S(2)}, u32[]{:S(2)}) collective-permute-start(bf16[576,128]{1,0:T(8,128)(2,1)S(1)} %get-tuple-element.221), channel_id=1, source_target_pairs={{0,64},{64,0},{128,192},{192,128},{1,65},{65,1},{129,193},{193,129... | collective-permute-start | bytes 442376 | tf_op jit(solution)/shard_map/ppermute | solution.py:217
  109.3 33.0 %collective-permute-start.10 = (bf16[4,576,128]{2,1,0:T(8,128)(2,1)S(1)}, bf16[4,576,128]{2,1,0:T(8,128)(2,1)S(1)}, u32[]{:S(2)}, u32[]{:S(2)}) collective-permute-start(bf16[4,576,128]{2,1,0:T(8,128)(2,1)S(1)} %pad_maximum_fusion.refs_4_), channel_id=1, source_target_pairs={{0,8},{8,16},{16,24},{24,0},{1,9},{9,17},{17,25},{25,1},{2,10},{10... | collective-permute-start | bytes 1769480 | tf_op jit(solution)/shard_map/ppermute | solution.py:223
  110.0 34.0 %collective-permute-start.11 = (bf16[4,576,128]{2,1,0:T(8,128)(2,1)S(1)}, bf16[4,576,128]{2,1,0:T(8,128)(2,1)}, u32[]{:S(2)}, u32[]{:S(2)}) collective-permute-start(bf16[4,576,128]{2,1,0:T(8,128)(2,1)S(1)} %pad_maximum_fusion.refs_4_), channel_id=1, source_target_pairs={{0,24},{8,0},{16,8},{24,16},{1,25},{9,1},{17,9},{25,17},{2,26},{10... | collective-permute-start | bytes 1769480 | tf_op jit(solution)/shard_map/ppermute | solution.py:223
  120.3 22.0 %collective-permute-start.12 = (bf16[16,32,512]{2,1,0:T(8,128)(2,1)S(1)}, bf16[16,32,512]{2,1,0:T(8,128)(2,1)S(1)}, u32[]{:S(2)}, u32[]{:S(2)}) collective-permute-start(bf16[16,32,512]{2,1,0:T(8,128)(2,1)S(1)} %get-tuple-element.174), channel_id=1, source_target_pairs={{0,1},{1,0},{2,3},{3,2},{4,5},{5,4},{6,7},{7,6},{8,9},{9,8},{10,11... | collective-permute-start | bytes 1572872 | tf_op jit(solution)/shard_map/ppermute | solution.py:471
  143.9 46.2 %all-to-all-start.3 = ((bf16[16,32,2048]{2,1,0:T(8,128)(2,1)}), bf16[16,32,2048]{2,1,0:T(8,128)(2,1)S(1)}, u32[]{:S(2)}, u32[]{:S(2)}) async-start(bf16[16,32,2048]{2,1,0:T(8,128)(2,1)} %copy-done.1), calls=%async_computation.3 | async-start | bytes 4194304 | tf_op jit(solution)/shard_map/all_to_all | solution.py:466
  152.4 28.6 %collective-permute-start.13 = (bf16[2,576,128]{2,1,0:T(8,128)(2,1)S(1)}, bf16[2,576,128]{2,1,0:T(8,128)(2,1)S(1)}, u32[]{:S(2)}, u32[]{:S(2)}) collective-permute-start(bf16[2,576,128]{2,1,0:T(8,128)(2,1)S(1)} %slice.62), channel_id=1, source_target_pairs={{0,8},{8,16},{16,24},{24,0},{1,9},{9,17},{17,25},{25,1},{2,10},{10... | collective-permute-start | bytes 884744 | tf_op jit(solution)/shard_map/ppermute | solution.py:223
  154.9 27.1 %collective-permute-start.14 = (bf16[2,576,128]{2,1,0:T(8,128)(2,1)S(1)}, bf16[2,576,128]{2,1,0:T(8,128)(2,1)S(1)}, u32[]{:S(2)}, u32[]{:S(2)}) collective-permute-start(bf16[2,576,128]{2,1,0:T(8,128)(2,1)S(1)} %slice.63), channel_id=1, source_target_pairs={{0,24},{8,0},{16,8},{24,16},{1,25},{9,1},{17,9},{25,17},{2,26},{10... | collective-permute-start | bytes 884744 | tf_op jit(solution)/shard_map/ppermute | solution.py:223
  155.5 38.0 %collective-permute-start.17 = (bf16[16,32,512]{2,1,0:T(8,128)(2,1)}, bf16[16,32,512]{2,1,0:T(8,128)(2,1)}, u32[]{:S(2)}, u32[]{:S(2)}) collective-permute-start(bf16[16,32,512]{2,1,0:T(8,128)(2,1)} %copy-done.29), channel_id=1, source_target_pairs={{0,3},{1,2},{2,1},{3,0},{4,7},{5,6},{6,5},{7,4},{8,11},{9,10},{10,... | collective-permute-start | bytes 1572872 | tf_op jit(solution)/shard_map/ppermute | solution.py:471
  157.7 43.7 %collective-permute-start.16 = (bf16[16,32,512]{2,1,0:T(8,128)(2,1)}, bf16[16,32,512]{2,1,0:T(8,128)(2,1)}, u32[]{:S(2)}, u32[]{:S(2)}) collective-permute-start(bf16[16,32,512]{2,1,0:T(8,128)(2,1)} %copy-done.28), channel_id=1, source_target_pairs={{0,2},{1,3},{2,0},{3,1},{4,6},{5,7},{6,4},{7,5},{8,10},{9,11},{10,... | collective-permute-start | bytes 1572872 | tf_op jit(solution)/shard_map/ppermute | solution.py:471
  193.4 10.3 %collective-permute-start.15 = (bf16[4,128,512]{2,1,0:T(8,128)(2,1)S(1)}, bf16[4,128,512]{2,1,0:T(8,128)(2,1)S(1)}, u32[]{:S(2)}, u32[]{:S(2)}) collective-permute-start(bf16[4,128,512]{2,1,0:T(8,128)(2,1)S(1)} %get-tuple-element.181), channel_id=1, source_target_pairs={{0,4},{4,0},{1,5},{5,1},{2,6},{6,2},{3,7},{7,3},{8,12},{12,8},{9,1... | collective-permute-start | bytes 1572872 | tf_op jit(solution)/shard_map/ppermute | solution.py:511
  204.6 11.9 %collective-permute-start.20 = (bf16[192,512]{1,0:T(8,128)(2,1)S(1)}, bf16[192,512]{1,0:T(8,128)(2,1)S(1)}, u32[]{:S(2)}, u32[]{:S(2)}) collective-permute-start(bf16[192,512]{1,0:T(8,128)(2,1)S(1)} %pad_maximum_fusion.3), channel_id=1, source_target_pairs={{0,3},{1,2},{2,1},{3,0},{4,7},{5,6},{6,5},{7,4},{8,11},{9,10},{10,... | collective-permute-start | bytes 589832 | tf_op jit(solution)/shard_map/ppermute | solution.py:471
  206.9 15.1 %collective-permute-start.19 = (bf16[192,512]{1,0:T(8,128)(2,1)S(1)}, bf16[192,512]{1,0:T(8,128)(2,1)S(1)}, u32[]{:S(2)}, u32[]{:S(2)}) collective-permute-start(bf16[192,512]{1,0:T(8,128)(2,1)S(1)} %pad_maximum_fusion.2), channel_id=1, source_target_pairs={{0,2},{1,3},{2,0},{3,1},{4,6},{5,7},{6,4},{7,5},{8,10},{9,11},{10,... | collective-permute-start | bytes 589832 | tf_op jit(solution)/shard_map/ppermute | solution.py:471
  207.0 14.9 %collective-permute-start.18 = (bf16[192,512]{1,0:T(8,128)(2,1)S(1)}, bf16[192,512]{1,0:T(8,128)(2,1)S(1)}, u32[]{:S(2)}, u32[]{:S(2)}) collective-permute-start(bf16[192,512]{1,0:T(8,128)(2,1)S(1)} %pad_maximum_fusion.1), channel_id=1, source_target_pairs={{0,1},{1,0},{2,3},{3,2},{4,5},{5,4},{6,7},{7,6},{8,9},{9,8},{10,11... | collective-permute-start | bytes 589832 | tf_op jit(solution)/shard_map/ppermute | solution.py:471
  209.3 16.0 %all-to-all-start.4 = ((bf16[16,32,512]{2,1,0:T(8,128)(2,1)}), bf16[16,32,512]{2,1,0:T(8,128)(2,1)S(1)}, u32[]{:S(2)}, u32[]{:S(2)}) async-start(bf16[16,32,512]{2,1,0:T(8,128)(2,1)} %add_convert_fusion), calls=%async_computation.4 | async-start | bytes 1048576 | tf_op jit(solution)/shard_map/all_to_all | solution.py:466
  227.1 9.6 %collective-permute-start.22 = (bf16[128,512]{1,0:T(8,128)(2,1)S(1)}, bf16[128,512]{1,0:T(8,128)(2,1)S(1)}, u32[]{:S(2)}, u32[]{:S(2)}) collective-permute-start(bf16[128,512]{1,0:T(8,128)(2,1)S(1)} %add_convert_fusion.2), channel_id=1, source_target_pairs={{0,32},{32,0},{1,33},{33,1},{2,34},{34,2},{3,35},{35,3},{4,36},{36... | collective-permute-start | bytes 393224 | tf_op jit(solution)/shard_map/ppermute | solution.py:524
  (41 other events, 364.6 us)

commit v11 on v10

--- a/solution.py
+++ b/solution.py
@@ -500,12 +500,11 @@
     far = ffn(info, rows, *experts, 1, n_t)
     far, rows = lax.optimization_barrier((tuple(far), rows))
     (near,) = ffn(info, rows, *experts, 0, 1)
-    summands = (far[0], *to_t(far, 1))
-    near, hot_w, summands = lax.optimization_barrier((near, hot_w, summands))
+    near, hot_w = lax.optimization_barrier((near, hot_w))
     near = exchange(near)
     half = hot_w[0].shape[0] // 2
     hot_w += (shift_x(hot_w[1][:half], 1), shift_x(hot_w[2][half:], -1))
-    far = total_of(summands + to_t(far, 2, 3))
+    far = total_of((far[0], *to_t(far, 1, 2, 3)))
     near_hot, far_hot = hot_ffn(info, (own_z, own_zc, own, own_c), hot_w, tok_dev // SPANS)
     mine, other = mix_rows(info, near_mix, near_hot_mix, near.reshape(n_slot, width), near_hot)
     got = lax.ppermute(other, "c", SWAP)

time: 240 us -> 234 us (0.975)
  waiting for transfers between devices: 97.9 us -> 88.6 us
  starting transfers between devices: 86.7 us -> 89.4 us
    ppermute x4, waiting for transfers between devices: 23.2 us -> 14.2 us  [shift_x(): return lax.ppermute(array, 'x', [(i, (i + step) % n_x) for i in range(n_x)])]
    ppermute x1, starting transfers between devices: 5.6 us -> 9.77 us  [per_device(): got = lax.ppermute(mine.astype(jnp.bfloat16), 'zh', SWAP)]
    unnamed x79 -> x77, local copies, waits for them, and re-layouts: 15.7 us -> 15.9 us
  transfers between devices with their start and end apart: 26 -> 26, of which waited for: 14 -> 13; matrix products, arithmetic and copies ran while one was open for 2% -> 2% of each run, Pallas kernels for 10% -> 11%
where the time goes in v11:
time: 234 us; the launch traced here: 231 us
  starting transfers between devices  89.4 us (38%)
  waiting for transfers between devices  88.6 us (38%)
  Pallas kernels  28.8 us (12%)
  local copies, waits for them, and re-layouts  18.7 us (8%)
  other arithmetic  4.46 us (2%)
    ppermute x3, waiting for transfers between devices, along_y(): column.append(lax.ppermute(chunk, 'y', [(i, i ^ k) for i in range(n_y)]))  31.8 us
    all_to_all x3, starting transfers between devices, exchange(): return lax.all_to_all(send, ('y', 'x'), 0, 0, tiled=True)  22.1 us
    ppermute x6, waiting for transfers between devices, to_t(): lax.ppermute(groups[k], 't', [(i, i ^ k) for i in pairs])  20.5 us
    ppermute x6, starting transfers between devices, to_t(): lax.ppermute(groups[k], 't', [(i, i ^ k) for i in pairs])  17 us
    unnamed x77, local copies, waits for them, and re-layouts  15.9 us
    ppermute x1, starting transfers between devices, own_span(): got = lax.ppermute(chunks[2:], 'zh', SWAP)  14.8 us
    ppermute x4, waiting for transfers between devices, shift_x(): return lax.ppermute(array, 'x', [(i, (i + step) % n_x) for i in range(n_x)])  14.2 us
    ppermute x1, starting transfers between devices, per_device(): got = lax.ppermute(mine.astype(jnp.bfloat16), 'zh', SWAP)  9.77 us
  transfers between devices with their start and end apart: 26, of which 13 were waited for; matrix products, arithmetic and copies ran while one was open for 2% of the time, Pallas kernels for 11%

profile of v11, /device:TPU:2, one launch (start us, length us, event | category | flops | bytes accessed | tf_op | source)
XLA Modules:
  0.0 231.0 jit_solution(16705804323042124126)
XLA Ops:
  0.7 3.3 %shard_map.75 = (bf16[16,288,128]{2,1,0:T(8,128)(2,1)S(1)}, bf16[16,288,128]{2,1,0:T(8,128)(2,1)S(1)}) custom-call(s32[9]{0:T(128)S(1)} %concatenate.23.info, bf16[2,192,2048]{2,1,0:T(8,128)(2,1)} %gate_ref.5, bf16[2,192,2048]{2,1,0:T(8,128)(2,1)} %up_ref.5, bf16[2,192,2048]{2,1,0:T(8,128)(2,1)} %down_ref.5), custom_call_target="tpu_custom_call" | custom-call | bytes 4718592 | tf_op jit(solution)/shard_map/pallas_call | solution.py:89
  4.3 7.3 %collective-permute-start.2 = (bf16[136,2048]{1,0:T(8,128)(2,1)S(1)}, bf16[136,2048]{1,0:T(8,128)(2,1)S(1)}, u32[]{:S(2)}, u32[]{:S(2)}) collective-permute-start(bf16[136,2048]{1,0:T(8,128)(2,1)S(1)} %fusion.1.a_ref.refs_2_), channel_id=1, source_target_pairs={{0,32},{32,0},{1,33},{33,1},{2,34},{34,2},{3,35},{35,3},{4,36},{36... | collective-permute-start | bytes 1671176 | tf_op jit(solution)/shard_map/ppermute | solution.py:487
  13.3 7.6 %all-to-all-start.1 = ((bf16[16,288,128]{2,1,0:T(8,128)(2,1)}), bf16[16,288,128]{2,1,0:T(8,128)(2,1)S(1)}, u32[]{:S(2)}, u32[]{:S(2)}) async-start(bf16[16,288,128]{2,1,0:T(8,128)(2,1)} %shard_map.76), calls=%async_computation.1 | async-start | bytes 2359296 | tf_op jit(solution)/shard_map/all_to_all | solution.py:169
  20.9 6.2 %collective-permute-done.2.a_ref.refs_0_ = bf16[136,2048]{1,0:T(8,128)(2,1)S(1)} collective-permute-done((bf16[136,2048]{1,0:T(8,128)(2,1)S(1)}, bf16[136,2048]{1,0:T(8,128)(2,1)S(1)}, u32[]{:S(2)}, u32[]{:S(2)}) %collective-permute-start.2) | collective-permute-done | bytes 557088 | tf_op jit(solution)/shard_map/ppermute | solution.py:487
  28.5 4.1 %shard_map.73 = (bf16[16,64,2048]{2,1,0:T(8,128)(2,1)S(1)}, bf16[512,256]{1,0:T(8,128)(2,1)S(1)}, bf16[64,256]{1,0:T(8,128)(2,1)S(1)}) custom-call(s32[9]{0:T(128)S(1)} %concatenate.23.info, bf16[136,2048]{1,0:T(8,128)(2,1)S(1)} %fusion.1.a_ref.refs_2_, bf16[136,2048]{1,0:T(8,128)(2,1)S(1)} %collective-permute-done.1.b_ref.refs_3_), custom_call_target="tpu_custom_call" | custom-call | flops 536870912 | bytes 3145728 | tf_op jit(solution)/shard_map/pallas_call | solution.py:348
  33.4 4.1 %shard_map.74 = (bf16[16,64,2048]{2,1,0:T(8,128)(2,1)S(1)}, bf16[512,256]{1,0:T(8,128)(2,1)S(1)}, bf16[64,256]{1,0:T(8,128)(2,1)S(1)}) custom-call(s32[9]{0:T(128)S(1)} %concatenate.23.info, bf16[136,2048]{1,0:T(8,128)(2,1)S(1)} %collective-permute-done.2.a_ref.refs_0_, ...), custom_call_target="tpu_custom_call", output_to_operand_aliasing={{0}: (3, {})} | custom-call | flops 536870912 | bytes 3145728 | tf_op jit(solution)/shard_map/pallas_call | solution.py:348
  40.9 7.5 %all-to-all-start.2 = ((bf16[16,64,2048]{2,1,0:T(8,128)(2,1)}), bf16[16,64,2048]{2,1,0:T(8,128)(2,1)}, u32[]{:S(2)}, u32[]{:S(2)}) async-start(bf16[16,64,2048]{2,1,0:T(8,128)(2,1)} %copy-done), calls=%async_computation.2 | async-start | bytes 8388608 | tf_op jit(solution)/shard_map/all_to_all | solution.py:466
  48.4 14.8 %collective-permute-start.5 = (bf16[2,288,128]{2,1,0:T(8,128)(2,1)S(1)}, bf16[2,288,128]{2,1,0:T(8,128)(2,1)S(1)}, u32[]{:S(2)}, u32[]{:S(2)}) collective-permute-start(bf16[2,288,128]{2,1,0:T(8,128)(2,1)S(1)} %slice.61), channel_id=1, source_target_pairs={{0,32},{32,0},{1,33},{33,1},{2,34},{34,2},{3,35},{35,3},{4,36},{36... | collective-permute-start | bytes 442376 | tf_op jit(solution)/shard_map/ppermute | solution.py:206
  63.2 4.0 %collective-permute-done.5.got_ref = bf16[2,288,128]{2,1,0:T(8,128)(2,1)S(1)} collective-permute-done((bf16[2,288,128]{2,1,0:T(8,128)(2,1)S(1)}, bf16[2,288,128]{2,1,0:T(8,128)(2,1)S(1)}, u32[]{:S(2)}, u32[]{:S(2)}) %collective-permute-start.5) | collective-permute-done | bytes 147488 | tf_op jit(solution)/shard_map/ppermute | solution.py:206
  73.5 30.8 %collective-permute-done.9 = bf16[576,128]{1,0:T(8,128)(2,1)S(1)} collective-permute-done((bf16[576,128]{1,0:T(8,128)(2,1)S(1)}, bf16[576,128]{1,0:T(8,128)(2,1)S(1)}, u32[]{:S(2)}, u32[]{:S(2)}) %collective-permute-start.9) | collective-permute-done | bytes 147488 | tf_op jit(solution)/shard_map/ppermute | solution.py:217
  105.4 3.7 %all-to-all-done.2.x_ref = bf16[16,64,2048]{2,1,0:T(8,128)(2,1)} async-done(((bf16[16,64,2048]{2,1,0:T(8,128)(2,1)}), bf16[16,64,2048]{2,1,0:T(8,128)(2,1)}, u32[]{:S(2)}, u32[]{:S(2)}) %all-to-all-start.2) | async-done | bytes 4194336 | tf_op jit(solution)/shard_map/all_to_all | solution.py:466
  109.8 3.5 %collective-permute-start.11 = (bf16[4,576,128]{2,1,0:T(8,128)(2,1)S(1)}, bf16[4,576,128]{2,1,0:T(8,128)(2,1)}, u32[]{:S(2)}, u32[]{:S(2)}) collective-permute-start(bf16[4,576,128]{2,1,0:T(8,128)(2,1)S(1)} %pad_maximum_fusion.refs_4_), channel_id=1, source_target_pairs={{0,24},{8,0},{16,8},{24,16},{1,25},{9,1},{17,9},{25,17},{2,26},{10... | collective-permute-start | bytes 1769480 | tf_op jit(solution)/shard_map/ppermute | solution.py:223
  113.3 4.6 %shard_map.79 = (bf16[16,32,512]{2,1,0:T(8,128)(2,1)S(1)}, bf16[16,32,512]{2,1,0:T(8,128)(2,1)S(1)}, bf16[16,32,512]{2,1,0:T(8,128)(2,1)S(1)}, bf16[16,32,512]{2,1,0:T(8,128)(2,1)S(1)}) custom-call(s32[9]{0:T(128)S(1)} %get-tuple-element.345, bf16[16,64,2048]{2,1,0:T(8,128)(2,1)} %all-to-all-done.2.x_ref, bf16[2,192,2048]{2,1,0:T(8,128)(2,1)S(1)} %copy-done.31, ...), custom_call_target="tpu_custom_call" | custom-call | flops 1207959552 | bytes 8912896 | tf_op jit(solution)/shard_map/pallas_call | solution.py:392
  121.1 4.1 %shard_map.80 = bf16[16,32,2048]{2,1,0:T(8,128)(2,1)S(1)} custom-call(s32[9]{0:T(128)S(1)} %get-tuple-element.345, bf16[16,64,2048]{2,1,0:T(8,128)(2,1)} %all-to-all-done.2.x_ref, bf16[2,192,2048]{2,1,0:T(8,128)(2,1)S(1)} %copy-done.31, bf16[2,192,2048]{2,1,0:T(8,128)(2,1)S(1)} %copy-done.32, bf16[2,192,2048]{2,1,0:T(8,128)(2,1)S(1)} %copy-done.33), custom_call_target="tpu_custom_call" | custom-call | flops 1207959552 | bytes 8912896 | tf_op jit(solution)/shard_map/pallas_call | solution.py:392
  127.5 7.4 %all-to-all-start.3 = ((bf16[16,32,2048]{2,1,0:T(8,128)(2,1)}), bf16[16,32,2048]{2,1,0:T(8,128)(2,1)S(1)}, u32[]{:S(2)}, u32[]{:S(2)}) async-start(bf16[16,32,2048]{2,1,0:T(8,128)(2,1)} %copy-done.1), calls=%async_computation.3 | async-start | bytes 4194304 | tf_op jit(solution)/shard_map/all_to_all | solution.py:466
  139.1 7.1 %collective-permute-start.17 = (bf16[16,32,512]{2,1,0:T(8,128)(2,1)}, bf16[16,32,512]{2,1,0:T(8,128)(2,1)}, u32[]{:S(2)}, u32[]{:S(2)}) collective-permute-start(bf16[16,32,512]{2,1,0:T(8,128)(2,1)} %copy-done.30), channel_id=1, source_target_pairs={{0,3},{1,2},{2,1},{3,0},{4,7},{5,6},{6,5},{7,4},{8,11},{9,10},{10,... | collective-permute-start | bytes 1572872 | tf_op jit(solution)/shard_map/ppermute | solution.py:471
  146.1 5.3 %collective-permute-start.16 = (bf16[16,32,512]{2,1,0:T(8,128)(2,1)}, bf16[16,32,512]{2,1,0:T(8,128)(2,1)}, u32[]{:S(2)}, u32[]{:S(2)}) collective-permute-start(bf16[16,32,512]{2,1,0:T(8,128)(2,1)} %copy-done.29), channel_id=1, source_target_pairs={{0,2},{1,3},{2,0},{3,1},{4,6},{5,7},{6,4},{7,5},{8,10},{9,11},{10,... | collective-permute-start | bytes 1572872 | tf_op jit(solution)/shard_map/ppermute | solution.py:471
  151.4 13.5 %collective-permute-done.12.refs_7_ = bf16[2,576,128]{2,1,0:T(8,128)(2,1)S(1)} collective-permute-done((bf16[2,576,128]{2,1,0:T(8,128)(2,1)S(1)}, bf16[2,576,128]{2,1,0:T(8,128)(2,1)S(1)}, u32[]{:S(2)}, u32[]{:S(2)}) %collective-permute-start.12) | collective-permute-done | bytes 294944 | tf_op jit(solution)/shard_map/ppermute | solution.py:223
  177.2 12.7 %collective-permute-done.16 = bf16[16,32,512]{2,1,0:T(8,128)(2,1)} collective-permute-done((bf16[16,32,512]{2,1,0:T(8,128)(2,1)}, bf16[16,32,512]{2,1,0:T(8,128)(2,1)}, u32[]{:S(2)}, u32[]{:S(2)}) %collective-permute-start.16) | collective-permute-done | bytes 524320 | tf_op jit(solution)/shard_map/ppermute | solution.py:471
  193.3 3.6 %collective-permute-start.20 = (bf16[192,512]{1,0:T(8,128)(2,1)S(1)}, bf16[192,512]{1,0:T(8,128)(2,1)S(1)}, u32[]{:S(2)}, u32[]{:S(2)}) collective-permute-start(bf16[192,512]{1,0:T(8,128)(2,1)S(1)} %pad_maximum_fusion.3), channel_id=1, source_target_pairs={{0,3},{1,2},{2,1},{3,0},{4,7},{5,6},{6,5},{7,4},{8,11},{9,10},{10,... | collective-permute-start | bytes 589832 | tf_op jit(solution)/shard_map/ppermute | solution.py:471
  198.0 7.2 %all-to-all-start.4 = ((bf16[16,32,512]{2,1,0:T(8,128)(2,1)}), bf16[16,32,512]{2,1,0:T(8,128)(2,1)S(1)}, u32[]{:S(2)}, u32[]{:S(2)}) async-start(bf16[16,32,512]{2,1,0:T(8,128)(2,1)} %add_convert_fusion), calls=%async_computation.4 | async-start | bytes 1048576 | tf_op jit(solution)/shard_map/all_to_all | solution.py:466
  205.2 7.7 %collective-permute-done.19 = bf16[192,512]{1,0:T(8,128)(2,1)S(1)} collective-permute-done((bf16[192,512]{1,0:T(8,128)(2,1)S(1)}, bf16[192,512]{1,0:T(8,128)(2,1)S(1)}, u32[]{:S(2)}, u32[]{:S(2)}) %collective-permute-start.19) | collective-permute-done | bytes 196640 | tf_op jit(solution)/shard_map/ppermute | solution.py:471
  216.7 9.8 %collective-permute-start.22 = (bf16[128,512]{1,0:T(8,128)(2,1)S(1)}, bf16[128,512]{1,0:T(8,128)(2,1)S(1)}, u32[]{:S(2)}, u32[]{:S(2)}) collective-permute-start(bf16[128,512]{1,0:T(8,128)(2,1)S(1)} %add_convert_fusion.2), channel_id=1, source_target_pairs={{0,32},{32,0},{1,33},{33,1},{2,34},{34,2},{3,35},{35,3},{4,36},{36... | collective-permute-start | bytes 393224 | tf_op jit(solution)/shard_map/ppermute | solution.py:523
  226.4 3.9 %collective-permute-done.22 = bf16[128,512]{1,0:T(8,128)(2,1)S(1)} collective-permute-done((bf16[128,512]{1,0:T(8,128)(2,1)S(1)}, bf16[128,512]{1,0:T(8,128)(2,1)S(1)}, u32[]{:S(2)}, u32[]{:S(2)}) %collective-permute-start.22) | collective-permute-done | bytes 131104 | tf_op jit(solution)/shard_map/ppermute | solution.py:523
  (140 shorter events, 46.1 us)
Async XLA Ops:
  4.1 7.5 %collective-permute-start.4 = (bf16[16,288,128]{2,1,0:T(8,128)(2,1)S(1)}, bf16[16,288,128]{2,1,0:T(8,128)(2,1)S(1)}, u32[]{:S(2)}, u32[]{:S(2)}) collective-permute-start(bf16[16,288,128]{2,1,0:T(8,128)(2,1)S(1)} %get-tuple-element.158), channel_id=1, source_target_pairs={{0,4},{4,0},{1,5},{5,1},{2,6},{6,2},{3,7},{7,3},{8,12},{12,8},{9,1... | collective-permute-start | bytes 3538952 | tf_op jit(solution)/shard_map/ppermute | solution.py:168
  4.3 22.8 %collective-permute-start.2 = (bf16[136,2048]{1,0:T(8,128)(2,1)S(1)}, bf16[136,2048]{1,0:T(8,128)(2,1)S(1)}, u32[]{:S(2)}, u32[]{:S(2)}) collective-permute-start(bf16[136,2048]{1,0:T(8,128)(2,1)S(1)} %fusion.1.a_ref.refs_2_), channel_id=1, source_target_pairs={{0,32},{32,0},{1,33},{33,1},{2,34},{34,2},{3,35},{35,3},{4,36},{36... | collective-permute-start | bytes 1671176 | tf_op jit(solution)/shard_map/ppermute | solution.py:487
  13.3 26.9 %all-to-all-start.1 = ((bf16[16,288,128]{2,1,0:T(8,128)(2,1)}), bf16[16,288,128]{2,1,0:T(8,128)(2,1)S(1)}, u32[]{:S(2)}, u32[]{:S(2)}) async-start(bf16[16,288,128]{2,1,0:T(8,128)(2,1)} %shard_map.76), calls=%async_computation.1 | async-start | bytes 2359296 | tf_op jit(solution)/shard_map/all_to_all | solution.py:169
  20.9 7.6 %collective-permute-start.1 = (bf16[136,2048]{1,0:T(8,128)(2,1)S(1)}, bf16[136,2048]{1,0:T(8,128)(2,1)S(1)}, u32[]{:S(2)}, u32[]{:S(2)}) collective-permute-start(bf16[136,2048]{1,0:T(8,128)(2,1)S(1)} %fusion.1.a_ref.refs_2_), channel_id=1, source_target_pairs={{0,4},{4,0},{1,5},{5,1},{2,6},{6,2},{3,7},{7,3},{8,12},{12,8},{9,1... | collective-permute-start | bytes 1671176 | tf_op jit(solution)/shard_map/ppermute | solution.py:488
  27.1 6.2 %collective-permute-start.3 = (bf16[136,2048]{1,0:T(8,128)(2,1)S(1)}, bf16[136,2048]{1,0:T(8,128)(2,1)S(1)}, u32[]{:S(2)}, u32[]{:S(2)}) collective-permute-start(bf16[136,2048]{1,0:T(8,128)(2,1)S(1)} %collective-permute-done.2.a_ref.refs_0_), channel_id=1, source_target_pairs={{0,4},{4,0},{1,5},{5,1},{2,6},{6,2},{3,7},{7,3},{8,12},{12,8},{9,1... | collective-permute-start | bytes 1671176 | tf_op jit(solution)/shard_map/ppermute | solution.py:493
  40.9 68.2 %all-to-all-start.2 = ((bf16[16,64,2048]{2,1,0:T(8,128)(2,1)}), bf16[16,64,2048]{2,1,0:T(8,128)(2,1)}, u32[]{:S(2)}, u32[]{:S(2)}) async-start(bf16[16,64,2048]{2,1,0:T(8,128)(2,1)} %copy-done), calls=%async_computation.2 | async-start | bytes 8388608 | tf_op jit(solution)/shard_map/all_to_all | solution.py:466
  48.4 18.9 %collective-permute-start.5 = (bf16[2,288,128]{2,1,0:T(8,128)(2,1)S(1)}, bf16[2,288,128]{2,1,0:T(8,128)(2,1)S(1)}, u32[]{:S(2)}, u32[]{:S(2)}) collective-permute-start(bf16[2,288,128]{2,1,0:T(8,128)(2,1)S(1)} %slice.61), channel_id=1, source_target_pairs={{0,32},{32,0},{1,33},{33,1},{2,34},{34,2},{3,35},{35,3},{4,36},{36... | collective-permute-start | bytes 442376 | tf_op jit(solution)/shard_map/ppermute | solution.py:206
  69.3 35.0 %collective-permute-start.9 = (bf16[576,128]{1,0:T(8,128)(2,1)S(1)}, bf16[576,128]{1,0:T(8,128)(2,1)S(1)}, u32[]{:S(2)}, u32[]{:S(2)}) collective-permute-start(bf16[576,128]{1,0:T(8,128)(2,1)S(1)} %get-tuple-element.217), channel_id=1, source_target_pairs={{0,192},{64,128},{128,64},{192,0},{1,193},{65,129},{129,65},{193,1... | collective-permute-start | bytes 442376 | tf_op jit(solution)/shard_map/ppermute | solution.py:217
  72.0 32.2 %collective-permute-start.8 = (bf16[576,128]{1,0:T(8,128)(2,1)S(1)}, bf16[576,128]{1,0:T(8,128)(2,1)S(1)}, u32[]{:S(2)}, u32[]{:S(2)}) collective-permute-start(bf16[576,128]{1,0:T(8,128)(2,1)S(1)} %get-tuple-element.217), channel_id=1, source_target_pairs={{0,128},{64,192},{128,0},{192,64},{1,129},{65,193},{129,1},{193,65... | collective-permute-start | bytes 442376 | tf_op jit(solution)/shard_map/ppermute | solution.py:217
  72.9 32.4 %collective-permute-start.7 = (bf16[576,128]{1,0:T(8,128)(2,1)S(1)}, bf16[576,128]{1,0:T(8,128)(2,1)S(1)}, u32[]{:S(2)}, u32[]{:S(2)}) collective-permute-start(bf16[576,128]{1,0:T(8,128)(2,1)S(1)} %get-tuple-element.217), channel_id=1, source_target_pairs={{0,64},{64,0},{128,192},{192,128},{1,65},{65,1},{129,193},{193,129... | collective-permute-start | bytes 442376 | tf_op jit(solution)/shard_map/ppermute | solution.py:217
  109.1 17.5 %collective-permute-start.10 = (bf16[4,576,128]{2,1,0:T(8,128)(2,1)S(1)}, bf16[4,576,128]{2,1,0:T(8,128)(2,1)S(1)}, u32[]{:S(2)}, u32[]{:S(2)}) collective-permute-start(bf16[4,576,128]{2,1,0:T(8,128)(2,1)S(1)} %pad_maximum_fusion.refs_4_), channel_id=1, source_target_pairs={{0,8},{8,16},{16,24},{24,0},{1,9},{9,17},{17,25},{25,1},{2,10},{10... | collective-permute-start | bytes 1769480 | tf_op jit(solution)/shard_map/ppermute | solution.py:223
  109.8 17.7 %collective-permute-start.11 = (bf16[4,576,128]{2,1,0:T(8,128)(2,1)S(1)}, bf16[4,576,128]{2,1,0:T(8,128)(2,1)}, u32[]{:S(2)}, u32[]{:S(2)}) collective-permute-start(bf16[4,576,128]{2,1,0:T(8,128)(2,1)S(1)} %pad_maximum_fusion.refs_4_), channel_id=1, source_target_pairs={{0,24},{8,0},{16,8},{24,16},{1,25},{9,1},{17,9},{25,17},{2,26},{10... | collective-permute-start | bytes 1769480 | tf_op jit(solution)/shard_map/ppermute | solution.py:223
  127.5 46.3 %all-to-all-start.3 = ((bf16[16,32,2048]{2,1,0:T(8,128)(2,1)}), bf16[16,32,2048]{2,1,0:T(8,128)(2,1)S(1)}, u32[]{:S(2)}, u32[]{:S(2)}) async-start(bf16[16,32,2048]{2,1,0:T(8,128)(2,1)} %copy-done.1), calls=%async_computation.3 | async-start | bytes 4194304 | tf_op jit(solution)/shard_map/all_to_all | solution.py:466
  135.9 29.1 %collective-permute-start.12 = (bf16[2,576,128]{2,1,0:T(8,128)(2,1)S(1)}, bf16[2,576,128]{2,1,0:T(8,128)(2,1)S(1)}, u32[]{:S(2)}, u32[]{:S(2)}) collective-permute-start(bf16[2,576,128]{2,1,0:T(8,128)(2,1)S(1)} %slice.62), channel_id=1, source_target_pairs={{0,8},{8,16},{16,24},{24,0},{1,9},{9,17},{17,25},{25,1},{2,10},{10... | collective-permute-start | bytes 884744 | tf_op jit(solution)/shard_map/ppermute | solution.py:223
  138.4 27.2 %collective-permute-start.13 = (bf16[2,576,128]{2,1,0:T(8,128)(2,1)S(1)}, bf16[2,576,128]{2,1,0:T(8,128)(2,1)S(1)}, u32[]{:S(2)}, u32[]{:S(2)}) collective-permute-start(bf16[2,576,128]{2,1,0:T(8,128)(2,1)S(1)} %slice.63), channel_id=1, source_target_pairs={{0,24},{8,0},{16,8},{24,16},{1,25},{9,1},{17,9},{25,17},{2,26},{10... | collective-permute-start | bytes 884744 | tf_op jit(solution)/shard_map/ppermute | solution.py:223
  139.1 38.2 %collective-permute-start.17 = (bf16[16,32,512]{2,1,0:T(8,128)(2,1)}, bf16[16,32,512]{2,1,0:T(8,128)(2,1)}, u32[]{:S(2)}, u32[]{:S(2)}) collective-permute-start(bf16[16,32,512]{2,1,0:T(8,128)(2,1)} %copy-done.30), channel_id=1, source_target_pairs={{0,3},{1,2},{2,1},{3,0},{4,7},{5,6},{6,5},{7,4},{8,11},{9,10},{10,... | collective-permute-start | bytes 1572872 | tf_op jit(solution)/shard_map/ppermute | solution.py:471
  146.1 43.8 %collective-permute-start.16 = (bf16[16,32,512]{2,1,0:T(8,128)(2,1)}, bf16[16,32,512]{2,1,0:T(8,128)(2,1)}, u32[]{:S(2)}, u32[]{:S(2)}) collective-permute-start(bf16[16,32,512]{2,1,0:T(8,128)(2,1)} %copy-done.29), channel_id=1, source_target_pairs={{0,2},{1,3},{2,0},{3,1},{4,6},{5,7},{6,4},{7,5},{8,10},{9,11},{10,... | collective-permute-start | bytes 1572872 | tf_op jit(solution)/shard_map/ppermute | solution.py:471
  151.4 38.5 %collective-permute-start.15 = (bf16[16,32,512]{2,1,0:T(8,128)(2,1)}, bf16[16,32,512]{2,1,0:T(8,128)(2,1)}, u32[]{:S(2)}, u32[]{:S(2)}) collective-permute-start(bf16[16,32,512]{2,1,0:T(8,128)(2,1)} %copy-done.28), channel_id=1, source_target_pairs={{0,1},{1,0},{2,3},{3,2},{4,5},{5,4},{6,7},{7,6},{8,9},{9,8},{10,11... | collective-permute-start | bytes 1572872 | tf_op jit(solution)/shard_map/ppermute | solution.py:471
  177.1 15.3 %collective-permute-start.14 = (bf16[4,128,512]{2,1,0:T(8,128)(2,1)S(1)}, bf16[4,128,512]{2,1,0:T(8,128)(2,1)S(1)}, u32[]{:S(2)}, u32[]{:S(2)}) collective-permute-start(bf16[4,128,512]{2,1,0:T(8,128)(2,1)S(1)} %get-tuple-element.177), channel_id=1, source_target_pairs={{0,4},{4,0},{1,5},{5,1},{2,6},{6,2},{3,7},{7,3},{8,12},{12,8},{9,1... | collective-permute-start | bytes 1572872 | tf_op jit(solution)/shard_map/ppermute | solution.py:510
  193.3 11.9 %collective-permute-start.20 = (bf16[192,512]{1,0:T(8,128)(2,1)S(1)}, bf16[192,512]{1,0:T(8,128)(2,1)S(1)}, u32[]{:S(2)}, u32[]{:S(2)}) collective-permute-start(bf16[192,512]{1,0:T(8,128)(2,1)S(1)} %pad_maximum_fusion.3), channel_id=1, source_target_pairs={{0,3},{1,2},{2,1},{3,0},{4,7},{5,6},{6,5},{7,4},{8,11},{9,10},{10,... | collective-permute-start | bytes 589832 | tf_op jit(solution)/shard_map/ppermute | solution.py:471
  196.9 16.0 %collective-permute-start.19 = (bf16[192,512]{1,0:T(8,128)(2,1)S(1)}, bf16[192,512]{1,0:T(8,128)(2,1)S(1)}, u32[]{:S(2)}, u32[]{:S(2)}) collective-permute-start(bf16[192,512]{1,0:T(8,128)(2,1)S(1)} %pad_maximum_fusion.2), channel_id=1, source_target_pairs={{0,2},{1,3},{2,0},{3,1},{4,6},{5,7},{6,4},{7,5},{8,10},{9,11},{10,... | collective-permute-start | bytes 589832 | tf_op jit(solution)/shard_map/ppermute | solution.py:471
  197.1 15.9 %collective-permute-start.18 = (bf16[192,512]{1,0:T(8,128)(2,1)S(1)}, bf16[192,512]{1,0:T(8,128)(2,1)S(1)}, u32[]{:S(2)}, u32[]{:S(2)}) collective-permute-start(bf16[192,512]{1,0:T(8,128)(2,1)S(1)} %pad_maximum_fusion.1), channel_id=1, source_target_pairs={{0,1},{1,0},{2,3},{3,2},{4,5},{5,4},{6,7},{7,6},{8,9},{9,8},{10,11... | collective-permute-start | bytes 589832 | tf_op jit(solution)/shard_map/ppermute | solution.py:471
  198.0 16.8 %all-to-all-start.4 = ((bf16[16,32,512]{2,1,0:T(8,128)(2,1)}), bf16[16,32,512]{2,1,0:T(8,128)(2,1)S(1)}, u32[]{:S(2)}, u32[]{:S(2)}) async-start(bf16[16,32,512]{2,1,0:T(8,128)(2,1)} %add_convert_fusion), calls=%async_computation.4 | async-start | bytes 1048576 | tf_op jit(solution)/shard_map/all_to_all | solution.py:466
  216.7 13.7 %collective-permute-start.22 = (bf16[128,512]{1,0:T(8,128)(2,1)S(1)}, bf16[128,512]{1,0:T(8,128)(2,1)S(1)}, u32[]{:S(2)}, u32[]{:S(2)}) collective-permute-start(bf16[128,512]{1,0:T(8,128)(2,1)S(1)} %add_convert_fusion.2), channel_id=1, source_target_pairs={{0,32},{32,0},{1,33},{33,1},{2,34},{34,2},{3,35},{35,3},{4,36},{36... | collective-permute-start | bytes 393224 | tf_op jit(solution)/shard_map/ppermute | solution.py:523
  (40 other events, 344.0 us)

commit v12 on v11

--- a/solution.py
+++ b/solution.py
@@ -504,7 +504,9 @@
     near = exchange(near)
     half = hot_w[0].shape[0] // 2
     hot_w += (shift_x(hot_w[1][:half], 1), shift_x(hot_w[2][half:], -1))
-    far = total_of((far[0], *to_t(far, 1, 2, 3)))
+    summands = (far[0], *to_t(far, 2))
+    hot_w, summands = lax.optimization_barrier((hot_w, summands))
+    far = total_of(summands + to_t(far, 3, 1))
     near_hot, far_hot = hot_ffn(info, (own_z, own_zc, own, own_c), hot_w, tok_dev // SPANS)
     mine, other = mix_rows(info, near_mix, near_hot_mix, near.reshape(n_slot, width), near_hot)
     got = lax.ppermute(other, "c", SWAP)

time: 234 us -> 234 us (level)
  starting transfers between devices: 89.4 us -> 86.2 us
  waiting for transfers between devices: 88.6 us -> 91.1 us
    ppermute x4, waiting for transfers between devices: 14.2 us -> 0.01 us  [shift_x(): return lax.ppermute(array, 'x', [(i, (i + step) % n_x) for i in range(n_x)])]
    ppermute x6, waiting for transfers between devices: 20.5 us -> 34.5 us  [to_t(): lax.ppermute(groups[k], 't', [(i, i ^ k) for i in pairs])]
    ppermute x1, starting transfers between devices: 9.77 us -> 5.6 us  [per_device(): got = lax.ppermute(mine.astype(jnp.bfloat16), 'zh', SWAP)]
    all_to_all x3, waiting for transfers between devices: 5.42 us -> 7.87 us  [exchange(): return lax.all_to_all(send, ('y', 'x'), 0, 0, tiled=True)]
    unnamed x77 -> x81, local copies, waits for them, and re-layouts: 15.9 us -> 16.6 us
  transfers between devices with their start and end apart: 26 -> 26, of which waited for: 13 -> 11; matrix products, arithmetic and copies ran while one was open for 2% -> 2% of each run, Pallas kernels for 11% -> 11%
where the time goes in v12:
time: 234 us; the launch traced here: 231 us
  waiting for transfers between devices  91.1 us (39%)
  starting transfers between devices  86.2 us (37%)
  Pallas kernels  28.8 us (12%)
  local copies, waits for them, and re-layouts  19.4 us (8%)
  other arithmetic  4.28 us (2%)
    ppermute x6, waiting for transfers between devices, to_t(): lax.ppermute(groups[k], 't', [(i, i ^ k) for i in pairs])  34.5 us
    ppermute x3, waiting for transfers between devices, along_y(): column.append(lax.ppermute(chunk, 'y', [(i, i ^ k) for i in range(n_y)]))  31.8 us
    all_to_all x3, starting transfers between devices, exchange(): return lax.all_to_all(send, ('y', 'x'), 0, 0, tiled=True)  22.1 us
    ppermute x6, starting transfers between devices, to_t(): lax.ppermute(groups[k], 't', [(i, i ^ k) for i in pairs])  17.9 us
    unnamed x81, local copies, waits for them, and re-layouts  16.6 us
    ppermute x1, starting transfers between devices, own_span(): got = lax.ppermute(chunks[2:], 'zh', SWAP)  14.8 us
    pallas_call x2, Pallas kernels, ffn(): pl.pallas_call(ffn_kernel, out_shape=[jax.ShapeDtypeStruct((n_src, rows,...  8.69 us
    pallas_call x2, Pallas kernels, route(): pl.pallas_call(route_kernel, out_shape=shapes, grid_spec=pltpu.PrefetchSc...  8.19 us
  transfers between devices with their start and end apart: 26, of which 11 were waited for; matrix products, arithmetic and copies ran while one was open for 2% of the time, Pallas kernels for 11%

profile of v12, /device:TPU:2, one launch (start us, length us, event | category | flops | bytes accessed | tf_op | source)
XLA Modules:
  0.0 230.8 jit_solution(6872135243190750118)
XLA Ops:
  0.7 3.3 %shard_map.75 = (bf16[16,288,128]{2,1,0:T(8,128)(2,1)S(1)}, bf16[16,288,128]{2,1,0:T(8,128)(2,1)S(1)}) custom-call(s32[9]{0:T(128)S(1)} %concatenate.23.info, bf16[2,192,2048]{2,1,0:T(8,128)(2,1)} %gate_ref.5, bf16[2,192,2048]{2,1,0:T(8,128)(2,1)} %up_ref.5, bf16[2,192,2048]{2,1,0:T(8,128)(2,1)} %down_ref.5), custom_call_target="tpu_custom_call" | custom-call | bytes 4718592 | tf_op jit(solution)/shard_map/pallas_call | solution.py:89
  4.3 7.3 %collective-permute-start.2 = (bf16[136,2048]{1,0:T(8,128)(2,1)S(1)}, bf16[136,2048]{1,0:T(8,128)(2,1)S(1)}, u32[]{:S(2)}, u32[]{:S(2)}) collective-permute-start(bf16[136,2048]{1,0:T(8,128)(2,1)S(1)} %fusion.1.a_ref.refs_2_), channel_id=1, source_target_pairs={{0,32},{32,0},{1,33},{33,1},{2,34},{34,2},{3,35},{35,3},{4,36},{36... | collective-permute-start | bytes 1671176 | tf_op jit(solution)/shard_map/ppermute | solution.py:487
  13.3 7.6 %all-to-all-start.1 = ((bf16[16,288,128]{2,1,0:T(8,128)(2,1)}), bf16[16,288,128]{2,1,0:T(8,128)(2,1)S(1)}, u32[]{:S(2)}, u32[]{:S(2)}) async-start(bf16[16,288,128]{2,1,0:T(8,128)(2,1)} %shard_map.76), calls=%async_computation.1 | async-start | bytes 2359296 | tf_op jit(solution)/shard_map/all_to_all | solution.py:169
  21.0 6.2 %collective-permute-done.2.a_ref.refs_0_ = bf16[136,2048]{1,0:T(8,128)(2,1)S(1)} collective-permute-done((bf16[136,2048]{1,0:T(8,128)(2,1)S(1)}, bf16[136,2048]{1,0:T(8,128)(2,1)S(1)}, u32[]{:S(2)}, u32[]{:S(2)}) %collective-permute-start.2) | collective-permute-done | bytes 557088 | tf_op jit(solution)/shard_map/ppermute | solution.py:487
  28.5 4.1 %shard_map.73 = (bf16[16,64,2048]{2,1,0:T(8,128)(2,1)S(1)}, bf16[512,256]{1,0:T(8,128)(2,1)S(1)}, bf16[64,256]{1,0:T(8,128)(2,1)S(1)}) custom-call(s32[9]{0:T(128)S(1)} %concatenate.23.info, bf16[136,2048]{1,0:T(8,128)(2,1)S(1)} %fusion.1.a_ref.refs_2_, bf16[136,2048]{1,0:T(8,128)(2,1)S(1)} %collective-permute-done.1.b_ref.refs_3_), custom_call_target="tpu_custom_call" | custom-call | flops 536870912 | bytes 3145728 | tf_op jit(solution)/shard_map/pallas_call | solution.py:348
  33.3 4.1 %shard_map.74 = (bf16[16,64,2048]{2,1,0:T(8,128)(2,1)S(1)}, bf16[512,256]{1,0:T(8,128)(2,1)S(1)}, bf16[64,256]{1,0:T(8,128)(2,1)S(1)}) custom-call(s32[9]{0:T(128)S(1)} %concatenate.23.info, bf16[136,2048]{1,0:T(8,128)(2,1)S(1)} %collective-permute-done.2.a_ref.refs_0_, ...), custom_call_target="tpu_custom_call", output_to_operand_aliasing={{0}: (3, {})} | custom-call | flops 536870912 | bytes 3145728 | tf_op jit(solution)/shard_map/pallas_call | solution.py:348
  40.8 7.5 %all-to-all-start.2 = ((bf16[16,64,2048]{2,1,0:T(8,128)(2,1)}), bf16[16,64,2048]{2,1,0:T(8,128)(2,1)}, u32[]{:S(2)}, u32[]{:S(2)}) async-start(bf16[16,64,2048]{2,1,0:T(8,128)(2,1)} %copy-done), calls=%async_computation.2 | async-start | bytes 8388608 | tf_op jit(solution)/shard_map/all_to_all | solution.py:466
  48.4 14.8 %collective-permute-start.5 = (bf16[2,288,128]{2,1,0:T(8,128)(2,1)S(1)}, bf16[2,288,128]{2,1,0:T(8,128)(2,1)S(1)}, u32[]{:S(2)}, u32[]{:S(2)}) collective-permute-start(bf16[2,288,128]{2,1,0:T(8,128)(2,1)S(1)} %slice.61), channel_id=1, source_target_pairs={{0,32},{32,0},{1,33},{33,1},{2,34},{34,2},{3,35},{35,3},{4,36},{36... | collective-permute-start | bytes 442376 | tf_op jit(solution)/shard_map/ppermute | solution.py:206
  63.2 4.0 %collective-permute-done.5.got_ref = bf16[2,288,128]{2,1,0:T(8,128)(2,1)S(1)} collective-permute-done((bf16[2,288,128]{2,1,0:T(8,128)(2,1)S(1)}, bf16[2,288,128]{2,1,0:T(8,128)(2,1)S(1)}, u32[]{:S(2)}, u32[]{:S(2)}) %collective-permute-start.5) | collective-permute-done | bytes 147488 | tf_op jit(solution)/shard_map/ppermute | solution.py:206
  69.2 2.8 %collective-permute-start.9 = (bf16[576,128]{1,0:T(8,128)(2,1)S(1)}, bf16[576,128]{1,0:T(8,128)(2,1)S(1)}, u32[]{:S(2)}, u32[]{:S(2)}) collective-permute-start(bf16[576,128]{1,0:T(8,128)(2,1)S(1)} %get-tuple-element.231), channel_id=1, source_target_pairs={{0,192},{64,128},{128,64},{192,0},{1,193},{65,129},{129,65},{193,1... | collective-permute-start | bytes 442376 | tf_op jit(solution)/shard_map/ppermute | solution.py:217
  73.4 30.8 %collective-permute-done.9 = bf16[576,128]{1,0:T(8,128)(2,1)S(1)} collective-permute-done((bf16[576,128]{1,0:T(8,128)(2,1)S(1)}, bf16[576,128]{1,0:T(8,128)(2,1)S(1)}, u32[]{:S(2)}, u32[]{:S(2)}) %collective-permute-start.9) | collective-permute-done | bytes 147488 | tf_op jit(solution)/shard_map/ppermute | solution.py:217
  105.3 3.7 %all-to-all-done.2.x_ref = bf16[16,64,2048]{2,1,0:T(8,128)(2,1)} async-done(((bf16[16,64,2048]{2,1,0:T(8,128)(2,1)}), bf16[16,64,2048]{2,1,0:T(8,128)(2,1)}, u32[]{:S(2)}, u32[]{:S(2)}) %all-to-all-start.2) | async-done | bytes 4194336 | tf_op jit(solution)/shard_map/all_to_all | solution.py:466
  109.7 3.5 %collective-permute-start.11 = (bf16[4,576,128]{2,1,0:T(8,128)(2,1)S(1)}, bf16[4,576,128]{2,1,0:T(8,128)(2,1)}, u32[]{:S(2)}, u32[]{:S(2)}) collective-permute-start(bf16[4,576,128]{2,1,0:T(8,128)(2,1)S(1)} %pad_maximum_fusion.refs_4_), channel_id=1, source_target_pairs={{0,24},{8,0},{16,8},{24,16},{1,25},{9,1},{17,9},{25,17},{2,26},{10... | collective-permute-start | bytes 1769480 | tf_op jit(solution)/shard_map/ppermute | solution.py:223
  113.3 4.6 %shard_map.79 = (bf16[16,32,512]{2,1,0:T(8,128)(2,1)S(1)}, bf16[16,32,512]{2,1,0:T(8,128)(2,1)S(1)}, bf16[16,32,512]{2,1,0:T(8,128)(2,1)S(1)}, bf16[16,32,512]{2,1,0:T(8,128)(2,1)S(1)}) custom-call(s32[9]{0:T(128)S(1)} %get-tuple-element.360, bf16[16,64,2048]{2,1,0:T(8,128)(2,1)} %all-to-all-done.2.x_ref, bf16[2,192,2048]{2,1,0:T(8,128)(2,1)S(1)} %copy-done.31, ...), custom_call_target="tpu_custom_call" | custom-call | flops 1207959552 | bytes 8912896 | tf_op jit(solution)/shard_map/pallas_call | solution.py:392
  121.1 4.1 %shard_map.80 = bf16[16,32,2048]{2,1,0:T(8,128)(2,1)S(1)} custom-call(s32[9]{0:T(128)S(1)} %get-tuple-element.360, bf16[16,64,2048]{2,1,0:T(8,128)(2,1)} %all-to-all-done.2.x_ref, bf16[2,192,2048]{2,1,0:T(8,128)(2,1)S(1)} %copy-done.31, bf16[2,192,2048]{2,1,0:T(8,128)(2,1)S(1)} %copy-done.32, bf16[2,192,2048]{2,1,0:T(8,128)(2,1)S(1)} %copy-done.33), custom_call_target="tpu_custom_call" | custom-call | flops 1207959552 | bytes 8912896 | tf_op jit(solution)/shard_map/pallas_call | solution.py:392
  127.4 7.4 %all-to-all-start.3 = ((bf16[16,32,2048]{2,1,0:T(8,128)(2,1)}), bf16[16,32,2048]{2,1,0:T(8,128)(2,1)S(1)}, u32[]{:S(2)}, u32[]{:S(2)}) async-start(bf16[16,32,2048]{2,1,0:T(8,128)(2,1)} %copy-done.1), calls=%async_computation.3 | async-start | bytes 4194304 | tf_op jit(solution)/shard_map/all_to_all | solution.py:466
  134.8 11.7 %collective-permute-start.14 = (bf16[16,32,512]{2,1,0:T(8,128)(2,1)}, bf16[16,32,512]{2,1,0:T(8,128)(2,1)S(1)}, u32[]{:S(2)}, u32[]{:S(2)}) collective-permute-start(bf16[16,32,512]{2,1,0:T(8,128)(2,1)} %copy-done.30), channel_id=1, source_target_pairs={{0,2},{1,3},{2,0},{3,1},{4,6},{5,7},{6,4},{7,5},{8,10},{9,11},{10,... | collective-permute-start | bytes 1572872 | tf_op jit(solution)/shard_map/ppermute | solution.py:471
  152.2 28.8 %collective-permute-done.14 = bf16[16,32,512]{2,1,0:T(8,128)(2,1)S(1)} collective-permute-done((bf16[16,32,512]{2,1,0:T(8,128)(2,1)}, bf16[16,32,512]{2,1,0:T(8,128)(2,1)S(1)}, u32[]{:S(2)}, u32[]{:S(2)}) %collective-permute-start.14) | collective-permute-done | bytes 524320 | tf_op jit(solution)/shard_map/ppermute | solution.py:471
  184.0 2.8 %shard_map.81 = (bf16[64,512]{1,0:T(8,128)(2,1)S(1)}, bf16[64,512]{1,0:T(8,128)(2,1)S(1)}, bf16[64,512]{1,0:T(8,128)(2,1)S(1)}, bf16[64,512]{1,0:T(8,128)(2,1)S(1)}, bf16[64,2048]{1,0:T(8,128)(2,1)S(1)}) custom-call(s32[9]{0:T(128)S(1)} %get-tuple-element.360, bf16[136,2048]{1,0:T(8,128)(2,1)S(1)} %copy-done.3, bf16[136,2048]{1,0:T(8,128)(2,1)S(1)} %copy-done.5, ...), custom_call_target="tpu_custom_call" | custom-call | flops 301989888 | bytes 3407872 | tf_op jit(solution)/shard_map/pallas_call | solution.py:263
  201.4 7.2 %all-to-all-start.4 = ((bf16[16,32,512]{2,1,0:T(8,128)(2,1)}), bf16[16,32,512]{2,1,0:T(8,128)(2,1)S(1)}, u32[]{:S(2)}, u32[]{:S(2)}) async-start(bf16[16,32,512]{2,1,0:T(8,128)(2,1)} %add_convert_fusion), calls=%async_computation.4 | async-start | bytes 1048576 | tf_op jit(solution)/shard_map/all_to_all | solution.py:466
  208.7 5.7 %collective-permute-done.19 = bf16[192,512]{1,0:T(8,128)(2,1)S(1)} collective-permute-done((bf16[192,512]{1,0:T(8,128)(2,1)S(1)}, bf16[192,512]{1,0:T(8,128)(2,1)S(1)}, u32[]{:S(2)}, u32[]{:S(2)}) %collective-permute-start.19) | collective-permute-done | bytes 196640 | tf_op jit(solution)/shard_map/ppermute | solution.py:471
  214.5 4.1 %all-to-all-done.4 = bf16[16,32,512]{2,1,0:T(8,128)(2,1)S(1)} async-done(((bf16[16,32,512]{2,1,0:T(8,128)(2,1)}), bf16[16,32,512]{2,1,0:T(8,128)(2,1)S(1)}, u32[]{:S(2)}, u32[]{:S(2)}) %all-to-all-start.4) | async-done | bytes 524320 | tf_op jit(solution)/shard_map/all_to_all | solution.py:466
  220.5 5.6 %collective-permute-start.22 = (bf16[128,512]{1,0:T(8,128)(2,1)S(1)}, bf16[128,512]{1,0:T(8,128)(2,1)S(1)}, u32[]{:S(2)}, u32[]{:S(2)}) collective-permute-start(bf16[128,512]{1,0:T(8,128)(2,1)S(1)} %add_convert_fusion.2), channel_id=1, source_target_pairs={{0,32},{32,0},{1,33},{33,1},{2,34},{34,2},{3,35},{35,3},{4,36},{36... | collective-permute-start | bytes 393224 | tf_op jit(solution)/shard_map/ppermute | solution.py:525
  226.1 4.0 %collective-permute-done.22 = bf16[128,512]{1,0:T(8,128)(2,1)S(1)} collective-permute-done((bf16[128,512]{1,0:T(8,128)(2,1)S(1)}, bf16[128,512]{1,0:T(8,128)(2,1)S(1)}, u32[]{:S(2)}, u32[]{:S(2)}) %collective-permute-start.22) | collective-permute-done | bytes 131104 | tf_op jit(solution)/shard_map/ppermute | solution.py:525
  (144 shorter events, 44.0 us)
Async XLA Ops:
  4.1 7.5 %collective-permute-start.4 = (bf16[16,288,128]{2,1,0:T(8,128)(2,1)S(1)}, bf16[16,288,128]{2,1,0:T(8,128)(2,1)S(1)}, u32[]{:S(2)}, u32[]{:S(2)}) collective-permute-start(bf16[16,288,128]{2,1,0:T(8,128)(2,1)S(1)} %get-tuple-element.165), channel_id=1, source_target_pairs={{0,4},{4,0},{1,5},{5,1},{2,6},{6,2},{3,7},{7,3},{8,12},{12,8},{9,1... | collective-permute-start | bytes 3538952 | tf_op jit(solution)/shard_map/ppermute | solution.py:168
  4.3 22.8 %collective-permute-start.2 = (bf16[136,2048]{1,0:T(8,128)(2,1)S(1)}, bf16[136,2048]{1,0:T(8,128)(2,1)S(1)}, u32[]{:S(2)}, u32[]{:S(2)}) collective-permute-start(bf16[136,2048]{1,0:T(8,128)(2,1)S(1)} %fusion.1.a_ref.refs_2_), channel_id=1, source_target_pairs={{0,32},{32,0},{1,33},{33,1},{2,34},{34,2},{3,35},{35,3},{4,36},{36... | collective-permute-start | bytes 1671176 | tf_op jit(solution)/shard_map/ppermute | solution.py:487
  13.3 26.8 %all-to-all-start.1 = ((bf16[16,288,128]{2,1,0:T(8,128)(2,1)}), bf16[16,288,128]{2,1,0:T(8,128)(2,1)S(1)}, u32[]{:S(2)}, u32[]{:S(2)}) async-start(bf16[16,288,128]{2,1,0:T(8,128)(2,1)} %shard_map.76), calls=%async_computation.1 | async-start | bytes 2359296 | tf_op jit(solution)/shard_map/all_to_all | solution.py:169
  20.9 7.5 %collective-permute-start.1 = (bf16[136,2048]{1,0:T(8,128)(2,1)S(1)}, bf16[136,2048]{1,0:T(8,128)(2,1)S(1)}, u32[]{:S(2)}, u32[]{:S(2)}) collective-permute-start(bf16[136,2048]{1,0:T(8,128)(2,1)S(1)} %fusion.1.a_ref.refs_2_), channel_id=1, source_target_pairs={{0,4},{4,0},{1,5},{5,1},{2,6},{6,2},{3,7},{7,3},{8,12},{12,8},{9,1... | collective-permute-start | bytes 1671176 | tf_op jit(solution)/shard_map/ppermute | solution.py:488
  27.1 6.2 %collective-permute-start.3 = (bf16[136,2048]{1,0:T(8,128)(2,1)S(1)}, bf16[136,2048]{1,0:T(8,128)(2,1)S(1)}, u32[]{:S(2)}, u32[]{:S(2)}) collective-permute-start(bf16[136,2048]{1,0:T(8,128)(2,1)S(1)} %collective-permute-done.2.a_ref.refs_0_), channel_id=1, source_target_pairs={{0,4},{4,0},{1,5},{5,1},{2,6},{6,2},{3,7},{7,3},{8,12},{12,8},{9,1... | collective-permute-start | bytes 1671176 | tf_op jit(solution)/shard_map/ppermute | solution.py:493
  40.8 68.2 %all-to-all-start.2 = ((bf16[16,64,2048]{2,1,0:T(8,128)(2,1)}), bf16[16,64,2048]{2,1,0:T(8,128)(2,1)}, u32[]{:S(2)}, u32[]{:S(2)}) async-start(bf16[16,64,2048]{2,1,0:T(8,128)(2,1)} %copy-done), calls=%async_computation.2 | async-start | bytes 8388608 | tf_op jit(solution)/shard_map/all_to_all | solution.py:466
  48.4 18.9 %collective-permute-start.5 = (bf16[2,288,128]{2,1,0:T(8,128)(2,1)S(1)}, bf16[2,288,128]{2,1,0:T(8,128)(2,1)S(1)}, u32[]{:S(2)}, u32[]{:S(2)}) collective-permute-start(bf16[2,288,128]{2,1,0:T(8,128)(2,1)S(1)} %slice.61), channel_id=1, source_target_pairs={{0,32},{32,0},{1,33},{33,1},{2,34},{34,2},{3,35},{35,3},{4,36},{36... | collective-permute-start | bytes 442376 | tf_op jit(solution)/shard_map/ppermute | solution.py:206
  69.2 35.0 %collective-permute-start.9 = (bf16[576,128]{1,0:T(8,128)(2,1)S(1)}, bf16[576,128]{1,0:T(8,128)(2,1)S(1)}, u32[]{:S(2)}, u32[]{:S(2)}) collective-permute-start(bf16[576,128]{1,0:T(8,128)(2,1)S(1)} %get-tuple-element.231), channel_id=1, source_target_pairs={{0,192},{64,128},{128,64},{192,0},{1,193},{65,129},{129,65},{193,1... | collective-permute-start | bytes 442376 | tf_op jit(solution)/shard_map/ppermute | solution.py:217
  72.0 32.2 %collective-permute-start.8 = (bf16[576,128]{1,0:T(8,128)(2,1)S(1)}, bf16[576,128]{1,0:T(8,128)(2,1)S(1)}, u32[]{:S(2)}, u32[]{:S(2)}) collective-permute-start(bf16[576,128]{1,0:T(8,128)(2,1)S(1)} %get-tuple-element.231), channel_id=1, source_target_pairs={{0,128},{64,192},{128,0},{192,64},{1,129},{65,193},{129,1},{193,65... | collective-permute-start | bytes 442376 | tf_op jit(solution)/shard_map/ppermute | solution.py:217
  72.8 32.4 %collective-permute-start.7 = (bf16[576,128]{1,0:T(8,128)(2,1)S(1)}, bf16[576,128]{1,0:T(8,128)(2,1)S(1)}, u32[]{:S(2)}, u32[]{:S(2)}) collective-permute-start(bf16[576,128]{1,0:T(8,128)(2,1)S(1)} %get-tuple-element.231), channel_id=1, source_target_pairs={{0,64},{64,0},{128,192},{192,128},{1,65},{65,1},{129,193},{193,129... | collective-permute-start | bytes 442376 | tf_op jit(solution)/shard_map/ppermute | solution.py:217
  109.1 17.5 %collective-permute-start.10 = (bf16[4,576,128]{2,1,0:T(8,128)(2,1)S(1)}, bf16[4,576,128]{2,1,0:T(8,128)(2,1)S(1)}, u32[]{:S(2)}, u32[]{:S(2)}) collective-permute-start(bf16[4,576,128]{2,1,0:T(8,128)(2,1)S(1)} %pad_maximum_fusion.refs_4_), channel_id=1, source_target_pairs={{0,8},{8,16},{16,24},{24,0},{1,9},{9,17},{17,25},{25,1},{2,10},{10... | collective-permute-start | bytes 1769480 | tf_op jit(solution)/shard_map/ppermute | solution.py:223
  109.7 17.6 %collective-permute-start.11 = (bf16[4,576,128]{2,1,0:T(8,128)(2,1)S(1)}, bf16[4,576,128]{2,1,0:T(8,128)(2,1)}, u32[]{:S(2)}, u32[]{:S(2)}) collective-permute-start(bf16[4,576,128]{2,1,0:T(8,128)(2,1)S(1)} %pad_maximum_fusion.refs_4_), channel_id=1, source_target_pairs={{0,24},{8,0},{16,8},{24,16},{1,25},{9,1},{17,9},{25,17},{2,26},{10... | collective-permute-start | bytes 1769480 | tf_op jit(solution)/shard_map/ppermute | solution.py:223
  127.4 62.7 %all-to-all-start.3 = ((bf16[16,32,2048]{2,1,0:T(8,128)(2,1)}), bf16[16,32,2048]{2,1,0:T(8,128)(2,1)S(1)}, u32[]{:S(2)}, u32[]{:S(2)}) async-start(bf16[16,32,2048]{2,1,0:T(8,128)(2,1)} %copy-done.1), calls=%async_computation.3 | async-start | bytes 4194304 | tf_op jit(solution)/shard_map/all_to_all | solution.py:466
  134.8 46.3 %collective-permute-start.14 = (bf16[16,32,512]{2,1,0:T(8,128)(2,1)}, bf16[16,32,512]{2,1,0:T(8,128)(2,1)S(1)}, u32[]{:S(2)}, u32[]{:S(2)}) collective-permute-start(bf16[16,32,512]{2,1,0:T(8,128)(2,1)} %copy-done.30), channel_id=1, source_target_pairs={{0,2},{1,3},{2,0},{3,1},{4,6},{5,7},{6,4},{7,5},{8,10},{9,11},{10,... | collective-permute-start | bytes 1572872 | tf_op jit(solution)/shard_map/ppermute | solution.py:471
  147.5 33.6 %collective-permute-start.12 = (bf16[2,576,128]{2,1,0:T(8,128)(2,1)S(1)}, bf16[2,576,128]{2,1,0:T(8,128)(2,1)S(1)}, u32[]{:S(2)}, u32[]{:S(2)}) collective-permute-start(bf16[2,576,128]{2,1,0:T(8,128)(2,1)S(1)} %slice.62), channel_id=1, source_target_pairs={{0,8},{8,16},{16,24},{24,0},{1,9},{9,17},{17,25},{25,1},{2,10},{10... | collective-permute-start | bytes 884744 | tf_op jit(solution)/shard_map/ppermute | solution.py:223
  150.0 31.9 %collective-permute-start.13 = (bf16[2,576,128]{2,1,0:T(8,128)(2,1)S(1)}, bf16[2,576,128]{2,1,0:T(8,128)(2,1)S(1)}, u32[]{:S(2)}, u32[]{:S(2)}) collective-permute-start(bf16[2,576,128]{2,1,0:T(8,128)(2,1)S(1)} %slice.63), channel_id=1, source_target_pairs={{0,24},{8,0},{16,8},{24,16},{1,25},{9,1},{17,9},{25,17},{2,26},{10... | collective-permute-start | bytes 884744 | tf_op jit(solution)/shard_map/ppermute | solution.py:223
  150.6 42.9 %collective-permute-start.17 = (bf16[16,32,512]{2,1,0:T(8,128)(2,1)}, bf16[16,32,512]{2,1,0:T(8,128)(2,1)}, u32[]{:S(2)}, u32[]{:S(2)}) collective-permute-start(bf16[16,32,512]{2,1,0:T(8,128)(2,1)} %copy-done.29), channel_id=1, source_target_pairs={{0,1},{1,0},{2,3},{3,2},{4,5},{5,4},{6,7},{7,6},{8,9},{9,8},{10,11... | collective-permute-start | bytes 1572872 | tf_op jit(solution)/shard_map/ppermute | solution.py:471
  150.6 42.9 %collective-permute-start.16 = (bf16[16,32,512]{2,1,0:T(8,128)(2,1)}, bf16[16,32,512]{2,1,0:T(8,128)(2,1)}, u32[]{:S(2)}, u32[]{:S(2)}) collective-permute-start(bf16[16,32,512]{2,1,0:T(8,128)(2,1)} %copy-done.28), channel_id=1, source_target_pairs={{0,3},{1,2},{2,1},{3,0},{4,7},{5,6},{6,5},{7,4},{8,11},{9,10},{10,... | collective-permute-start | bytes 1572872 | tf_op jit(solution)/shard_map/ppermute | solution.py:471
  193.4 2.5 %collective-permute-start.15 = (bf16[4,128,512]{2,1,0:T(8,128)(2,1)S(1)}, bf16[4,128,512]{2,1,0:T(8,128)(2,1)S(1)}, u32[]{:S(2)}, u32[]{:S(2)}) collective-permute-start(bf16[4,128,512]{2,1,0:T(8,128)(2,1)S(1)} %get-tuple-element.191), channel_id=1, source_target_pairs={{0,4},{4,0},{1,5},{5,1},{2,6},{6,2},{3,7},{7,3},{8,12},{12,8},{9,1... | collective-permute-start | bytes 1572872 | tf_op jit(solution)/shard_map/ppermute | solution.py:512
  196.7 11.9 %collective-permute-start.20 = (bf16[192,512]{1,0:T(8,128)(2,1)S(1)}, bf16[192,512]{1,0:T(8,128)(2,1)S(1)}, u32[]{:S(2)}, u32[]{:S(2)}) collective-permute-start(bf16[192,512]{1,0:T(8,128)(2,1)S(1)} %pad_maximum_fusion.3), channel_id=1, source_target_pairs={{0,3},{1,2},{2,1},{3,0},{4,7},{5,6},{6,5},{7,4},{8,11},{9,10},{10,... | collective-permute-start | bytes 589832 | tf_op jit(solution)/shard_map/ppermute | solution.py:471
  199.0 15.4 %collective-permute-start.19 = (bf16[192,512]{1,0:T(8,128)(2,1)S(1)}, bf16[192,512]{1,0:T(8,128)(2,1)S(1)}, u32[]{:S(2)}, u32[]{:S(2)}) collective-permute-start(bf16[192,512]{1,0:T(8,128)(2,1)S(1)} %pad_maximum_fusion.2), channel_id=1, source_target_pairs={{0,2},{1,3},{2,0},{3,1},{4,6},{5,7},{6,4},{7,5},{8,10},{9,11},{10,... | collective-permute-start | bytes 589832 | tf_op jit(solution)/shard_map/ppermute | solution.py:471
  199.2 15.2 %collective-permute-start.18 = (bf16[192,512]{1,0:T(8,128)(2,1)S(1)}, bf16[192,512]{1,0:T(8,128)(2,1)S(1)}, u32[]{:S(2)}, u32[]{:S(2)}) collective-permute-start(bf16[192,512]{1,0:T(8,128)(2,1)S(1)} %pad_maximum_fusion.1), channel_id=1, source_target_pairs={{0,1},{1,0},{2,3},{3,2},{4,5},{5,4},{6,7},{7,6},{8,9},{9,8},{10,11... | collective-permute-start | bytes 589832 | tf_op jit(solution)/shard_map/ppermute | solution.py:471
  201.4 17.2 %all-to-all-start.4 = ((bf16[16,32,512]{2,1,0:T(8,128)(2,1)}), bf16[16,32,512]{2,1,0:T(8,128)(2,1)S(1)}, u32[]{:S(2)}, u32[]{:S(2)}) async-start(bf16[16,32,512]{2,1,0:T(8,128)(2,1)} %add_convert_fusion), calls=%async_computation.4 | async-start | bytes 1048576 | tf_op jit(solution)/shard_map/all_to_all | solution.py:466
  220.5 9.6 %collective-permute-start.22 = (bf16[128,512]{1,0:T(8,128)(2,1)S(1)}, bf16[128,512]{1,0:T(8,128)(2,1)S(1)}, u32[]{:S(2)}, u32[]{:S(2)}) collective-permute-start(bf16[128,512]{1,0:T(8,128)(2,1)S(1)} %add_convert_fusion.2), channel_id=1, source_target_pairs={{0,32},{32,0},{1,33},{33,1},{2,34},{34,2},{3,35},{35,3},{4,36},{36... | collective-permute-start | bytes 393224 | tf_op jit(solution)/shard_map/ppermute | solution.py:525
  (42 other events, 382.3 us)
